TPU v7x, 128 devices: a whole 4x4x4 slice. The times are simulated.
128 devices in a mesh: head: 8 (over y_lo, z), key: 16 (over x, y_hi, core).
Axes of the slice: x: 4, y: 4 (y_hi: 2, y_lo: 2; y = y_hi * 2 + y_lo), z: 4, core: 2. Of those that a mesh axis runs over, the one named last changes fastest.
Arguments:
- q_latent: bfloat16 [128, 512, 576], P('head'), may hold values from -48 to 48
- k_latent: bfloat16 [16384, 576], P('key'), may hold values from -6 to 6
- q_index: bfloat16 [512, 8192], P('head'), may hold values from -8 to 8
- k_index: bfloat16 [16384, 128], P('key'), may hold values from -6 to 6
- head_weight: float32 [512, 64], P('head'), may hold values from -4 to 4, as said below
- loss_weight: float32 [512], P('head'), may hold values from 4096 to 32768
- query_pos: int32 [512], replicated, may hold values from 0 to 16383, as said below
- key_start: int32 [512], replicated, may hold values from 0 to 16383, as said below
Outputs:
- grad_query: float32 [512, 8192], P('head', 'key')
- grad_key: float32 [16384, 128], P('key')
- grad_weight: float32 [512, 64], P('head', 'key')
Inputs may be any that keep to these rules, and one draw needn't show every extreme that they name: `head_weight`: indexer head weights, of either sign. Query t sees the keys key_start[t] to query_pos[t]; some query sits at position 16383 and some at 0. key_start[t] <= query_pos[t] for every query t; some query starts at 0 and some at 16383.
All inputs are finite; a program needn't handle non-finite values.
Results may differ from a plain program's by a relative error of at most 0.0028.
Values sent between devices are 32-bit elements; how exact they have to be, the bound alone decides.
No kernel may reach another device: no remote copies, remote signals or barrier semaphores. Data moves between devices by JAX's collectives and lax.ppermute only.
A program may use at most 128 MiB of HBM per device.

v0:
```python
import math

import jax
import jax.numpy as jnp
from jax import lax
from jax.sharding import PartitionSpec as P

H = 128
QK_DIM = 192


masked_low = -1e30


def sent_to_all(x, axis):
    copies = jnp.broadcast_to(x, (lax.axis_size(axis), *x.shape))
    return lax.all_to_all(copies, axis, split_axis=0, concat_axis=0, tiled=True)


def all_in_one(x, axis):
    leaves = jax.tree.leaves(x)
    order = sorted(range(len(leaves)), key=lambda k: -leaves[k].size)
    width = (1, *leaves[order[0]].shape)[-1]
    lines = [
        jnp.pad(leaves[k].reshape(-1), (0, -leaves[k].size % width)).reshape(-1, width)
        for k in order
    ]
    both, at, found = (sent_to_all(jnp.concatenate(lines), axis), 0, {})
    for k, line in zip(order, lines):
        piece = both[:, at : at + len(line)].reshape(len(both), -1)
        found[k] = piece[:, : leaves[k].size].reshape(-1, *leaves[k].shape)
        at += len(line)
    numbers = iter(range(len(leaves)))
    return jax.tree.map(lambda _: found[next(numbers)], x)


def joined_by_halves(pieces, combine):
    while len(jax.tree.leaves(pieces)[0]) > 1:
        pieces = jax.vmap(combine)(
            *(jax.tree.map(lambda part: part[side::2], pieces) for side in (0, 1))
        )
    return jax.tree.map(lambda part: part[0], pieces)


def combined_all(x, axis, combine):
    pieces = all_in_one(x, axis)
    return joined_by_halves(pieces, combine)


def in_blocks(x, dim, count):
    shape = x.shape
    pieces = x.reshape(*shape[:dim], count, shape[dim] // count, *shape[dim + 1 :])
    return jnp.moveaxis(pieces, dim, 0)


def sent_and_summed(x, axis, dim):
    count = lax.axis_size(axis)
    pieces = lax.all_to_all(in_blocks(x, dim, count), axis, 0, 0, tiled=True)
    return jnp.sum(pieces, axis=0)


def taken_together(x, axis):
    return sent_to_all(x, axis).sum(axis=0)


def local_stats(scores, seen_mask):
    masked = jnp.where(seen_mask, scores, masked_low)
    highest = jnp.max(masked, axis=-1)
    exponents = jnp.where(seen_mask, jnp.exp(scores - highest[..., None]), 0.0)
    return (highest, jnp.sum(exponents, axis=-1))


def combine_all(former, latter):
    merged = []
    for offset in range(0, len(former), 2):
        highest = jnp.maximum(former[offset], latter[offset])
        combined = former[offset + 1] * jnp.exp(former[offset] - highest) + latter[
            offset + 1
        ] * jnp.exp(latter[offset] - highest)
        merged.append(highest)
        merged.append(combined)
    return tuple(merged)


def shards(q_latent, k_latent, q_index, k_index, head_weight, loss_weight, query_pos, key_start):
    keys_here = k_latent.shape[0]
    rows_here, index_width = q_index.shape
    index_heads = head_weight.shape[1]
    index_dim = k_index.shape[1]
    score_scale = 1.0 / math.sqrt(QK_DIM)
    index_scale = 1.0 / math.sqrt(index_dim)
    positions = lax.axis_index("key") * keys_here + jnp.arange(keys_here, dtype=jnp.int32)
    visible = (positions[None, :] >= key_start[:, None]) & (
        positions[None, :] <= query_pos[:, None]
    )

    def main_scores(q_rows):
        return (
            jnp.einsum("qd,sd->qs", q_rows, k_latent, preferred_element_type=jnp.float32)
            * score_scale
        )

    main_high, main_sum = lax.map(
        lambda q_head: local_stats(main_scores(q_head), visible), q_latent
    )
    row_start = lax.axis_index("head") * rows_here
    own_pos = lax.dynamic_slice_in_dim(query_pos, row_start, rows_here)
    own_start = lax.dynamic_slice_in_dim(key_start, row_start, rows_here)
    own_visible = (positions[None, :] >= own_start[:, None]) & (
        positions[None, :] <= own_pos[:, None]
    )
    q_heads = q_index.reshape(rows_here, index_heads, index_dim)
    head_dots = jnp.einsum("qjd,sd->qjs", q_heads, k_index, preferred_element_type=jnp.float32)
    rectified = jnp.maximum(head_dots, 0.0)
    index_scores = jnp.sum(head_weight[:, :, None] * rectified, axis=1) * index_scale
    index_high, index_sum = local_stats(index_scores, own_visible)
    main_high, main_sum = combined_all((main_high, main_sum), "key", combine_all)
    index_high, index_sum = combined_all((index_high, index_sum), "key", combine_all)

    def add_head(running, entries):
        scores = main_scores(entries[0])
        probabilities = (
            jnp.where(visible, jnp.exp(scores - entries[1][:, None]), 0.0) / entries[2][:, None]
        )
        return (running + probabilities, None)

    start_value = jnp.zeros((q_latent.shape[1], keys_here), jnp.float32)
    summed, _ = lax.scan(add_head, start_value, (q_latent, main_high, main_sum))
    target = sent_and_summed(summed, "head", 0)
    target = target / H
    index_probs = (
        jnp.where(own_visible, jnp.exp(index_scores - index_high[:, None]), 0.0)
        / index_sum[:, None]
    )
    grad_scores = jnp.where(own_visible, loss_weight[:, None] * (index_probs - target), 0.0)
    head_coef = head_weight * index_scale
    head_grad = jnp.where(
        head_dots > 0.0, grad_scores[:, None, :] * head_coef[:, :, None], 0.0
    ).astype(jnp.bfloat16)
    query_part = jnp.einsum(
        "qjs,sd->qjd", head_grad, k_index, preferred_element_type=jnp.float32
    ).reshape(rows_here, index_width)
    key_part = jnp.einsum("qjs,qjd->sd", head_grad, q_heads, preferred_element_type=jnp.float32)
    weight_part = jnp.sum(grad_scores[:, None, :] * rectified, axis=2)
    grad_query, grad_weight = (
        sent_and_summed(query_part, "key", 1),
        sent_and_summed(weight_part, "key", 1),
    )
    grad_key = taken_together(key_part, "head")
    return (grad_query, grad_key, grad_weight * index_scale)


def solution(mesh):
    return jax.shard_map(
        shards,
        mesh=mesh,
        in_specs=(
            P("head", None, None),
            P("key", None),
            P("head", None),
            P("key", None),
            P("head", None),
            P("head"),
            P(),
            P(),
        ),
        out_specs=(P("head", "key"), P("key", None), P("head", "key")),
        check_vma=False,
    )
```

profile of v0, /device:TPU:1, one launch (start us, length us, event | category | flops | bytes accessed | tf_op | source)
XLA Modules:
  0.0 308.7 jit_solution(3595171685359491797)
XLA Ops:
  0.7 59.6 %while.24 = (s32[]{:T(128)}, f32[16,512]{1,0:T(8,128)S(1)}, f32[16,512]{1,0:T(8,128)S(1)}, bf16[16,512,576]{1,2,0:T(8,128)(2,1)}, bf16[1024,576]{0,1:T(8,128)(2,...) while((s32[]{:T(128)}, f32[16,512]{1,0:T(8,128)S(1)}, ...), condition=%wide.region_6.7_spmd.clone, body=%wide.region_3.6_spmd.clone.sunk | while | flops 610794496 | bytes 6011057 | solution.py:103
  0.7 2.7 select_reduce_fusion.6
  4.5 2.7 select_reduce_fusion.6
  8.2 2.7 select_reduce_fusion.6
  19.4 2.7 select_reduce_fusion.6
  23.1 2.7 select_reduce_fusion.6
  26.8 2.7 select_reduce_fusion.6
  30.5 2.7 select_reduce_fusion.6
  34.2 2.7 select_reduce_fusion.6
  38.0 2.7 select_reduce_fusion.6
  41.7 2.7 select_reduce_fusion.6
  45.4 2.7 select_reduce_fusion.6
  49.1 2.7 select_reduce_fusion.6
  52.9 2.7 select_reduce_fusion.6
  56.6 2.7 select_reduce_fusion.6
  61.4 8.6 %all-to-all-start.1 = ((f32[16,32,512]{2,1,0:T(8,128)}), f32[16,32,512]{2,1,0:T(8,128)S(1)}, u32[]{:S(2)}, u32[]{:S(2)}) async-start(f32[16,32,512]{2,1,0:T(8,128)} %broadcast_in_dim.61), calls=%async_computation.1 | async-start | bytes 2097152 | tf_op jit(solution)/shard_map/all_to_all | solution.py:17
  70.5 7.0 %multiply_reduce_fusion.1 = (f32[64,1024]{1,0:T(8,128)S(1)}, f32[64,64,1024]{2,1,0:T(8,128)}) fusion(f32[64,64]{1,0:T(8,128)S(1)} %copy-done.7, bf16[64,64,128]{2,1,0:T(8,128)(2,1)S(1)} %bitcast.68, bf16[1024,128]{1,0:T(8,128)(2,1)S(1)} %copy-done), kind=kOutput, calls=%fused_computation.17 | convolution fusion | flops 1086259200 | bytes 18366464 | tf_op jit(solution)/shard_map/qjd,sd->qjs/dot_general | solution.py:113
  78.7 8.3 %all-to-all-done.1 = f32[16,32,512]{2,1,0:T(8,128)S(1)} async-done(((f32[16,32,512]{2,1,0:T(8,128)}), f32[16,32,512]{2,1,0:T(8,128)S(1)}, u32[]{:S(2)}, u32[]{:S(2)}) %all-to-all-start.1) | async-done | bytes 1048608 | tf_op jit(solution)/shard_map/all_to_all | solution.py:17
  87.0 4.4 %all-to-all-start = ((f32[16,1,128]{2,1,0:T(1,128)}), f32[16,1,128]{2,1,0:T(1,128)S(1)}, u32[]{:S(2)}, u32[]{:S(2)}) async-start(f32[16,1,128]{2,1,0:T(1,128)} %reshape.153), calls=%async_computation | async-start | bytes 16384 | tf_op jit(solution)/shard_map/all_to_all | solution.py:17
  93.0 58.1 %while.25 = (s32[]{:T(128)}, f32[512,1024]{1,0:T(8,128)S(1)}, bf16[16,512,576]{1,2,0:T(8,128)(2,1)}, bf16[1024,576]{0,1:T(8,128)(2,1)}, f32[16,512]{1,0:T(8,128)...) while((s32[]{:T(128)}, f32[512,1024]{1,0:T(8,128)S(1)}, ...), condition=%wide.region_8.9_spmd.clone, body=%wide.region_7.8_spmd.clone.sunk | while | flops 608698368 | bytes 5984391 | solution.py:128
  93.0 3.6 %select_add_fusion.2 = f32[512,1024]{1,0:T(8,128)S(1)} fusion(f32[512,1024]{1,0:T(8,128)S(1)} %get-tuple-element.346, bf16[1024,576]{0,1:T(8,128)(2,1)} %get-tuple-element.359, s32[1024]{0:T(1024)S(1)} %get-tuple-element.364, f32[512]{0:T(512)S(1)} %bitcast.75, f32[512]{0:T(512)S(1)} %bitcast.76, s32[512]{0:T(512)S(1)} %get-tuple-element.363, ...), kind=kOutput, calls=%fused_computation.9.clone.1 | convolution fusion | flops 608698368 | bytes 5976069 | tf_op jit(solution)/shard_map/while/body/eval_jaxpr/qd,sd->qs/dot_general | solution.py:99
  96.6 3.6 %select_add_fusion.2 = f32[512,1024]{1,0:T(8,128)S(1)} fusion(f32[512,1024]{1,0:T(8,128)S(1)} %get-tuple-element.346, bf16[1024,576]{0,1:T(8,128)(2,1)} %get-tuple-element.359, s32[1024]{0:T(1024)S(1)} %get-tuple-element.364, f32[512]{0:T(512)S(1)} %bitcast.75, f32[512]{0:T(512)S(1)} %bitcast.76, s32[512]{0:T(512)S(1)} %get-tuple-element.363, ...), kind=kOutput, calls=%fused_computation.9.clone.1 | convolution fusion | flops 608698368 | bytes 5976069 | tf_op jit(solution)/shard_map/while/body/eval_jaxpr/qd,sd->qs/dot_general | solution.py:99
  100.3 3.6 %select_add_fusion.2 = f32[512,1024]{1,0:T(8,128)S(1)} fusion(f32[512,1024]{1,0:T(8,128)S(1)} %get-tuple-element.346, bf16[1024,576]{0,1:T(8,128)(2,1)} %get-tuple-element.359, s32[1024]{0:T(1024)S(1)} %get-tuple-element.364, f32[512]{0:T(512)S(1)} %bitcast.75, f32[512]{0:T(512)S(1)} %bitcast.76, s32[512]{0:T(512)S(1)} %get-tuple-element.363, ...), kind=kOutput, calls=%fused_computation.9.clone.1 | convolution fusion | flops 608698368 | bytes 5976069 | tf_op jit(solution)/shard_map/while/body/eval_jaxpr/qd,sd->qs/dot_general | solution.py:99
  103.9 3.6 %select_add_fusion.2 = f32[512,1024]{1,0:T(8,128)S(1)} fusion(f32[512,1024]{1,0:T(8,128)S(1)} %get-tuple-element.346, bf16[1024,576]{0,1:T(8,128)(2,1)} %get-tuple-element.359, s32[1024]{0:T(1024)S(1)} %get-tuple-element.364, f32[512]{0:T(512)S(1)} %bitcast.75, f32[512]{0:T(512)S(1)} %bitcast.76, s32[512]{0:T(512)S(1)} %get-tuple-element.363, ...), kind=kOutput, calls=%fused_computation.9.clone.1 | convolution fusion | flops 608698368 | bytes 5976069 | tf_op jit(solution)/shard_map/while/body/eval_jaxpr/qd,sd->qs/dot_general | solution.py:99
  107.5 3.6 %select_add_fusion.2 = f32[512,1024]{1,0:T(8,128)S(1)} fusion(f32[512,1024]{1,0:T(8,128)S(1)} %get-tuple-element.346, bf16[1024,576]{0,1:T(8,128)(2,1)} %get-tuple-element.359, s32[1024]{0:T(1024)S(1)} %get-tuple-element.364, f32[512]{0:T(512)S(1)} %bitcast.75, f32[512]{0:T(512)S(1)} %bitcast.76, s32[512]{0:T(512)S(1)} %get-tuple-element.363, ...), kind=kOutput, calls=%fused_computation.9.clone.1 | convolution fusion | flops 608698368 | bytes 5976069 | tf_op jit(solution)/shard_map/while/body/eval_jaxpr/qd,sd->qs/dot_general | solution.py:99
  111.2 3.6 %select_add_fusion.2 = f32[512,1024]{1,0:T(8,128)S(1)} fusion(f32[512,1024]{1,0:T(8,128)S(1)} %get-tuple-element.346, bf16[1024,576]{0,1:T(8,128)(2,1)} %get-tuple-element.359, s32[1024]{0:T(1024)S(1)} %get-tuple-element.364, f32[512]{0:T(512)S(1)} %bitcast.75, f32[512]{0:T(512)S(1)} %bitcast.76, s32[512]{0:T(512)S(1)} %get-tuple-element.363, ...), kind=kOutput, calls=%fused_computation.9.clone.1 | convolution fusion | flops 608698368 | bytes 5976069 | tf_op jit(solution)/shard_map/while/body/eval_jaxpr/qd,sd->qs/dot_general | solution.py:99
  114.8 3.6 %select_add_fusion.2 = f32[512,1024]{1,0:T(8,128)S(1)} fusion(f32[512,1024]{1,0:T(8,128)S(1)} %get-tuple-element.346, bf16[1024,576]{0,1:T(8,128)(2,1)} %get-tuple-element.359, s32[1024]{0:T(1024)S(1)} %get-tuple-element.364, f32[512]{0:T(512)S(1)} %bitcast.75, f32[512]{0:T(512)S(1)} %bitcast.76, s32[512]{0:T(512)S(1)} %get-tuple-element.363, ...), kind=kOutput, calls=%fused_computation.9.clone.1 | convolution fusion | flops 608698368 | bytes 5976069 | tf_op jit(solution)/shard_map/while/body/eval_jaxpr/qd,sd->qs/dot_general | solution.py:99
  118.4 3.6 %select_add_fusion.2 = f32[512,1024]{1,0:T(8,128)S(1)} fusion(f32[512,1024]{1,0:T(8,128)S(1)} %get-tuple-element.346, bf16[1024,576]{0,1:T(8,128)(2,1)} %get-tuple-element.359, s32[1024]{0:T(1024)S(1)} %get-tuple-element.364, f32[512]{0:T(512)S(1)} %bitcast.75, f32[512]{0:T(512)S(1)} %bitcast.76, s32[512]{0:T(512)S(1)} %get-tuple-element.363, ...), kind=kOutput, calls=%fused_computation.9.clone.1 | convolution fusion | flops 608698368 | bytes 5976069 | tf_op jit(solution)/shard_map/while/body/eval_jaxpr/qd,sd->qs/dot_general | solution.py:99
  122.1 3.6 %select_add_fusion.2 = f32[512,1024]{1,0:T(8,128)S(1)} fusion(f32[512,1024]{1,0:T(8,128)S(1)} %get-tuple-element.346, bf16[1024,576]{0,1:T(8,128)(2,1)} %get-tuple-element.359, s32[1024]{0:T(1024)S(1)} %get-tuple-element.364, f32[512]{0:T(512)S(1)} %bitcast.75, f32[512]{0:T(512)S(1)} %bitcast.76, s32[512]{0:T(512)S(1)} %get-tuple-element.363, ...), kind=kOutput, calls=%fused_computation.9.clone.1 | convolution fusion | flops 608698368 | bytes 5976069 | tf_op jit(solution)/shard_map/while/body/eval_jaxpr/qd,sd->qs/dot_general | solution.py:99
  125.7 3.6 %select_add_fusion.2 = f32[512,1024]{1,0:T(8,128)S(1)} fusion(f32[512,1024]{1,0:T(8,128)S(1)} %get-tuple-element.346, bf16[1024,576]{0,1:T(8,128)(2,1)} %get-tuple-element.359, s32[1024]{0:T(1024)S(1)} %get-tuple-element.364, f32[512]{0:T(512)S(1)} %bitcast.75, f32[512]{0:T(512)S(1)} %bitcast.76, s32[512]{0:T(512)S(1)} %get-tuple-element.363, ...), kind=kOutput, calls=%fused_computation.9.clone.1 | convolution fusion | flops 608698368 | bytes 5976069 | tf_op jit(solution)/shard_map/while/body/eval_jaxpr/qd,sd->qs/dot_general | solution.py:99
  129.3 3.6 %select_add_fusion.2 = f32[512,1024]{1,0:T(8,128)S(1)} fusion(f32[512,1024]{1,0:T(8,128)S(1)} %get-tuple-element.346, bf16[1024,576]{0,1:T(8,128)(2,1)} %get-tuple-element.359, s32[1024]{0:T(1024)S(1)} %get-tuple-element.364, f32[512]{0:T(512)S(1)} %bitcast.75, f32[512]{0:T(512)S(1)} %bitcast.76, s32[512]{0:T(512)S(1)} %get-tuple-element.363, ...), kind=kOutput, calls=%fused_computation.9.clone.1 | convolution fusion | flops 608698368 | bytes 5976069 | tf_op jit(solution)/shard_map/while/body/eval_jaxpr/qd,sd->qs/dot_general | solution.py:99
  133.0 3.6 %select_add_fusion.2 = f32[512,1024]{1,0:T(8,128)S(1)} fusion(f32[512,1024]{1,0:T(8,128)S(1)} %get-tuple-element.346, bf16[1024,576]{0,1:T(8,128)(2,1)} %get-tuple-element.359, s32[1024]{0:T(1024)S(1)} %get-tuple-element.364, f32[512]{0:T(512)S(1)} %bitcast.75, f32[512]{0:T(512)S(1)} %bitcast.76, s32[512]{0:T(512)S(1)} %get-tuple-element.363, ...), kind=kOutput, calls=%fused_computation.9.clone.1 | convolution fusion | flops 608698368 | bytes 5976069 | tf_op jit(solution)/shard_map/while/body/eval_jaxpr/qd,sd->qs/dot_general | solution.py:99
  136.6 3.6 %select_add_fusion.2 = f32[512,1024]{1,0:T(8,128)S(1)} fusion(f32[512,1024]{1,0:T(8,128)S(1)} %get-tuple-element.346, bf16[1024,576]{0,1:T(8,128)(2,1)} %get-tuple-element.359, s32[1024]{0:T(1024)S(1)} %get-tuple-element.364, f32[512]{0:T(512)S(1)} %bitcast.75, f32[512]{0:T(512)S(1)} %bitcast.76, s32[512]{0:T(512)S(1)} %get-tuple-element.363, ...), kind=kOutput, calls=%fused_computation.9.clone.1 | convolution fusion | flops 608698368 | bytes 5976069 | tf_op jit(solution)/shard_map/while/body/eval_jaxpr/qd,sd->qs/dot_general | solution.py:99
  140.2 3.6 %select_add_fusion.2 = f32[512,1024]{1,0:T(8,128)S(1)} fusion(f32[512,1024]{1,0:T(8,128)S(1)} %get-tuple-element.346, bf16[1024,576]{0,1:T(8,128)(2,1)} %get-tuple-element.359, s32[1024]{0:T(1024)S(1)} %get-tuple-element.364, f32[512]{0:T(512)S(1)} %bitcast.75, f32[512]{0:T(512)S(1)} %bitcast.76, s32[512]{0:T(512)S(1)} %get-tuple-element.363, ...), kind=kOutput, calls=%fused_computation.9.clone.1 | convolution fusion | flops 608698368 | bytes 5976069 | tf_op jit(solution)/shard_map/while/body/eval_jaxpr/qd,sd->qs/dot_general | solution.py:99
  143.9 3.6 %select_add_fusion.2 = f32[512,1024]{1,0:T(8,128)S(1)} fusion(f32[512,1024]{1,0:T(8,128)S(1)} %get-tuple-element.346, bf16[1024,576]{0,1:T(8,128)(2,1)} %get-tuple-element.359, s32[1024]{0:T(1024)S(1)} %get-tuple-element.364, f32[512]{0:T(512)S(1)} %bitcast.75, f32[512]{0:T(512)S(1)} %bitcast.76, s32[512]{0:T(512)S(1)} %get-tuple-element.363, ...), kind=kOutput, calls=%fused_computation.9.clone.1 | convolution fusion | flops 608698368 | bytes 5976069 | tf_op jit(solution)/shard_map/while/body/eval_jaxpr/qd,sd->qs/dot_general | solution.py:99
  147.5 3.6 %select_add_fusion.2 = f32[512,1024]{1,0:T(8,128)S(1)} fusion(f32[512,1024]{1,0:T(8,128)S(1)} %get-tuple-element.346, bf16[1024,576]{0,1:T(8,128)(2,1)} %get-tuple-element.359, s32[1024]{0:T(1024)S(1)} %get-tuple-element.364, f32[512]{0:T(512)S(1)} %bitcast.75, f32[512]{0:T(512)S(1)} %bitcast.76, s32[512]{0:T(512)S(1)} %get-tuple-element.363, ...), kind=kOutput, calls=%fused_computation.9.clone.1 | convolution fusion | flops 608698368 | bytes 5976069 | tf_op jit(solution)/shard_map/while/body/eval_jaxpr/qd,sd->qs/dot_general | solution.py:99
  152.4 5.1 %all-to-all-start.2 = ((f32[8,64,1024]{2,1,0:T(8,128)}), f32[8,64,1024]{2,1,0:T(8,128)S(1)}, u32[]{:S(2)}, u32[]{:S(2)}) async-start(f32[8,64,1024]{2,1,0:T(8,128)} %bitcast.70), calls=%async_computation.2 | async-start | bytes 4194304 | tf_op jit(solution)/shard_map/all_to_all | solution.py:58
  159.2 24.6 %all-to-all-done.2 = f32[8,64,1024]{2,1,0:T(8,128)S(1)} async-done(((f32[8,64,1024]{2,1,0:T(8,128)}), f32[8,64,1024]{2,1,0:T(8,128)S(1)}, u32[]{:S(2)}, u32[]{:S(2)}) %all-to-all-start.2) | async-done | bytes 2097184 | tf_op jit(solution)/shard_map/all_to_all | solution.py:58
  184.1 7.5 %multiply_reduce_fusion = f32[64,64]{1,0:T(8,128)S(1)} fusion(f32[64,64,1024]{2,1,0:T(8,128)} %get-tuple-element.191, f32[64,1024]{1,0:T(8,128)S(1)} %multiply_select_fusion), kind=kLoop, calls=%fused_computation.15 | loop fusion | flops 12578816 | bytes 17055744 | tf_op jit(solution)/shard_map/reduce_sum | solution.py:144
  192.5 8.3 %all-to-all-start.5 = ((f32[16,1,256]{2,1,0:T(1,128)}), f32[16,1,256]{2,1,0:T(1,128)S(1)}, u32[]{:S(2)}, u32[]{:S(2)}) async-start(f32[16,1,256]{2,1,0:T(1,128)} %reshape.155), calls=%async_computation.5 | async-start | bytes 32768 | tf_op jit(solution)/shard_map/all_to_all | solution.py:58
  200.8 8.3 %fusion.11 = f32[64,64,128]{2,1,0:T(8,128)} fusion(f32[64,64,1024]{2,1,0:T(8,128)} %get-tuple-element.191, f32[64,64]{1,0:T(8,128)S(1)} %broadcast_multiply_fusion, f32[64,1024]{1,0:T(8,128)S(1)} %multiply_select_fusion, bf16[1024,128]{1,0:T(8,128)(2,1)S(1)} %copy-done), kind=kOutput, calls=%fused_computation.20 | convolution fusion | flops 1090519040 | bytes 19415040 | tf_op jit(solution)/shard_map/qjs,sd->qjd/dot_general | solution.py:140
  213.3 7.3 %all-to-all-start.3 = ((f32[16,64,512]{2,1,0:T(8,128)}), f32[16,64,512]{2,1,0:T(8,128)S(1)}, u32[]{:S(2)}, u32[]{:S(2)}) async-start(f32[16,64,512]{2,1,0:T(8,128)} %bitcast.67), calls=%async_computation.3 | async-start | bytes 4194304 | tf_op jit(solution)/shard_map/all_to_all | solution.py:58
  220.7 8.3 %convolution_bitcast_fusion = f32[1024,128]{1,0:T(8,128)} fusion(bf16[64,64,128]{2,1,0:T(8,128)(2,1)S(1)} %bitcast.69, f32[64,64,1024]{2,1,0:T(8,128)} %get-tuple-element.191, f32[64,64]{1,0:T(8,128)S(1)} %broadcast_multiply_fusion, f32[64,1024]{1,0:T(8,128)} %copy-done.5), kind=kOutput, calls=%fused_computation.19 | convolution fusion | flops 1090519040 | bytes 18628608 | tf_op jit(solution)/shard_map/qjs,qjd->sd/dot_general | solution.py:143
  229.0 20.0 %all-to-all-done.3 = f32[16,64,512]{2,1,0:T(8,128)S(1)} async-done(((f32[16,64,512]{2,1,0:T(8,128)}), f32[16,64,512]{2,1,0:T(8,128)S(1)}, u32[]{:S(2)}, u32[]{:S(2)}) %all-to-all-start.3) | async-done | bytes 2097184 | tf_op jit(solution)/shard_map/all_to_all | solution.py:58
  249.0 3.3 %broadcast_in_dim.62 = f32[8,1024,128]{2,1,0:T(8,128)} broadcast(f32[1024,128]{1,0:T(8,128)} %convolution_bitcast_fusion), dimensions={1,2} | broadcast | bytes 4718592 | tf_op jit(solution)/shard_map/broadcast_in_dim | solution.py:16
  252.2 4.6 %all-to-all-start.4 = ((f32[8,1024,128]{2,1,0:T(8,128)}), f32[8,1024,128]{2,1,0:T(8,128)}, u32[]{:S(2)}, u32[]{:S(2)}) async-start(f32[8,1024,128]{2,1,0:T(8,128)} %broadcast_in_dim.62), calls=%async_computation.4 | async-start | bytes 8388608 | tf_op jit(solution)/shard_map/all_to_all | solution.py:17
  259.0 46.5 %all-to-all-done.4 = f32[8,1024,128]{2,1,0:T(8,128)} async-done(((f32[8,1024,128]{2,1,0:T(8,128)}), f32[8,1024,128]{2,1,0:T(8,128)}, u32[]{:S(2)}, u32[]{:S(2)}) %all-to-all-start.4) | async-done | bytes 4194336 | tf_op jit(solution)/shard_map/all_to_all | solution.py:17
  305.5 3.2 %reduce_sum.76 = f32[1024,128]{1,0:T(8,128)} reduce(f32[8,1024,128]{2,1,0:T(8,128)} %all-to-all-done.4, f32[]{:T(128)} %constant.36.clone.1), dimensions={0}, to_apply=%region_11.12 | reduce | flops 917504 | bytes 4718596 | tf_op jit(solution)/shard_map/reduce_sum | solution.py:63
  (205 shorter events, 35.7 us)
Async XLA Ops:
  0.6 69.8 %copy-start = (bf16[1024,128]{1,0:T(8,128)(2,1)S(1)}, bf16[1024,128]{1,0:T(8,128)(2,1)}, u32[]{:S(2)}) copy-start(bf16[1024,128]{1,0:T(8,128)(2,1)} %param.15) | copy-start | bytes 786436
  0.7 2.8 copy-start.8
  0.7 2.8 copy-start.10
  4.4 2.7 copy-start.8
  4.5 2.7 copy-start.10
  8.2 2.7 copy-start.8
  8.2 2.7 copy-start.10
  11.9 2.7 copy-start.8
  11.9 2.7 copy-start.10
  15.6 2.7 copy-start.8
  15.6 2.7 copy-start.10
  19.3 2.7 copy-start.8
  19.3 2.7 copy-start.10
  23.1 2.7 copy-start.8
  23.1 2.7 copy-start.10
  26.8 2.7 copy-start.8
  26.8 2.7 copy-start.10
  30.5 2.7 copy-start.8
  30.5 2.7 copy-start.10
  34.2 2.7 copy-start.8
  34.2 2.7 copy-start.10
  37.9 2.7 copy-start.8
  38.0 2.7 copy-start.10
  41.7 2.7 copy-start.8
  41.7 2.7 copy-start.10
  45.4 2.7 copy-start.8
  45.4 2.7 copy-start.10
  49.1 2.7 copy-start.8
  49.1 2.7 copy-start.10
  52.8 2.7 copy-start.8
  52.8 2.7 copy-start.10
  56.6 2.7 copy-start.8
  56.6 2.7 copy-start.10
  60.3 9.7 %copy-start.11 = (s32[512]{0:T(512)S(1)}, s32[512]{0:T(512)}, u32[]{:S(2)}) copy-start(s32[512]{0:T(512)} %get-tuple-element.380) | copy-start | bytes 6148
  60.3 9.8 %copy-start.9 = (s32[512]{0:T(512)S(1)}, s32[512]{0:T(512)}, u32[]{:S(2)}) copy-start(s32[512]{0:T(512)} %get-tuple-element.379) | copy-start | bytes 6148
  60.3 9.9 %copy-start.6 = (bf16[64,8192]{1,0:T(8,128)(2,1)S(1)}, bf16[64,8192]{1,0:T(8,128)(2,1)}, u32[]{:S(2)}) copy-start(bf16[64,8192]{1,0:T(8,128)(2,1)} %param.14) | copy-start | bytes 3145732
  61.4 9.0 %copy-start.7 = (f32[64,64]{1,0:T(8,128)S(1)}, f32[64,64]{1,0:T(8,128)}, u32[]{:S(2)}) copy-start(f32[64,64]{1,0:T(8,128)} %param.16) | copy-start | bytes 49156
  61.4 25.5 %all-to-all-start.1 = ((f32[16,32,512]{2,1,0:T(8,128)}), f32[16,32,512]{2,1,0:T(8,128)S(1)}, u32[]{:S(2)}, u32[]{:S(2)}) async-start(f32[16,32,512]{2,1,0:T(8,128)} %broadcast_in_dim.61), calls=%async_computation.1 | async-start | bytes 2097152 | tf_op jit(solution)/shard_map/all_to_all | solution.py:17
  70.4 7.1 %copy-start.1 = (bf16[8,8,64,128]{3,2,1,0:T(8,128)(2,1)}, bf16[8,8,64,128]{3,2,1,0:T(8,128)(2,1)S(1)}, u32[]{:S(2)}) copy-start(bf16[8,8,64,128]{3,2,1,0:T(8,128)(2,1)S(1)} %copy.22) | copy-start | bytes 3145732
  87.0 64.2 %all-to-all-start = ((f32[16,1,128]{2,1,0:T(1,128)}), f32[16,1,128]{2,1,0:T(1,128)S(1)}, u32[]{:S(2)}, u32[]{:S(2)}) async-start(f32[16,1,128]{2,1,0:T(1,128)} %reshape.153), calls=%async_computation | async-start | bytes 16384 | tf_op jit(solution)/shard_map/all_to_all | solution.py:17
  91.4 1.6 copy-start.3
  152.4 31.3 %all-to-all-start.2 = ((f32[8,64,1024]{2,1,0:T(8,128)}), f32[8,64,1024]{2,1,0:T(8,128)S(1)}, u32[]{:S(2)}, u32[]{:S(2)}) async-start(f32[8,64,1024]{2,1,0:T(8,128)} %bitcast.70), calls=%async_computation.2 | async-start | bytes 4194304 | tf_op jit(solution)/shard_map/all_to_all | solution.py:58
  157.6 26.3 %copy-start.12 = (f32[64]{0:T(128)S(1)}, f32[64]{0:T(128)}, u32[]{:S(2)}) copy-start(f32[64]{0:T(128)} %param.17) | copy-start | bytes 772
  184.1 16.6 %copy-start.5 = (f32[64,1024]{1,0:T(8,128)}, f32[64,1024]{1,0:T(8,128)S(1)}, u32[]{:S(2)}) copy-start(f32[64,1024]{1,0:T(8,128)S(1)} %multiply_select_fusion) | copy-start | bytes 786436
  192.5 20.9 %all-to-all-start.5 = ((f32[16,1,256]{2,1,0:T(1,128)}), f32[16,1,256]{2,1,0:T(1,128)S(1)}, u32[]{:S(2)}, u32[]{:S(2)}) async-start(f32[16,1,256]{2,1,0:T(1,128)} %reshape.155), calls=%async_computation.5 | async-start | bytes 32768 | tf_op jit(solution)/shard_map/all_to_all | solution.py:58
  213.3 7.3 %copy-start.2 = (bf16[8,8,64,128]{3,2,1,0:T(8,128)(2,1)S(1)}, bf16[8,8,64,128]{3,2,1,0:T(8,128)(2,1)}, u32[]{:S(2)}) copy-start(bf16[8,8,64,128]{3,2,1,0:T(8,128)(2,1)} %copy-done.1) | copy-start | bytes 3145732
  213.3 35.6 %all-to-all-start.3 = ((f32[16,64,512]{2,1,0:T(8,128)}), f32[16,64,512]{2,1,0:T(8,128)S(1)}, u32[]{:S(2)}, u32[]{:S(2)}) async-start(f32[16,64,512]{2,1,0:T(8,128)} %bitcast.67), calls=%async_computation.3 | async-start | bytes 4194304 | tf_op jit(solution)/shard_map/all_to_all | solution.py:58
  252.2 53.2 %all-to-all-start.4 = ((f32[8,1024,128]{2,1,0:T(8,128)}), f32[8,1024,128]{2,1,0:T(8,128)}, u32[]{:S(2)}, u32[]{:S(2)}) async-start(f32[8,1024,128]{2,1,0:T(8,128)} %broadcast_in_dim.62), calls=%async_computation.4 | async-start | bytes 8388608 | tf_op jit(solution)/shard_map/all_to_all | solution.py:17
  (1 other events, 1.3 us)
where the time goes:
time: 310 us; the launch traced here: 309 us
  matrix products  124 us (40%)
  waiting for transfers between devices  99.3 us (32%)
  starting transfers between devices  38.2 us (12%)
  other arithmetic  27.7 us (9%)
  local copies, waits for them, and re-layouts  16.6 us (5%)
    dot_general x32, matrix products, main_scores(): jnp.einsum('qd,sd->qs', q_rows, k_latent, preferred_element_type=jnp.floa...  101 us
    all_to_all x3, waiting for transfers between devices, sent_to_all(): return lax.all_to_all(copies, axis, split_axis=0, concat_axis=0, tiled=True)  54.7 us
    all_to_all x3, waiting for transfers between devices, sent_and_summed(): pieces = lax.all_to_all(in_blocks(x, dim, count), axis, 0, 0, tiled=True)  44.6 us
    all_to_all x3, starting transfers between devices, sent_and_summed(): pieces = lax.all_to_all(in_blocks(x, dim, count), axis, 0, 0, tiled=True)  20.7 us
    all_to_all x3, starting transfers between devices, sent_to_all(): return lax.all_to_all(copies, axis, split_axis=0, concat_axis=0, tiled=True)  17.5 us
    reduce_sum x17, other arithmetic, local_stats(): return (highest, jnp.sum(exponents, axis=-1))  13.3 us
    dot_general x1, matrix products, shards(): jnp.einsum('qjs,qjd->sd', head_grad, q_heads, preferred_element_type=jnp....  8.32 us
    dot_general x1, matrix products, shards(): jnp.einsum('qjs,sd->qjd', head_grad, k_index, preferred_element_type=jnp....  8.29 us
  transfers between devices with their start and end apart: 6, of which 4 were waited for; matrix products, arithmetic and copies ran while one was open for 30% of the time, Pallas kernels for 0%

commit v1 on v0

v1 whole, which is shorter than its diff:
```python
import functools
import math

import jax
import jax.numpy as jnp
from jax import lax
from jax.experimental import pallas as pl
from jax.experimental.pallas import tpu as pltpu
from jax.sharding import PartitionSpec as P

H = 128
QK_DIM = 192
LOG2E = 1.4426950408889634
LOW = -1e30
FLOOR = -1e29
CHUNK = 256
GROUP = 4


def eye_of(n):
    rows = lax.broadcasted_iota(jnp.int32, (n, n), 0)
    return rows == lax.broadcasted_iota(jnp.int32, (n, n), 1)


def as_column(row):
    n = row.shape[1]
    return jnp.sum(jnp.where(eye_of(n), row, jnp.zeros_like(row)), axis=1, keepdims=True)


def as_row(column):
    n = column.shape[0]
    return jnp.sum(jnp.where(eye_of(n), column, jnp.zeros_like(column)), axis=0, keepdims=True)


def joined_lse(a, b):
    high = jnp.maximum(a, b)
    return high + jnp.log2(jnp.exp2(a - high) + jnp.exp2(b - high))


def main_kernel(base_ref, kt_ref, qt_ref, start_ref, pos_ref, e_ref, m_ref, lse_ref, k_ref, bias_ref):
    h = pl.program_id(0)
    keys, queries = bias_ref.shape
    chunks = keys // CHUNK
    scale = LOG2E / math.sqrt(QK_DIM)

    @pl.when(h == 0)
    def _():
        k_ref[...] = kt_ref[...].T
        s = base_ref[0] + lax.broadcasted_iota(jnp.int32, (keys, queries), 0)
        seen = (s >= start_ref[...]) & (s <= pos_ref[...])
        bias_ref[...] = jnp.where(seen, 0.0, LOW)

    qt = qt_ref[0]
    highs, sums = [], []
    for c in range(chunks):
        here = pl.ds(c * CHUNK, CHUNK)
        s = jnp.dot(k_ref[here, :], qt, preferred_element_type=jnp.float32)
        s = s * scale + bias_ref[here, :]
        high = jnp.maximum(jnp.max(s, axis=0, keepdims=True), FLOOR)
        e = jnp.exp2(s - high).astype(jnp.bfloat16)
        e_ref[0, here, :] = e
        highs.append(high)
        sums.append(jnp.sum(e.astype(jnp.float32), axis=0, keepdims=True))
        m_ref[pl.ds(h * chunks + c, 1), :] = high
    top = functools.reduce(jnp.maximum, highs)
    total = sum(l * jnp.exp2(m - top) for l, m in zip(sums, highs))
    lse_ref[pl.ds(h, 1), :] = jnp.where(total > 0.0, top + jnp.log2(total), FLOOR)


def main_forward(base, kt, qt, start, pos):
    heads, lat, queries = qt.shape
    keys = kt.shape[1]
    chunks = keys // CHUNK
    return pl.pallas_call(
        main_kernel,
        grid=(heads,),
        in_specs=[
            pl.BlockSpec(memory_space=pltpu.SMEM),
            pl.BlockSpec((lat, keys), lambda h: (0, 0)),
            pl.BlockSpec((1, lat, queries), lambda h: (h, 0, 0)),
            pl.BlockSpec((1, queries), lambda h: (0, 0)),
            pl.BlockSpec((1, queries), lambda h: (0, 0)),
        ],
        out_specs=[
            pl.BlockSpec((1, keys, queries), lambda h: (h, 0, 0)),
            pl.BlockSpec((heads * chunks, queries), lambda h: (0, 0)),
            pl.BlockSpec((heads, queries), lambda h: (0, 0)),
        ],
        out_shape=[
            jax.ShapeDtypeStruct((heads, keys, queries), jnp.bfloat16),
            jax.ShapeDtypeStruct((heads * chunks, queries), jnp.float32),
            jax.ShapeDtypeStruct((heads, queries), jnp.float32),
        ],
        scratch_shapes=[
            pltpu.VMEM((keys, lat), jnp.bfloat16),
            pltpu.VMEM((keys, queries), jnp.float32),
        ],
        cost_estimate=pl.CostEstimate(
            flops=2 * heads * keys * queries * lat, bytes_accessed=26 << 20, transcendentals=heads * keys * queries
        ),
        name="main_forward",
    )(base, kt, qt, start, pos)


def index_kernel(base_ref, q_ref, kt_ref, w_ref, start_ref, pos_ref, s_ref, lse_ref):
    c = pl.program_id(0)
    rows, width = s_ref.shape[0], CHUNK
    heads = w_ref.shape[1]
    dim = kt_ref.shape[0]
    here = pl.ds(pl.multiple_of(c * width, width), width)
    kt = kt_ref[:, here]
    total = jnp.zeros((rows, width), jnp.float32)
    for j in range(heads):
        d = jnp.dot(q_ref[:, j * dim : (j + 1) * dim], kt, preferred_element_type=jnp.float32)
        total = total + w_ref[:, j : j + 1] * jnp.maximum(d, 0.0)
    s = base_ref[0] + c * width + lax.broadcasted_iota(jnp.int32, (rows, width), 1)
    seen = (s >= as_column(start_ref[...])) & (s <= as_column(pos_ref[...]))
    s_ref[:, here] = jnp.where(seen, total * (LOG2E / math.sqrt(dim)), LOW)

    @pl.when(c == pl.num_programs(0) - 1)
    def _():
        scores = s_ref[...]
        high = jnp.maximum(jnp.max(scores, axis=1, keepdims=True), FLOOR)
        total = jnp.sum(jnp.exp2(scores - high), axis=1, keepdims=True)
        lse_ref[...] = as_row(jnp.where(total > 0.0, high + jnp.log2(total), FLOOR))


def index_forward(base, q, kt, w, start, pos):
    rows, width = q.shape
    dim, keys = kt.shape
    heads = w.shape[1]
    whole = lambda *shape: pl.BlockSpec(shape, lambda c: (0,) * len(shape))
    return pl.pallas_call(
        index_kernel,
        grid=(keys // CHUNK,),
        in_specs=[
            pl.BlockSpec(memory_space=pltpu.SMEM),
            whole(rows, width),
            whole(dim, keys),
            whole(rows, heads),
            whole(1, rows),
            whole(1, rows),
        ],
        out_specs=[whole(rows, keys), whole(1, rows)],
        out_shape=[
            jax.ShapeDtypeStruct((rows, keys), jnp.float32),
            jax.ShapeDtypeStruct((1, rows), jnp.float32),
        ],
        cost_estimate=pl.CostEstimate(flops=2 * rows * width * keys, bytes_accessed=2 << 20, transcendentals=rows * keys),
        name="index_forward",
    )(base, q, kt, w, start, pos)


def sum_kernel(e_ref, m_ref, lse_ref, t_ref):
    c = pl.program_id(0)
    heads, width, queries = e_ref.shape
    chunks = pl.num_programs(0)
    owners, rows, _ = t_ref.shape
    lanes = 128
    weights = [jnp.exp2(m_ref[pl.ds(h * chunks + c, 1), :] - lse_ref[h : h + 1, :]) for h in range(heads)]
    for b in range(queries // lanes):
        cols = slice(b * lanes, (b + 1) * lanes)
        for r in range(width // 128):
            at = pl.ds(r * 128, 128)
            total = e_ref[0, at, cols].astype(jnp.float32) * weights[0][:, cols]
            for h in range(1, heads):
                total = total + e_ref[h, at, cols].astype(jnp.float32) * weights[h][:, cols]
            flipped = total.T
            for o in range(lanes // rows):
                t_ref[b * (lanes // rows) + o, :, at] = flipped[o * rows : (o + 1) * rows]


def weighted_sum(e, m, lse, owners):
    heads, keys, queries = e.shape
    chunks = keys // CHUNK
    rows = queries // owners
    return pl.pallas_call(
        sum_kernel,
        grid=(chunks,),
        in_specs=[
            pl.BlockSpec((heads, CHUNK, queries), lambda c: (0, c, 0)),
            pl.BlockSpec((heads * chunks, queries), lambda c: (0, 0)),
            pl.BlockSpec((heads, queries), lambda c: (0, 0)),
        ],
        out_specs=pl.BlockSpec((owners, rows, CHUNK), lambda c: (0, 0, c)),
        out_shape=jax.ShapeDtypeStruct((owners, rows, keys), jnp.float32),
        cost_estimate=pl.CostEstimate(
            flops=2 * heads * keys * queries, bytes_accessed=18 << 20, transcendentals=heads * chunks * queries
        ),
        name="weighted_sum",
    )(e, m, lse)


def back_kernel(t_ref, s_ref, lse_ref, c_ref, q_ref, k_ref, kt_ref, w_ref, gq_ref, gk_ref, g_ref, gkt_ref):
    i = pl.program_id(0)
    rows, keys = g_ref.shape
    dim = kt_ref.shape[0]
    index_scale = 1.0 / math.sqrt(dim)

    @pl.when(i == 0)
    def _():
        target = jnp.sum(t_ref[...], axis=0) * (1.0 / H)
        scores = s_ref[...]
        probs = jnp.exp2(scores - as_column(lse_ref[...]))
        g_ref[...] = jnp.where(scores > FLOOR, as_column(c_ref[...]) * (probs - target), 0.0)
        gkt_ref[...] = jnp.zeros_like(gkt_ref)

    q = jnp.concatenate([q_ref[:, j * dim : (j + 1) * dim] for j in range(GROUP)], axis=0)
    d = jnp.dot(q, kt_ref[...], preferred_element_type=jnp.float32)
    g = g_ref[...]
    parts, sums = [], []
    for j in range(GROUP):
        dots = d[j * rows : (j + 1) * rows]
        kept = jnp.where(dots > 0.0, g, 0.0)
        coef = w_ref[0][:, j : j + 1] * index_scale
        parts.append((kept * coef).astype(jnp.bfloat16))
        sums.append(as_row(jnp.sum(kept * dots, axis=1, keepdims=True)))
    head_grad = jnp.concatenate(parts, axis=0)
    gq = jnp.dot(head_grad, k_ref[...], preferred_element_type=jnp.float32)
    for j in range(GROUP):
        gq_ref[0, :rows, j * dim : (j + 1) * dim] = gq[j * rows : (j + 1) * rows]
        gq_ref[0, rows + j : rows + j + 1, :rows] = sums[j] * index_scale
    gkt_ref[...] += lax.dot_general(q, head_grad, (((0,), (0,)), ((), ())), preferred_element_type=jnp.float32)

    @pl.when(i == pl.num_programs(0) - 1)
    def _():
        gk_ref[...] = gkt_ref[...].T


def backward(t, s, lse, c, q, k, kt, w):
    rows, width = q.shape
    keys, dim = k.shape
    steps = width // (dim * GROUP)
    whole = lambda *shape: pl.BlockSpec(shape, lambda i: (0,) * len(shape))
    w = jnp.moveaxis(w.reshape(rows, steps, GROUP), 1, 0)
    return pl.pallas_call(
        back_kernel,
        grid=(steps,),
        in_specs=[
            whole(*t.shape),
            whole(rows, keys),
            whole(1, rows),
            whole(1, rows),
            pl.BlockSpec((rows, dim * GROUP), lambda i: (0, i)),
            whole(keys, dim),
            whole(dim, keys),
            pl.BlockSpec((1, rows, GROUP), lambda i: (i, 0, 0)),
        ],
        out_specs=[
            pl.BlockSpec((1, rows + 8, dim * GROUP), lambda i: (i, 0, 0)),
            whole(keys, dim),
        ],
        out_shape=[
            jax.ShapeDtypeStruct((steps, rows + 8, dim * GROUP), jnp.float32),
            jax.ShapeDtypeStruct((keys, dim), jnp.float32),
        ],
        scratch_shapes=[pltpu.VMEM((rows, keys), jnp.float32), pltpu.VMEM((dim, keys), jnp.float32)],
        cost_estimate=pl.CostEstimate(flops=6 * rows * width * keys, bytes_accessed=8 << 20, transcendentals=rows * keys),
        name="backward",
    )(t, s, lse, c, q, k, kt, w)


def joined_over_key(x):
    n = lax.axis_size("key")
    for mask in (1, 2):
        x = joined_lse(x, lax.ppermute(x, "key", [(i, i ^ mask) for i in range(n)]))
    others = [lax.ppermute(x, "key", [(i, (i + 4 * k) % n) for i in range(n)]) for k in (1, 2, 3)]
    high = functools.reduce(jnp.maximum, others, x)
    return high + jnp.log2(sum(jnp.exp2(y - high) for y in [x, *others]))


def shards(q_latent, k_latent, q_index, k_index, head_weight, loss_weight, query_pos, key_start):
    keys = k_latent.shape[0]
    rows = q_index.shape[0]
    owners = lax.axis_size("head")
    base = (lax.axis_index("key") * keys).astype(jnp.int32).reshape(1)
    own = lax.axis_index("head") * rows
    start, pos = key_start.reshape(1, -1), query_pos.reshape(1, -1)
    own_start = lax.dynamic_slice_in_dim(start, own, rows, axis=1)
    own_pos = lax.dynamic_slice_in_dim(pos, own, rows, axis=1)
    kt_index = k_index.T
    e, high, lse = main_forward(base, k_latent.T, jnp.swapaxes(q_latent, 1, 2), start, pos)
    scores, index_lse = index_forward(base, q_index, kt_index, head_weight, own_start, own_pos)
    lse = joined_over_key(lse)
    index_lse = joined_over_key(index_lse)
    partial = weighted_sum(e, high, lse, owners)
    blocks = lax.all_to_all(partial, "head", 0, 0, tiled=True)
    gq, gk = backward(blocks, scores, index_lse, loss_weight.reshape(1, -1), q_index, k_index, kt_index, head_weight)
    gq = jnp.sum(lax.all_to_all(gq, "key", 0, 0, tiled=True), axis=0)
    gk = gk.reshape(owners, -1, gk.shape[1])
    gk = jnp.sum(lax.all_to_all(gk, "head", 0, 0, tiled=True), axis=0)
    gk = lax.all_to_all(jnp.broadcast_to(gk, (owners, *gk.shape)), "head", 0, 0, tiled=True)
    return (gq[:rows], gk.reshape(keys, -1), gq[rows : rows + GROUP, :rows].T)


def solution(mesh):
    return jax.shard_map(
        shards,
        mesh=mesh,
        in_specs=(
            P("head", None, None),
            P("key", None),
            P("head", None),
            P("key", None),
            P("head", None),
            P("head"),
            P(),
            P(),
        ),
        out_specs=(P("head", "key"), P("key", None), P("head", "key")),
        check_vma=False,
    )
```

time: 310 us -> 170 us (0.55)
  matrix products: 124 us -> 0 us
  waiting for transfers between devices: 99.3 us -> 44.8 us
  Pallas kernels: 0 us -> 52.9 us
  other arithmetic: 27.7 us -> 2.93 us
  blocking collectives: 0 us -> 21.3 us
  local copies, waits for them, and re-layouts: 16.6 us -> 6.66 us
    dot_general x35 -> x0, matrix products: 124 us -> none  [the longest x32 101 us: main_scores(): jnp.einsum('qd,sd->qs', q_rows, k_latent, preferred_element_type=jnp.floa...]
    all_to_all x6 -> x2, waiting for transfers between devices: 99.3 us -> 31.1 us  [the longest x1 31.1 us: shards(): gq = jnp.sum(lax.all_to_all(gq, 'key', 0, 0, tiled=True), axis=0)]
    pallas_call x0 -> x4, Pallas kernels: none -> 52.9 us  [the longest x1 23.8 us: main_forward(): pl.pallas_call(main_kernel, grid=(heads,), in_specs=[pl.BlockSpec(memory_...]
    reduce_sum x22 -> x2, other arithmetic: 25.1 us -> 0.22 us  [the longest x1 0.19 us: shards(): gq = jnp.sum(lax.all_to_all(gq, 'key', 0, 0, tiled=True), axis=0)]
    all_to_all x0 -> x2, blocking collectives: none -> 21.3 us  [the longest x1 11.4 us: shards(): gk = jnp.sum(lax.all_to_all(gk, 'head', 0, 0, tiled=True), axis=0)]
    ppermute x0 -> x10, starting transfers between devices: none -> 19.8 us  [the longest x4 10.7 us: joined_over_key(): x = joined_lse(x, lax.ppermute(x, 'key', [(i, i ^ mask) for i in range(n)]))]
    all_to_all x6 -> x2, starting transfers between devices: 38.2 us -> 19.2 us  [the longest x1 13.1 us: shards(): gq = jnp.sum(lax.all_to_all(gq, 'key', 0, 0, tiled=True), axis=0)]
    ppermute x0 -> x10, waiting for transfers between devices: none -> 13.7 us  [the longest x4 10.7 us: joined_over_key(): x = joined_lse(x, lax.ppermute(x, 'key', [(i, i ^ mask) for i in range(n)]))]
  transfers between devices with their start and end apart: 6 -> 12, of which waited for: 4 -> 8; matrix products, arithmetic and copies ran while one was open for 30% -> 3% of each run, Pallas kernels for 0% -> 3%
where the time goes in v1:
time: 170 us; the launch traced here: 168 us
  Pallas kernels  52.9 us (31%)
  waiting for transfers between devices  44.8 us (26%)
  starting transfers between devices  39 us (23%)
  blocking collectives  21.3 us (13%)
  local copies, waits for them, and re-layouts  6.66 us (4%)
  other arithmetic  2.93 us (2%)
    all_to_all x1, waiting for transfers between devices, shards(): gq = jnp.sum(lax.all_to_all(gq, 'key', 0, 0, tiled=True), axis=0)  31.1 us
    pallas_call x1, Pallas kernels, main_forward(): pl.pallas_call(main_kernel, grid=(heads,), in_specs=[pl.BlockSpec(memory_...  23.8 us
    pallas_call x1, Pallas kernels, backward(): pl.pallas_call(back_kernel, grid=(steps,), in_specs=[whole(*t.shape), who...  14.7 us
    all_to_all x1, starting transfers between devices, shards(): gq = jnp.sum(lax.all_to_all(gq, 'key', 0, 0, tiled=True), axis=0)  13.1 us
    all_to_all x1, blocking collectives, shards(): gk = jnp.sum(lax.all_to_all(gk, 'head', 0, 0, tiled=True), axis=0)  11.4 us
    ppermute x4, waiting for transfers between devices, joined_over_key(): x = joined_lse(x, lax.ppermute(x, 'key', [(i, i ^ mask) for i in range(n)]))  10.7 us
    ppermute x4, starting transfers between devices, joined_over_key(): x = joined_lse(x, lax.ppermute(x, 'key', [(i, i ^ mask) for i in range(n)]))  10.7 us
    all_to_all x1, blocking collectives, shards(): lax.all_to_all(jnp.broadcast_to(gk, (owners, *gk.shape)), 'head', 0, 0, t...  9.89 us
  transfers between devices with their start and end apart: 12, of which 8 were waited for; matrix products, arithmetic and copies ran while one was open for 3% of the time, Pallas kernels for 3%

profile of v1, /device:TPU:1, one launch (start us, length us, event | category | flops | bytes accessed | tf_op | source)
XLA Modules:
  0.0 168.4 jit_solution(1861827721729214481)
XLA Ops:
  0.6 23.8 %main_forward.1 = (bf16[16,1024,512]{2,1,0:T(8,128)(2,1)}, f32[64,512]{1,0:T(8,128)}, f32[16,512]{1,0:T(8,128)}) custom-call(s32[1]{0:T(128)} %bitcast.base_ref, bf16[576,1024]{1,0:T(8,128)(2,1)} %bitcast.26, bf16[16,576,512]{2,1,0:T(8,128)(2,1)} %bitcast.25, s32[1,512]{1,0:T(1,128)} %bitcast.23, s32[1,512]{1,0:T(1,128)} %bitcast.24), custom_call_target="tpu_custom_call" | custom-call | flops 9663676416 | bytes 27262976 | tf_op jit(solution)/shard_map/main_forward/pallas_call | solution.py:74
  24.5 1.4 collective-permute-start
  25.8 1.1 collective-permute-done
  26.9 0.8 multiply_add_fusion.2
  27.7 3.1 %collective-permute-start.1 = (f32[16,512]{1,0:T(8,128)S(1)}, f32[16,512]{1,0:T(8,128)S(1)}, u32[]{:S(2)}, u32[]{:S(2)}) collective-permute-start(f32[16,512]{1,0:T(8,128)S(1)} %multiply_add_fusion.2), channel_id=1, source_target_pairs={{0,2},{1,3},{2,0},{3,1},{4,6},{5,7},{6,4},{7,5},{8,10},{9,11},{10,... | collective-permute-start | bytes 98312 | tf_op jit(solution)/shard_map/ppermute | solution.py:266
  30.8 1.3 collective-permute-done.1
  32.2 1.3 collective-permute-start.2
  33.5 2.4 %collective-permute-start.3 = (f32[16,512]{1,0:T(8,128)S(1)}, f32[16,512]{1,0:T(8,128)S(1)}, u32[]{:S(2)}, u32[]{:S(2)}) collective-permute-start(f32[16,512]{1,0:T(8,128)S(1)} %multiply_add_fusion.1), channel_id=1, source_target_pairs={{0,8},{1,9},{2,10},{3,11},{4,12},{5,13},{6,14},{7,15},{8,0},{9,1},... | collective-permute-start | bytes 98312 | tf_op jit(solution)/shard_map/ppermute | solution.py:267
  35.9 1.2 collective-permute-start.4
  37.1 0.0 collective-permute-done.2
  37.1 0.7 collective-permute-done.3
  37.8 1.0 collective-permute-done.4
  38.8 0.7 multiply_add_fusion.lse_ref
  39.5 8.8 %weighted_sum.1 = f32[8,64,1024]{2,1,0:T(8,128)} custom-call(bf16[16,1024,512]{2,1,0:T(8,128)(2,1)} %get-tuple-element.10.e_ref, f32[64,512]{1,0:T(8,128)} %get-tuple-element.11.m_ref, f32[16,512]{1,0:T(8,128)} %multiply_add_fusion.lse_ref), custom_call_target="tpu_custom_call" | custom-call | flops 16777216 | bytes 18874368 | tf_op jit(solution)/shard_map/weighted_sum/pallas_call | solution.py:177
  48.3 0.0 copy-start.1
  48.3 6.1 %all-to-all-start = ((f32[8,64,1024]{2,1,0:T(8,128)}), f32[8,64,1024]{2,1,0:T(8,128)S(1)}, u32[]{:S(2)}, u32[]{:S(2)}) async-start(f32[8,64,1024]{2,1,0:T(8,128)} %weighted_sum.1), calls=%async_computation | async-start | bytes 4194304 | tf_op jit(solution)/shard_map/all_to_all | solution.py:287
  54.4 0.0 copy-start.2
  54.4 0.0 copy-done.1
  54.4 0.9 copy.12
  55.2 1.3 dynamic-slice_bitcast_fusion
  56.5 5.6 %index_forward.1 = (f32[64,1024]{1,0:T(8,128)}, f32[1,64]{1,0:T(1,128)}) custom-call(s32[1]{0:T(128)} %bitcast.base_ref, bf16[64,8192]{1,0:T(8,128)(2,1)} %q_ref.3, bf16[128,1024]{1,0:T(8,128)(2,1)} %bitcast.20, f32[64,64]{1,0:T(8,128)} %w_ref.1, s32[1,64]{1,0:T(1,128)} %get-tuple-element.18.start_ref, s32[1,64]{1,0:T(1,128)} %get-tuple-element.17.pos_ref), custom_call_target="tpu_custom_call" | custom-call | flops 1073741824 | bytes 2097152 | tf_op jit(solution)/shard_map/index_forward/pallas_call | solution.py:133
  62.1 3.5 %collective-permute-start.5 = (f32[1,64]{1,0:T(1,128)}, f32[1,64]{1,0:T(1,128)S(1)}, u32[]{:S(2)}, u32[]{:S(2)}) collective-permute-start(f32[1,64]{1,0:T(1,128)} %get-tuple-element.14), channel_id=1, source_target_pairs={{0,1},{1,0},{2,3},{3,2},{4,5},{5,4},{6,7},{7,6},{8,9},{9,8},{10,11... | collective-permute-start | bytes 776 | tf_op jit(solution)/shard_map/ppermute | solution.py:266
  65.6 0.9 collective-permute-done.5
  66.5 0.7 multiply_add_fusion.5
  67.2 2.7 %collective-permute-start.6 = (f32[1,64]{1,0:T(1,128)S(1)}, f32[1,64]{1,0:T(1,128)S(1)}, u32[]{:S(2)}, u32[]{:S(2)}) collective-permute-start(f32[1,64]{1,0:T(1,128)S(1)} %multiply_add_fusion.5), channel_id=1, source_target_pairs={{0,2},{1,3},{2,0},{3,1},{4,6},{5,7},{6,4},{7,5},{8,10},{9,11},{10,... | collective-permute-start | bytes 776 | tf_op jit(solution)/shard_map/ppermute | solution.py:266
  69.9 7.5 %collective-permute-done.6 = f32[1,64]{1,0:T(1,128)S(1)} collective-permute-done((f32[1,64]{1,0:T(1,128)S(1)}, f32[1,64]{1,0:T(1,128)S(1)}, u32[]{:S(2)}, u32[]{:S(2)}) %collective-permute-start.6) | collective-permute-done | bytes 288 | tf_op jit(solution)/shard_map/ppermute | solution.py:266
  77.4 0.6 collective-permute-start.7
  78.0 3.6 %collective-permute-start.8 = (f32[1,64]{1,0:T(1,128)S(1)}, f32[1,64]{1,0:T(1,128)S(1)}, u32[]{:S(2)}, u32[]{:S(2)}) collective-permute-start(f32[1,64]{1,0:T(1,128)S(1)} %multiply_add_fusion.4), channel_id=1, source_target_pairs={{0,8},{1,9},{2,10},{3,11},{4,12},{5,13},{6,14},{7,15},{8,0},{9,1},... | collective-permute-start | bytes 776 | tf_op jit(solution)/shard_map/ppermute | solution.py:267
  81.6 0.0 collective-permute-start.9
  81.6 0.0 copy-done.2
  81.6 0.1 copy.13
  81.6 1.1 copy.14
  82.7 0.0 collective-permute-done.7
  82.7 0.0 collective-permute-done.8
  82.7 1.3 collective-permute-done.9
  84.0 0.5 multiply_add_fusion.3.lse_ref
  84.5 0.0 all-to-all-done.t_ref
  84.5 0.0 copy-start
  84.5 1.3 copy-done
  85.8 14.7 %backward.1 = (f32[16,72,512]{2,1,0:T(8,128)}, f32[1024,128]{1,0:T(8,128)}) custom-call(f32[8,64,1024]{2,1,0:T(8,128)} %copy-done, f32[64,1024]{1,0:T(8,128)} %get-tuple-element.13.s_ref, f32[1,64]{1,0:T(1,128)} %multiply_add_fusion.3.lse_ref, f32[1,64]{1,0:T(1,128)} %bitcast.27, bf16[64,8192]{1,0:T(8,128)(2,1)} %q_ref.3, bf16[1024,128]{1,0:T(8,128)(2,1)} %k_ref.1, ...), custom_call_target="tpu_custom_call" | custom-call | flops 3221225472 | bytes 8388608 | tf_op jit(solution)/shard_map/backward/pallas_call | solution.py:236
  100.5 11.4 %all_to_all.20 = f32[8,128,128]{2,1,0:T(8,128)S(1)} all-to-all(f32[8,128,128]{2,1,0:T(8,128)} %bitcast.19), channel_id=1, replica_groups=mesh['head'=8,'key'=16] {'head'}, dimensions={0} | all-to-all | bytes 1048576 | tf_op jit(solution)/shard_map/all_to_all | solution.py:291
  112.0 9.9 %all_to_all.21 = f32[8,128,128]{2,1,0:T(8,128)S(1)} all-to-all(f32[8,128,128]{2,1,0:T(8,128)S(1)} %broadcast_in_dim.3), channel_id=1, replica_groups=mesh['head'=8,'key'=16] {'head'}, dimensions={0} | all-to-all | bytes 1048576 | tf_op jit(solution)/shard_map/all_to_all | solution.py:292
  121.9 13.1 %all-to-all-start.1 = ((f32[16,72,512]{2,1,0:T(8,128)}), f32[16,72,512]{2,1,0:T(8,128)S(1)}, u32[]{:S(2)}, u32[]{:S(2)}) async-start(f32[16,72,512]{2,1,0:T(8,128)} %get-tuple-element.15), calls=%async_computation.1 | async-start | bytes 4718592 | tf_op jit(solution)/shard_map/all_to_all | solution.py:289
  135.0 31.1 %all-to-all-done.1 = f32[16,72,512]{2,1,0:T(8,128)S(1)} async-done(((f32[16,72,512]{2,1,0:T(8,128)}), f32[16,72,512]{2,1,0:T(8,128)S(1)}, u32[]{:S(2)}, u32[]{:S(2)}) %all-to-all-start.1) | async-done | bytes 2359328 | tf_op jit(solution)/shard_map/all_to_all | solution.py:289
  166.2 0.2 reduce_sum.18
  166.3 0.7 slice.8
  167.0 0.6 slice_bitcast_fusion
  167.6 0.8 copy.16
  (4 shorter events, 0.1 us)
Async XLA Ops:
  24.5 2.5 %collective-permute-start = (f32[16,512]{1,0:T(8,128)}, f32[16,512]{1,0:T(8,128)S(1)}, u32[]{:S(2)}, u32[]{:S(2)}) collective-permute-start(f32[16,512]{1,0:T(8,128)} %get-tuple-element.12), channel_id=1, source_target_pairs={{0,1},{1,0},{2,3},{3,2},{4,5},{5,4},{6,7},{7,6},{8,9},{9,8},{10,11... | collective-permute-start | bytes 98312 | tf_op jit(solution)/shard_map/ppermute | solution.py:266
  27.7 4.4 %collective-permute-start.1 = (f32[16,512]{1,0:T(8,128)S(1)}, f32[16,512]{1,0:T(8,128)S(1)}, u32[]{:S(2)}, u32[]{:S(2)}) collective-permute-start(f32[16,512]{1,0:T(8,128)S(1)} %multiply_add_fusion.2), channel_id=1, source_target_pairs={{0,2},{1,3},{2,0},{3,1},{4,6},{5,7},{6,4},{7,5},{8,10},{9,11},{10,... | collective-permute-start | bytes 98312 | tf_op jit(solution)/shard_map/ppermute | solution.py:266
  32.2 4.9 %collective-permute-start.2 = (f32[16,512]{1,0:T(8,128)S(1)}, f32[16,512]{1,0:T(8,128)S(1)}, u32[]{:S(2)}, u32[]{:S(2)}) collective-permute-start(f32[16,512]{1,0:T(8,128)S(1)} %multiply_add_fusion.1), channel_id=1, source_target_pairs={{0,4},{1,5},{2,6},{3,7},{4,8},{5,9},{6,10},{7,11},{8,12},{9,13},{1... | collective-permute-start | bytes 98312 | tf_op jit(solution)/shard_map/ppermute | solution.py:267
  33.5 4.3 %collective-permute-start.3 = (f32[16,512]{1,0:T(8,128)S(1)}, f32[16,512]{1,0:T(8,128)S(1)}, u32[]{:S(2)}, u32[]{:S(2)}) collective-permute-start(f32[16,512]{1,0:T(8,128)S(1)} %multiply_add_fusion.1), channel_id=1, source_target_pairs={{0,8},{1,9},{2,10},{3,11},{4,12},{5,13},{6,14},{7,15},{8,0},{9,1},... | collective-permute-start | bytes 98312 | tf_op jit(solution)/shard_map/ppermute | solution.py:267
  35.9 2.9 %collective-permute-start.4 = (f32[16,512]{1,0:T(8,128)S(1)}, f32[16,512]{1,0:T(8,128)S(1)}, u32[]{:S(2)}, u32[]{:S(2)}) collective-permute-start(f32[16,512]{1,0:T(8,128)S(1)} %multiply_add_fusion.1), channel_id=1, source_target_pairs={{0,12},{1,13},{2,14},{3,15},{4,0},{5,1},{6,2},{7,3},{8,4},{9,5},{1... | collective-permute-start | bytes 98312 | tf_op jit(solution)/shard_map/ppermute | solution.py:267
  48.3 6.1 %copy-start.1 = (bf16[1024,128]{1,0:T(8,128)(2,1)S(1)}, bf16[1024,128]{1,0:T(8,128)(2,1)}, u32[]{:S(2)}) copy-start(bf16[1024,128]{1,0:T(8,128)(2,1)} %k_ref.1) | copy-start | bytes 786436
  48.3 36.2 %all-to-all-start = ((f32[8,64,1024]{2,1,0:T(8,128)}), f32[8,64,1024]{2,1,0:T(8,128)S(1)}, u32[]{:S(2)}, u32[]{:S(2)}) async-start(f32[8,64,1024]{2,1,0:T(8,128)} %weighted_sum.1), calls=%async_computation | async-start | bytes 4194304 | tf_op jit(solution)/shard_map/all_to_all | solution.py:287
  54.4 27.2 %copy-start.2 = (f32[64,64]{1,0:T(8,128)S(1)}, f32[64,64]{1,0:T(8,128)}, u32[]{:S(2)}) copy-start(f32[64,64]{1,0:T(8,128)} %w_ref.1) | copy-start | bytes 49156
  62.1 4.4 %collective-permute-start.5 = (f32[1,64]{1,0:T(1,128)}, f32[1,64]{1,0:T(1,128)S(1)}, u32[]{:S(2)}, u32[]{:S(2)}) collective-permute-start(f32[1,64]{1,0:T(1,128)} %get-tuple-element.14), channel_id=1, source_target_pairs={{0,1},{1,0},{2,3},{3,2},{4,5},{5,4},{6,7},{7,6},{8,9},{9,8},{10,11... | collective-permute-start | bytes 776 | tf_op jit(solution)/shard_map/ppermute | solution.py:266
  67.2 10.1 %collective-permute-start.6 = (f32[1,64]{1,0:T(1,128)S(1)}, f32[1,64]{1,0:T(1,128)S(1)}, u32[]{:S(2)}, u32[]{:S(2)}) collective-permute-start(f32[1,64]{1,0:T(1,128)S(1)} %multiply_add_fusion.5), channel_id=1, source_target_pairs={{0,2},{1,3},{2,0},{3,1},{4,6},{5,7},{6,4},{7,5},{8,10},{9,11},{10,... | collective-permute-start | bytes 776 | tf_op jit(solution)/shard_map/ppermute | solution.py:266
  77.4 5.3 %collective-permute-start.7 = (f32[1,64]{1,0:T(1,128)S(1)}, f32[1,64]{1,0:T(1,128)S(1)}, u32[]{:S(2)}, u32[]{:S(2)}) collective-permute-start(f32[1,64]{1,0:T(1,128)S(1)} %multiply_add_fusion.4), channel_id=1, source_target_pairs={{0,4},{1,5},{2,6},{3,7},{4,8},{5,9},{6,10},{7,11},{8,12},{9,13},{1... | collective-permute-start | bytes 776 | tf_op jit(solution)/shard_map/ppermute | solution.py:267
  78.0 4.7 %collective-permute-start.8 = (f32[1,64]{1,0:T(1,128)S(1)}, f32[1,64]{1,0:T(1,128)S(1)}, u32[]{:S(2)}, u32[]{:S(2)}) collective-permute-start(f32[1,64]{1,0:T(1,128)S(1)} %multiply_add_fusion.4), channel_id=1, source_target_pairs={{0,8},{1,9},{2,10},{3,11},{4,12},{5,13},{6,14},{7,15},{8,0},{9,1},... | collective-permute-start | bytes 776 | tf_op jit(solution)/shard_map/ppermute | solution.py:267
  81.6 2.4 %collective-permute-start.9 = (f32[1,64]{1,0:T(1,128)S(1)}, f32[1,64]{1,0:T(1,128)S(1)}, u32[]{:S(2)}, u32[]{:S(2)}) collective-permute-start(f32[1,64]{1,0:T(1,128)S(1)} %multiply_add_fusion.4), channel_id=1, source_target_pairs={{0,12},{1,13},{2,14},{3,15},{4,0},{5,1},{6,2},{7,3},{8,4},{9,5},{1... | collective-permute-start | bytes 776 | tf_op jit(solution)/shard_map/ppermute | solution.py:267
  84.5 1.3 copy-start
  121.9 44.2 %all-to-all-start.1 = ((f32[16,72,512]{2,1,0:T(8,128)}), f32[16,72,512]{2,1,0:T(8,128)S(1)}, u32[]{:S(2)}, u32[]{:S(2)}) async-start(f32[16,72,512]{2,1,0:T(8,128)} %get-tuple-element.15), calls=%async_computation.1 | async-start | bytes 4718592 | tf_op jit(solution)/shard_map/all_to_all | solution.py:289

commit v2 on v1

v2 whole, which is shorter than its diff:
```python
import functools
import math

import jax
import jax.numpy as jnp
from jax import lax
from jax.experimental import pallas as pl
from jax.experimental.pallas import tpu as pltpu
from jax.sharding import PartitionSpec as P


H = 128
QK_DIM = 192
LOG2E = 1.4426950408889634
LOW = -1e30
FLOOR = -1e29
CHUNK = 256
GROUP = 4
PARTS = 2
MASKS = (1, 3, 4)
MASKS_OF = [(r >> 2) * MASKS[0] ^ (r >> 1 & 1) * MASKS[1] ^ (r & 1) * MASKS[2] for r in range(8)]


def eye_of(n):
    rows = lax.broadcasted_iota(jnp.int32, (n, n), 0)
    return rows == lax.broadcasted_iota(jnp.int32, (n, n), 1)


def as_column(row):
    n = row.shape[1]
    return jnp.sum(jnp.where(eye_of(n), row, jnp.zeros_like(row)), axis=1, keepdims=True)


def as_row(column):
    n = column.shape[0]
    return jnp.sum(jnp.where(eye_of(n), column, jnp.zeros_like(column)), axis=0, keepdims=True)


def main_kernel(base_ref, kt_ref, qt_ref, start_ref, pos_ref, e_ref, m_ref, lse_ref, k_ref, bias_ref, part_ref):
    h = pl.program_id(0)
    keys, queries = bias_ref.shape
    chunks = keys // CHUNK
    scale = LOG2E / math.sqrt(QK_DIM)

    @pl.when(h == 0)
    def _():
        k_ref[...] = kt_ref[...].T
        s = base_ref[0] + lax.broadcasted_iota(jnp.int32, (keys, queries), 0)
        seen = (s >= start_ref[...]) & (s <= pos_ref[...])
        bias_ref[...] = jnp.where(seen, 0.0, LOW)

    qt = qt_ref[0]
    highs, sums = [], []
    for c in range(chunks):
        here = pl.ds(c * CHUNK, CHUNK)
        s = jnp.dot(k_ref[here, :], qt, preferred_element_type=jnp.float32)
        s = s * scale + bias_ref[here, :]
        high = jnp.maximum(jnp.max(s, axis=0, keepdims=True), FLOOR)
        e = jnp.exp2(s - high)
        e_ref[0, here, :] = e.astype(jnp.bfloat16)
        highs.append(high)
        sums.append(jnp.sum(e, axis=0, keepdims=True))
        m_ref[pl.ds(h * chunks + c, 1), :] = high
    top = functools.reduce(jnp.maximum, highs)
    total = sum(l * jnp.exp2(m - top) for l, m in zip(sums, highs))
    part_ref[pl.ds(h, 1), :] = jnp.where(total > 0.0, top + jnp.log2(total), FLOOR)

    @pl.when(h == pl.num_programs(0) - 1)
    def _():
        for i in range(lse_ref.shape[0]):
            lse_ref[i] = part_ref[...]


def main_forward(base, kt, qt, start, pos, peers):
    heads, lat, queries = qt.shape
    keys = kt.shape[1]
    chunks = keys // CHUNK
    return pl.pallas_call(
        main_kernel,
        grid=(heads,),
        in_specs=[
            pl.BlockSpec(memory_space=pltpu.SMEM),
            pl.BlockSpec((lat, keys), lambda h: (0, 0)),
            pl.BlockSpec((1, lat, queries), lambda h: (h, 0, 0)),
            pl.BlockSpec((1, queries), lambda h: (0, 0)),
            pl.BlockSpec((1, queries), lambda h: (0, 0)),
        ],
        out_specs=[
            pl.BlockSpec((1, keys, queries), lambda h: (h, 0, 0)),
            pl.BlockSpec((heads * chunks, queries), lambda h: (0, 0)),
            pl.BlockSpec((peers, heads, queries), lambda h: (0, 0, 0)),
        ],
        out_shape=[
            jax.ShapeDtypeStruct((heads, keys, queries), jnp.bfloat16),
            jax.ShapeDtypeStruct((heads * chunks, queries), jnp.float32),
            jax.ShapeDtypeStruct((peers, heads, queries), jnp.float32),
        ],
        scratch_shapes=[
            pltpu.VMEM((keys, lat), jnp.bfloat16),
            pltpu.VMEM((keys, queries), jnp.float32),
            pltpu.VMEM((heads, queries), jnp.float32),
        ],
        cost_estimate=pl.CostEstimate(
            flops=2 * heads * keys * queries * lat, bytes_accessed=26 << 20, transcendentals=heads * keys * queries
        ),
        name="main_forward",
    )(base, kt, qt, start, pos)


def index_kernel(base_ref, q_ref, kt_ref, w_ref, start_ref, pos_ref, s_ref, lse_ref):
    c = pl.program_id(0)
    rows, width = s_ref.shape[0], CHUNK
    heads = w_ref.shape[1]
    dim = kt_ref.shape[0]
    here = pl.ds(pl.multiple_of(c * width, width), width)
    kt = kt_ref[:, here]
    total = jnp.zeros((rows, width), jnp.float32)
    for j in range(heads):
        d = jnp.dot(q_ref[:, j * dim : (j + 1) * dim], kt, preferred_element_type=jnp.float32)
        total = total + w_ref[:, j : j + 1] * jnp.maximum(d, 0.0)
    s = base_ref[0] + c * width + lax.broadcasted_iota(jnp.int32, (rows, width), 1)
    seen = (s >= as_column(start_ref[...])) & (s <= as_column(pos_ref[...]))
    s_ref[:, here] = jnp.where(seen, total * (LOG2E / math.sqrt(dim)), LOW)

    @pl.when(c == pl.num_programs(0) - 1)
    def _():
        scores = s_ref[...]
        high = jnp.maximum(jnp.max(scores, axis=1, keepdims=True), FLOOR)
        total = jnp.sum(jnp.exp2(scores - high), axis=1, keepdims=True)
        lse_ref[...] = as_row(jnp.where(total > 0.0, high + jnp.log2(total), FLOOR))


def index_forward(base, q, kt, w, start, pos):
    rows, width = q.shape
    dim, keys = kt.shape
    heads = w.shape[1]
    whole = lambda *shape: pl.BlockSpec(shape, lambda c: (0,) * len(shape))
    return pl.pallas_call(
        index_kernel,
        grid=(keys // CHUNK,),
        in_specs=[
            pl.BlockSpec(memory_space=pltpu.SMEM),
            whole(rows, width),
            whole(dim, keys),
            whole(rows, heads),
            whole(1, rows),
            whole(1, rows),
        ],
        out_specs=[whole(rows, keys), whole(1, rows)],
        out_shape=[
            jax.ShapeDtypeStruct((rows, keys), jnp.float32),
            jax.ShapeDtypeStruct((1, rows), jnp.float32),
        ],
        cost_estimate=pl.CostEstimate(flops=2 * rows * width * keys, bytes_accessed=2 << 20, transcendentals=rows * keys),
        name="index_forward",
    )(base, q, kt, w, start, pos)


def sum_kernel(first, e_ref, m_ref, stats_ref, t_ref, lse_ref):
    c = pl.program_id(0)
    heads, width, queries = e_ref.shape
    rows = t_ref.shape[1]
    chunks = m_ref.shape[0] // heads
    lanes = 128

    @pl.when(c == 0)
    def _():
        stats = [stats_ref[i] for i in range(stats_ref.shape[0])]
        high = functools.reduce(jnp.maximum, stats)
        lse_ref[...] = high + jnp.log2(sum(jnp.exp2(x - high) for x in stats))

    chunk = (first + c) * width // CHUNK
    weights = [jnp.exp2(m_ref[pl.ds(h * chunks + chunk, 1), :] - lse_ref[h : h + 1, :]) for h in range(heads)]
    for b in range(queries // lanes):
        cols = slice(b * lanes, (b + 1) * lanes)
        total = e_ref[0, :, cols].astype(jnp.float32) * weights[0][:, cols]
        for h in range(1, heads):
            total = total + e_ref[h, :, cols].astype(jnp.float32) * weights[h][:, cols]
        flipped = total.T
        for o in range(lanes // rows):
            t_ref[b * (lanes // rows) + o] = flipped[o * rows : (o + 1) * rows]


def weighted_sum(e, m, stats, owners, part):
    heads, keys, queries = e.shape
    rows = queries // owners
    width = 128
    steps = keys // PARTS // width
    first = part * steps
    return pl.pallas_call(
        functools.partial(sum_kernel, first),
        grid=(steps,),
        in_specs=[
            pl.BlockSpec((heads, width, queries), lambda c: (0, first + c, 0)),
            pl.BlockSpec(m.shape, lambda c: (0, 0)),
            pl.BlockSpec(stats.shape, lambda c: (0, 0, 0)),
        ],
        out_specs=pl.BlockSpec((owners, rows, width), lambda c: (0, 0, c)),
        out_shape=jax.ShapeDtypeStruct((owners, rows, keys // PARTS), jnp.float32),
        scratch_shapes=[pltpu.VMEM((heads, queries), jnp.float32)],
        cost_estimate=pl.CostEstimate(
            flops=2 * heads * keys * queries // PARTS, bytes_accessed=18 << 19, transcendentals=heads * queries
        ),
    )(e, m, stats)


def back_kernel(has_former, has_keys, splits, *refs):
    place_ref, t_ref, s_ref, stats_ref, c_ref, q_ref, k_ref, kt_ref, w_ref, *refs = refs
    if has_former:
        former_ref, *refs = refs
    if has_keys:
        fk_ref, *refs = refs
    gq_ref, gk_ref, g_ref, gkt_ref, turned_ref = refs
    i = pl.program_id(0)
    rows, _ = g_ref.shape
    dim = kt_ref.shape[0]
    index_scale = 1.0 / math.sqrt(dim)

    @pl.when(i == 0)
    def _():
        target = jnp.sum(t_ref[...], axis=0) * (1.0 / H)
        scores = s_ref[...]
        probs = jnp.exp2(scores - as_column(stats_ref[...]))
        g_ref[...] = jnp.where(scores > FLOOR, as_column(c_ref[...]) * (probs - target), 0.0)
        gkt_ref[...] = jnp.zeros_like(gkt_ref)

    q = jnp.concatenate([q_ref[:, j * dim : (j + 1) * dim] for j in range(GROUP)], axis=0)
    d = jnp.dot(q, kt_ref[...], preferred_element_type=jnp.float32)
    g = g_ref[...]
    parts, sums = [], []
    for j in range(GROUP):
        dots = d[j * rows : (j + 1) * rows]
        kept = jnp.where(dots > 0.0, g, 0.0)
        coef = w_ref[0][:, j : j + 1] * index_scale
        parts.append((kept * coef).astype(jnp.bfloat16))
        sums.append(as_row(jnp.sum(kept * dots, axis=1, keepdims=True)))
    head_grad = jnp.concatenate(parts, axis=0)
    gq = jnp.dot(head_grad, k_ref[...], preferred_element_type=jnp.float32)
    pad = jnp.zeros((1, dim * GROUP - rows), jnp.float32)
    low = jnp.concatenate([jnp.concatenate([x * index_scale, pad], axis=1) for x in sums], axis=0)
    low = jnp.concatenate([low, jnp.zeros((8 - GROUP, dim * GROUP), jnp.float32)], axis=0)
    gq = jnp.concatenate([gq[j * rows : (j + 1) * rows] for j in range(GROUP)], axis=1)
    if has_former:
        gq, low = gq + former_ref[0, :rows], low + former_ref[0, rows:]
    gq_ref[0, :rows] = gq
    gq_ref[0, rows:] = low
    gkt_ref[...] += lax.dot_general(q, head_grad, (((0,), (0,)), ((), ())), preferred_element_type=jnp.float32)

    @pl.when(i == pl.num_programs(0) - 1)
    def _():
        gk = gkt_ref[...].T.reshape(turned_ref.shape)
        if has_keys:
            gk = gk + fk_ref[...]
        if splits:
            turned_ref[...] = gk
            for r in range(len(MASKS_OF)):
                gk_ref[r] = turned_ref[place_ref[1] ^ MASKS_OF[r]]
        else:
            gk_ref[...] = gk


def backward(place, t, s, stats, c, q, k, kt, w, part, dests, owners, former=None, gk=None):
    rows, width = q.shape
    keys, dim = k.shape
    keys = keys // PARTS
    steps = width // (dim * GROUP)
    count = steps if dests is None else steps // 2
    if dests is None:
        dest = lambda i, place: i
    elif dests == "far":
        dest = lambda i, place: 2 * i + 1 - place[0]
    else:
        dest = lambda i, place: 2 * i + place[0]
    whole = lambda *shape: pl.BlockSpec(shape, lambda i, place: (0,) * len(shape))
    w = jnp.moveaxis(w.reshape(rows, steps, GROUP), 1, 0)
    block = (1, rows + 8, dim * GROUP)
    in_specs = [
        whole(*t.shape),
        pl.BlockSpec((rows, keys), lambda i, place: (0, part)),
        whole(*stats.shape),
        whole(1, rows),
        pl.BlockSpec((rows, dim * GROUP), lambda i, place: (0, dest(i, place))),
        pl.BlockSpec((keys, dim), lambda i, place: (part, 0)),
        pl.BlockSpec((dim, keys), lambda i, place: (0, part)),
        pl.BlockSpec((1, rows, GROUP), lambda i, place: (dest(i, place), 0, 0)),
    ]
    args = [t, s, stats, c, q, k, kt, w]
    if former is not None:
        in_specs.append(pl.BlockSpec(block, lambda i, place: (dest(i, place), 0, 0)))
        args.append(former)
    shape = (owners, keys // owners, dim)
    if gk is not None:
        in_specs.append(whole(*shape))
        args.append(gk)
    return pl.pallas_call(
        functools.partial(back_kernel, former is not None, gk is not None, dests != "far"),
        grid_spec=pltpu.PrefetchScalarGridSpec(
            num_scalar_prefetch=1,
            grid=(count,),
            in_specs=in_specs,
            out_specs=[pl.BlockSpec(block, lambda i, place: (i, 0, 0)), whole(*shape)],
            scratch_shapes=[
                pltpu.VMEM((rows, keys), jnp.float32),
                pltpu.VMEM((dim, keys), jnp.float32),
                pltpu.VMEM(shape, jnp.float32),
            ],
        ),
        out_shape=[
            jax.ShapeDtypeStruct((count, rows + 8, dim * GROUP), jnp.float32),
            jax.ShapeDtypeStruct(shape, jnp.float32),
        ],
        cost_estimate=pl.CostEstimate(
            flops=6 * rows * width * keys * count // steps, bytes_accessed=4 << 20, transcendentals=rows * keys
        ),
    )(place, *args)


def end_kernel(x_ref, gq_ref, gw_ref):
    rows = gq_ref.shape[0]
    total = jnp.sum(x_ref[...], axis=0)
    gq_ref[...] = total[:rows]
    gw_ref[...] = total[rows : rows + GROUP, :rows]


def ended(x):
    _, rows, width = x.shape
    rows -= 8
    return pl.pallas_call(
        end_kernel,
        out_shape=[
            jax.ShapeDtypeStruct((rows, width), jnp.float32),
            jax.ShapeDtypeStruct((GROUP, rows), jnp.float32),
        ],
        name="end",
    )(x)


def join_kernel(place_ref, near_ref, far_ref, out_ref):
    half = near_ref.shape[0]
    parts, _, rows, _ = out_ref.shape
    for n, ref in enumerate((near_ref, far_ref)):
        for r in range(half):
            for p in range(parts):
                out_ref[p, place_ref[1] ^ MASKS_OF[n * half + r]] = ref[r, p * rows : (p + 1) * rows]


def joined(place, near, far):
    half, rows, dim = near.shape
    vmem = pl.BlockSpec(memory_space=pltpu.VMEM)
    return pl.pallas_call(
        join_kernel,
        in_specs=[pl.BlockSpec(memory_space=pltpu.SMEM), vmem, vmem],
        out_specs=vmem,
        out_shape=jax.ShapeDtypeStruct((PARTS, 2 * half, rows // PARTS, dim), jnp.float32),
        name="join",
    )(place, near, far)


def exchanged(x, axis, groups=None):
    return lax.all_to_all(x, axis, 0, 0, axis_index_groups=groups, tiled=True)


def flipped(x, axis, mask):
    return lax.ppermute(x, axis, [(i, i ^ mask) for i in range(lax.axis_size(axis))])


def summed(x):
    for mask in MASKS:
        half = x.shape[0] // 2
        x = x[:half] + flipped(x[half:], "head", mask)
    return x


def gathered(x):
    for mask in MASKS[:0:-1]:
        x = jnp.concatenate([x, flipped(x, "head", mask)], axis=0)
    return x, flipped(x, "head", MASKS[0])


def joined_lse(a, b):
    high = jnp.maximum(a, b)
    return high + jnp.log2(jnp.exp2(a - high) + jnp.exp2(b - high))


def joined_over_key(x):
    n = lax.axis_size("key")
    for mask in (1, 2):
        x = joined_lse(x, flipped(x, "key", mask))
    others = [lax.ppermute(x, "key", [(i, (i + 4 * k) % n) for i in range(n)]) for k in (1, 2, 3)]
    high = functools.reduce(jnp.maximum, others, x)
    return high + jnp.log2(sum(jnp.exp2(y - high) for y in [x, *others]))


def shards(q_latent, k_latent, q_index, k_index, head_weight, loss_weight, query_pos, key_start):
    keys = k_latent.shape[0]
    rows = q_index.shape[0]
    owners, peers = lax.axis_size("head"), lax.axis_size("key")
    at_key, at_head = (lax.axis_index(name).astype(jnp.int32) for name in ("key", "head"))
    base, place = (at_key * keys).reshape(1), jnp.stack([at_key % 2, at_head])
    own = at_head * rows
    start, pos = key_start.reshape(1, -1), query_pos.reshape(1, -1)
    own_start = lax.dynamic_slice_in_dim(start, own, rows, axis=1)
    own_pos = lax.dynamic_slice_in_dim(pos, own, rows, axis=1)
    kt_index = k_index.T
    e, high, lse = main_forward(base, k_latent.T, jnp.swapaxes(q_latent, 1, 2), start, pos, peers)
    stats = exchanged(lse, "key")
    scores, index_lse = index_forward(base, q_index, kt_index, head_weight, own_start, own_pos)
    targets = []
    for part in range(PARTS):
        partial = weighted_sum(e, high, stats, owners, part)
        targets.append(exchanged(partial, "head"))
    index_stats = joined_over_key(index_lse)

    def back(part, dests, *former):
        fixed = (scores, index_stats, loss_weight.reshape(1, -1), q_index, k_index, kt_index, head_weight)
        return backward(place, targets[part], *fixed, part, dests, owners, *former)

    gq_0, gk_0 = back(0, None)
    gk_0 = summed(gk_0)
    targets[1], gk_0 = lax.optimization_barrier((targets[1], gk_0))
    far, gk_1 = back(1, "far", gq_0)
    moved = flipped(far, "key", 1)
    near, gk_1 = back(1, "near", gq_0, gk_1)
    groups = [list(range(c, peers, 2)) for c in (0, 1)]
    gq = exchanged(near + moved, "key", groups)
    gk_1 = summed(gk_1)
    gk = joined(place, *gathered(jnp.concatenate([gk_0, gk_1], axis=1))).reshape(keys, -1)
    gq, gw = ended(gq)
    return (gq, gk, gw.T)


def solution(mesh):
    return jax.shard_map(
        shards,
        mesh=mesh,
        in_specs=(
            P("head", None, None),
            P("key", None),
            P("head", None),
            P("key", None),
            P("head", None),
            P("head"),
            P(),
            P(),
        ),
        out_specs=(P("head", "key"), P("key", None), P("head", "key")),
        check_vma=False,
    )
```

time: 170 us -> 200 us (1.18)
  the two profiles are of different devices: /device:TPU:1 before, /device:TPU:4 now
where the time goes in v2:
time: 200 us; the launch traced here: 198 us
  Pallas kernels  76.6 us (38%)
  waiting for transfers between devices  65.1 us (33%)
  starting transfers between devices  40.4 us (20%)
  local copies, waits for them, and re-layouts  9.68 us (5%)
  other arithmetic  5.29 us (3%)
    ppermute x12, waiting for transfers between devices, flipped(): lax.ppermute(x, axis, [(i, i ^ mask) for i in range(lax.axis_size(axis))])  54.5 us
    pallas_call x3, Pallas kernels, backward(): pl.pallas_call(functools.partial(back_kernel, former is not None, gk is n...  30.9 us
    pallas_call x1, Pallas kernels, main_forward(): pl.pallas_call(main_kernel, grid=(heads,), in_specs=[pl.BlockSpec(memory_...  24 us
    all_to_all x4, starting transfers between devices, exchanged(): return lax.all_to_all(x, axis, 0, 0, axis_index_groups=groups, tiled=True)  23.3 us
    pallas_call x2, Pallas kernels, weighted_sum(): pl.pallas_call(functools.partial(sum_kernel, first), grid=(steps,), in_sp...  12.2 us
    ppermute x12, starting transfers between devices, flipped(): lax.ppermute(x, axis, [(i, i ^ mask) for i in range(lax.axis_size(axis))])  11.9 us
    all_to_all x4, waiting for transfers between devices, exchanged(): return lax.all_to_all(x, axis, 0, 0, axis_index_groups=groups, tiled=True)  9.87 us
    pallas_call x1, Pallas kernels, index_forward(): pl.pallas_call(index_kernel, grid=(keys // CHUNK,), in_specs=[pl.BlockSpe...  5.62 us
  transfers between devices with their start and end apart: 19, of which 11 were waited for; matrix products, arithmetic and copies ran while one was open for 5% of the time, Pallas kernels for 11%

profile of v2, /device:TPU:4, one launch (start us, length us, event | category | flops | bytes accessed | tf_op | source)
XLA Modules:
  0.0 197.8 jit_solution(8851867457144259387)
XLA Ops:
  0.6 24.0 %main_forward.1 = (bf16[16,1024,512]{2,1,0:T(8,128)(2,1)}, f32[64,512]{1,0:T(8,128)}, f32[16,16,512]{2,1,0:T(8,128)}) custom-call(s32[1]{0:T(128)} %bitcast.2.base_ref, bf16[576,1024]{1,0:T(8,128)(2,1)} %bitcast.32, bf16[16,576,512]{2,1,0:T(8,128)(2,1)} %bitcast.31, s32[1,512]{1,0:T(1,128)} %bitcast.29, s32[1,512]{1,0:T(1,128)} %bitcast.30), custom_call_target="tpu_custom_call" | custom-call | flops 9663676416 | bytes 27262976 | tf_op jit(solution)/shard_map/main_forward/pallas_call | solution.py:78
  24.6 7.5 %all-to-all-start = ((f32[16,16,512]{2,1,0:T(8,128)}), f32[16,16,512]{2,1,0:T(8,128)S(1)}, u32[]{:S(2)}, u32[]{:S(2)}) async-start(f32[16,16,512]{2,1,0:T(8,128)} %get-tuple-element.20), calls=%async_computation | async-start | bytes 1048576 | tf_op jit(solution)/shard_map/all_to_all | solution.py:360
  32.1 9.9 %all-to-all-done.stats_ref = f32[16,16,512]{2,1,0:T(8,128)S(1)} async-done(((f32[16,16,512]{2,1,0:T(8,128)}), f32[16,16,512]{2,1,0:T(8,128)S(1)}, u32[]{:S(2)}, u32[]{:S(2)}) %all-to-all-start) | async-done | bytes 524320 | tf_op jit(solution)/shard_map/all_to_all | solution.py:360
  41.9 0.8 copy-done.1
  42.7 6.1 %shard_map.104 = f32[8,64,512]{2,1,0:T(8,128)} custom-call(bf16[16,1024,512]{2,1,0:T(8,128)(2,1)} %get-tuple-element.18.e_ref, f32[64,512]{1,0:T(8,128)} %get-tuple-element.19.m_ref, f32[16,16,512]{2,1,0:T(8,128)} %copy-done.1), custom_call_target="tpu_custom_call" | custom-call | flops 8388608 | bytes 9437184 | tf_op jit(solution)/shard_map/pallas_call | solution.py:190
  48.9 5.6 %all-to-all-start.2 = ((f32[8,64,512]{2,1,0:T(8,128)}), f32[8,64,512]{2,1,0:T(8,128)S(1)}, u32[]{:S(2)}, u32[]{:S(2)}) async-start(f32[8,64,512]{2,1,0:T(8,128)} %shard_map.104), calls=%async_computation.2 | async-start | bytes 2097152 | tf_op jit(solution)/shard_map/all_to_all | solution.py:360
  54.4 1.3 dynamic-slice_bitcast_fusion
  55.8 0.9 copy.12
  56.6 5.6 %index_forward.1 = (f32[64,1024]{1,0:T(8,128)}, f32[1,64]{1,0:T(1,128)}) custom-call(s32[1]{0:T(128)} %bitcast.2.base_ref, bf16[64,8192]{1,0:T(8,128)(2,1)} %refs_5_.5, bf16[128,1024]{1,0:T(8,128)(2,1)} %bitcast.20, f32[64,64]{1,0:T(8,128)} %w_ref.1, s32[1,64]{1,0:T(1,128)} %get-tuple-element.34.start_ref, s32[1,64]{1,0:T(1,128)} %get-tuple-element.33.pos_ref), custom_call_target="tpu_custom_call" | custom-call | flops 1073741824 | bytes 2097152 | tf_op jit(solution)/shard_map/index_forward/pallas_call | solution.py:138
  62.2 1.4 collective-permute-done
  63.6 0.6 multiply_add_fusion.2
  64.2 1.4 collective-permute-start.1
  65.6 0.6 pad_add_fusion.refs_0_.place_ref
  66.2 3.1 %collective-permute-done.1 = f32[1,64]{1,0:T(1,128)S(1)} collective-permute-done((f32[1,64]{1,0:T(1,128)S(1)}, f32[1,64]{1,0:T(1,128)S(1)}, u32[]{:S(2)}, u32[]{:S(2)}) %collective-permute-start.1) | collective-permute-done | bytes 288 | tf_op jit(solution)/shard_map/ppermute | solution.py:364
  69.4 0.8 collective-permute-start.4
  70.1 2.7 %collective-permute-start.3 = (f32[1,64]{1,0:T(1,128)S(1)}, f32[1,64]{1,0:T(1,128)S(1)}, u32[]{:S(2)}, u32[]{:S(2)}) collective-permute-start(f32[1,64]{1,0:T(1,128)S(1)} %multiply_add_fusion.1), channel_id=1, source_target_pairs={{0,8},{1,9},{2,10},{3,11},{4,12},{5,13},{6,14},{7,15},{8,0},{9,1},... | collective-permute-start | bytes 776 | tf_op jit(solution)/shard_map/ppermute | solution.py:389
  72.9 1.8 collective-permute-start.2
  74.7 1.1 copy.14
  75.8 0.7 collective-permute-done.2
  77.0 1.0 copy-done.4
  77.9 13.5 %shard_map.105 = (f32[16,72,512]{2,1,0:T(8,128)}, f32[8,64,128]{2,1,0:T(8,128)}) custom-call(s32[2]{0:T(128)} %pad_add_fusion.refs_0_.place_ref, f32[8,64,512]{2,1,0:T(8,128)} %copy-done.4, f32[64,1024]{1,0:T(8,128)} %get-tuple-element.21.refs_2_, f32[1,64]{1,0:T(1,128)} %multiply_add_fusion.refs_3_, f32[1,64]{1,0:T(1,128)} %bitcast.26, ...), custom_call_target="tpu_custom_call" | custom-call | flops 1610612736 | bytes 4194304 | tf_op jit(solution)/shard_map/pallas_call | solution.py:295
  91.5 0.9 slice.37
  92.4 2.1 %collective-permute-start.5 = (f32[4,64,128]{2,1,0:T(8,128)S(1)}, f32[4,64,128]{2,1,0:T(8,128)S(1)}, u32[]{:S(2)}, u32[]{:S(2)}) collective-permute-start(f32[4,64,128]{2,1,0:T(8,128)S(1)} %slice.37), channel_id=1, source_target_pairs={{0,16},{16,0},{32,48},{48,32},{64,80},{80,64},{96,112},{112,96},{1... | collective-permute-start | bytes 393224 | tf_op jit(solution)/shard_map/ppermute | solution.py:364
  94.5 6.1 %shard_map.103 = f32[8,64,512]{2,1,0:T(8,128)} custom-call(bf16[16,1024,512]{2,1,0:T(8,128)(2,1)} %get-tuple-element.18.e_ref, f32[64,512]{1,0:T(8,128)} %get-tuple-element.19.m_ref, f32[16,16,512]{2,1,0:T(8,128)} %copy-done.1), custom_call_target="tpu_custom_call" | custom-call | flops 8388608 | bytes 9437184 | tf_op jit(solution)/shard_map/pallas_call | solution.py:190
  100.6 5.0 %all-to-all-start.1 = ((f32[8,64,512]{2,1,0:T(8,128)}), f32[8,64,512]{2,1,0:T(8,128)S(1)}, u32[]{:S(2)}, u32[]{:S(2)}) async-start(f32[8,64,512]{2,1,0:T(8,128)} %shard_map.103), calls=%async_computation.1 | async-start | bytes 2097152 | tf_op jit(solution)/shard_map/all_to_all | solution.py:360
  105.6 3.3 %collective-permute-start.6 = (f32[2,64,128]{2,1,0:T(8,128)S(1)}, f32[2,64,128]{2,1,0:T(8,128)S(1)}, u32[]{:S(2)}, u32[]{:S(2)}) collective-permute-start(f32[2,64,128]{2,1,0:T(8,128)S(1)} %slice.49), channel_id=1, source_target_pairs={{0,48},{16,32},{32,16},{48,0},{64,112},{80,96},{96,80},{112,64},{1... | collective-permute-start | bytes 196616 | tf_op jit(solution)/shard_map/ppermute | solution.py:364
  108.9 10.3 %collective-permute-done.6 = f32[2,64,128]{2,1,0:T(8,128)S(1)} collective-permute-done((f32[2,64,128]{2,1,0:T(8,128)S(1)}, f32[2,64,128]{2,1,0:T(8,128)S(1)}, u32[]{:S(2)}, u32[]{:S(2)}) %collective-permute-start.6) | collective-permute-done | bytes 65568 | tf_op jit(solution)/shard_map/ppermute | solution.py:364
  119.2 1.5 collective-permute-start.7
  120.8 2.4 %collective-permute-done.7 = f32[1,64,128]{2,1,0:T(8,128)S(1)} collective-permute-done((f32[1,64,128]{2,1,0:T(8,128)S(1)}, f32[1,64,128]{2,1,0:T(8,128)S(1)}, u32[]{:S(2)}, u32[]{:S(2)}) %collective-permute-start.7) | collective-permute-done | bytes 32800 | tf_op jit(solution)/shard_map/ppermute | solution.py:364
  123.2 1.0 copy-done
  124.2 8.6 %shard_map.106 = (f32[8,72,512]{2,1,0:T(8,128)}, f32[8,64,128]{2,1,0:T(8,128)}) custom-call(s32[2]{0:T(128)} %pad_add_fusion.refs_0_.place_ref, f32[8,64,512]{2,1,0:T(8,128)} %copy-done, f32[64,1024]{1,0:T(8,128)} %get-tuple-element.21.refs_2_, f32[1,64]{1,0:T(1,128)} %multiply_add_fusion.refs_3_, f32[1,64]{1,0:T(1,128)} %bitcast.27, ...), custom_call_target="tpu_custom_call" | custom-call | flops 805306368 | bytes 4194304 | tf_op jit(solution)/shard_map/pallas_call | solution.py:295
  132.8 8.8 %shard_map.107 = (f32[8,72,512]{2,1,0:T(8,128)}, f32[8,64,128]{2,1,0:T(8,128)}) custom-call(s32[2]{0:T(128)} %pad_add_fusion.refs_0_.place_ref, f32[8,64,512]{2,1,0:T(8,128)} %copy-done, f32[64,1024]{1,0:T(8,128)} %get-tuple-element.21.refs_2_, f32[1,64]{1,0:T(1,128)} %multiply_add_fusion.refs_3_, f32[1,64]{1,0:T(1,128)} %bitcast.28, ...), custom_call_target="tpu_custom_call" | custom-call | flops 805306368 | bytes 4194304 | tf_op jit(solution)/shard_map/pallas_call | solution.py:295
  141.6 0.9 slice.43
  142.8 5.7 %collective-permute-done.9 = f32[4,64,128]{2,1,0:T(8,128)S(1)} collective-permute-done((f32[4,64,128]{2,1,0:T(8,128)S(1)}, f32[4,64,128]{2,1,0:T(8,128)S(1)}, u32[]{:S(2)}, u32[]{:S(2)}) %collective-permute-start.9) | collective-permute-done | bytes 131104 | tf_op jit(solution)/shard_map/ppermute | solution.py:364
  148.5 0.9 slice_add_fusion
  149.8 5.2 %collective-permute-done.10 = f32[2,64,128]{2,1,0:T(8,128)S(1)} collective-permute-done((f32[2,64,128]{2,1,0:T(8,128)S(1)}, f32[2,64,128]{2,1,0:T(8,128)S(1)}, u32[]{:S(2)}, u32[]{:S(2)}) %collective-permute-start.10) | collective-permute-done | bytes 65568 | tf_op jit(solution)/shard_map/ppermute | solution.py:364
  155.0 1.5 collective-permute-start.11
  156.6 2.6 %add.66 = f32[8,72,512]{2,1,0:T(8,128)} add(f32[8,72,512]{2,1,0:T(8,128)} %get-tuple-element.27, f32[8,72,512]{2,1,0:T(8,128)S(1)} %collective-permute-done.8) | non-fusion elementwise | flops 294912 | bytes 3538944 | tf_op jit(solution)/shard_map/add | solution.py:425
  159.1 5.3 %all-to-all-start.3 = ((f32[8,72,512]{2,1,0:T(8,128)}), f32[8,72,512]{2,1,0:T(8,128)S(1)}, u32[]{:S(2)}, u32[]{:S(2)}) async-start(f32[8,72,512]{2,1,0:T(8,128)} %add.66), calls=%async_computation.3 | async-start | bytes 2359296 | tf_op jit(solution)/shard_map/all_to_all | solution.py:360
  164.5 0.6 collective-permute-start.12
  165.1 12.9 %collective-permute-done.12 = f32[1,128,128]{2,1,0:T(8,128)S(1)} collective-permute-done((f32[1,128,128]{2,1,0:T(8,128)S(1)}, f32[1,128,128]{2,1,0:T(8,128)S(1)}, u32[]{:S(2)}, u32[]{:S(2)}) %collective-permute-start.12) | collective-permute-done | bytes 65568 | tf_op jit(solution)/shard_map/ppermute | solution.py:364
  178.0 0.5 collective-permute-start.13
  178.5 6.2 %collective-permute-done.13 = f32[2,128,128]{2,1,0:T(8,128)S(1)} collective-permute-done((f32[2,128,128]{2,1,0:T(8,128)S(1)}, f32[2,128,128]{2,1,0:T(8,128)S(1)}, u32[]{:S(2)}, u32[]{:S(2)}) %collective-permute-start.13) | collective-permute-done | bytes 131104 | tf_op jit(solution)/shard_map/ppermute | solution.py:364
  184.8 7.4 %collective-permute-done.14.far_ref = f32[4,128,128]{2,1,0:T(8,128)S(1)} collective-permute-done((f32[4,128,128]{2,1,0:T(8,128)S(1)}, f32[4,128,128]{2,1,0:T(8,128)S(1)}, u32[]{:S(2)}, u32[]{:S(2)}) %collective-permute-start.14) | collective-permute-done | bytes 262176 | tf_op jit(solution)/shard_map/ppermute | solution.py:364
  192.2 0.7 copy-done.7
  192.9 1.9 join.1
  194.8 1.1 copy-done.2
  195.8 2.0 end.1
  (41 shorter events, 1.6 us)
Async XLA Ops:
  24.6 17.3 %all-to-all-start = ((f32[16,16,512]{2,1,0:T(8,128)}), f32[16,16,512]{2,1,0:T(8,128)S(1)}, u32[]{:S(2)}, u32[]{:S(2)}) async-start(f32[16,16,512]{2,1,0:T(8,128)} %get-tuple-element.20), calls=%async_computation | async-start | bytes 1048576 | tf_op jit(solution)/shard_map/all_to_all | solution.py:360
  41.9 0.8 copy-start.1
  48.9 6.9 %copy-start.3 = (bf16[1024,128]{1,0:T(8,128)(2,1)S(1)}, bf16[1024,128]{1,0:T(8,128)(2,1)}, u32[]{:S(2)}) copy-start(bf16[1024,128]{1,0:T(8,128)(2,1)} %refs_6_.5) | copy-start | bytes 786436
  48.9 28.1 %all-to-all-start.2 = ((f32[8,64,512]{2,1,0:T(8,128)}), f32[8,64,512]{2,1,0:T(8,128)S(1)}, u32[]{:S(2)}, u32[]{:S(2)}) async-start(f32[8,64,512]{2,1,0:T(8,128)} %shard_map.104), calls=%async_computation.2 | async-start | bytes 2097152 | tf_op jit(solution)/shard_map/all_to_all | solution.py:360
  56.6 18.0 %copy-start.8 = (f32[64,64]{1,0:T(8,128)S(1)}, f32[64,64]{1,0:T(8,128)}, u32[]{:S(2)}) copy-start(f32[64,64]{1,0:T(8,128)} %w_ref.1) | copy-start | bytes 49156
  62.2 1.4 collective-permute-start
  64.2 5.2 %collective-permute-start.1 = (f32[1,64]{1,0:T(1,128)S(1)}, f32[1,64]{1,0:T(1,128)S(1)}, u32[]{:S(2)}, u32[]{:S(2)}) collective-permute-start(f32[1,64]{1,0:T(1,128)S(1)} %multiply_add_fusion.2), channel_id=1, source_target_pairs={{0,2},{1,3},{2,0},{3,1},{4,6},{5,7},{6,4},{7,5},{8,10},{9,11},{10,... | collective-permute-start | bytes 776 | tf_op jit(solution)/shard_map/ppermute | solution.py:364
  69.4 6.4 %collective-permute-start.4 = (f32[1,64]{1,0:T(1,128)S(1)}, f32[1,64]{1,0:T(1,128)S(1)}, u32[]{:S(2)}, u32[]{:S(2)}) collective-permute-start(f32[1,64]{1,0:T(1,128)S(1)} %multiply_add_fusion.1), channel_id=1, source_target_pairs={{0,12},{1,13},{2,14},{3,15},{4,0},{5,1},{6,2},{7,3},{8,4},{9,5},{1... | collective-permute-start | bytes 776 | tf_op jit(solution)/shard_map/ppermute | solution.py:389
  70.1 5.6 %collective-permute-start.3 = (f32[1,64]{1,0:T(1,128)S(1)}, f32[1,64]{1,0:T(1,128)S(1)}, u32[]{:S(2)}, u32[]{:S(2)}) collective-permute-start(f32[1,64]{1,0:T(1,128)S(1)} %multiply_add_fusion.1), channel_id=1, source_target_pairs={{0,8},{1,9},{2,10},{3,11},{4,12},{5,13},{6,14},{7,15},{8,0},{9,1},... | collective-permute-start | bytes 776 | tf_op jit(solution)/shard_map/ppermute | solution.py:389
  72.9 3.6 %collective-permute-start.2 = (f32[1,64]{1,0:T(1,128)S(1)}, f32[1,64]{1,0:T(1,128)S(1)}, u32[]{:S(2)}, u32[]{:S(2)}) collective-permute-start(f32[1,64]{1,0:T(1,128)S(1)} %multiply_add_fusion.1), channel_id=1, source_target_pairs={{0,4},{1,5},{2,6},{3,7},{4,8},{5,9},{6,10},{7,11},{8,12},{9,13},{1... | collective-permute-start | bytes 776 | tf_op jit(solution)/shard_map/ppermute | solution.py:389
  77.0 1.0 copy-start.4
  92.4 13.2 %collective-permute-start.5 = (f32[4,64,128]{2,1,0:T(8,128)S(1)}, f32[4,64,128]{2,1,0:T(8,128)S(1)}, u32[]{:S(2)}, u32[]{:S(2)}) collective-permute-start(f32[4,64,128]{2,1,0:T(8,128)S(1)} %slice.37), channel_id=1, source_target_pairs={{0,16},{16,0},{32,48},{48,32},{64,80},{80,64},{96,112},{112,96},{1... | collective-permute-start | bytes 393224 | tf_op jit(solution)/shard_map/ppermute | solution.py:364
  100.6 5.0 %copy-start.6 = (f32[8,64,128]{2,1,0:T(8,128)S(1)}, f32[8,64,128]{2,1,0:T(8,128)}, u32[]{:S(2)}) copy-start(f32[8,64,128]{2,1,0:T(8,128)} %get-tuple-element.23) | copy-start | bytes 786436
  100.6 22.7 %all-to-all-start.1 = ((f32[8,64,512]{2,1,0:T(8,128)}), f32[8,64,512]{2,1,0:T(8,128)S(1)}, u32[]{:S(2)}, u32[]{:S(2)}) async-start(f32[8,64,512]{2,1,0:T(8,128)} %shard_map.103), calls=%async_computation.1 | async-start | bytes 2097152 | tf_op jit(solution)/shard_map/all_to_all | solution.py:360
  105.6 13.6 %collective-permute-start.6 = (f32[2,64,128]{2,1,0:T(8,128)S(1)}, f32[2,64,128]{2,1,0:T(8,128)S(1)}, u32[]{:S(2)}, u32[]{:S(2)}) collective-permute-start(f32[2,64,128]{2,1,0:T(8,128)S(1)} %slice.49), channel_id=1, source_target_pairs={{0,48},{16,32},{32,16},{48,0},{64,112},{80,96},{96,80},{112,64},{1... | collective-permute-start | bytes 196616 | tf_op jit(solution)/shard_map/ppermute | solution.py:364
  119.2 4.0 %collective-permute-start.7 = (f32[1,64,128]{2,1,0:T(8,128)S(1)}, f32[1,64,128]{2,1,0:T(8,128)S(1)}, u32[]{:S(2)}, u32[]{:S(2)}) collective-permute-start(f32[1,64,128]{2,1,0:T(8,128)S(1)} %slice.51), channel_id=1, source_target_pairs={{0,64},{16,80},{32,96},{48,112},{64,0},{80,16},{96,32},{112,48},{1... | collective-permute-start | bytes 98312 | tf_op jit(solution)/shard_map/ppermute | solution.py:364
  123.2 1.0 copy-start
  132.8 23.8 %collective-permute-start.8 = (f32[8,72,512]{2,1,0:T(8,128)}, f32[8,72,512]{2,1,0:T(8,128)S(1)}, u32[]{:S(2)}, u32[]{:S(2)}) collective-permute-start(f32[8,72,512]{2,1,0:T(8,128)} %get-tuple-element.28), channel_id=1, source_target_pairs={{0,1},{1,0},{2,3},{3,2},{4,5},{5,4},{6,7},{7,6},{8,9},{9,8},{10,11... | collective-permute-start | bytes 3538952 | tf_op jit(solution)/shard_map/ppermute | solution.py:364
  142.5 6.0 %collective-permute-start.9 = (f32[4,64,128]{2,1,0:T(8,128)S(1)}, f32[4,64,128]{2,1,0:T(8,128)S(1)}, u32[]{:S(2)}, u32[]{:S(2)}) collective-permute-start(f32[4,64,128]{2,1,0:T(8,128)S(1)} %slice.43), channel_id=1, source_target_pairs={{0,16},{16,0},{32,48},{48,32},{64,80},{80,64},{96,112},{112,96},{1... | collective-permute-start | bytes 393224 | tf_op jit(solution)/shard_map/ppermute | solution.py:364
  149.4 5.6 %collective-permute-start.10 = (f32[2,64,128]{2,1,0:T(8,128)S(1)}, f32[2,64,128]{2,1,0:T(8,128)S(1)}, u32[]{:S(2)}, u32[]{:S(2)}) collective-permute-start(f32[2,64,128]{2,1,0:T(8,128)S(1)} %slice.53), channel_id=1, source_target_pairs={{0,48},{16,32},{32,16},{48,0},{64,112},{80,96},{96,80},{112,64},{1... | collective-permute-start | bytes 196616 | tf_op jit(solution)/shard_map/ppermute | solution.py:364
  155.0 9.4 %collective-permute-start.11 = (f32[1,64,128]{2,1,0:T(8,128)S(1)}, f32[1,64,128]{2,1,0:T(8,128)S(1)}, u32[]{:S(2)}, u32[]{:S(2)}) collective-permute-start(f32[1,64,128]{2,1,0:T(8,128)S(1)} %slice.55), channel_id=1, source_target_pairs={{0,64},{16,80},{32,96},{48,112},{64,0},{80,16},{96,32},{112,48},{1... | collective-permute-start | bytes 98312 | tf_op jit(solution)/shard_map/ppermute | solution.py:364
  159.1 35.7 %all-to-all-start.3 = ((f32[8,72,512]{2,1,0:T(8,128)}), f32[8,72,512]{2,1,0:T(8,128)S(1)}, u32[]{:S(2)}, u32[]{:S(2)}) async-start(f32[8,72,512]{2,1,0:T(8,128)} %add.66), calls=%async_computation.3 | async-start | bytes 2359296 | tf_op jit(solution)/shard_map/all_to_all | solution.py:360
  164.5 13.5 %collective-permute-start.12 = (f32[1,128,128]{2,1,0:T(8,128)S(1)}, f32[1,128,128]{2,1,0:T(8,128)S(1)}, u32[]{:S(2)}, u32[]{:S(2)}) collective-permute-start(f32[1,128,128]{2,1,0:T(8,128)S(1)} %pad_maximum_fusion.2), channel_id=1, source_target_pairs={{0,64},{16,80},{32,96},{48,112},{64,0},{80,16},{96,32},{112,48},{1... | collective-permute-start | bytes 196616 | tf_op jit(solution)/shard_map/ppermute | solution.py:364
  178.0 6.7 %collective-permute-start.13 = (f32[2,128,128]{2,1,0:T(8,128)S(1)}, f32[2,128,128]{2,1,0:T(8,128)S(1)}, u32[]{:S(2)}, u32[]{:S(2)}) collective-permute-start(f32[2,128,128]{2,1,0:T(8,128)S(1)} %pad_maximum_fusion.1), channel_id=1, source_target_pairs={{0,48},{16,32},{32,16},{48,0},{64,112},{80,96},{96,80},{112,64},{1... | collective-permute-start | bytes 393224 | tf_op jit(solution)/shard_map/ppermute | solution.py:364
  184.7 7.5 %copy-start.5 = (f32[4,128,128]{2,1,0:T(8,128)}, f32[4,128,128]{2,1,0:T(8,128)S(1)}, u32[]{:S(2)}) copy-start(f32[4,128,128]{2,1,0:T(8,128)S(1)} %pad_maximum_fusion.near_ref) | copy-start | bytes 786436
  184.7 7.5 %collective-permute-start.14 = (f32[4,128,128]{2,1,0:T(8,128)S(1)}, f32[4,128,128]{2,1,0:T(8,128)S(1)}, u32[]{:S(2)}, u32[]{:S(2)}) collective-permute-start(f32[4,128,128]{2,1,0:T(8,128)S(1)} %pad_maximum_fusion.near_ref), channel_id=1, source_target_pairs={{0,16},{16,0},{32,48},{48,32},{64,80},{80,64},{96,112},{112,96},{1... | collective-permute-start | bytes 786440 | tf_op jit(solution)/shard_map/ppermute | solution.py:364
  192.2 0.7 copy-start.7
  194.8 1.1 copy-start.2

commit v3 on v2

--- a/solution.py
+++ b/solution.py
@@ -17,8 +17,8 @@
 CHUNK = 256
 GROUP = 4
 PARTS = 2
-MASKS = (1, 3, 4)
-MASKS_OF = [(r >> 2) * MASKS[0] ^ (r >> 1 & 1) * MASKS[1] ^ (r & 1) * MASKS[2] for r in range(8)]
+ROUNDS = 4
+VMEM = 48 << 20
 
 
 def eye_of(n):
@@ -127,10 +127,12 @@
         scores = s_ref[...]
         high = jnp.maximum(jnp.max(scores, axis=1, keepdims=True), FLOOR)
         total = jnp.sum(jnp.exp2(scores - high), axis=1, keepdims=True)
-        lse_ref[...] = as_row(jnp.where(total > 0.0, high + jnp.log2(total), FLOOR))
-
-
-def index_forward(base, q, kt, w, start, pos):
+        row = as_row(jnp.where(total > 0.0, high + jnp.log2(total), FLOOR))
+        row = jnp.concatenate([row, jnp.zeros_like(row)], axis=1)
+        lse_ref[...] = jnp.broadcast_to(row[None], lse_ref.shape)
+
+
+def index_forward(base, q, kt, w, start, pos, peers):
     rows, width = q.shape
     dim, keys = kt.shape
     heads = w.shape[1]
@@ -146,10 +148,10 @@
             whole(1, rows),
             whole(1, rows),
         ],
-        out_specs=[whole(rows, keys), whole(1, rows)],
+        out_specs=[whole(rows, keys), whole(peers, 8, 2 * rows)],
         out_shape=[
             jax.ShapeDtypeStruct((rows, keys), jnp.float32),
-            jax.ShapeDtypeStruct((1, rows), jnp.float32),
+            jax.ShapeDtypeStruct((peers, 8, 2 * rows), jnp.float32),
         ],
         cost_estimate=pl.CostEstimate(flops=2 * rows * width * keys, bytes_accessed=2 << 20, transcendentals=rows * keys),
         name="index_forward",
@@ -198,119 +200,134 @@
         out_specs=pl.BlockSpec((owners, rows, width), lambda c: (0, 0, c)),
         out_shape=jax.ShapeDtypeStruct((owners, rows, keys // PARTS), jnp.float32),
         scratch_shapes=[pltpu.VMEM((heads, queries), jnp.float32)],
+        compiler_params=pltpu.CompilerParams(vmem_limit_bytes=VMEM),
         cost_estimate=pl.CostEstimate(
             flops=2 * heads * keys * queries // PARTS, bytes_accessed=18 << 19, transcendentals=heads * queries
         ),
     )(e, m, stats)
 
 
-def back_kernel(has_former, has_keys, splits, *refs):
-    place_ref, t_ref, s_ref, stats_ref, c_ref, q_ref, k_ref, kt_ref, w_ref, *refs = refs
-    if has_former:
-        former_ref, *refs = refs
-    if has_keys:
-        fk_ref, *refs = refs
-    gq_ref, gk_ref, g_ref, gkt_ref, turned_ref = refs
-    i = pl.program_id(0)
+def back_kernel(last, place_ref, t_ref, s_ref, stats_ref, c_ref, q_ref, k_ref, kt_ref, w_ref, *refs):
+    if last:
+        former_ref, fk_ref, far_ref, near_ref, *gk_refs, g_ref, gkt_ref, turned_ref = refs
+    else:
+        gq_ref, gk_ref, g_ref, gkt_ref = refs
+    i, steps = pl.program_id(0), pl.num_programs(0)
     rows, _ = g_ref.shape
     dim = kt_ref.shape[0]
+    width = dim * GROUP
     index_scale = 1.0 / math.sqrt(dim)
+    dest = far_first(i, steps, place_ref) if last else i
 
     @pl.when(i == 0)
     def _():
         target = jnp.sum(t_ref[...], axis=0) * (1.0 / H)
         scores = s_ref[...]
-        probs = jnp.exp2(scores - as_column(stats_ref[...]))
+        stats = [stats_ref[n, 0:1, :rows] for n in range(stats_ref.shape[0])]
+        high = functools.reduce(jnp.maximum, stats)
+        lse = high + jnp.log2(sum(jnp.exp2(x - high) for x in stats))
+        probs = jnp.exp2(scores - as_column(lse))
         g_ref[...] = jnp.where(scores > FLOOR, as_column(c_ref[...]) * (probs - target), 0.0)
         gkt_ref[...] = jnp.zeros_like(gkt_ref)
 
-    q = jnp.concatenate([q_ref[:, j * dim : (j + 1) * dim] for j in range(GROUP)], axis=0)
+    q = q_ref[:, pl.ds(pl.multiple_of(dest * width, width), width)]
+    q = jnp.concatenate([q[:, j * dim : (j + 1) * dim] for j in range(GROUP)], axis=0)
     d = jnp.dot(q, kt_ref[...], preferred_element_type=jnp.float32)
     g = g_ref[...]
+    w = w_ref[dest]
     parts, sums = [], []
     for j in range(GROUP):
         dots = d[j * rows : (j + 1) * rows]
         kept = jnp.where(dots > 0.0, g, 0.0)
-        coef = w_ref[0][:, j : j + 1] * index_scale
-        parts.append((kept * coef).astype(jnp.bfloat16))
+        parts.append((kept * (w[:, j : j + 1] * index_scale)).astype(jnp.bfloat16))
         sums.append(as_row(jnp.sum(kept * dots, axis=1, keepdims=True)))
     head_grad = jnp.concatenate(parts, axis=0)
     gq = jnp.dot(head_grad, k_ref[...], preferred_element_type=jnp.float32)
-    pad = jnp.zeros((1, dim * GROUP - rows), jnp.float32)
-    low = jnp.concatenate([jnp.concatenate([x * index_scale, pad], axis=1) for x in sums], axis=0)
-    low = jnp.concatenate([low, jnp.zeros((8 - GROUP, dim * GROUP), jnp.float32)], axis=0)
+    pad = jnp.zeros((1, width - rows), jnp.float32)
+    low = [jnp.concatenate([x * index_scale, pad], axis=1) for x in sums]
+    low = jnp.concatenate([*low, jnp.zeros((8 - GROUP, width), jnp.float32)], axis=0)
     gq = jnp.concatenate([gq[j * rows : (j + 1) * rows] for j in range(GROUP)], axis=1)
-    if has_former:
-        gq, low = gq + former_ref[0, :rows], low + former_ref[0, rows:]
-    gq_ref[0, :rows] = gq
-    gq_ref[0, rows:] = low
+    gq = jnp.concatenate([gq, low], axis=0)
     gkt_ref[...] += lax.dot_general(q, head_grad, (((0,), (0,)), ((), ())), preferred_element_type=jnp.float32)
-
-    @pl.when(i == pl.num_programs(0) - 1)
-    def _():
-        gk = gkt_ref[...].T.reshape(turned_ref.shape)
-        if has_keys:
-            gk = gk + fk_ref[...]
-        if splits:
-            turned_ref[...] = gk
-            for r in range(len(MASKS_OF)):
-                gk_ref[r] = turned_ref[place_ref[1] ^ MASKS_OF[r]]
-        else:
-            gk_ref[...] = gk
-
-
-def backward(place, t, s, stats, c, q, k, kt, w, part, dests, owners, former=None, gk=None):
+    if not last:
+        gq_ref[0] = gq
+
+        @pl.when(i == steps - 1)
+        def _():
+            gk_ref[...] = gkt_ref[...].T.reshape(gk_ref.shape)
+
+        return
+    gq = gq + former_ref[0]
+
+    @pl.when(i < steps // 2)
+    def _():
+        far_ref[0] = gq
+
+    @pl.when(i >= steps // 2)
+    def _():
+        near_ref[0] = gq
+
+    @pl.when(i == steps - 1)
+    def _():
+        turned_ref[...] = gkt_ref[...].T.reshape(turned_ref.shape)
+        rounds, lines = len(gk_refs), turned_ref.shape[1]
+        for n, ref in enumerate(gk_refs):
+            for y in range(ref.shape[0]):
+                owner = y * rounds + (place_ref[1] + n) % rounds
+                ref[y, :lines] = fk_ref[owner]
+                ref[y, lines:] = turned_ref[owner]
+
+
+def far_first(i, steps, place):
+    half = steps // 2
+    return 2 * (i % half) + jnp.where(i < half, 1 - place[0], place[0])
+
+
+def backward(place, t, s, stats, c, q, k, kt, w, part, owners, former=None):
     rows, width = q.shape
     keys, dim = k.shape
     keys = keys // PARTS
     steps = width // (dim * GROUP)
-    count = steps if dests is None else steps // 2
-    if dests is None:
-        dest = lambda i, place: i
-    elif dests == "far":
-        dest = lambda i, place: 2 * i + 1 - place[0]
-    else:
-        dest = lambda i, place: 2 * i + place[0]
+    last = former is not None
     whole = lambda *shape: pl.BlockSpec(shape, lambda i, place: (0,) * len(shape))
     w = jnp.moveaxis(w.reshape(rows, steps, GROUP), 1, 0)
-    block = (1, rows + 8, dim * GROUP)
+    block, shape = (1, rows + 8, dim * GROUP), (owners, keys // owners, dim)
+    array = lambda *shape: jax.ShapeDtypeStruct(shape, jnp.float32)
     in_specs = [
         whole(*t.shape),
         pl.BlockSpec((rows, keys), lambda i, place: (0, part)),
         whole(*stats.shape),
         whole(1, rows),
-        pl.BlockSpec((rows, dim * GROUP), lambda i, place: (0, dest(i, place))),
+        whole(rows, width),
         pl.BlockSpec((keys, dim), lambda i, place: (part, 0)),
         pl.BlockSpec((dim, keys), lambda i, place: (0, part)),
-        pl.BlockSpec((1, rows, GROUP), lambda i, place: (dest(i, place), 0, 0)),
+        whole(*w.shape),
     ]
     args = [t, s, stats, c, q, k, kt, w]
-    if former is not None:
-        in_specs.append(pl.BlockSpec(block, lambda i, place: (dest(i, place), 0, 0)))
-        args.append(former)
-    shape = (owners, keys // owners, dim)
-    if gk is not None:
-        in_specs.append(whole(*shape))
-        args.append(gk)
-    return pl.pallas_call(
-        functools.partial(back_kernel, former is not None, gk is not None, dests != "far"),
+    scratch = [pltpu.VMEM((rows, keys), jnp.float32), pltpu.VMEM((dim, keys), jnp.float32)]
+    if last:
+        half = steps // 2
+        in_specs += [pl.BlockSpec(block, lambda i, place: (far_first(i, steps, place), 0, 0)), whole(*shape)]
+        args += former
+        scratch.append(pltpu.VMEM(shape, jnp.float32))
+        piece = (owners // ROUNDS, PARTS * shape[1], dim)
+        out_specs = [
+            pl.BlockSpec(block, lambda i, place: (jnp.minimum(i, half - 1), 0, 0)),
+            pl.BlockSpec(block, lambda i, place: (jnp.maximum(i - half, 0), 0, 0)),
+        ] + [whole(*piece)] * ROUNDS
+        out_shape = [array(half, *block[1:])] * 2 + [array(*piece)] * ROUNDS
+    else:
+        out_specs = [pl.BlockSpec(block, lambda i, place: (i, 0, 0)), whole(*shape)]
+        out_shape = [array(steps, *block[1:]), array(*shape)]
+    return pl.pallas_call(
+        functools.partial(back_kernel, last),
         grid_spec=pltpu.PrefetchScalarGridSpec(
-            num_scalar_prefetch=1,
-            grid=(count,),
-            in_specs=in_specs,
-            out_specs=[pl.BlockSpec(block, lambda i, place: (i, 0, 0)), whole(*shape)],
-            scratch_shapes=[
-                pltpu.VMEM((rows, keys), jnp.float32),
-                pltpu.VMEM((dim, keys), jnp.float32),
-                pltpu.VMEM(shape, jnp.float32),
-            ],
+            num_scalar_prefetch=1, grid=(steps,), in_specs=in_specs, out_specs=out_specs, scratch_shapes=scratch
         ),
-        out_shape=[
-            jax.ShapeDtypeStruct((count, rows + 8, dim * GROUP), jnp.float32),
-            jax.ShapeDtypeStruct(shape, jnp.float32),
-        ],
+        out_shape=out_shape,
+        compiler_params=pltpu.CompilerParams(vmem_limit_bytes=VMEM),
         cost_estimate=pl.CostEstimate(
-            flops=6 * rows * width * keys * count // steps, bytes_accessed=4 << 20, transcendentals=rows * keys
+            flops=6 * rows * width * keys, bytes_accessed=4 << 20, transcendentals=rows * keys
         ),
     )(place, *args)
 
@@ -331,29 +348,33 @@
             jax.ShapeDtypeStruct((rows, width), jnp.float32),
             jax.ShapeDtypeStruct((GROUP, rows), jnp.float32),
         ],
+        compiler_params=pltpu.CompilerParams(vmem_limit_bytes=VMEM),
         name="end",
     )(x)
 
 
-def join_kernel(place_ref, near_ref, far_ref, out_ref):
-    half = near_ref.shape[0]
+def join_kernel(place_ref, *refs):
+    *in_refs, out_ref = refs
     parts, _, rows, _ = out_ref.shape
-    for n, ref in enumerate((near_ref, far_ref)):
-        for r in range(half):
+    rounds = len(in_refs)
+    for n, ref in enumerate(in_refs):
+        for y in range(ref.shape[0]):
             for p in range(parts):
-                out_ref[p, place_ref[1] ^ MASKS_OF[n * half + r]] = ref[r, p * rows : (p + 1) * rows]
-
-
-def joined(place, near, far):
-    half, rows, dim = near.shape
+                owner = y * rounds + (place_ref[1] + rounds - n) % rounds
+                out_ref[p, owner] = ref[y, p * rows : (p + 1) * rows]
+
+
+def joined(place, pieces):
+    count, rows, dim = pieces[0].shape
     vmem = pl.BlockSpec(memory_space=pltpu.VMEM)
     return pl.pallas_call(
         join_kernel,
-        in_specs=[pl.BlockSpec(memory_space=pltpu.SMEM), vmem, vmem],
+        in_specs=[pl.BlockSpec(memory_space=pltpu.SMEM)] + [vmem] * len(pieces),
         out_specs=vmem,
-        out_shape=jax.ShapeDtypeStruct((PARTS, 2 * half, rows // PARTS, dim), jnp.float32),
+        out_shape=jax.ShapeDtypeStruct((PARTS, count * len(pieces), rows // PARTS, dim), jnp.float32),
+        compiler_params=pltpu.CompilerParams(vmem_limit_bytes=VMEM),
         name="join",
-    )(place, near, far)
+    )(place, *pieces)
 
 
 def exchanged(x, axis, groups=None):
@@ -364,31 +385,9 @@
     return lax.ppermute(x, axis, [(i, i ^ mask) for i in range(lax.axis_size(axis))])
 
 
-def summed(x):
-    for mask in MASKS:
-        half = x.shape[0] // 2
-        x = x[:half] + flipped(x[half:], "head", mask)
-    return x
-
-
-def gathered(x):
-    for mask in MASKS[:0:-1]:
-        x = jnp.concatenate([x, flipped(x, "head", mask)], axis=0)
-    return x, flipped(x, "head", MASKS[0])
-
-
-def joined_lse(a, b):
-    high = jnp.maximum(a, b)
-    return high + jnp.log2(jnp.exp2(a - high) + jnp.exp2(b - high))
-
-
-def joined_over_key(x):
-    n = lax.axis_size("key")
-    for mask in (1, 2):
-        x = joined_lse(x, flipped(x, "key", mask))
-    others = [lax.ppermute(x, "key", [(i, (i + 4 * k) % n) for i in range(n)]) for k in (1, 2, 3)]
-    high = functools.reduce(jnp.maximum, others, x)
-    return high + jnp.log2(sum(jnp.exp2(y - high) for y in [x, *others]))
+def turned(x, k):
+    n = lax.axis_size("head")
+    return lax.ppermute(x, "head", [(i, i // ROUNDS * ROUNDS + (i + k) % ROUNDS) for i in range(n)])
 
 
 def shards(q_latent, k_latent, q_index, k_index, head_weight, loss_weight, query_pos, key_start):
@@ -404,27 +403,25 @@
     kt_index = k_index.T
     e, high, lse = main_forward(base, k_latent.T, jnp.swapaxes(q_latent, 1, 2), start, pos, peers)
     stats = exchanged(lse, "key")
-    scores, index_lse = index_forward(base, q_index, kt_index, head_weight, own_start, own_pos)
+    scores, index_lse = index_forward(base, q_index, kt_index, head_weight, own_start, own_pos, peers)
+    index_stats = exchanged(index_lse, "key")
     targets = []
     for part in range(PARTS):
         partial = weighted_sum(e, high, stats, owners, part)
         targets.append(exchanged(partial, "head"))
-    index_stats = joined_over_key(index_lse)
-
-    def back(part, dests, *former):
+
+    def back(part, *former):
         fixed = (scores, index_stats, loss_weight.reshape(1, -1), q_index, k_index, kt_index, head_weight)
-        return backward(place, targets[part], *fixed, part, dests, owners, *former)
-
-    gq_0, gk_0 = back(0, None)
-    gk_0 = summed(gk_0)
-    targets[1], gk_0 = lax.optimization_barrier((targets[1], gk_0))
-    far, gk_1 = back(1, "far", gq_0)
+        return backward(place, targets[part], *fixed, part, owners, *former)
+
+    former = back(0)
+    far, near, *pieces = back(1, former)
     moved = flipped(far, "key", 1)
-    near, gk_1 = back(1, "near", gq_0, gk_1)
     groups = [list(range(c, peers, 2)) for c in (0, 1)]
     gq = exchanged(near + moved, "key", groups)
-    gk_1 = summed(gk_1)
-    gk = joined(place, *gathered(jnp.concatenate([gk_0, gk_1], axis=1))).reshape(keys, -1)
+    gk = sum([turned(x, k) for k, x in enumerate(pieces) if k], pieces[0])
+    gk = gk + flipped(gk, "head", ROUNDS)
+    gk = joined(place, [gk] + [turned(gk, k) for k in range(1, ROUNDS)]).reshape(keys, -1)
     gq, gw = ended(gq)
     return (gq, gk, gw.T)
 

time: 200 us -> 158 us (0.79)
  the two profiles are of different devices: /device:TPU:4 before, /device:TPU:1 now
where the time goes in v3:
time: 158 us; the launch traced here: 156 us
  Pallas kernels  64.8 us (41%)
  waiting for transfers between devices  39.7 us (25%)
  starting transfers between devices  37.9 us (24%)
  local copies, waits for them, and re-layouts  10.5 us (7%)
  other arithmetic  2.68 us (2%)
    all_to_all x5, starting transfers between devices, exchanged(): return lax.all_to_all(x, axis, 0, 0, axis_index_groups=groups, tiled=True)  27.8 us
    pallas_call x1, Pallas kernels, main_forward(): pl.pallas_call(main_kernel, grid=(heads,), in_specs=[pl.BlockSpec(memory_...  24 us
    pallas_call x2, Pallas kernels, backward(): pl.pallas_call(functools.partial(back_kernel, last), grid_spec=pltpu.Pref...  21.1 us
    all_to_all x5, waiting for transfers between devices, exchanged(): return lax.all_to_all(x, axis, 0, 0, axis_index_groups=groups, tiled=True)  17.1 us
    ppermute x6, waiting for transfers between devices, turned(): lax.ppermute(x, 'head', [(i, i // ROUNDS * ROUNDS + (i + k) % ROUNDS) for...  14 us
    pallas_call x2, Pallas kernels, weighted_sum(): pl.pallas_call(functools.partial(sum_kernel, first), grid=(steps,), in_sp...  12 us
    unnamed x42, local copies, waits for them, and re-layouts  8.87 us
    ppermute x2, waiting for transfers between devices, flipped(): lax.ppermute(x, axis, [(i, i ^ mask) for i in range(lax.axis_size(axis))])  8.63 us
  transfers between devices with their start and end apart: 13, of which 12 were waited for; matrix products, arithmetic and copies ran while one was open for 2% of the time, Pallas kernels for 17%

profile of v3, /device:TPU:1, one launch (start us, length us, event | category | flops | bytes accessed | tf_op | source)
XLA Modules:
  0.0 156.3 jit_solution(7655165952108539451)
XLA Ops:
  0.6 24.0 %main_forward.1 = (bf16[16,1024,512]{2,1,0:T(8,128)(2,1)}, f32[64,512]{1,0:T(8,128)}, f32[16,16,512]{2,1,0:T(8,128)}) custom-call(s32[1]{0:T(128)} %bitcast.2.base_ref, bf16[576,1024]{1,0:T(8,128)(2,1)} %bitcast.29, bf16[16,576,512]{2,1,0:T(8,128)(2,1)} %bitcast.28, s32[1,512]{1,0:T(1,128)} %bitcast.26, s32[1,512]{1,0:T(1,128)} %bitcast.27), custom_call_target="tpu_custom_call" | custom-call | flops 9663676416 | bytes 27262976 | tf_op jit(solution)/shard_map/main_forward/pallas_call | solution.py:78
  24.6 8.6 %all-to-all-start = ((f32[16,16,512]{2,1,0:T(8,128)}), f32[16,16,512]{2,1,0:T(8,128)S(1)}, u32[]{:S(2)}, u32[]{:S(2)}) async-start(f32[16,16,512]{2,1,0:T(8,128)} %get-tuple-element.20), calls=%async_computation | async-start | bytes 1048576 | tf_op jit(solution)/shard_map/all_to_all | solution.py:381
  33.2 0.9 copy.12
  34.1 1.3 dynamic-slice_bitcast_fusion
  35.4 5.6 %index_forward.1 = (f32[64,1024]{1,0:T(8,128)}, f32[16,8,128]{2,1,0:T(8,128)}) custom-call(s32[1]{0:T(128)} %bitcast.2.base_ref, bf16[64,8192]{1,0:T(8,128)(2,1)} %q_ref.5, bf16[128,1024]{1,0:T(8,128)(2,1)} %bitcast.19, f32[64,64]{1,0:T(8,128)} %w_ref.1, s32[1,64]{1,0:T(1,128)} %get-tuple-element.34.start_ref, s32[1,64]{1,0:T(1,128)} %get-tuple-element.33.pos_ref), custom_call_target="tpu_custom_call" | custom-call | flops 1073741824 | bytes 2097152 | tf_op jit(solution)/shard_map/index_forward/pallas_call | solution.py:140
  41.0 3.4 %all-to-all-done.stats_ref = f32[16,16,512]{2,1,0:T(8,128)S(1)} async-done(((f32[16,16,512]{2,1,0:T(8,128)}), f32[16,16,512]{2,1,0:T(8,128)S(1)}, u32[]{:S(2)}, u32[]{:S(2)}) %all-to-all-start) | async-done | bytes 524320 | tf_op jit(solution)/shard_map/all_to_all | solution.py:381
  44.4 4.5 %all-to-all-start.2 = ((f32[16,8,128]{2,1,0:T(8,128)}), f32[16,8,128]{2,1,0:T(8,128)S(1)}, u32[]{:S(2)}, u32[]{:S(2)}) async-start(f32[16,8,128]{2,1,0:T(8,128)} %get-tuple-element.22), calls=%async_computation.2 | async-start | bytes 131072 | tf_op jit(solution)/shard_map/all_to_all | solution.py:381
  48.9 6.0 %shard_map.104 = f32[8,64,512]{2,1,0:T(8,128)} custom-call(bf16[16,1024,512]{2,1,0:T(8,128)(2,1)} %get-tuple-element.18.e_ref, f32[64,512]{1,0:T(8,128)S(1)} %copy-done.6, f32[16,16,512]{2,1,0:T(8,128)S(1)} %all-to-all-done.stats_ref), custom_call_target="tpu_custom_call" | custom-call | flops 8388608 | bytes 9437184 | tf_op jit(solution)/shard_map/pallas_call | solution.py:192
  54.9 1.4 all-to-all-done.2.stats_ref
  56.3 5.1 %all-to-all-start.3 = ((f32[8,64,512]{2,1,0:T(8,128)}), f32[8,64,512]{2,1,0:T(8,128)S(1)}, u32[]{:S(2)}, u32[]{:S(2)}) async-start(f32[8,64,512]{2,1,0:T(8,128)} %shard_map.104), calls=%async_computation.3 | async-start | bytes 2097152 | tf_op jit(solution)/shard_map/all_to_all | solution.py:381
  61.5 6.0 %shard_map.103 = f32[8,64,512]{2,1,0:T(8,128)} custom-call(bf16[16,1024,512]{2,1,0:T(8,128)(2,1)} %get-tuple-element.18.e_ref, f32[64,512]{1,0:T(8,128)S(1)} %copy-done.6, f32[16,16,512]{2,1,0:T(8,128)S(1)} %all-to-all-done.stats_ref), custom_call_target="tpu_custom_call" | custom-call | flops 8388608 | bytes 9437184 | tf_op jit(solution)/shard_map/pallas_call | solution.py:192
  67.5 8.9 %all-to-all-done.3.t_ref = f32[8,64,512]{2,1,0:T(8,128)S(1)} async-done(((f32[8,64,512]{2,1,0:T(8,128)}), f32[8,64,512]{2,1,0:T(8,128)S(1)}, u32[]{:S(2)}, u32[]{:S(2)}) %all-to-all-start.3) | async-done | bytes 1048608 | tf_op jit(solution)/shard_map/all_to_all | solution.py:381
  76.5 1.0 copy-done.4
  77.4 3.7 %all-to-all-start.1 = ((f32[8,64,512]{2,1,0:T(8,128)}), f32[8,64,512]{2,1,0:T(8,128)S(1)}, u32[]{:S(2)}, u32[]{:S(2)}) async-start(f32[8,64,512]{2,1,0:T(8,128)} %shard_map.103), calls=%async_computation.1 | async-start | bytes 2097152 | tf_op jit(solution)/shard_map/all_to_all | solution.py:381
  81.1 0.1 copy.13
  81.2 0.2 copy.14
  81.4 0.1 pad_add_fusion.place_ref
  81.5 1.2 copy-done.5
  82.8 7.8 %shard_map.105 = (f32[16,72,512]{2,1,0:T(8,128)S(1)}, f32[8,64,128]{2,1,0:T(8,128)S(1)}) custom-call(s32[2]{0:T(128)S(1)} %pad_add_fusion.place_ref, f32[8,64,512]{2,1,0:T(8,128)S(1)} %copy-done.5, f32[64,1024]{1,0:T(8,128)S(1)} %copy-done.7, f32[16,8,128]{2,1,0:T(8,128)S(1)} %all-to-all-done.2.stats_ref, f32[1,64]{1,0:T(1,128)S(1)} %bitcast.22, ...), custom_call_target="tpu_custom_call" | custom-call | flops 1610612736 | bytes 4194304 | tf_op jit(solution)/shard_map/pallas_call | solution.py:322
  90.5 1.4 copy-done
  92.0 0.7 copy-done.8
  92.7 3.4 %all-to-all-done.1.t_ref = f32[8,64,512]{2,1,0:T(8,128)S(1)} async-done(((f32[8,64,512]{2,1,0:T(8,128)}), f32[8,64,512]{2,1,0:T(8,128)S(1)}, u32[]{:S(2)}, u32[]{:S(2)}) %all-to-all-start.1) | async-done | bytes 1048608 | tf_op jit(solution)/shard_map/all_to_all | solution.py:381
  96.1 0.9 copy-done.9
  97.0 13.3 %shard_map.106 = (f32[8,72,512]{2,1,0:T(8,128)S(1)}, f32[8,72,512]{2,1,0:T(8,128)}, f32[2,128,128]{2,1,0:T(8,128)S(1)}, f32[2,128,128]{2,1,0:T(8,128)S(1)}, f32[...) custom-call(s32[2]{0:T(128)S(1)} %pad_add_fusion.place_ref, f32[8,64,512]{2,1,0:T(8,128)S(1)} %all-to-all-done.1.t_ref, ...), custom_call_target="tpu_custom_call" | custom-call | flops 1610612736 | bytes 4194304 | tf_op jit(solution)/shard_map/pallas_call | solution.py:322
  110.3 0.6 copy-done.10
  111.0 0.7 copy-done.13
  111.6 0.7 copy-done.15
  112.3 0.6 copy-done.17
  112.9 0.8 collective-permute-start
  113.7 2.5 %collective-permute-done = f32[8,72,512]{2,1,0:T(8,128)S(1)} collective-permute-done((f32[8,72,512]{2,1,0:T(8,128)S(1)}, f32[8,72,512]{2,1,0:T(8,128)S(1)}, u32[]{:S(2)}, u32[]{:S(2)}) %collective-permute-start) | collective-permute-done | bytes 1179680 | tf_op jit(solution)/shard_map/ppermute | solution.py:385
  116.2 2.5 %add.25 = f32[8,72,512]{2,1,0:T(8,128)} add(f32[8,72,512]{2,1,0:T(8,128)} %get-tuple-element.25, f32[8,72,512]{2,1,0:T(8,128)S(1)} %collective-permute-done) | non-fusion elementwise | flops 294912 | bytes 3538944 | tf_op jit(solution)/shard_map/add | solution.py:421
  118.8 6.0 %all-to-all-start.4 = ((f32[8,72,512]{2,1,0:T(8,128)}), f32[8,72,512]{2,1,0:T(8,128)S(1)}, u32[]{:S(2)}, u32[]{:S(2)}) async-start(f32[8,72,512]{2,1,0:T(8,128)} %add.25), calls=%async_computation.4 | async-start | bytes 2359296 | tf_op jit(solution)/shard_map/all_to_all | solution.py:381
  124.7 0.7 collective-permute-start.1
  125.4 1.8 %collective-permute-start.2 = (f32[2,128,128]{2,1,0:T(8,128)S(1)}, f32[2,128,128]{2,1,0:T(8,128)S(1)}, u32[]{:S(2)}, u32[]{:S(2)}) collective-permute-start(f32[2,128,128]{2,1,0:T(8,128)S(1)} %copy-done.16), channel_id=1, source_target_pairs={{0,32},{16,48},{32,0},{48,16},{64,96},{80,112},{96,64},{112,80},{1... | collective-permute-start | bytes 393224 | tf_op jit(solution)/shard_map/ppermute | solution.py:390
  127.2 1.2 collective-permute-start.3
  128.5 2.2 %collective-permute-done.1 = f32[2,128,128]{2,1,0:T(8,128)S(1)} collective-permute-done((f32[2,128,128]{2,1,0:T(8,128)S(1)}, f32[2,128,128]{2,1,0:T(8,128)S(1)}, u32[]{:S(2)}, u32[]{:S(2)}) %collective-permute-start.1) | collective-permute-done | bytes 131104 | tf_op jit(solution)/shard_map/ppermute | solution.py:390
  130.6 2.3 %collective-permute-done.2 = f32[2,128,128]{2,1,0:T(8,128)S(1)} collective-permute-done((f32[2,128,128]{2,1,0:T(8,128)S(1)}, f32[2,128,128]{2,1,0:T(8,128)S(1)}, u32[]{:S(2)}, u32[]{:S(2)}) %collective-permute-start.2) | collective-permute-done | bytes 131104 | tf_op jit(solution)/shard_map/ppermute | solution.py:390
  133.0 0.5 collective-permute-done.3
  133.6 0.8 collective-permute-start.4
  134.4 6.2 %collective-permute-done.4 = f32[2,128,128]{2,1,0:T(8,128)S(1)} collective-permute-done((f32[2,128,128]{2,1,0:T(8,128)S(1)}, f32[2,128,128]{2,1,0:T(8,128)S(1)}, u32[]{:S(2)}, u32[]{:S(2)}) %collective-permute-start.4) | collective-permute-done | bytes 131104 | tf_op jit(solution)/shard_map/ppermute | solution.py:385
  140.5 4.0 %collective-permute-start.7 = (f32[2,128,128]{2,1,0:T(8,128)S(1)}, f32[2,128,128]{2,1,0:T(8,128)S(1)}, u32[]{:S(2)}, u32[]{:S(2)}) collective-permute-start(f32[2,128,128]{2,1,0:T(8,128)S(1)} %add.29.refs_0_), channel_id=1, source_target_pairs={{0,48},{16,0},{32,16},{48,32},{64,112},{80,64},{96,80},{112,96},{1... | collective-permute-start | bytes 393224 | tf_op jit(solution)/shard_map/ppermute | solution.py:390
  144.6 0.5 collective-permute-start.6
  145.1 0.2 collective-permute-start.5
  145.3 4.6 %collective-permute-done.7.refs_3_ = f32[2,128,128]{2,1,0:T(8,128)S(1)} collective-permute-done((f32[2,128,128]{2,1,0:T(8,128)S(1)}, f32[2,128,128]{2,1,0:T(8,128)S(1)}, u32[]{:S(2)}, u32[]{:S(2)}) %collective-permute-start.7) | collective-permute-done | bytes 131104 | tf_op jit(solution)/shard_map/ppermute | solution.py:390
  149.9 0.5 collective-permute-done.6.refs_2_
  150.3 3.8 %collective-permute-done.5.refs_1_ = f32[2,128,128]{2,1,0:T(8,128)S(1)} collective-permute-done((f32[2,128,128]{2,1,0:T(8,128)S(1)}, f32[2,128,128]{2,1,0:T(8,128)S(1)}, u32[]{:S(2)}, u32[]{:S(2)}) %collective-permute-start.5) | collective-permute-done | bytes 131104 | tf_op jit(solution)/shard_map/ppermute | solution.py:390
  154.2 1.4 join.1
  155.5 0.7 end.1
  (34 shorter events, 0.1 us)
Async XLA Ops:
  24.6 8.6 %copy-start.2 = (bf16[1024,128]{1,0:T(8,128)(2,1)S(1)}, bf16[1024,128]{1,0:T(8,128)(2,1)}, u32[]{:S(2)}) copy-start(bf16[1024,128]{1,0:T(8,128)(2,1)} %k_ref.3) | copy-start | bytes 786436
  24.6 19.8 %all-to-all-start = ((f32[16,16,512]{2,1,0:T(8,128)}), f32[16,16,512]{2,1,0:T(8,128)S(1)}, u32[]{:S(2)}, u32[]{:S(2)}) async-start(f32[16,16,512]{2,1,0:T(8,128)} %get-tuple-element.20), calls=%async_computation | async-start | bytes 1048576 | tf_op jit(solution)/shard_map/all_to_all | solution.py:381
  35.4 13.5 %copy-start.6 = (f32[64,512]{1,0:T(8,128)S(1)}, f32[64,512]{1,0:T(8,128)}, u32[]{:S(2)}) copy-start(f32[64,512]{1,0:T(8,128)} %get-tuple-element.19.m_ref) | copy-start | bytes 393220
  44.4 11.9 %all-to-all-start.2 = ((f32[16,8,128]{2,1,0:T(8,128)}), f32[16,8,128]{2,1,0:T(8,128)S(1)}, u32[]{:S(2)}, u32[]{:S(2)}) async-start(f32[16,8,128]{2,1,0:T(8,128)} %get-tuple-element.22), calls=%async_computation.2 | async-start | bytes 131072 | tf_op jit(solution)/shard_map/all_to_all | solution.py:381
  56.3 20.1 %all-to-all-start.3 = ((f32[8,64,512]{2,1,0:T(8,128)}), f32[8,64,512]{2,1,0:T(8,128)S(1)}, u32[]{:S(2)}, u32[]{:S(2)}) async-start(f32[8,64,512]{2,1,0:T(8,128)} %shard_map.104), calls=%async_computation.3 | async-start | bytes 2097152 | tf_op jit(solution)/shard_map/all_to_all | solution.py:381
  67.5 13.6 %copy-start.19 = (f32[64,64]{1,0:T(8,128)S(1)}, f32[64,64]{1,0:T(8,128)}, u32[]{:S(2)}) copy-start(f32[64,64]{1,0:T(8,128)} %w_ref.1) | copy-start | bytes 49156
  67.5 14.0 %copy-start.1 = (bf16[64,8192]{1,0:T(8,128)(2,1)S(1)}, bf16[64,8192]{1,0:T(8,128)(2,1)}, u32[]{:S(2)}) copy-start(bf16[64,8192]{1,0:T(8,128)(2,1)} %q_ref.5) | copy-start | bytes 3145732
  67.5 14.0 %copy-start.3 = (bf16[1024,128]{0,1:T(8,128)(2,1)S(1)}, bf16[1024,128]{0,1:T(8,128)(2,1)}, u32[]{:S(2)}) copy-start(bf16[1024,128]{0,1:T(8,128)(2,1)} %copy.12) | copy-start | bytes 786436
  67.5 14.0 %copy-start.7 = (f32[64,1024]{1,0:T(8,128)S(1)}, f32[64,1024]{1,0:T(8,128)}, u32[]{:S(2)}) copy-start(f32[64,1024]{1,0:T(8,128)} %get-tuple-element.21.s_ref) | copy-start | bytes 786436
  67.5 14.0 %copy-start.12 = (f32[64]{0:T(128)S(1)}, f32[64]{0:T(128)}, u32[]{:S(2)}) copy-start(f32[64]{0:T(128)} %param.13) | copy-start | bytes 772
  76.4 1.0 copy-start.4
  77.4 18.6 %all-to-all-start.1 = ((f32[8,64,512]{2,1,0:T(8,128)}), f32[8,64,512]{2,1,0:T(8,128)S(1)}, u32[]{:S(2)}, u32[]{:S(2)}) async-start(f32[8,64,512]{2,1,0:T(8,128)} %shard_map.103), calls=%async_computation.1 | async-start | bytes 2097152 | tf_op jit(solution)/shard_map/all_to_all | solution.py:381
  81.5 1.2 copy-start.5
  90.5 1.4 copy-start
  92.0 0.7 copy-start.8
  96.1 1.0 copy-start.9
  110.3 0.6 copy-start.10
  111.0 0.7 copy-start.13
  111.6 0.7 copy-start.15
  112.3 0.7 copy-start.17
  112.9 3.3 %collective-permute-start = (f32[8,72,512]{2,1,0:T(8,128)S(1)}, f32[8,72,512]{2,1,0:T(8,128)S(1)}, u32[]{:S(2)}, u32[]{:S(2)}) collective-permute-start(f32[8,72,512]{2,1,0:T(8,128)S(1)} %get-tuple-element.26), channel_id=1, source_target_pairs={{0,1},{1,0},{2,3},{3,2},{4,5},{5,4},{6,7},{7,6},{8,9},{9,8},{10,11... | collective-permute-start | bytes 3538952 | tf_op jit(solution)/shard_map/ppermute | solution.py:385
  118.7 6.0 %copy-start.18 = (f32[2,128,128]{2,1,0:T(8,128)S(1)}, f32[2,128,128]{2,1,0:T(8,128)}, u32[]{:S(2)}) copy-start(f32[2,128,128]{2,1,0:T(8,128)} %copy-done.17) | copy-start | bytes 393220
  118.8 6.6 %copy-start.16 = (f32[2,128,128]{2,1,0:T(8,128)S(1)}, f32[2,128,128]{2,1,0:T(8,128)}, u32[]{:S(2)}) copy-start(f32[2,128,128]{2,1,0:T(8,128)} %copy-done.15) | copy-start | bytes 393220
  118.8 8.5 %copy-start.14 = (f32[2,128,128]{2,1,0:T(8,128)S(1)}, f32[2,128,128]{2,1,0:T(8,128)}, u32[]{:S(2)}) copy-start(f32[2,128,128]{2,1,0:T(8,128)} %copy-done.13) | copy-start | bytes 393220
  118.8 14.8 %copy-start.11 = (f32[2,128,128]{2,1,0:T(8,128)S(1)}, f32[2,128,128]{2,1,0:T(8,128)}, u32[]{:S(2)}) copy-start(f32[2,128,128]{2,1,0:T(8,128)} %copy-done.10) | copy-start | bytes 393220
  118.8 36.8 %all-to-all-start.4 = ((f32[8,72,512]{2,1,0:T(8,128)}), f32[8,72,512]{2,1,0:T(8,128)S(1)}, u32[]{:S(2)}, u32[]{:S(2)}) async-start(f32[8,72,512]{2,1,0:T(8,128)} %add.25), calls=%async_computation.4 | async-start | bytes 2359296 | tf_op jit(solution)/shard_map/all_to_all | solution.py:381
  124.7 5.9 %collective-permute-start.1 = (f32[2,128,128]{2,1,0:T(8,128)S(1)}, f32[2,128,128]{2,1,0:T(8,128)S(1)}, u32[]{:S(2)}, u32[]{:S(2)}) collective-permute-start(f32[2,128,128]{2,1,0:T(8,128)S(1)} %copy-done.18), channel_id=1, source_target_pairs={{0,16},{16,32},{32,48},{48,0},{64,80},{80,96},{96,112},{112,64},{1... | collective-permute-start | bytes 393224 | tf_op jit(solution)/shard_map/ppermute | solution.py:390
  125.4 7.6 %collective-permute-start.2 = (f32[2,128,128]{2,1,0:T(8,128)S(1)}, f32[2,128,128]{2,1,0:T(8,128)S(1)}, u32[]{:S(2)}, u32[]{:S(2)}) collective-permute-start(f32[2,128,128]{2,1,0:T(8,128)S(1)} %copy-done.16), channel_id=1, source_target_pairs={{0,32},{16,48},{32,0},{48,16},{64,96},{80,112},{96,64},{112,80},{1... | collective-permute-start | bytes 393224 | tf_op jit(solution)/shard_map/ppermute | solution.py:390
  127.2 6.3 %collective-permute-start.3 = (f32[2,128,128]{2,1,0:T(8,128)S(1)}, f32[2,128,128]{2,1,0:T(8,128)S(1)}, u32[]{:S(2)}, u32[]{:S(2)}) collective-permute-start(f32[2,128,128]{2,1,0:T(8,128)S(1)} %copy-done.14), channel_id=1, source_target_pairs={{0,48},{16,0},{32,16},{48,32},{64,112},{80,64},{96,80},{112,96},{1... | collective-permute-start | bytes 393224 | tf_op jit(solution)/shard_map/ppermute | solution.py:390
  133.6 7.0 %collective-permute-start.4 = (f32[2,128,128]{2,1,0:T(8,128)S(1)}, f32[2,128,128]{2,1,0:T(8,128)S(1)}, u32[]{:S(2)}, u32[]{:S(2)}) collective-permute-start(f32[2,128,128]{2,1,0:T(8,128)S(1)} %add_add_fusion), channel_id=1, source_target_pairs={{0,64},{16,80},{32,96},{48,112},{64,0},{80,16},{96,32},{112,48},{1... | collective-permute-start | bytes 393224 | tf_op jit(solution)/shard_map/ppermute | solution.py:385
  140.5 9.3 %collective-permute-start.7 = (f32[2,128,128]{2,1,0:T(8,128)S(1)}, f32[2,128,128]{2,1,0:T(8,128)S(1)}, u32[]{:S(2)}, u32[]{:S(2)}) collective-permute-start(f32[2,128,128]{2,1,0:T(8,128)S(1)} %add.29.refs_0_), channel_id=1, source_target_pairs={{0,48},{16,0},{32,16},{48,32},{64,112},{80,64},{96,80},{112,96},{1... | collective-permute-start | bytes 393224 | tf_op jit(solution)/shard_map/ppermute | solution.py:390
  144.6 5.8 %collective-permute-start.6 = (f32[2,128,128]{2,1,0:T(8,128)S(1)}, f32[2,128,128]{2,1,0:T(8,128)S(1)}, u32[]{:S(2)}, u32[]{:S(2)}) collective-permute-start(f32[2,128,128]{2,1,0:T(8,128)S(1)} %add.29.refs_0_), channel_id=1, source_target_pairs={{0,32},{16,48},{32,0},{48,16},{64,96},{80,112},{96,64},{112,80},{1... | collective-permute-start | bytes 393224 | tf_op jit(solution)/shard_map/ppermute | solution.py:390
  145.1 9.1 %collective-permute-start.5 = (f32[2,128,128]{2,1,0:T(8,128)S(1)}, f32[2,128,128]{2,1,0:T(8,128)S(1)}, u32[]{:S(2)}, u32[]{:S(2)}) collective-permute-start(f32[2,128,128]{2,1,0:T(8,128)S(1)} %add.29.refs_0_), channel_id=1, source_target_pairs={{0,16},{16,32},{32,48},{48,0},{64,80},{80,96},{96,112},{112,64},{1... | collective-permute-start | bytes 393224 | tf_op jit(solution)/shard_map/ppermute | solution.py:390

commit v4 on v3

--- a/solution.py
+++ b/solution.py
@@ -15,6 +15,8 @@
 LOW = -1e30
 FLOOR = -1e29
 CHUNK = 256
+TILE = 256
+RUN = 4
 GROUP = 4
 PARTS = 2
 ROUNDS = 4
@@ -36,75 +38,140 @@
     return jnp.sum(jnp.where(eye_of(n), column, jnp.zeros_like(column)), axis=0, keepdims=True)
 
 
-def main_kernel(base_ref, kt_ref, qt_ref, start_ref, pos_ref, e_ref, m_ref, lse_ref, k_ref, bias_ref, part_ref):
-    h = pl.program_id(0)
-    keys, queries = bias_ref.shape
+def split_dot(x, onehot, dims, pieces):
+    total = 0.0
+    for _ in range(pieces):
+        high = x.astype(jnp.bfloat16)
+        x = x - high.astype(jnp.float32)
+        total = total + lax.dot_general(*dims(high, onehot), preferred_element_type=jnp.float32)
+    return total
+
+
+def in_use(t, info):
+    return (t == 0) | (info[1] > t * TILE)
+
+
+def main_kernel(info_ref, kt_ref, q0_ref, *refs):
+    qt_refs, refs = refs[:RUN], refs[RUN:]
+    start_ref, pos_ref, e_ref, sel_ref, m_ref, lse_ref, k_ref, bias_ref, part_ref, picked_ref = refs
+    step, steps = pl.program_id(0), pl.num_programs(0)
+    heads = part_ref.shape[1]
+    tiles = bias_ref.shape[0]
+    keys, queries = k_ref.shape[0], start_ref.shape[1]
     chunks = keys // CHUNK
     scale = LOG2E / math.sqrt(QK_DIM)
-
-    @pl.when(h == 0)
+    first = info_ref[0]
+
+    def pick(t, q):
+        return jnp.dot(q, sel_ref[t], preferred_element_type=jnp.float32).astype(jnp.bfloat16)
+
+    def any_seen():
+        return (start_ref[...] < first + keys) & (pos_ref[...] >= first)
+
+    @pl.when(step == 0)
     def _():
         k_ref[...] = kt_ref[...].T
-        s = base_ref[0] + lax.broadcasted_iota(jnp.int32, (keys, queries), 0)
-        seen = (s >= start_ref[...]) & (s <= pos_ref[...])
-        bias_ref[...] = jnp.where(seen, 0.0, LOW)
-
-    qt = qt_ref[0]
-    highs, sums = [], []
-    for c in range(chunks):
-        here = pl.ds(c * CHUNK, CHUNK)
-        s = jnp.dot(k_ref[here, :], qt, preferred_element_type=jnp.float32)
-        s = s * scale + bias_ref[here, :]
-        high = jnp.maximum(jnp.max(s, axis=0, keepdims=True), FLOOR)
-        e = jnp.exp2(s - high)
-        e_ref[0, here, :] = e.astype(jnp.bfloat16)
-        highs.append(high)
-        sums.append(jnp.sum(e, axis=0, keepdims=True))
-        m_ref[pl.ds(h * chunks + c, 1), :] = high
-    top = functools.reduce(jnp.maximum, highs)
-    total = sum(l * jnp.exp2(m - top) for l, m in zip(sums, highs))
-    part_ref[pl.ds(h, 1), :] = jnp.where(total > 0.0, top + jnp.log2(total), FLOOR)
-
-    @pl.when(h == pl.num_programs(0) - 1)
-    def _():
+
+    def prepare(t):
+        seen = any_seen()
+        rows = lax.broadcasted_iota(jnp.int32, (queries, queries), 0)
+        before = rows < lax.broadcasted_iota(jnp.int32, (queries, queries), 1)
+        rank = jnp.dot(
+            jnp.broadcast_to(seen.astype(jnp.float32), (8, queries)).astype(jnp.bfloat16),
+            before.astype(jnp.bfloat16),
+            preferred_element_type=jnp.float32,
+        )[0:1]
+        rank = as_column(jnp.where(seen, rank, -1.0))
+        places = t * TILE + lax.broadcasted_iota(jnp.int32, (queries, TILE), 1)
+        chosen = rank == places.astype(jnp.float32)
+        sel_ref[t] = chosen.astype(jnp.bfloat16)
+        left, right = start_ref[...].astype(jnp.float32), pos_ref[...].astype(jnp.float32) + 1.0
+        left = jnp.sum(jnp.where(chosen, as_column(left), 0.0), axis=0, keepdims=True)
+        right = jnp.sum(jnp.where(chosen, as_column(right), 0.0), axis=0, keepdims=True)
+        s = (first + lax.broadcasted_iota(jnp.int32, (keys, TILE), 0)).astype(jnp.float32)
+        bias_ref[t] = jnp.where((s >= left) & (s < right), 0.0, LOW)
+        picked_ref[t, 0] = pick(t, q0_ref[0])
+
+    def score(t, n):
+        h = step * RUN + n
+        qt = picked_ref[t, n % 2]
+        highs, sums = [], []
+        for c in range(chunks):
+            here = pl.ds(c * CHUNK, CHUNK)
+            s = jnp.dot(k_ref[here, :], qt, preferred_element_type=jnp.float32)
+            if c == chunks - 1:
+                picked_ref[t, (n + 1) % 2] = pick(t, qt_refs[n][0])
+            s = s * scale + bias_ref[t, here, :]
+            high = jnp.maximum(jnp.max(s, axis=0, keepdims=True), FLOOR)
+            e = jnp.exp2(s - high)
+            e_ref[t, n, here, :] = e.astype(jnp.bfloat16)
+            highs.append(high)
+            sums.append(jnp.sum(e, axis=0, keepdims=True))
+            m_ref[pl.ds((t * heads + h) * chunks + c, 1), :] = high
+        top = functools.reduce(jnp.maximum, highs)
+        total = sum(l * jnp.exp2(m - top) for l, m in zip(sums, highs))
+        part_ref[t, pl.ds(h, 1), :] = jnp.where(total > 0.0, top + jnp.log2(total), 0.0)
+
+    def scores(t):
+        for n in range(RUN):
+            score(t, n)
+
+    def send(t):
+        dims = lambda x, y: (x, y, (((1,), (1,)), ((), ())))
+        lse = split_dot(part_ref[t], sel_ref[t], dims, 3)
+        lse = jnp.where(any_seen(), lse, FLOOR) if t == 0 else lse_ref[0] + lse
         for i in range(lse_ref.shape[0]):
-            lse_ref[i] = part_ref[...]
-
-
-def main_forward(base, kt, qt, start, pos, peers):
+            lse_ref[i] = lse
+
+    for t in range(tiles):
+        used = in_use(t, info_ref)
+        pl.when(used & (step == 0))(functools.partial(prepare, t))
+        pl.when(used)(functools.partial(scores, t)) if t else scores(t)
+        pl.when(used & (step == steps - 1))(functools.partial(send, t))
+
+
+def main_forward(info, kt, qt, start, pos, peers):
     heads, lat, queries = qt.shape
     keys = kt.shape[1]
-    chunks = keys // CHUNK
+    chunks, tiles = keys // CHUNK, queries // TILE
+    whole = lambda *shape: pl.BlockSpec(shape, lambda i, info: (0,) * len(shape))
+    later = lambda n, i, info: (jnp.minimum(i * RUN + n, heads - 1), 0, 0)
     return pl.pallas_call(
         main_kernel,
-        grid=(heads,),
-        in_specs=[
-            pl.BlockSpec(memory_space=pltpu.SMEM),
-            pl.BlockSpec((lat, keys), lambda h: (0, 0)),
-            pl.BlockSpec((1, lat, queries), lambda h: (h, 0, 0)),
-            pl.BlockSpec((1, queries), lambda h: (0, 0)),
-            pl.BlockSpec((1, queries), lambda h: (0, 0)),
-        ],
-        out_specs=[
-            pl.BlockSpec((1, keys, queries), lambda h: (h, 0, 0)),
-            pl.BlockSpec((heads * chunks, queries), lambda h: (0, 0)),
-            pl.BlockSpec((peers, heads, queries), lambda h: (0, 0, 0)),
-        ],
+        grid_spec=pltpu.PrefetchScalarGridSpec(
+            num_scalar_prefetch=1,
+            grid=(heads // RUN,),
+            in_specs=[
+                whole(lat, keys),
+                whole(1, lat, queries),
+                *(pl.BlockSpec((1, lat, queries), functools.partial(later, n)) for n in range(1, RUN + 1)),
+                whole(1, queries),
+                whole(1, queries),
+            ],
+            out_specs=[
+                pl.BlockSpec((tiles, RUN, keys, TILE), lambda i, info: (0, i, 0, 0)),
+                whole(tiles, queries, TILE),
+                whole(tiles * heads * chunks, TILE),
+                whole(peers, heads, queries),
+            ],
+            scratch_shapes=[
+                pltpu.VMEM((keys, lat), jnp.bfloat16),
+                pltpu.VMEM((tiles, keys, TILE), jnp.float32),
+                pltpu.VMEM((tiles, heads, TILE), jnp.float32),
+                pltpu.VMEM((tiles, 2, lat, TILE), jnp.bfloat16),
+            ],
+        ),
         out_shape=[
-            jax.ShapeDtypeStruct((heads, keys, queries), jnp.bfloat16),
-            jax.ShapeDtypeStruct((heads * chunks, queries), jnp.float32),
+            jax.ShapeDtypeStruct((tiles, heads, keys, TILE), jnp.bfloat16),
+            jax.ShapeDtypeStruct((tiles, queries, TILE), jnp.bfloat16),
+            jax.ShapeDtypeStruct((tiles * heads * chunks, TILE), jnp.float32),
             jax.ShapeDtypeStruct((peers, heads, queries), jnp.float32),
-        ],
-        scratch_shapes=[
-            pltpu.VMEM((keys, lat), jnp.bfloat16),
-            pltpu.VMEM((keys, queries), jnp.float32),
-            pltpu.VMEM((heads, queries), jnp.float32),
         ],
         cost_estimate=pl.CostEstimate(
             flops=2 * heads * keys * queries * lat, bytes_accessed=26 << 20, transcendentals=heads * keys * queries
         ),
         name="main_forward",
-    )(base, kt, qt, start, pos)
+    )(info, kt, *([qt] * (RUN + 1)), start, pos)
 
 
 def index_kernel(base_ref, q_ref, kt_ref, w_ref, start_ref, pos_ref, s_ref, lse_ref):
@@ -158,53 +225,72 @@
     )(base, q, kt, w, start, pos)
 
 
-def sum_kernel(first, e_ref, m_ref, stats_ref, t_ref, lse_ref):
-    c = pl.program_id(0)
-    heads, width, queries = e_ref.shape
-    rows = t_ref.shape[1]
-    chunks = m_ref.shape[0] // heads
+def sum_kernel(first, info_ref, e_ref, sel_ref, m_ref, stats_ref, t_ref, lse_ref):
+    c, t = pl.program_id(0), pl.program_id(1)
+    _, heads, width, _ = e_ref.shape
+    owners, rows, _ = t_ref.shape
+    chunks = m_ref.shape[0] // heads // pl.num_programs(1)
     lanes = 128
 
-    @pl.when(c == 0)
+    @pl.when(in_use(t, info_ref) & (c == 0))
     def _():
         stats = [stats_ref[i] for i in range(stats_ref.shape[0])]
         high = functools.reduce(jnp.maximum, stats)
-        lse_ref[...] = high + jnp.log2(sum(jnp.exp2(x - high) for x in stats))
-
-    chunk = (first + c) * width // CHUNK
-    weights = [jnp.exp2(m_ref[pl.ds(h * chunks + chunk, 1), :] - lse_ref[h : h + 1, :]) for h in range(heads)]
-    for b in range(queries // lanes):
-        cols = slice(b * lanes, (b + 1) * lanes)
-        total = e_ref[0, :, cols].astype(jnp.float32) * weights[0][:, cols]
-        for h in range(1, heads):
-            total = total + e_ref[h, :, cols].astype(jnp.float32) * weights[h][:, cols]
-        flipped = total.T
-        for o in range(lanes // rows):
-            t_ref[b * (lanes // rows) + o] = flipped[o * rows : (o + 1) * rows]
-
-
-def weighted_sum(e, m, stats, owners, part):
-    heads, keys, queries = e.shape
+        lse = high + jnp.log2(sum(jnp.exp2(x - high) for x in stats))
+        lse_ref[t] = split_dot(lse, sel_ref[0], lambda x, y: (x, y, (((1,), (0,)), ((), ()))), 3)
+
+    @pl.when(in_use(t, info_ref))
+    def _():
+        lse = lse_ref[t]
+        row = t * heads * chunks + first + c
+        weights = [jnp.exp2(m_ref[pl.ds(row + h * chunks, 1), :] - lse[h : h + 1]) for h in range(heads)]
+        strips = []
+        for r in range(width // lanes):
+            at = slice(r * lanes, (r + 1) * lanes)
+            total = e_ref[0, 0, at, :].astype(jnp.float32) * weights[0]
+            for h in range(1, heads):
+                total = total + e_ref[0, h, at, :].astype(jnp.float32) * weights[h]
+            strips.append(total)
+        total = jnp.concatenate(strips, axis=0)
+        dense = split_dot(total, sel_ref[0], lambda x, y: (y, x, (((1,), (1,)), ((), ()))), 2)
+        dense = dense.reshape(owners, rows, width)
+
+        @pl.when(t == 0)
+        def _():
+            t_ref[...] = dense
+
+        @pl.when(t > 0)
+        def _():
+            t_ref[...] += dense
+
+
+def weighted_sum(info, e, sel, m, stats, owners, part):
+    tiles, heads, keys, tile = e.shape
+    queries = sel.shape[1]
     rows = queries // owners
-    width = 128
-    steps = keys // PARTS // width
+    steps = keys // PARTS // CHUNK
     first = part * steps
+    used = lambda t, info: jnp.where(in_use(t, info), t, 0)
     return pl.pallas_call(
         functools.partial(sum_kernel, first),
-        grid=(steps,),
-        in_specs=[
-            pl.BlockSpec((heads, width, queries), lambda c: (0, first + c, 0)),
-            pl.BlockSpec(m.shape, lambda c: (0, 0)),
-            pl.BlockSpec(stats.shape, lambda c: (0, 0, 0)),
-        ],
-        out_specs=pl.BlockSpec((owners, rows, width), lambda c: (0, 0, c)),
+        grid_spec=pltpu.PrefetchScalarGridSpec(
+            num_scalar_prefetch=1,
+            grid=(steps, tiles),
+            in_specs=[
+                pl.BlockSpec((1, heads, CHUNK, tile), lambda c, t, info: (used(t, info), 0, first + c, 0)),
+                pl.BlockSpec((1, queries, tile), lambda c, t, info: (used(t, info), 0, 0)),
+                pl.BlockSpec(m.shape, lambda c, t, info: (0, 0)),
+                pl.BlockSpec(stats.shape, lambda c, t, info: (0, 0, 0)),
+            ],
+            out_specs=pl.BlockSpec((owners, rows, CHUNK), lambda c, t, info: (0, 0, c)),
+            scratch_shapes=[pltpu.VMEM((tiles, heads, tile), jnp.float32)],
+        ),
         out_shape=jax.ShapeDtypeStruct((owners, rows, keys // PARTS), jnp.float32),
-        scratch_shapes=[pltpu.VMEM((heads, queries), jnp.float32)],
         compiler_params=pltpu.CompilerParams(vmem_limit_bytes=VMEM),
         cost_estimate=pl.CostEstimate(
             flops=2 * heads * keys * queries // PARTS, bytes_accessed=18 << 19, transcendentals=heads * queries
         ),
-    )(e, m, stats)
+    )(info, e, sel, m, stats)
 
 
 def back_kernel(last, place_ref, t_ref, s_ref, stats_ref, c_ref, q_ref, k_ref, kt_ref, w_ref, *refs):
@@ -257,7 +343,7 @@
             gk_ref[...] = gkt_ref[...].T.reshape(gk_ref.shape)
 
         return
-    gq = gq + former_ref[0]
+    gq = gq + former_ref[dest]
 
     @pl.when(i < steps // 2)
     def _():
@@ -307,7 +393,7 @@
     scratch = [pltpu.VMEM((rows, keys), jnp.float32), pltpu.VMEM((dim, keys), jnp.float32)]
     if last:
         half = steps // 2
-        in_specs += [pl.BlockSpec(block, lambda i, place: (far_first(i, steps, place), 0, 0)), whole(*shape)]
+        in_specs += [whole(*former[0].shape), whole(*shape)]
         args += former
         scratch.append(pltpu.VMEM(shape, jnp.float32))
         piece = (owners // ROUNDS, PARTS * shape[1], dim)
@@ -325,7 +411,6 @@
             num_scalar_prefetch=1, grid=(steps,), in_specs=in_specs, out_specs=out_specs, scratch_shapes=scratch
         ),
         out_shape=out_shape,
-        compiler_params=pltpu.CompilerParams(vmem_limit_bytes=VMEM),
         cost_estimate=pl.CostEstimate(
             flops=6 * rows * width * keys, bytes_accessed=4 << 20, transcendentals=rows * keys
         ),
@@ -401,13 +486,15 @@
     own_start = lax.dynamic_slice_in_dim(start, own, rows, axis=1)
     own_pos = lax.dynamic_slice_in_dim(pos, own, rows, axis=1)
     kt_index = k_index.T
-    e, high, lse = main_forward(base, k_latent.T, jnp.swapaxes(q_latent, 1, 2), start, pos, peers)
+    count = jnp.sum((key_start < base + keys) & (query_pos >= base), dtype=jnp.int32)
+    info = jnp.stack([at_key * keys, count])
+    e, sel, high, lse = main_forward(info, k_latent.T, jnp.swapaxes(q_latent, 1, 2), start, pos, peers)
     stats = exchanged(lse, "key")
     scores, index_lse = index_forward(base, q_index, kt_index, head_weight, own_start, own_pos, peers)
     index_stats = exchanged(index_lse, "key")
     targets = []
     for part in range(PARTS):
-        partial = weighted_sum(e, high, stats, owners, part)
+        partial = weighted_sum(info, e, sel, high, stats, owners, part)
         targets.append(exchanged(partial, "head"))
 
     def back(part, *former):
@@ -419,7 +506,8 @@
     moved = flipped(far, "key", 1)
     groups = [list(range(c, peers, 2)) for c in (0, 1)]
     gq = exchanged(near + moved, "key", groups)
-    gk = sum([turned(x, k) for k, x in enumerate(pieces) if k], pieces[0])
+    pieces = [turned(x, k) if k else x for k, x in enumerate(pieces)]
+    gk = sum(pieces[1:], pieces[0])
     gk = gk + flipped(gk, "head", ROUNDS)
     gk = joined(place, [gk] + [turned(gk, k) for k in range(1, ROUNDS)]).reshape(keys, -1)
     gq, gw = ended(gq)

time: 158 us -> 152 us (0.962)
  local copies, waits for them, and re-layouts: 10.5 us -> 4.37 us
  waiting for transfers between devices: 39.7 us -> 34.6 us
  other arithmetic: 2.68 us -> 5.84 us
  starting transfers between devices: 37.9 us -> 39.6 us
    unnamed x42 -> x28, local copies, waits for them, and re-layouts: 8.87 us -> 1.99 us
    pallas_call x2, Pallas kernels: 21.1 us -> 25.2 us  [backward(): pl.pallas_call(functools.partial(back_kernel, last), grid_spec=pltpu.Pref...]
    all_to_all x5, waiting for transfers between devices: 17.1 us -> 13.3 us  [exchanged(): return lax.all_to_all(x, axis, 0, 0, axis_index_groups=groups, tiled=True)]
    pallas_call x3, Pallas kernels: 36 us -> 32.3 us  [the longest x1 19 us: main_forward(): pl.pallas_call(main_kernel, grid_spec=pltpu.PrefetchScalarGridSpec(num_sc...]
    ppermute x6, waiting for transfers between devices: 14 us -> 12.3 us  [turned(): lax.ppermute(x, 'head', [(i, i // ROUNDS * ROUNDS + (i + k) % ROUNDS) for...]
  transfers between devices with their start and end apart: 13 -> 13, of which waited for: 12 -> 11; matrix products, arithmetic and copies ran while one was open for 2% -> 3% of each run, Pallas kernels for 17% -> 22%
where the time goes in v4:
time: 152 us; the launch traced here: 150 us
  Pallas kernels  65.3 us (43%)
  starting transfers between devices  39.6 us (26%)
  waiting for transfers between devices  34.6 us (23%)
  other arithmetic  5.84 us (4%)
  local copies, waits for them, and re-layouts  4.37 us (3%)
    all_to_all x5, starting transfers between devices, exchanged(): return lax.all_to_all(x, axis, 0, 0, axis_index_groups=groups, tiled=True)  28.6 us
    pallas_call x2, Pallas kernels, backward(): pl.pallas_call(functools.partial(back_kernel, last), grid_spec=pltpu.Pref...  25.2 us
    pallas_call x1, Pallas kernels, main_forward(): pl.pallas_call(main_kernel, grid_spec=pltpu.PrefetchScalarGridSpec(num_sc...  19 us
    all_to_all x5, waiting for transfers between devices, exchanged(): return lax.all_to_all(x, axis, 0, 0, axis_index_groups=groups, tiled=True)  13.3 us
    pallas_call x2, Pallas kernels, weighted_sum(): pl.pallas_call(functools.partial(sum_kernel, first), grid_spec=pltpu.Pref...  13.3 us
    ppermute x6, waiting for transfers between devices, turned(): lax.ppermute(x, 'head', [(i, i // ROUNDS * ROUNDS + (i + k) % ROUNDS) for...  12.3 us
    ppermute x6, starting transfers between devices, turned(): lax.ppermute(x, 'head', [(i, i // ROUNDS * ROUNDS + (i + k) % ROUNDS) for...  9.41 us
    ppermute x2, waiting for transfers between devices, flipped(): lax.ppermute(x, axis, [(i, i ^ mask) for i in range(lax.axis_size(axis))])  8.93 us
  transfers between devices with their start and end apart: 13, of which 11 were waited for; matrix products, arithmetic and copies ran while one was open for 3% of the time, Pallas kernels for 22%

profile of v4, /device:TPU:1, one launch (start us, length us, event | category | flops | bytes accessed | tf_op | source)
XLA Modules:
  0.0 150.4 jit_solution(10439186718121067875)
XLA Ops:
  0.6 1.3 convert_reduce_fusion
  2.0 1.3 pad_add_fusion.1.info_ref
  3.3 19.0 %main_forward.1 = (bf16[2,16,1024,256]{3,2,1,0:T(8,128)(2,1)}, bf16[2,512,256]{2,1,0:T(8,128)(2,1)}, f32[128,256]{1,0:T(8,128)}, f32[16,16,512]{2,1,0:T(8,128)}) custom-call(s32[2]{0:T(128)} %pad_add_fusion.1.info_ref, bf16[576,1024]{1,0:T(8,128)(2,1)} %bitcast.26, bf16[16,576,512]{2,1,0:T(8,128)(2,1)} %bitcast.19, bf16[16,576,512]{2,1,0:T(8,128)(2,1)} %bitcast.20, ...), custom_call_target="tpu_custom_call" | custom-call | flops 9663676416 | bytes 27262976 | tf_op jit(solution)/shard_map/main_forward/pallas_call | solution.py:139
  22.2 0.0 copy-start.5
  22.3 8.6 %all-to-all-start = ((f32[16,16,512]{2,1,0:T(8,128)}), f32[16,16,512]{2,1,0:T(8,128)S(1)}, u32[]{:S(2)}, u32[]{:S(2)}) async-start(f32[16,16,512]{2,1,0:T(8,128)} %get-tuple-element.22), calls=%async_computation | async-start | bytes 1048576 | tf_op jit(solution)/shard_map/all_to_all | solution.py:466
  30.8 0.9 copy.12
  31.7 1.3 dynamic-slice_bitcast_fusion
  33.1 5.7 %index_forward.1 = (f32[64,1024]{1,0:T(8,128)}, f32[16,8,128]{2,1,0:T(8,128)}) custom-call(s32[1]{0:T(128)} %bitcast.2.base_ref, bf16[64,8192]{1,0:T(8,128)(2,1)} %q_ref.5, bf16[128,1024]{1,0:T(8,128)(2,1)} %bitcast.27, f32[64,64]{1,0:T(8,128)} %w_ref.1, s32[1,64]{1,0:T(1,128)} %get-tuple-element.36.start_ref, s32[1,64]{1,0:T(1,128)} %get-tuple-element.35.pos_ref), custom_call_target="tpu_custom_call" | custom-call | flops 1073741824 | bytes 2097152 | tf_op jit(solution)/shard_map/index_forward/pallas_call | solution.py:207
  38.8 3.3 %all-to-all-done.stats_ref = f32[16,16,512]{2,1,0:T(8,128)S(1)} async-done(((f32[16,16,512]{2,1,0:T(8,128)}), f32[16,16,512]{2,1,0:T(8,128)S(1)}, u32[]{:S(2)}, u32[]{:S(2)}) %all-to-all-start) | async-done | bytes 524320 | tf_op jit(solution)/shard_map/all_to_all | solution.py:466
  42.0 4.5 %all-to-all-start.2 = ((f32[16,8,128]{2,1,0:T(8,128)}), f32[16,8,128]{2,1,0:T(8,128)S(1)}, u32[]{:S(2)}, u32[]{:S(2)}) async-start(f32[16,8,128]{2,1,0:T(8,128)} %get-tuple-element.24), calls=%async_computation.2 | async-start | bytes 131072 | tf_op jit(solution)/shard_map/all_to_all | solution.py:466
  46.6 0.0 copy-done
  46.6 0.0 copy-done.1
  46.6 0.0 copy-done.2
  46.6 6.7 %shard_map.104 = f32[8,64,512]{2,1,0:T(8,128)} custom-call(s32[2]{0:T(128)S(1)} %copy-done.2, bf16[2,16,1024,256]{3,2,1,0:T(8,128)(2,1)} %get-tuple-element.19.e_ref, bf16[2,512,256]{2,1,0:T(8,128)(2,1)S(1)} %copy-done, f32[128,256]{1,0:T(8,128)S(1)} %copy-done.1, f32[16,16,512]{2,1,0:T(8,128)S(1)} %all-to-all-done.stats_ref), custom_call_target="tpu_custom_call" | custom-call | flops 8388608 | bytes 9437184 | tf_op jit(solution)/shard_map/pallas_call | solution.py:274
  53.2 0.7 all-to-all-done.2.stats_ref
  54.0 5.1 %all-to-all-start.3 = ((f32[8,64,512]{2,1,0:T(8,128)}), f32[8,64,512]{2,1,0:T(8,128)S(1)}, u32[]{:S(2)}, u32[]{:S(2)}) async-start(f32[8,64,512]{2,1,0:T(8,128)} %shard_map.104), calls=%async_computation.3 | async-start | bytes 2097152 | tf_op jit(solution)/shard_map/all_to_all | solution.py:466
  59.1 6.7 %shard_map.103 = f32[8,64,512]{2,1,0:T(8,128)} custom-call(s32[2]{0:T(128)S(1)} %copy-done.2, bf16[2,16,1024,256]{3,2,1,0:T(8,128)(2,1)} %get-tuple-element.19.e_ref, bf16[2,512,256]{2,1,0:T(8,128)(2,1)S(1)} %copy-done, f32[128,256]{1,0:T(8,128)S(1)} %copy-done.1, f32[16,16,512]{2,1,0:T(8,128)S(1)} %all-to-all-done.stats_ref), custom_call_target="tpu_custom_call" | custom-call | flops 8388608 | bytes 9437184 | tf_op jit(solution)/shard_map/pallas_call | solution.py:274
  65.8 8.3 %all-to-all-done.3.t_ref = f32[8,64,512]{2,1,0:T(8,128)S(1)} async-done(((f32[8,64,512]{2,1,0:T(8,128)}), f32[8,64,512]{2,1,0:T(8,128)S(1)}, u32[]{:S(2)}, u32[]{:S(2)}) %all-to-all-start.3) | async-done | bytes 1048608 | tf_op jit(solution)/shard_map/all_to_all | solution.py:466
  74.1 3.7 %all-to-all-start.1 = ((f32[8,64,512]{2,1,0:T(8,128)}), f32[8,64,512]{2,1,0:T(8,128)S(1)}, u32[]{:S(2)}, u32[]{:S(2)}) async-start(f32[8,64,512]{2,1,0:T(8,128)} %shard_map.103), calls=%async_computation.1 | async-start | bytes 2097152 | tf_op jit(solution)/shard_map/all_to_all | solution.py:466
  77.8 0.0 copy-done.9
  77.9 0.1 copy.13
  77.9 1.1 copy.14
  79.0 0.6 pad_add_fusion.place_ref
  79.6 12.1 %shard_map.105 = (f32[16,72,512]{2,1,0:T(8,128)}, f32[8,64,128]{2,1,0:T(8,128)}) custom-call(s32[2]{0:T(128)} %pad_add_fusion.place_ref, f32[8,64,512]{2,1,0:T(8,128)} %copy-done.6, f32[64,1024]{1,0:T(8,128)} %get-tuple-element.23.s_ref, f32[16,8,128]{2,1,0:T(8,128)} %copy-done.7, f32[1,64]{1,0:T(1,128)} %bitcast.34, bf16[64,8192]{1,0:T(8,128)(2,1)} %q_ref.5, ...), custom_call_target="tpu_custom_call" | custom-call | flops 1610612736 | bytes 4194304 | tf_op jit(solution)/shard_map/pallas_call | solution.py:408
  91.7 1.1 all-to-all-done.1.t_ref
  92.7 1.0 copy-done.4
  93.7 13.1 %shard_map.106 = (f32[8,72,512]{2,1,0:T(8,128)}, f32[8,72,512]{2,1,0:T(8,128)}, f32[2,128,128]{2,1,0:T(8,128)}, f32[2,128,128]{2,1,0:T(8,128)}, f32[2,128,128]{2,1,0:T(8,128)}, /*index=5*/f32[2,128,128]{2,1,0:T(8,128)}) custom-call(s32[2]{0:T(128)} %pad_add_fusion.place_ref, f32[8,64,512]{2,1,0:T(8,128)} %copy-done.4, f32[64,1024]{1,0:T(8,128)} %get-tuple-element.23.s_ref, ...), custom_call_target="tpu_custom_call" | custom-call | flops 1610612736 | bytes 4194304 | tf_op jit(solution)/shard_map/pallas_call | solution.py:408
  106.8 0.9 collective-permute-start
  107.7 2.7 %collective-permute-done = f32[8,72,512]{2,1,0:T(8,128)S(1)} collective-permute-done((f32[8,72,512]{2,1,0:T(8,128)}, f32[8,72,512]{2,1,0:T(8,128)S(1)}, u32[]{:S(2)}, u32[]{:S(2)}) %collective-permute-start) | collective-permute-done | bytes 1179680 | tf_op jit(solution)/shard_map/ppermute | solution.py:470
  110.4 2.5 %add.29 = f32[8,72,512]{2,1,0:T(8,128)} add(f32[8,72,512]{2,1,0:T(8,128)} %get-tuple-element.27, f32[8,72,512]{2,1,0:T(8,128)S(1)} %collective-permute-done) | non-fusion elementwise | flops 294912 | bytes 3538944 | tf_op jit(solution)/shard_map/add | solution.py:508
  113.0 6.6 %all-to-all-start.4 = ((f32[8,72,512]{2,1,0:T(8,128)}), f32[8,72,512]{2,1,0:T(8,128)S(1)}, u32[]{:S(2)}, u32[]{:S(2)}) async-start(f32[8,72,512]{2,1,0:T(8,128)} %add.29), calls=%async_computation.4 | async-start | bytes 2359296 | tf_op jit(solution)/shard_map/all_to_all | solution.py:466
  119.6 0.6 collective-permute-start.1
  120.2 2.4 %collective-permute-start.2 = (f32[2,128,128]{2,1,0:T(8,128)S(1)}, f32[2,128,128]{2,1,0:T(8,128)S(1)}, u32[]{:S(2)}, u32[]{:S(2)}) collective-permute-start(f32[2,128,128]{2,1,0:T(8,128)S(1)} %copy-done.11), channel_id=1, source_target_pairs={{0,32},{16,48},{32,0},{48,16},{64,96},{80,112},{96,64},{112,80},{1... | collective-permute-start | bytes 393224 | tf_op jit(solution)/shard_map/ppermute | solution.py:475
  122.6 1.2 collective-permute-start.3
  123.8 1.5 collective-permute-done.1
  125.3 3.1 %collective-permute-done.2 = f32[2,128,128]{2,1,0:T(8,128)S(1)} collective-permute-done((f32[2,128,128]{2,1,0:T(8,128)S(1)}, f32[2,128,128]{2,1,0:T(8,128)S(1)}, u32[]{:S(2)}, u32[]{:S(2)}) %collective-permute-start.2) | collective-permute-done | bytes 131104 | tf_op jit(solution)/shard_map/ppermute | solution.py:475
  128.3 0.1 collective-permute-done.3
  128.4 0.7 collective-permute-start.4
  129.1 6.2 %collective-permute-done.4 = f32[2,128,128]{2,1,0:T(8,128)S(1)} collective-permute-done((f32[2,128,128]{2,1,0:T(8,128)S(1)}, f32[2,128,128]{2,1,0:T(8,128)S(1)}, u32[]{:S(2)}, u32[]{:S(2)}) %collective-permute-start.4) | collective-permute-done | bytes 131104 | tf_op jit(solution)/shard_map/ppermute | solution.py:470
  135.4 3.8 %collective-permute-start.7 = (f32[2,128,128]{2,1,0:T(8,128)S(1)}, f32[2,128,128]{2,1,0:T(8,128)S(1)}, u32[]{:S(2)}, u32[]{:S(2)}) collective-permute-start(f32[2,128,128]{2,1,0:T(8,128)S(1)} %add.33.refs_0_), channel_id=1, source_target_pairs={{0,48},{16,0},{32,16},{48,32},{64,112},{80,64},{96,80},{112,96},{1... | collective-permute-start | bytes 393224 | tf_op jit(solution)/shard_map/ppermute | solution.py:475
  139.2 1.4 collective-permute-start.6
  140.6 0.0 collective-permute-start.5
  140.6 1.5 collective-permute-done.7.refs_3_
  142.1 2.5 %collective-permute-done.6.refs_2_ = f32[2,128,128]{2,1,0:T(8,128)S(1)} collective-permute-done((f32[2,128,128]{2,1,0:T(8,128)S(1)}, f32[2,128,128]{2,1,0:T(8,128)S(1)}, u32[]{:S(2)}, u32[]{:S(2)}) %collective-permute-start.6) | collective-permute-done | bytes 131104 | tf_op jit(solution)/shard_map/ppermute | solution.py:475
  144.6 3.7 %collective-permute-done.5.refs_1_ = f32[2,128,128]{2,1,0:T(8,128)S(1)} collective-permute-done((f32[2,128,128]{2,1,0:T(8,128)S(1)}, f32[2,128,128]{2,1,0:T(8,128)S(1)}, u32[]{:S(2)}, u32[]{:S(2)}) %collective-permute-start.5) | collective-permute-done | bytes 131104 | tf_op jit(solution)/shard_map/ppermute | solution.py:475
  148.3 1.4 join.1
  149.7 0.0 all-to-all-done.4.x_ref
  149.7 0.7 end.1
  (22 shorter events, 0.1 us)
Async XLA Ops:
  22.2 8.6 %copy-start.5 = (bf16[1024,128]{1,0:T(8,128)(2,1)S(1)}, bf16[1024,128]{1,0:T(8,128)(2,1)}, u32[]{:S(2)}) copy-start(bf16[1024,128]{1,0:T(8,128)(2,1)} %k_ref.3) | copy-start | bytes 786436
  22.3 19.8 %all-to-all-start = ((f32[16,16,512]{2,1,0:T(8,128)}), f32[16,16,512]{2,1,0:T(8,128)S(1)}, u32[]{:S(2)}, u32[]{:S(2)}) async-start(f32[16,16,512]{2,1,0:T(8,128)} %get-tuple-element.22), calls=%async_computation | async-start | bytes 1048576 | tf_op jit(solution)/shard_map/all_to_all | solution.py:466
  33.0 13.5 %copy-start = (bf16[2,512,256]{2,1,0:T(8,128)(2,1)S(1)}, bf16[2,512,256]{2,1,0:T(8,128)(2,1)}, u32[]{:S(2)}) copy-start(bf16[2,512,256]{2,1,0:T(8,128)(2,1)} %get-tuple-element.20.sel_ref) | copy-start | bytes 1572868
  33.1 13.5 %copy-start.1 = (f32[128,256]{1,0:T(8,128)S(1)}, f32[128,256]{1,0:T(8,128)}, u32[]{:S(2)}) copy-start(f32[128,256]{1,0:T(8,128)} %get-tuple-element.21.m_ref) | copy-start | bytes 393220
  33.1 13.5 %copy-start.2 = (s32[2]{0:T(128)S(1)}, s32[2]{0:T(128)}, u32[]{:S(2)}) copy-start(s32[2]{0:T(128)} %pad_add_fusion.1.info_ref) | copy-start | bytes 28
  42.0 11.9 %all-to-all-start.2 = ((f32[16,8,128]{2,1,0:T(8,128)}), f32[16,8,128]{2,1,0:T(8,128)S(1)}, u32[]{:S(2)}, u32[]{:S(2)}) async-start(f32[16,8,128]{2,1,0:T(8,128)} %get-tuple-element.24), calls=%async_computation.2 | async-start | bytes 131072 | tf_op jit(solution)/shard_map/all_to_all | solution.py:466
  54.0 11.8 %copy-start.7 = (f32[16,8,128]{2,1,0:T(8,128)}, f32[16,8,128]{2,1,0:T(8,128)S(1)}, u32[]{:S(2)}) copy-start(f32[16,8,128]{2,1,0:T(8,128)S(1)} %all-to-all-done.2.stats_ref) | copy-start | bytes 196612
  54.0 20.1 %all-to-all-start.3 = ((f32[8,64,512]{2,1,0:T(8,128)}), f32[8,64,512]{2,1,0:T(8,128)S(1)}, u32[]{:S(2)}, u32[]{:S(2)}) async-start(f32[8,64,512]{2,1,0:T(8,128)} %shard_map.104), calls=%async_computation.3 | async-start | bytes 2097152 | tf_op jit(solution)/shard_map/all_to_all | solution.py:466
  65.8 12.0 %copy-start.9 = (f32[64,64]{1,0:T(8,128)S(1)}, f32[64,64]{1,0:T(8,128)}, u32[]{:S(2)}) copy-start(f32[64,64]{1,0:T(8,128)} %w_ref.1) | copy-start | bytes 49156
  74.1 4.9 %copy-start.6 = (f32[8,64,512]{2,1,0:T(8,128)}, f32[8,64,512]{2,1,0:T(8,128)S(1)}, u32[]{:S(2)}) copy-start(f32[8,64,512]{2,1,0:T(8,128)S(1)} %all-to-all-done.3.t_ref) | copy-start | bytes 3145732
  74.1 18.6 %all-to-all-start.1 = ((f32[8,64,512]{2,1,0:T(8,128)}), f32[8,64,512]{2,1,0:T(8,128)S(1)}, u32[]{:S(2)}, u32[]{:S(2)}) async-start(f32[8,64,512]{2,1,0:T(8,128)} %shard_map.103), calls=%async_computation.1 | async-start | bytes 2097152 | tf_op jit(solution)/shard_map/all_to_all | solution.py:466
  92.7 1.0 copy-start.4
  106.8 3.6 %collective-permute-start = (f32[8,72,512]{2,1,0:T(8,128)}, f32[8,72,512]{2,1,0:T(8,128)S(1)}, u32[]{:S(2)}, u32[]{:S(2)}) collective-permute-start(f32[8,72,512]{2,1,0:T(8,128)} %get-tuple-element.28), channel_id=1, source_target_pairs={{0,1},{1,0},{2,3},{3,2},{4,5},{5,4},{6,7},{7,6},{8,9},{9,8},{10,11... | collective-permute-start | bytes 3538952 | tf_op jit(solution)/shard_map/ppermute | solution.py:470
  113.0 6.6 %copy-start.12 = (f32[2,128,128]{2,1,0:T(8,128)S(1)}, f32[2,128,128]{2,1,0:T(8,128)}, u32[]{:S(2)}) copy-start(f32[2,128,128]{2,1,0:T(8,128)} %get-tuple-element.31) | copy-start | bytes 393220
  113.0 7.3 %copy-start.11 = (f32[2,128,128]{2,1,0:T(8,128)S(1)}, f32[2,128,128]{2,1,0:T(8,128)}, u32[]{:S(2)}) copy-start(f32[2,128,128]{2,1,0:T(8,128)} %get-tuple-element.32) | copy-start | bytes 393220
  113.0 9.6 %copy-start.10 = (f32[2,128,128]{2,1,0:T(8,128)S(1)}, f32[2,128,128]{2,1,0:T(8,128)}, u32[]{:S(2)}) copy-start(f32[2,128,128]{2,1,0:T(8,128)} %get-tuple-element.33) | copy-start | bytes 393220
  113.0 15.4 %copy-start.8 = (f32[2,128,128]{2,1,0:T(8,128)S(1)}, f32[2,128,128]{2,1,0:T(8,128)}, u32[]{:S(2)}) copy-start(f32[2,128,128]{2,1,0:T(8,128)} %get-tuple-element.30) | copy-start | bytes 393220
  113.0 35.3 %copy-start.3 = (s32[2]{0:T(128)S(1)}, s32[2]{0:T(128)}, u32[]{:S(2)}) copy-start(s32[2]{0:T(128)} %pad_add_fusion.place_ref) | copy-start | bytes 28
  113.0 36.7 %all-to-all-start.4 = ((f32[8,72,512]{2,1,0:T(8,128)}), f32[8,72,512]{2,1,0:T(8,128)S(1)}, u32[]{:S(2)}, u32[]{:S(2)}) async-start(f32[8,72,512]{2,1,0:T(8,128)} %add.29), calls=%async_computation.4 | async-start | bytes 2359296 | tf_op jit(solution)/shard_map/all_to_all | solution.py:466
  119.6 5.7 %collective-permute-start.1 = (f32[2,128,128]{2,1,0:T(8,128)S(1)}, f32[2,128,128]{2,1,0:T(8,128)S(1)}, u32[]{:S(2)}, u32[]{:S(2)}) collective-permute-start(f32[2,128,128]{2,1,0:T(8,128)S(1)} %copy-done.12), channel_id=1, source_target_pairs={{0,16},{16,32},{32,48},{48,0},{64,80},{80,96},{96,112},{112,64},{1... | collective-permute-start | bytes 393224 | tf_op jit(solution)/shard_map/ppermute | solution.py:475
  120.2 8.1 %collective-permute-start.2 = (f32[2,128,128]{2,1,0:T(8,128)S(1)}, f32[2,128,128]{2,1,0:T(8,128)S(1)}, u32[]{:S(2)}, u32[]{:S(2)}) collective-permute-start(f32[2,128,128]{2,1,0:T(8,128)S(1)} %copy-done.11), channel_id=1, source_target_pairs={{0,32},{16,48},{32,0},{48,16},{64,96},{80,112},{96,64},{112,80},{1... | collective-permute-start | bytes 393224 | tf_op jit(solution)/shard_map/ppermute | solution.py:475
  122.6 5.8 %collective-permute-start.3 = (f32[2,128,128]{2,1,0:T(8,128)S(1)}, f32[2,128,128]{2,1,0:T(8,128)S(1)}, u32[]{:S(2)}, u32[]{:S(2)}) collective-permute-start(f32[2,128,128]{2,1,0:T(8,128)S(1)} %copy-done.10), channel_id=1, source_target_pairs={{0,48},{16,0},{32,16},{48,32},{64,112},{80,64},{96,80},{112,96},{1... | collective-permute-start | bytes 393224 | tf_op jit(solution)/shard_map/ppermute | solution.py:475
  128.4 6.9 %collective-permute-start.4 = (f32[2,128,128]{2,1,0:T(8,128)S(1)}, f32[2,128,128]{2,1,0:T(8,128)S(1)}, u32[]{:S(2)}, u32[]{:S(2)}) collective-permute-start(f32[2,128,128]{2,1,0:T(8,128)S(1)} %add_add_fusion), channel_id=1, source_target_pairs={{0,64},{16,80},{32,96},{48,112},{64,0},{80,16},{96,32},{112,48},{1... | collective-permute-start | bytes 393224 | tf_op jit(solution)/shard_map/ppermute | solution.py:470
  135.4 6.7 %collective-permute-start.7 = (f32[2,128,128]{2,1,0:T(8,128)S(1)}, f32[2,128,128]{2,1,0:T(8,128)S(1)}, u32[]{:S(2)}, u32[]{:S(2)}) collective-permute-start(f32[2,128,128]{2,1,0:T(8,128)S(1)} %add.33.refs_0_), channel_id=1, source_target_pairs={{0,48},{16,0},{32,16},{48,32},{64,112},{80,64},{96,80},{112,96},{1... | collective-permute-start | bytes 393224 | tf_op jit(solution)/shard_map/ppermute | solution.py:475
  139.2 5.4 %collective-permute-start.6 = (f32[2,128,128]{2,1,0:T(8,128)S(1)}, f32[2,128,128]{2,1,0:T(8,128)S(1)}, u32[]{:S(2)}, u32[]{:S(2)}) collective-permute-start(f32[2,128,128]{2,1,0:T(8,128)S(1)} %add.33.refs_0_), channel_id=1, source_target_pairs={{0,32},{16,48},{32,0},{48,16},{64,96},{80,112},{96,64},{112,80},{1... | collective-permute-start | bytes 393224 | tf_op jit(solution)/shard_map/ppermute | solution.py:475
  140.6 7.7 %collective-permute-start.5 = (f32[2,128,128]{2,1,0:T(8,128)S(1)}, f32[2,128,128]{2,1,0:T(8,128)S(1)}, u32[]{:S(2)}, u32[]{:S(2)}) collective-permute-start(f32[2,128,128]{2,1,0:T(8,128)S(1)} %add.33.refs_0_), channel_id=1, source_target_pairs={{0,16},{16,32},{32,48},{48,0},{64,80},{80,96},{96,112},{112,64},{1... | collective-permute-start | bytes 393224 | tf_op jit(solution)/shard_map/ppermute | solution.py:475

commit v5 on v4

--- a/solution.py
+++ b/solution.py
@@ -48,19 +48,19 @@
 
 
 def in_use(t, info):
-    return (t == 0) | (info[1] > t * TILE)
-
-
-def main_kernel(info_ref, kt_ref, q0_ref, *refs):
+    return (t == 0) | (info[0] > t * TILE)
+
+
+def main_kernel(base_ref, kt_ref, q0_ref, *refs):
     qt_refs, refs = refs[:RUN], refs[RUN:]
-    start_ref, pos_ref, e_ref, sel_ref, m_ref, lse_ref, k_ref, bias_ref, part_ref, picked_ref = refs
+    start_ref, pos_ref, e_ref, sel_ref, m_ref, lse_ref, k_ref, bias_ref, part_ref, picked_ref, count_ref = refs
     step, steps = pl.program_id(0), pl.num_programs(0)
     heads = part_ref.shape[1]
     tiles = bias_ref.shape[0]
     keys, queries = k_ref.shape[0], start_ref.shape[1]
     chunks = keys // CHUNK
     scale = LOG2E / math.sqrt(QK_DIM)
-    first = info_ref[0]
+    first = base_ref[0]
 
     def pick(t, q):
         return jnp.dot(q, sel_ref[t], preferred_element_type=jnp.float32).astype(jnp.bfloat16)
@@ -71,6 +71,7 @@
     @pl.when(step == 0)
     def _():
         k_ref[...] = kt_ref[...].T
+        count_ref[0] = jnp.sum(any_seen().astype(jnp.int32))
 
     def prepare(t):
         seen = any_seen()
@@ -124,13 +125,13 @@
             lse_ref[i] = lse
 
     for t in range(tiles):
-        used = in_use(t, info_ref)
+        used = in_use(t, count_ref)
         pl.when(used & (step == 0))(functools.partial(prepare, t))
         pl.when(used)(functools.partial(scores, t)) if t else scores(t)
         pl.when(used & (step == steps - 1))(functools.partial(send, t))
 
 
-def main_forward(info, kt, qt, start, pos, peers):
+def main_forward(base, kt, qt, start, pos, peers):
     heads, lat, queries = qt.shape
     keys = kt.shape[1]
     chunks, tiles = keys // CHUNK, queries // TILE
@@ -159,6 +160,7 @@
                 pltpu.VMEM((tiles, keys, TILE), jnp.float32),
                 pltpu.VMEM((tiles, heads, TILE), jnp.float32),
                 pltpu.VMEM((tiles, 2, lat, TILE), jnp.bfloat16),
+                pltpu.SMEM((1,), jnp.int32),
             ],
         ),
         out_shape=[
@@ -171,7 +173,7 @@
             flops=2 * heads * keys * queries * lat, bytes_accessed=26 << 20, transcendentals=heads * keys * queries
         ),
         name="main_forward",
-    )(info, kt, *([qt] * (RUN + 1)), start, pos)
+    )(base, kt, *([qt] * (RUN + 1)), start, pos)
 
 
 def index_kernel(base_ref, q_ref, kt_ref, w_ref, start_ref, pos_ref, s_ref, lse_ref):
@@ -411,21 +413,41 @@
             num_scalar_prefetch=1, grid=(steps,), in_specs=in_specs, out_specs=out_specs, scratch_shapes=scratch
         ),
         out_shape=out_shape,
+        compiler_params=pltpu.CompilerParams(vmem_limit_bytes=VMEM),
         cost_estimate=pl.CostEstimate(
             flops=6 * rows * width * keys, bytes_accessed=4 << 20, transcendentals=rows * keys
         ),
     )(place, *args)
 
 
-def end_kernel(x_ref, gq_ref, gw_ref):
+def half_kernel(place_ref, x_ref, own_ref, other_ref):
+    mine = place_ref[2]
+    total = lambda half: functools.reduce(jnp.add, [x_ref[n, half] for n in range(x_ref.shape[0])])
+    own_ref[...] = total(mine)
+    other_ref[...] = total(1 - mine)
+
+
+def halves(place, x):
+    vmem = pl.BlockSpec(memory_space=pltpu.VMEM)
+    return pl.pallas_call(
+        half_kernel,
+        in_specs=[pl.BlockSpec(memory_space=pltpu.SMEM), vmem],
+        out_specs=[vmem, vmem],
+        out_shape=[jax.ShapeDtypeStruct(x.shape[2:], jnp.float32)] * 2,
+        compiler_params=pltpu.CompilerParams(vmem_limit_bytes=VMEM),
+        name="halves",
+    )(place, x)
+
+
+def end_kernel(x_ref, y_ref, gq_ref, gw_ref):
     rows = gq_ref.shape[0]
-    total = jnp.sum(x_ref[...], axis=0)
+    total = x_ref[...] + y_ref[...]
     gq_ref[...] = total[:rows]
     gw_ref[...] = total[rows : rows + GROUP, :rows]
 
 
-def ended(x):
-    _, rows, width = x.shape
+def ended(x, y):
+    rows, width = x.shape
     rows -= 8
     return pl.pallas_call(
         end_kernel,
@@ -435,7 +457,7 @@
         ],
         compiler_params=pltpu.CompilerParams(vmem_limit_bytes=VMEM),
         name="end",
-    )(x)
+    )(x, y)
 
 
 def join_kernel(place_ref, *refs):
@@ -480,15 +502,15 @@
     rows = q_index.shape[0]
     owners, peers = lax.axis_size("head"), lax.axis_size("key")
     at_key, at_head = (lax.axis_index(name).astype(jnp.int32) for name in ("key", "head"))
-    base, place = (at_key * keys).reshape(1), jnp.stack([at_key % 2, at_head])
+    base, place = (at_key * keys).reshape(1), jnp.stack([at_key % 2, at_head, at_key // 2 % 2])
     own = at_head * rows
     start, pos = key_start.reshape(1, -1), query_pos.reshape(1, -1)
     own_start = lax.dynamic_slice_in_dim(start, own, rows, axis=1)
     own_pos = lax.dynamic_slice_in_dim(pos, own, rows, axis=1)
     kt_index = k_index.T
     count = jnp.sum((key_start < base + keys) & (query_pos >= base), dtype=jnp.int32)
-    info = jnp.stack([at_key * keys, count])
-    e, sel, high, lse = main_forward(info, k_latent.T, jnp.swapaxes(q_latent, 1, 2), start, pos, peers)
+    info = count.reshape(1)
+    e, sel, high, lse = main_forward(base, k_latent.T, jnp.swapaxes(q_latent, 1, 2), start, pos, peers)
     stats = exchanged(lse, "key")
     scores, index_lse = index_forward(base, q_index, kt_index, head_weight, own_start, own_pos, peers)
     index_stats = exchanged(index_lse, "key")
@@ -504,13 +526,15 @@
     former = back(0)
     far, near, *pieces = back(1, former)
     moved = flipped(far, "key", 1)
-    groups = [list(range(c, peers, 2)) for c in (0, 1)]
-    gq = exchanged(near + moved, "key", groups)
+    groups = [list(range(c, peers, 4)) for c in range(4)]
+    gq = near + moved
+    gq = exchanged(gq.reshape(peers // 4, 2, *gq.shape[1:]), "key", groups)
     pieces = [turned(x, k) if k else x for k, x in enumerate(pieces)]
     gk = sum(pieces[1:], pieces[0])
     gk = gk + flipped(gk, "head", ROUNDS)
     gk = joined(place, [gk] + [turned(gk, k) for k in range(1, ROUNDS)]).reshape(keys, -1)
-    gq, gw = ended(gq)
+    mine, other = halves(place, gq)
+    gq, gw = ended(mine, flipped(other, "key", 2))
     return (gq, gk, gw.T)
 
 

time: 152 us -> 145 us (0.954)
  Pallas kernels: 65.3 us -> 60 us
  other arithmetic: 5.84 us -> 3.27 us
  starting transfers between devices: 39.6 us -> 37.7 us
    all_to_all x5, waiting for transfers between devices: 13.3 us -> 21.7 us  [exchanged(): return lax.all_to_all(x, axis, 0, 0, axis_index_groups=groups, tiled=True)]
    ppermute x2 -> x3, waiting for transfers between devices: 8.93 us -> 2.48 us  [flipped(): lax.ppermute(x, axis, [(i, i ^ mask) for i in range(lax.axis_size(axis))])]
    pallas_call x2, Pallas kernels: 25.2 us -> 20.1 us  [backward(): pl.pallas_call(functools.partial(back_kernel, last), grid_spec=pltpu.Pref...]
    ppermute x2 -> x3, starting transfers between devices: 1.58 us -> 5.57 us  [flipped(): lax.ppermute(x, axis, [(i, i ^ mask) for i in range(lax.axis_size(axis))])]
    ppermute x6, starting transfers between devices: 9.41 us -> 6.01 us  [turned(): lax.ppermute(x, 'head', [(i, i // ROUNDS * ROUNDS + (i + k) % ROUNDS) for...]
    all_to_all x5, starting transfers between devices: 28.6 us -> 26.1 us  [exchanged(): return lax.all_to_all(x, axis, 0, 0, axis_index_groups=groups, tiled=True)]
    unnamed x28 -> x44, local copies, waits for them, and re-layouts: 1.99 us -> 4.1 us
    another operation x2 -> x1, other arithmetic: 1.91 us -> 0.08 us  [shards(): jnp.stack([at_key % 2, at_head, at_key // 2 % 2])]
  transfers between devices with their start and end apart: 13 -> 14, of which waited for: 11 -> 12; matrix products, arithmetic and copies ran while one was open for 3% -> 2% of each run, Pallas kernels for 22% -> 21%
where the time goes in v5:
time: 145 us; the launch traced here: 142 us
  Pallas kernels  60 us (41%)
  starting transfers between devices  37.7 us (26%)
  waiting for transfers between devices  35.5 us (24%)
  local copies, waits for them, and re-layouts  5 us (3%)
  other arithmetic  3.27 us (2%)
    all_to_all x5, starting transfers between devices, exchanged(): return lax.all_to_all(x, axis, 0, 0, axis_index_groups=groups, tiled=True)  26.1 us
    all_to_all x5, waiting for transfers between devices, exchanged(): return lax.all_to_all(x, axis, 0, 0, axis_index_groups=groups, tiled=True)  21.7 us
    pallas_call x2, Pallas kernels, backward(): pl.pallas_call(functools.partial(back_kernel, last), grid_spec=pltpu.Pref...  20.1 us
    pallas_call x1, Pallas kernels, main_forward(): pl.pallas_call(main_kernel, grid_spec=pltpu.PrefetchScalarGridSpec(num_sc...  18.3 us
    pallas_call x2, Pallas kernels, weighted_sum(): pl.pallas_call(functools.partial(sum_kernel, first), grid_spec=pltpu.Pref...  13.3 us
    ppermute x6, waiting for transfers between devices, turned(): lax.ppermute(x, 'head', [(i, i // ROUNDS * ROUNDS + (i + k) % ROUNDS) for...  11.3 us
    ppermute x6, starting transfers between devices, turned(): lax.ppermute(x, 'head', [(i, i // ROUNDS * ROUNDS + (i + k) % ROUNDS) for...  6.01 us
    pallas_call x1, Pallas kernels, index_forward(): pl.pallas_call(index_kernel, grid=(keys // CHUNK,), in_specs=[pl.BlockSpe...  5.66 us
  transfers between devices with their start and end apart: 14, of which 12 were waited for; matrix products, arithmetic and copies ran while one was open for 2% of the time, Pallas kernels for 21%

profile of v5, /device:TPU:1, one launch (start us, length us, event | category | flops | bytes accessed | tf_op | source)
XLA Modules:
  0.0 142.4 jit_solution(17102302843614447256)
XLA Ops:
  0.6 18.3 %main_forward.1 = (bf16[2,16,1024,256]{3,2,1,0:T(8,128)(2,1)}, bf16[2,512,256]{2,1,0:T(8,128)(2,1)}, f32[128,256]{1,0:T(8,128)}, f32[16,16,512]{2,1,0:T(8,128)}) custom-call(s32[1]{0:T(128)} %bitcast.3.base_ref, bf16[576,1024]{1,0:T(8,128)(2,1)} %bitcast.33, bf16[16,576,512]{2,1,0:T(8,128)(2,1)} %bitcast.28, bf16[16,576,512]{2,1,0:T(8,128)(2,1)} %bitcast.29, ...), custom_call_target="tpu_custom_call" | custom-call | flops 9663676416 | bytes 27262976 | tf_op jit(solution)/shard_map/main_forward/pallas_call | solution.py:140
  19.0 0.0 copy-start.3
  19.0 8.6 %all-to-all-start = ((f32[16,16,512]{2,1,0:T(8,128)}), f32[16,16,512]{2,1,0:T(8,128)S(1)}, u32[]{:S(2)}, u32[]{:S(2)}) async-start(f32[16,16,512]{2,1,0:T(8,128)} %get-tuple-element.24), calls=%async_computation | async-start | bytes 1048576 | tf_op jit(solution)/shard_map/all_to_all | solution.py:488
  27.6 0.9 copy.12
  28.5 0.6 dynamic-slice_bitcast_fusion
  29.1 5.7 %index_forward.1 = (f32[64,1024]{1,0:T(8,128)}, f32[16,8,128]{2,1,0:T(8,128)}) custom-call(s32[1]{0:T(128)} %bitcast.3.base_ref, bf16[64,8192]{1,0:T(8,128)(2,1)} %q_ref.5, bf16[128,1024]{1,0:T(8,128)(2,1)} %bitcast.23, f32[64,64]{1,0:T(8,128)} %w_ref.1, s32[1,64]{1,0:T(1,128)} %get-tuple-element.40.start_ref, s32[1,64]{1,0:T(1,128)} %get-tuple-element.39.pos_ref), custom_call_target="tpu_custom_call" | custom-call | flops 1073741824 | bytes 2097152 | tf_op jit(solution)/shard_map/index_forward/pallas_call | solution.py:209
  34.8 4.0 %all-to-all-done.stats_ref = f32[16,16,512]{2,1,0:T(8,128)S(1)} async-done(((f32[16,16,512]{2,1,0:T(8,128)}), f32[16,16,512]{2,1,0:T(8,128)S(1)}, u32[]{:S(2)}, u32[]{:S(2)}) %all-to-all-start) | async-done | bytes 524320 | tf_op jit(solution)/shard_map/all_to_all | solution.py:488
  38.8 4.5 %all-to-all-start.2 = ((f32[16,8,128]{2,1,0:T(8,128)}), f32[16,8,128]{2,1,0:T(8,128)S(1)}, u32[]{:S(2)}, u32[]{:S(2)}) async-start(f32[16,8,128]{2,1,0:T(8,128)} %get-tuple-element.26), calls=%async_computation.2 | async-start | bytes 131072 | tf_op jit(solution)/shard_map/all_to_all | solution.py:488
  43.3 0.6 convert_reduce_fusion
  43.9 6.6 %shard_map.104 = f32[8,64,512]{2,1,0:T(8,128)} custom-call(s32[1]{0:T(128)} %bitcast.5.info_ref, bf16[2,16,1024,256]{3,2,1,0:T(8,128)(2,1)} %get-tuple-element.21.e_ref, bf16[2,512,256]{2,1,0:T(8,128)(2,1)S(1)} %copy-done.1, f32[128,256]{1,0:T(8,128)S(1)} %copy-done.5, f32[16,16,512]{2,1,0:T(8,128)S(1)} %all-to-all-done.stats_ref), custom_call_target="tpu_custom_call" | custom-call | flops 8388608 | bytes 9437184 | tf_op jit(solution)/shard_map/pallas_call | solution.py:276
  50.5 0.2 all-to-all-done.2.stats_ref
  50.7 5.2 %all-to-all-start.3 = ((f32[8,64,512]{2,1,0:T(8,128)}), f32[8,64,512]{2,1,0:T(8,128)}, u32[]{:S(2)}, u32[]{:S(2)}) async-start(f32[8,64,512]{2,1,0:T(8,128)} %shard_map.104), calls=%async_computation.3 | async-start | bytes 2097152 | tf_op jit(solution)/shard_map/all_to_all | solution.py:488
  55.9 6.7 %shard_map.103 = f32[8,64,512]{2,1,0:T(8,128)} custom-call(s32[1]{0:T(128)} %bitcast.5.info_ref, bf16[2,16,1024,256]{3,2,1,0:T(8,128)(2,1)} %get-tuple-element.21.e_ref, bf16[2,512,256]{2,1,0:T(8,128)(2,1)S(1)} %copy-done.1, f32[128,256]{1,0:T(8,128)S(1)} %copy-done.5, f32[16,16,512]{2,1,0:T(8,128)S(1)} %all-to-all-done.stats_ref), custom_call_target="tpu_custom_call" | custom-call | flops 8388608 | bytes 9437184 | tf_op jit(solution)/shard_map/pallas_call | solution.py:276
  62.6 0.0 copy-start.11
  62.6 8.6 %all-to-all-done.3.t_ref = f32[8,64,512]{2,1,0:T(8,128)} async-done(((f32[8,64,512]{2,1,0:T(8,128)}), f32[8,64,512]{2,1,0:T(8,128)}, u32[]{:S(2)}, u32[]{:S(2)}) %all-to-all-start.3) | async-done | bytes 1048608 | tf_op jit(solution)/shard_map/all_to_all | solution.py:488
  71.2 3.7 %all-to-all-start.1 = ((f32[8,64,512]{2,1,0:T(8,128)}), f32[8,64,512]{2,1,0:T(8,128)S(1)}, u32[]{:S(2)}, u32[]{:S(2)}) async-start(f32[8,64,512]{2,1,0:T(8,128)} %shard_map.103), calls=%async_computation.1 | async-start | bytes 2097152 | tf_op jit(solution)/shard_map/all_to_all | solution.py:488
  74.9 0.1 copy.13
  75.0 0.2 copy.14
  75.3 0.1 pad_add_fusion.place_ref
  75.4 9.0 %shard_map.105 = (f32[16,72,512]{2,1,0:T(8,128)S(1)}, f32[8,64,128]{2,1,0:T(8,128)S(1)}) custom-call(s32[3]{0:T(128)S(1)} %pad_add_fusion.place_ref, f32[8,64,512]{2,1,0:T(8,128)} %all-to-all-done.3.t_ref, f32[64,1024]{1,0:T(8,128)S(1)} %copy-done.6, f32[16,8,128]{2,1,0:T(8,128)S(1)} %all-to-all-done.2.stats_ref, f32[1,64]{1,0:T(1,128)S(1)} %bitcast.26, ...), custom_call_target="tpu_custom_call" | custom-call | flops 1610612736 | bytes 4194304 | tf_op jit(solution)/shard_map/pallas_call | solution.py:410
  84.4 1.4 copy-done
  85.8 0.7 copy-done.7
  86.5 3.1 %all-to-all-done.1.t_ref = f32[8,64,512]{2,1,0:T(8,128)S(1)} async-done(((f32[8,64,512]{2,1,0:T(8,128)}), f32[8,64,512]{2,1,0:T(8,128)S(1)}, u32[]{:S(2)}, u32[]{:S(2)}) %all-to-all-start.1) | async-done | bytes 1048608 | tf_op jit(solution)/shard_map/all_to_all | solution.py:488
  89.6 0.9 copy-done.8
  90.6 11.1 %shard_map.106 = (f32[8,72,512]{2,1,0:T(8,128)S(1)}, f32[8,72,512]{2,1,0:T(8,128)}, f32[2,128,128]{2,1,0:T(8,128)S(1)}, f32[2,128,128]{2,1,0:T(8,128)S(1)}, f32[...) custom-call(s32[3]{0:T(128)S(1)} %pad_add_fusion.place_ref, f32[8,64,512]{2,1,0:T(8,128)S(1)} %all-to-all-done.1.t_ref, ...), custom_call_target="tpu_custom_call" | custom-call | flops 1610612736 | bytes 4194304 | tf_op jit(solution)/shard_map/pallas_call | solution.py:410
  101.6 0.9 collective-permute-start
  102.6 2.5 %collective-permute-done = f32[8,72,512]{2,1,0:T(8,128)S(1)} collective-permute-done((f32[8,72,512]{2,1,0:T(8,128)S(1)}, f32[8,72,512]{2,1,0:T(8,128)S(1)}, u32[]{:S(2)}, u32[]{:S(2)}) %collective-permute-start) | collective-permute-done | bytes 1179680 | tf_op jit(solution)/shard_map/ppermute | solution.py:492
  105.0 2.6 %add.34 = f32[8,72,512]{2,1,0:T(8,128)} add(f32[8,72,512]{2,1,0:T(8,128)} %get-tuple-element.29, f32[8,72,512]{2,1,0:T(8,128)S(1)} %collective-permute-done) | non-fusion elementwise | flops 294912 | bytes 3538944 | tf_op jit(solution)/shard_map/add | solution.py:530
  107.6 0.0 copy-start.15
  107.7 4.1 %all-to-all-start.4 = ((f32[4,2,72,512]{3,2,1,0:T(8,128)}), f32[4,2,72,512]{3,2,1,0:T(8,128)S(1)}, u32[]{:S(2)}, u32[]{:S(2)}) async-start(f32[4,2,72,512]{3,2,1,0:T(8,128)} %bitcast.16), calls=%async_computation.4 | async-start | bytes 2359296 | tf_op jit(solution)/shard_map/all_to_all | solution.py:488
  111.8 0.6 collective-permute-start.2
  112.4 1.7 %collective-permute-start.3 = (f32[2,128,128]{2,1,0:T(8,128)S(1)}, f32[2,128,128]{2,1,0:T(8,128)S(1)}, u32[]{:S(2)}, u32[]{:S(2)}) collective-permute-start(f32[2,128,128]{2,1,0:T(8,128)S(1)} %copy-done.15), channel_id=1, source_target_pairs={{0,32},{16,48},{32,0},{48,16},{64,96},{80,112},{96,64},{112,80},{1... | collective-permute-start | bytes 393224 | tf_op jit(solution)/shard_map/ppermute | solution.py:497
  114.1 1.3 collective-permute-start.4
  115.4 2.3 %collective-permute-done.2 = f32[2,128,128]{2,1,0:T(8,128)S(1)} collective-permute-done((f32[2,128,128]{2,1,0:T(8,128)S(1)}, f32[2,128,128]{2,1,0:T(8,128)S(1)}, u32[]{:S(2)}, u32[]{:S(2)}) %collective-permute-start.2) | collective-permute-done | bytes 131104 | tf_op jit(solution)/shard_map/ppermute | solution.py:497
  117.8 2.1 %collective-permute-done.3 = f32[2,128,128]{2,1,0:T(8,128)S(1)} collective-permute-done((f32[2,128,128]{2,1,0:T(8,128)S(1)}, f32[2,128,128]{2,1,0:T(8,128)S(1)}, u32[]{:S(2)}, u32[]{:S(2)}) %collective-permute-start.3) | collective-permute-done | bytes 131104 | tf_op jit(solution)/shard_map/ppermute | solution.py:497
  119.9 0.7 collective-permute-done.4
  120.6 1.3 collective-permute-start.5
  121.9 5.9 %all-to-all-done.4.x_ref = f32[4,2,72,512]{3,2,1,0:T(8,128)S(1)} async-done(((f32[4,2,72,512]{3,2,1,0:T(8,128)}), f32[4,2,72,512]{3,2,1,0:T(8,128)S(1)}, u32[]{:S(2)}, u32[]{:S(2)}) %all-to-all-start.4) | async-done | bytes 1179680 | tf_op jit(solution)/shard_map/all_to_all | solution.py:488
  127.7 0.6 halves.1
  128.4 3.4 %collective-permute-start.1 = (f32[72,512]{1,0:T(8,128)S(1)}, f32[72,512]{1,0:T(8,128)S(1)}, u32[]{:S(2)}, u32[]{:S(2)}) collective-permute-start(f32[72,512]{1,0:T(8,128)S(1)} %get-tuple-element.32), channel_id=1, source_target_pairs={{0,2},{1,3},{2,0},{3,1},{4,6},{5,7},{6,4},{7,5},{8,10},{9,11},{10,... | collective-permute-start | bytes 442376 | tf_op jit(solution)/shard_map/ppermute | solution.py:492
  131.7 1.3 collective-permute-start.8
  133.0 1.0 collective-permute-start.7
  134.0 0.1 collective-permute-start.6
  134.1 1.8 %collective-permute-done.8.refs_3_ = f32[2,128,128]{2,1,0:T(8,128)S(1)} collective-permute-done((f32[2,128,128]{2,1,0:T(8,128)S(1)}, f32[2,128,128]{2,1,0:T(8,128)S(1)}, u32[]{:S(2)}, u32[]{:S(2)}) %collective-permute-start.8) | collective-permute-done | bytes 131104 | tf_op jit(solution)/shard_map/ppermute | solution.py:497
  135.9 2.5 %collective-permute-done.7.refs_2_ = f32[2,128,128]{2,1,0:T(8,128)S(1)} collective-permute-done((f32[2,128,128]{2,1,0:T(8,128)S(1)}, f32[2,128,128]{2,1,0:T(8,128)S(1)}, u32[]{:S(2)}, u32[]{:S(2)}) %collective-permute-start.7) | collective-permute-done | bytes 131104 | tf_op jit(solution)/shard_map/ppermute | solution.py:497
  138.4 1.9 %collective-permute-done.6.refs_1_ = f32[2,128,128]{2,1,0:T(8,128)S(1)} collective-permute-done((f32[2,128,128]{2,1,0:T(8,128)S(1)}, f32[2,128,128]{2,1,0:T(8,128)S(1)}, u32[]{:S(2)}, u32[]{:S(2)}) %collective-permute-start.6) | collective-permute-done | bytes 131104 | tf_op jit(solution)/shard_map/ppermute | solution.py:497
  140.3 1.4 join.1
  141.7 0.7 end.1
  (40 shorter events, 0.1 us)
Async XLA Ops:
  19.0 8.6 %copy-start.3 = (bf16[1024,128]{1,0:T(8,128)(2,1)S(1)}, bf16[1024,128]{1,0:T(8,128)(2,1)}, u32[]{:S(2)}) copy-start(bf16[1024,128]{1,0:T(8,128)(2,1)} %k_ref.3) | copy-start | bytes 786436
  19.0 9.5 %copy-start.19 = (s32[512]{0:T(512)S(1)}, s32[512]{0:T(512)}, u32[]{:S(2)}) copy-start(s32[512]{0:T(512)} %param.14) | copy-start | bytes 6148
  19.0 9.5 %copy-start.20 = (s32[512]{0:T(512)S(1)}, s32[512]{0:T(512)}, u32[]{:S(2)}) copy-start(s32[512]{0:T(512)} %param.15) | copy-start | bytes 6148
  19.0 19.8 %all-to-all-start = ((f32[16,16,512]{2,1,0:T(8,128)}), f32[16,16,512]{2,1,0:T(8,128)S(1)}, u32[]{:S(2)}, u32[]{:S(2)}) async-start(f32[16,16,512]{2,1,0:T(8,128)} %get-tuple-element.24), calls=%async_computation | async-start | bytes 1048576 | tf_op jit(solution)/shard_map/all_to_all | solution.py:488
  29.1 14.8 %copy-start.1 = (bf16[2,512,256]{2,1,0:T(8,128)(2,1)S(1)}, bf16[2,512,256]{2,1,0:T(8,128)(2,1)}, u32[]{:S(2)}) copy-start(bf16[2,512,256]{2,1,0:T(8,128)(2,1)} %get-tuple-element.22.sel_ref) | copy-start | bytes 1572868
  29.1 14.8 %copy-start.5 = (f32[128,256]{1,0:T(8,128)S(1)}, f32[128,256]{1,0:T(8,128)}, u32[]{:S(2)}) copy-start(f32[128,256]{1,0:T(8,128)} %get-tuple-element.23.m_ref) | copy-start | bytes 393220
  38.8 11.9 %all-to-all-start.2 = ((f32[16,8,128]{2,1,0:T(8,128)}), f32[16,8,128]{2,1,0:T(8,128)S(1)}, u32[]{:S(2)}, u32[]{:S(2)}) async-start(f32[16,8,128]{2,1,0:T(8,128)} %get-tuple-element.26), calls=%async_computation.2 | async-start | bytes 131072 | tf_op jit(solution)/shard_map/all_to_all | solution.py:488
  50.7 20.4 %all-to-all-start.3 = ((f32[8,64,512]{2,1,0:T(8,128)}), f32[8,64,512]{2,1,0:T(8,128)}, u32[]{:S(2)}, u32[]{:S(2)}) async-start(f32[8,64,512]{2,1,0:T(8,128)} %shard_map.104), calls=%async_computation.3 | async-start | bytes 2097152 | tf_op jit(solution)/shard_map/all_to_all | solution.py:488
  62.6 12.4 %copy-start.18 = (f32[64,64]{1,0:T(8,128)S(1)}, f32[64,64]{1,0:T(8,128)}, u32[]{:S(2)}) copy-start(f32[64,64]{1,0:T(8,128)} %w_ref.1) | copy-start | bytes 49156
  62.6 12.8 %copy-start.2 = (bf16[64,8192]{1,0:T(8,128)(2,1)S(1)}, bf16[64,8192]{1,0:T(8,128)(2,1)}, u32[]{:S(2)}) copy-start(bf16[64,8192]{1,0:T(8,128)(2,1)} %q_ref.5) | copy-start | bytes 3145732
  62.6 12.8 %copy-start.4 = (bf16[1024,128]{0,1:T(8,128)(2,1)S(1)}, bf16[1024,128]{0,1:T(8,128)(2,1)}, u32[]{:S(2)}) copy-start(bf16[1024,128]{0,1:T(8,128)(2,1)} %copy.12) | copy-start | bytes 786436
  62.6 12.8 %copy-start.6 = (f32[64,1024]{1,0:T(8,128)S(1)}, f32[64,1024]{1,0:T(8,128)}, u32[]{:S(2)}) copy-start(f32[64,1024]{1,0:T(8,128)} %get-tuple-element.25.s_ref) | copy-start | bytes 786436
  62.6 12.8 %copy-start.11 = (f32[64]{0:T(128)S(1)}, f32[64]{0:T(128)}, u32[]{:S(2)}) copy-start(f32[64]{0:T(128)} %param.13) | copy-start | bytes 772
  71.2 18.4 %all-to-all-start.1 = ((f32[8,64,512]{2,1,0:T(8,128)}), f32[8,64,512]{2,1,0:T(8,128)S(1)}, u32[]{:S(2)}, u32[]{:S(2)}) async-start(f32[8,64,512]{2,1,0:T(8,128)} %shard_map.103), calls=%async_computation.1 | async-start | bytes 2097152 | tf_op jit(solution)/shard_map/all_to_all | solution.py:488
  84.4 1.4 %copy-start = (f32[16,72,512]{2,1,0:T(8,128)}, f32[16,72,512]{2,1,0:T(8,128)S(1)}, u32[]{:S(2)}) copy-start(f32[16,72,512]{2,1,0:T(8,128)S(1)} %get-tuple-element.27.refs_0_) | copy-start | bytes 7077892
  85.8 0.7 copy-start.7
  89.6 1.0 copy-start.8
  101.6 6.0 %copy-start.9 = (f32[2,128,128]{2,1,0:T(8,128)}, f32[2,128,128]{2,1,0:T(8,128)S(1)}, u32[]{:S(2)}) copy-start(f32[2,128,128]{2,1,0:T(8,128)S(1)} %get-tuple-element.34) | copy-start | bytes 393220
  101.6 6.0 %copy-start.12 = (f32[2,128,128]{2,1,0:T(8,128)}, f32[2,128,128]{2,1,0:T(8,128)S(1)}, u32[]{:S(2)}) copy-start(f32[2,128,128]{2,1,0:T(8,128)S(1)} %get-tuple-element.37) | copy-start | bytes 393220
  101.6 6.0 %copy-start.14 = (f32[2,128,128]{2,1,0:T(8,128)}, f32[2,128,128]{2,1,0:T(8,128)S(1)}, u32[]{:S(2)}) copy-start(f32[2,128,128]{2,1,0:T(8,128)S(1)} %get-tuple-element.36) | copy-start | bytes 393220
  101.6 6.0 %copy-start.16 = (f32[2,128,128]{2,1,0:T(8,128)}, f32[2,128,128]{2,1,0:T(8,128)S(1)}, u32[]{:S(2)}) copy-start(f32[2,128,128]{2,1,0:T(8,128)S(1)} %get-tuple-element.35) | copy-start | bytes 393220
  101.6 3.4 %collective-permute-start = (f32[8,72,512]{2,1,0:T(8,128)S(1)}, f32[8,72,512]{2,1,0:T(8,128)S(1)}, u32[]{:S(2)}, u32[]{:S(2)}) collective-permute-start(f32[8,72,512]{2,1,0:T(8,128)S(1)} %get-tuple-element.30), channel_id=1, source_target_pairs={{0,1},{1,0},{2,3},{3,2},{4,5},{5,4},{6,7},{7,6},{8,9},{9,8},{10,11... | collective-permute-start | bytes 3538952 | tf_op jit(solution)/shard_map/ppermute | solution.py:492
  107.6 4.2 %copy-start.17 = (f32[2,128,128]{2,1,0:T(8,128)S(1)}, f32[2,128,128]{2,1,0:T(8,128)}, u32[]{:S(2)}) copy-start(f32[2,128,128]{2,1,0:T(8,128)} %copy-done.16) | copy-start | bytes 393220
  107.6 4.8 %copy-start.15 = (f32[2,128,128]{2,1,0:T(8,128)S(1)}, f32[2,128,128]{2,1,0:T(8,128)}, u32[]{:S(2)}) copy-start(f32[2,128,128]{2,1,0:T(8,128)} %copy-done.14) | copy-start | bytes 393220
  107.6 6.5 %copy-start.13 = (f32[2,128,128]{2,1,0:T(8,128)S(1)}, f32[2,128,128]{2,1,0:T(8,128)}, u32[]{:S(2)}) copy-start(f32[2,128,128]{2,1,0:T(8,128)} %copy-done.12) | copy-start | bytes 393220
  107.6 12.9 %copy-start.10 = (f32[2,128,128]{2,1,0:T(8,128)S(1)}, f32[2,128,128]{2,1,0:T(8,128)}, u32[]{:S(2)}) copy-start(f32[2,128,128]{2,1,0:T(8,128)} %copy-done.9) | copy-start | bytes 393220
  107.7 20.1 %all-to-all-start.4 = ((f32[4,2,72,512]{3,2,1,0:T(8,128)}), f32[4,2,72,512]{3,2,1,0:T(8,128)S(1)}, u32[]{:S(2)}, u32[]{:S(2)}) async-start(f32[4,2,72,512]{3,2,1,0:T(8,128)} %bitcast.16), calls=%async_computation.4 | async-start | bytes 2359296 | tf_op jit(solution)/shard_map/all_to_all | solution.py:488
  111.8 6.0 %collective-permute-start.2 = (f32[2,128,128]{2,1,0:T(8,128)S(1)}, f32[2,128,128]{2,1,0:T(8,128)S(1)}, u32[]{:S(2)}, u32[]{:S(2)}) collective-permute-start(f32[2,128,128]{2,1,0:T(8,128)S(1)} %copy-done.17), channel_id=1, source_target_pairs={{0,16},{16,32},{32,48},{48,0},{64,80},{80,96},{96,112},{112,64},{1... | collective-permute-start | bytes 393224 | tf_op jit(solution)/shard_map/ppermute | solution.py:497
  112.4 7.5 %collective-permute-start.3 = (f32[2,128,128]{2,1,0:T(8,128)S(1)}, f32[2,128,128]{2,1,0:T(8,128)S(1)}, u32[]{:S(2)}, u32[]{:S(2)}) collective-permute-start(f32[2,128,128]{2,1,0:T(8,128)S(1)} %copy-done.15), channel_id=1, source_target_pairs={{0,32},{16,48},{32,0},{48,16},{64,96},{80,112},{96,64},{112,80},{1... | collective-permute-start | bytes 393224 | tf_op jit(solution)/shard_map/ppermute | solution.py:497
  114.1 6.4 %collective-permute-start.4 = (f32[2,128,128]{2,1,0:T(8,128)S(1)}, f32[2,128,128]{2,1,0:T(8,128)S(1)}, u32[]{:S(2)}, u32[]{:S(2)}) collective-permute-start(f32[2,128,128]{2,1,0:T(8,128)S(1)} %copy-done.13), channel_id=1, source_target_pairs={{0,48},{16,0},{32,16},{48,32},{64,112},{80,64},{96,80},{112,96},{1... | collective-permute-start | bytes 393224 | tf_op jit(solution)/shard_map/ppermute | solution.py:497
  120.6 11.1 %collective-permute-start.5 = (f32[2,128,128]{2,1,0:T(8,128)S(1)}, f32[2,128,128]{2,1,0:T(8,128)S(1)}, u32[]{:S(2)}, u32[]{:S(2)}) collective-permute-start(f32[2,128,128]{2,1,0:T(8,128)S(1)} %add_add_fusion), channel_id=1, source_target_pairs={{0,64},{16,80},{32,96},{48,112},{64,0},{80,16},{96,32},{112,48},{1... | collective-permute-start | bytes 393224 | tf_op jit(solution)/shard_map/ppermute | solution.py:492
  128.4 13.3 %collective-permute-start.1 = (f32[72,512]{1,0:T(8,128)S(1)}, f32[72,512]{1,0:T(8,128)S(1)}, u32[]{:S(2)}, u32[]{:S(2)}) collective-permute-start(f32[72,512]{1,0:T(8,128)S(1)} %get-tuple-element.32), channel_id=1, source_target_pairs={{0,2},{1,3},{2,0},{3,1},{4,6},{5,7},{6,4},{7,5},{8,10},{9,11},{10,... | collective-permute-start | bytes 442376 | tf_op jit(solution)/shard_map/ppermute | solution.py:492
  131.7 4.2 %collective-permute-start.8 = (f32[2,128,128]{2,1,0:T(8,128)S(1)}, f32[2,128,128]{2,1,0:T(8,128)S(1)}, u32[]{:S(2)}, u32[]{:S(2)}) collective-permute-start(f32[2,128,128]{2,1,0:T(8,128)S(1)} %add.38.refs_0_), channel_id=1, source_target_pairs={{0,48},{16,0},{32,16},{48,32},{64,112},{80,64},{96,80},{112,96},{1... | collective-permute-start | bytes 393224 | tf_op jit(solution)/shard_map/ppermute | solution.py:497
  133.0 5.4 %collective-permute-start.7 = (f32[2,128,128]{2,1,0:T(8,128)S(1)}, f32[2,128,128]{2,1,0:T(8,128)S(1)}, u32[]{:S(2)}, u32[]{:S(2)}) collective-permute-start(f32[2,128,128]{2,1,0:T(8,128)S(1)} %add.38.refs_0_), channel_id=1, source_target_pairs={{0,32},{16,48},{32,0},{48,16},{64,96},{80,112},{96,64},{112,80},{1... | collective-permute-start | bytes 393224 | tf_op jit(solution)/shard_map/ppermute | solution.py:497
  134.0 6.3 %collective-permute-start.6 = (f32[2,128,128]{2,1,0:T(8,128)S(1)}, f32[2,128,128]{2,1,0:T(8,128)S(1)}, u32[]{:S(2)}, u32[]{:S(2)}) collective-permute-start(f32[2,128,128]{2,1,0:T(8,128)S(1)} %add.38.refs_0_), channel_id=1, source_target_pairs={{0,16},{16,32},{32,48},{48,0},{64,80},{80,96},{96,112},{112,64},{1... | collective-permute-start | bytes 393224 | tf_op jit(solution)/shard_map/ppermute | solution.py:497

commit v6 on v5

--- a/solution.py
+++ b/solution.py
@@ -120,9 +120,7 @@
     def send(t):
         dims = lambda x, y: (x, y, (((1,), (1,)), ((), ())))
         lse = split_dot(part_ref[t], sel_ref[t], dims, 3)
-        lse = jnp.where(any_seen(), lse, FLOOR) if t == 0 else lse_ref[0] + lse
-        for i in range(lse_ref.shape[0]):
-            lse_ref[i] = lse
+        lse_ref[...] = jnp.where(any_seen(), lse, FLOOR) if t == 0 else lse_ref[...] + lse
 
     for t in range(tiles):
         used = in_use(t, count_ref)
@@ -131,7 +129,7 @@
         pl.when(used & (step == steps - 1))(functools.partial(send, t))
 
 
-def main_forward(base, kt, qt, start, pos, peers):
+def main_forward(base, kt, qt, start, pos):
     heads, lat, queries = qt.shape
     keys = kt.shape[1]
     chunks, tiles = keys // CHUNK, queries // TILE
@@ -153,7 +151,7 @@
                 pl.BlockSpec((tiles, RUN, keys, TILE), lambda i, info: (0, i, 0, 0)),
                 whole(tiles, queries, TILE),
                 whole(tiles * heads * chunks, TILE),
-                whole(peers, heads, queries),
+                whole(heads, queries),
             ],
             scratch_shapes=[
                 pltpu.VMEM((keys, lat), jnp.bfloat16),
@@ -167,7 +165,7 @@
             jax.ShapeDtypeStruct((tiles, heads, keys, TILE), jnp.bfloat16),
             jax.ShapeDtypeStruct((tiles, queries, TILE), jnp.bfloat16),
             jax.ShapeDtypeStruct((tiles * heads * chunks, TILE), jnp.float32),
-            jax.ShapeDtypeStruct((peers, heads, queries), jnp.float32),
+            jax.ShapeDtypeStruct((heads, queries), jnp.float32),
         ],
         cost_estimate=pl.CostEstimate(
             flops=2 * heads * keys * queries * lat, bytes_accessed=26 << 20, transcendentals=heads * keys * queries
@@ -492,6 +490,11 @@
     return lax.ppermute(x, axis, [(i, i ^ mask) for i in range(lax.axis_size(axis))])
 
 
+def joined_lse(a, b):
+    high = jnp.maximum(a, b)
+    return high + jnp.log2(jnp.exp2(a - high) + jnp.exp2(b - high))
+
+
 def turned(x, k):
     n = lax.axis_size("head")
     return lax.ppermute(x, "head", [(i, i // ROUNDS * ROUNDS + (i + k) % ROUNDS) for i in range(n)])
@@ -510,8 +513,10 @@
     kt_index = k_index.T
     count = jnp.sum((key_start < base + keys) & (query_pos >= base), dtype=jnp.int32)
     info = count.reshape(1)
-    e, sel, high, lse = main_forward(base, k_latent.T, jnp.swapaxes(q_latent, 1, 2), start, pos, peers)
-    stats = exchanged(lse, "key")
+    e, sel, high, lse = main_forward(base, k_latent.T, jnp.swapaxes(q_latent, 1, 2), start, pos)
+    cores = [list(range(c, peers, 2)) for c in (0, 1)]
+    lse = joined_lse(lse, flipped(lse, "key", 1))
+    stats = exchanged(jnp.broadcast_to(lse, (peers // 2, *lse.shape)), "key", cores)
     scores, index_lse = index_forward(base, q_index, kt_index, head_weight, own_start, own_pos, peers)
     index_stats = exchanged(index_lse, "key")
     targets = []

time: 145 us -> 146 us (level)
  waiting for transfers between devices: 35.5 us -> 32.3 us
  starting transfers between devices: 37.7 us -> 40.7 us
    all_to_all x5, waiting for transfers between devices: 21.7 us -> 17.6 us  [exchanged(): return lax.all_to_all(x, axis, 0, 0, axis_index_groups=groups, tiled=True)]
    ppermute x3 -> x4, starting transfers between devices: 5.57 us -> 7.1 us  [flipped(): lax.ppermute(x, axis, [(i, i ^ mask) for i in range(lax.axis_size(axis))])]
    all_to_all x5, starting transfers between devices: 26.1 us -> 27.6 us  [exchanged(): return lax.all_to_all(x, axis, 0, 0, axis_index_groups=groups, tiled=True)]
    ppermute x3 -> x4, waiting for transfers between devices: 2.48 us -> 3.55 us  [flipped(): lax.ppermute(x, axis, [(i, i ^ mask) for i in range(lax.axis_size(axis))])]
  transfers between devices with their start and end apart: 14 -> 15, of which waited for: 12 -> 12; matrix products, arithmetic and copies ran while one was open for 2% -> 2% of each run, Pallas kernels for 21% -> 21%
where the time goes in v6:
time: 146 us; the launch traced here: 144 us
  Pallas kernels  60 us (41%)
  starting transfers between devices  40.7 us (28%)
  waiting for transfers between devices  32.3 us (22%)
  local copies, waits for them, and re-layouts  5.73 us (4%)
  other arithmetic  4.15 us (3%)
    all_to_all x5, starting transfers between devices, exchanged(): return lax.all_to_all(x, axis, 0, 0, axis_index_groups=groups, tiled=True)  27.6 us
    pallas_call x2, Pallas kernels, backward(): pl.pallas_call(functools.partial(back_kernel, last), grid_spec=pltpu.Pref...  20.1 us
    pallas_call x1, Pallas kernels, main_forward(): pl.pallas_call(main_kernel, grid_spec=pltpu.PrefetchScalarGridSpec(num_sc...  18.1 us
    all_to_all x5, waiting for transfers between devices, exchanged(): return lax.all_to_all(x, axis, 0, 0, axis_index_groups=groups, tiled=True)  17.6 us
    pallas_call x2, Pallas kernels, weighted_sum(): pl.pallas_call(functools.partial(sum_kernel, first), grid_spec=pltpu.Pref...  13.5 us
    ppermute x6, waiting for transfers between devices, turned(): lax.ppermute(x, 'head', [(i, i // ROUNDS * ROUNDS + (i + k) % ROUNDS) for...  11.1 us
    ppermute x4, starting transfers between devices, flipped(): lax.ppermute(x, axis, [(i, i ^ mask) for i in range(lax.axis_size(axis))])  7.1 us
    ppermute x6, starting transfers between devices, turned(): lax.ppermute(x, 'head', [(i, i // ROUNDS * ROUNDS + (i + k) % ROUNDS) for...  6.06 us
  transfers between devices with their start and end apart: 15, of which 12 were waited for; matrix products, arithmetic and copies ran while one was open for 2% of the time, Pallas kernels for 21%

profile of v6, /device:TPU:1, one launch (start us, length us, event | category | flops | bytes accessed | tf_op | source)
XLA Modules:
  0.0 143.8 jit_solution(7842656870874047353)
XLA Ops:
  0.6 18.1 %main_forward.1 = (bf16[2,16,1024,256]{3,2,1,0:T(8,128)(2,1)}, bf16[2,512,256]{2,1,0:T(8,128)(2,1)}, f32[128,256]{1,0:T(8,128)}, f32[16,512]{1,0:T(8,128)}) custom-call(s32[1]{0:T(128)} %bitcast.3.base_ref, bf16[576,1024]{1,0:T(8,128)(2,1)} %bitcast.33, bf16[16,576,512]{2,1,0:T(8,128)(2,1)} %bitcast.28, bf16[16,576,512]{2,1,0:T(8,128)(2,1)} %bitcast.29, ...), custom_call_target="tpu_custom_call" | custom-call | flops 9663676416 | bytes 27262976 | tf_op jit(solution)/shard_map/main_forward/pallas_call | solution.py:138
  18.8 1.5 %collective-permute-start = (f32[16,512]{1,0:T(8,128)}, f32[16,512]{1,0:T(8,128)S(1)}, u32[]{:S(2)}, u32[]{:S(2)}) collective-permute-start(f32[16,512]{1,0:T(8,128)} %get-tuple-element.24), channel_id=1, source_target_pairs={{0,1},{1,0},{2,3},{3,2},{4,5},{5,4},{6,7},{7,6},{8,9},{9,8},{10,11... | collective-permute-start | bytes 98312 | tf_op jit(solution)/shard_map/ppermute | solution.py:490
  20.3 1.1 collective-permute-done
  21.3 0.8 multiply_add_fusion
  22.1 0.7 broadcast_in_dim.3
  22.9 6.8 %all-to-all-start = ((f32[8,16,512]{2,1,0:T(8,128)}), f32[8,16,512]{2,1,0:T(8,128)S(1)}, u32[]{:S(2)}, u32[]{:S(2)}) async-start(f32[8,16,512]{2,1,0:T(8,128)} %broadcast_in_dim.3), calls=%async_computation | async-start | bytes 524288 | tf_op jit(solution)/shard_map/all_to_all | solution.py:486
  29.6 0.9 copy.12
  30.5 0.7 dynamic-slice_bitcast_fusion
  31.1 5.7 %index_forward.1 = (f32[64,1024]{1,0:T(8,128)}, f32[16,8,128]{2,1,0:T(8,128)}) custom-call(s32[1]{0:T(128)} %bitcast.3.base_ref, bf16[64,8192]{1,0:T(8,128)(2,1)} %q_ref.5, bf16[128,1024]{1,0:T(8,128)(2,1)} %bitcast.23, f32[64,64]{1,0:T(8,128)} %w_ref.1, s32[1,64]{1,0:T(1,128)} %get-tuple-element.40.start_ref, s32[1,64]{1,0:T(1,128)} %get-tuple-element.39.pos_ref), custom_call_target="tpu_custom_call" | custom-call | flops 1073741824 | bytes 2097152 | tf_op jit(solution)/shard_map/index_forward/pallas_call | solution.py:207
  36.8 0.3 all-to-all-done.stats_ref
  37.1 7.6 %all-to-all-start.2 = ((f32[16,8,128]{2,1,0:T(8,128)}), f32[16,8,128]{2,1,0:T(8,128)S(1)}, u32[]{:S(2)}, u32[]{:S(2)}) async-start(f32[16,8,128]{2,1,0:T(8,128)} %get-tuple-element.26), calls=%async_computation.2 | async-start | bytes 131072 | tf_op jit(solution)/shard_map/all_to_all | solution.py:486
  44.6 0.7 convert_reduce_fusion
  45.3 6.7 %shard_map.104 = f32[8,64,512]{2,1,0:T(8,128)} custom-call(s32[1]{0:T(128)} %bitcast.5.info_ref, bf16[2,16,1024,256]{3,2,1,0:T(8,128)(2,1)} %get-tuple-element.21.e_ref, bf16[2,512,256]{2,1,0:T(8,128)(2,1)S(1)} %copy-done.1, f32[128,256]{1,0:T(8,128)S(1)} %copy-done.5, f32[8,16,512]{2,1,0:T(8,128)S(1)} %all-to-all-done.stats_ref), custom_call_target="tpu_custom_call" | custom-call | flops 8388608 | bytes 9437184 | tf_op jit(solution)/shard_map/pallas_call | solution.py:274
  52.1 5.1 %all-to-all-start.3 = ((f32[8,64,512]{2,1,0:T(8,128)}), f32[8,64,512]{2,1,0:T(8,128)}, u32[]{:S(2)}, u32[]{:S(2)}) async-start(f32[8,64,512]{2,1,0:T(8,128)} %shard_map.104), calls=%async_computation.3 | async-start | bytes 2097152 | tf_op jit(solution)/shard_map/all_to_all | solution.py:486
  57.2 6.8 %shard_map.103 = f32[8,64,512]{2,1,0:T(8,128)} custom-call(s32[1]{0:T(128)} %bitcast.5.info_ref, bf16[2,16,1024,256]{3,2,1,0:T(8,128)(2,1)} %get-tuple-element.21.e_ref, bf16[2,512,256]{2,1,0:T(8,128)(2,1)S(1)} %copy-done.1, f32[128,256]{1,0:T(8,128)S(1)} %copy-done.5, f32[8,16,512]{2,1,0:T(8,128)S(1)} %all-to-all-done.stats_ref), custom_call_target="tpu_custom_call" | custom-call | flops 8388608 | bytes 9437184 | tf_op jit(solution)/shard_map/pallas_call | solution.py:274
  64.0 8.5 %all-to-all-done.3.t_ref = f32[8,64,512]{2,1,0:T(8,128)} async-done(((f32[8,64,512]{2,1,0:T(8,128)}), f32[8,64,512]{2,1,0:T(8,128)}, u32[]{:S(2)}, u32[]{:S(2)}) %all-to-all-start.3) | async-done | bytes 1048608 | tf_op jit(solution)/shard_map/all_to_all | solution.py:486
  72.5 3.7 %all-to-all-start.1 = ((f32[8,64,512]{2,1,0:T(8,128)}), f32[8,64,512]{2,1,0:T(8,128)S(1)}, u32[]{:S(2)}, u32[]{:S(2)}) async-start(f32[8,64,512]{2,1,0:T(8,128)} %shard_map.103), calls=%async_computation.1 | async-start | bytes 2097152 | tf_op jit(solution)/shard_map/all_to_all | solution.py:486
  76.3 0.1 copy.13
  76.4 0.2 copy.14
  76.6 0.1 pad_add_fusion.place_ref
  76.7 9.0 %shard_map.105 = (f32[16,72,512]{2,1,0:T(8,128)S(1)}, f32[8,64,128]{2,1,0:T(8,128)S(1)}) custom-call(s32[3]{0:T(128)S(1)} %pad_add_fusion.place_ref, f32[8,64,512]{2,1,0:T(8,128)} %all-to-all-done.3.t_ref, f32[64,1024]{1,0:T(8,128)S(1)} %copy-done.6, f32[16,8,128]{2,1,0:T(8,128)S(1)} %all-to-all-done.2.stats_ref, f32[1,64]{1,0:T(1,128)S(1)} %bitcast.26, ...), custom_call_target="tpu_custom_call" | custom-call | flops 1610612736 | bytes 4194304 | tf_op jit(solution)/shard_map/pallas_call | solution.py:408
  85.7 1.4 copy-done
  87.2 0.7 copy-done.7
  87.9 3.1 %all-to-all-done.1.t_ref = f32[8,64,512]{2,1,0:T(8,128)S(1)} async-done(((f32[8,64,512]{2,1,0:T(8,128)}), f32[8,64,512]{2,1,0:T(8,128)S(1)}, u32[]{:S(2)}, u32[]{:S(2)}) %all-to-all-start.1) | async-done | bytes 1048608 | tf_op jit(solution)/shard_map/all_to_all | solution.py:486
  90.9 0.9 copy-done.8
  91.9 11.1 %shard_map.106 = (f32[8,72,512]{2,1,0:T(8,128)S(1)}, f32[8,72,512]{2,1,0:T(8,128)}, f32[2,128,128]{2,1,0:T(8,128)S(1)}, f32[2,128,128]{2,1,0:T(8,128)S(1)}, f32[...) custom-call(s32[3]{0:T(128)S(1)} %pad_add_fusion.place_ref, f32[8,64,512]{2,1,0:T(8,128)S(1)} %all-to-all-done.1.t_ref, ...), custom_call_target="tpu_custom_call" | custom-call | flops 1610612736 | bytes 4194304 | tf_op jit(solution)/shard_map/pallas_call | solution.py:408
  103.0 0.8 collective-permute-start.1
  103.8 2.5 %collective-permute-done.1 = f32[8,72,512]{2,1,0:T(8,128)S(1)} collective-permute-done((f32[8,72,512]{2,1,0:T(8,128)S(1)}, f32[8,72,512]{2,1,0:T(8,128)S(1)}, u32[]{:S(2)}, u32[]{:S(2)}) %collective-permute-start.1) | collective-permute-done | bytes 1179680 | tf_op jit(solution)/shard_map/ppermute | solution.py:490
  106.3 2.5 %add.42 = f32[8,72,512]{2,1,0:T(8,128)} add(f32[8,72,512]{2,1,0:T(8,128)} %get-tuple-element.29, f32[8,72,512]{2,1,0:T(8,128)S(1)} %collective-permute-done.1) | non-fusion elementwise | flops 294912 | bytes 3538944 | tf_op jit(solution)/shard_map/add | solution.py:535
  108.9 4.4 %all-to-all-start.4 = ((f32[4,2,72,512]{3,2,1,0:T(8,128)}), f32[4,2,72,512]{3,2,1,0:T(8,128)S(1)}, u32[]{:S(2)}, u32[]{:S(2)}) async-start(f32[4,2,72,512]{3,2,1,0:T(8,128)} %bitcast.16), calls=%async_computation.4 | async-start | bytes 2359296 | tf_op jit(solution)/shard_map/all_to_all | solution.py:486
  113.3 0.5 collective-permute-start.3
  113.8 1.9 %collective-permute-start.4 = (f32[2,128,128]{2,1,0:T(8,128)S(1)}, f32[2,128,128]{2,1,0:T(8,128)S(1)}, u32[]{:S(2)}, u32[]{:S(2)}) collective-permute-start(f32[2,128,128]{2,1,0:T(8,128)S(1)} %copy-done.15), channel_id=1, source_target_pairs={{0,32},{16,48},{32,0},{48,16},{64,96},{80,112},{96,64},{112,80},{1... | collective-permute-start | bytes 393224 | tf_op jit(solution)/shard_map/ppermute | solution.py:500
  115.7 1.2 collective-permute-start.5
  117.0 2.2 %collective-permute-done.3 = f32[2,128,128]{2,1,0:T(8,128)S(1)} collective-permute-done((f32[2,128,128]{2,1,0:T(8,128)S(1)}, f32[2,128,128]{2,1,0:T(8,128)S(1)}, u32[]{:S(2)}, u32[]{:S(2)}) %collective-permute-start.3) | collective-permute-done | bytes 131104 | tf_op jit(solution)/shard_map/ppermute | solution.py:500
  119.1 2.3 %collective-permute-done.4 = f32[2,128,128]{2,1,0:T(8,128)S(1)} collective-permute-done((f32[2,128,128]{2,1,0:T(8,128)S(1)}, f32[2,128,128]{2,1,0:T(8,128)S(1)}, u32[]{:S(2)}, u32[]{:S(2)}) %collective-permute-start.4) | collective-permute-done | bytes 131104 | tf_op jit(solution)/shard_map/ppermute | solution.py:500
  121.5 0.5 collective-permute-done.5
  122.0 1.4 %collective-permute-start.6 = (f32[2,128,128]{2,1,0:T(8,128)S(1)}, f32[2,128,128]{2,1,0:T(8,128)S(1)}, u32[]{:S(2)}, u32[]{:S(2)}) collective-permute-start(f32[2,128,128]{2,1,0:T(8,128)S(1)} %add_add_fusion), channel_id=1, source_target_pairs={{0,64},{16,80},{32,96},{48,112},{64,0},{80,16},{96,32},{112,48},{1... | collective-permute-start | bytes 393224 | tf_op jit(solution)/shard_map/ppermute | solution.py:490
  123.5 5.7 %all-to-all-done.4.x_ref = f32[4,2,72,512]{3,2,1,0:T(8,128)S(1)} async-done(((f32[4,2,72,512]{3,2,1,0:T(8,128)}), f32[4,2,72,512]{3,2,1,0:T(8,128)S(1)}, u32[]{:S(2)}, u32[]{:S(2)}) %all-to-all-start.4) | async-done | bytes 1179680 | tf_op jit(solution)/shard_map/all_to_all | solution.py:486
  129.2 0.6 halves.1
  129.8 3.3 %collective-permute-start.2 = (f32[72,512]{1,0:T(8,128)S(1)}, f32[72,512]{1,0:T(8,128)S(1)}, u32[]{:S(2)}, u32[]{:S(2)}) collective-permute-start(f32[72,512]{1,0:T(8,128)S(1)} %get-tuple-element.32), channel_id=1, source_target_pairs={{0,2},{1,3},{2,0},{3,1},{4,6},{5,7},{6,4},{7,5},{8,10},{9,11},{10,... | collective-permute-start | bytes 442376 | tf_op jit(solution)/shard_map/ppermute | solution.py:490
  133.2 1.2 collective-permute-start.9
  134.4 1.1 collective-permute-start.8
  135.5 0.1 collective-permute-start.7
  135.6 1.8 %collective-permute-done.9.refs_3_ = f32[2,128,128]{2,1,0:T(8,128)S(1)} collective-permute-done((f32[2,128,128]{2,1,0:T(8,128)S(1)}, f32[2,128,128]{2,1,0:T(8,128)S(1)}, u32[]{:S(2)}, u32[]{:S(2)}) %collective-permute-start.9) | collective-permute-done | bytes 131104 | tf_op jit(solution)/shard_map/ppermute | solution.py:500
  137.4 2.4 %collective-permute-done.8.refs_2_ = f32[2,128,128]{2,1,0:T(8,128)S(1)} collective-permute-done((f32[2,128,128]{2,1,0:T(8,128)S(1)}, f32[2,128,128]{2,1,0:T(8,128)S(1)}, u32[]{:S(2)}, u32[]{:S(2)}) %collective-permute-start.8) | collective-permute-done | bytes 131104 | tf_op jit(solution)/shard_map/ppermute | solution.py:500
  139.8 1.9 %collective-permute-done.7.refs_1_ = f32[2,128,128]{2,1,0:T(8,128)S(1)} collective-permute-done((f32[2,128,128]{2,1,0:T(8,128)S(1)}, f32[2,128,128]{2,1,0:T(8,128)S(1)}, u32[]{:S(2)}, u32[]{:S(2)}) %collective-permute-start.7) | collective-permute-done | bytes 131104 | tf_op jit(solution)/shard_map/ppermute | solution.py:500
  141.7 1.4 join.1
  143.1 0.7 end.1
  (44 shorter events, 0.1 us)
Async XLA Ops:
  0.6 29.0 %copy-start.3 = (bf16[1024,128]{1,0:T(8,128)(2,1)S(1)}, bf16[1024,128]{1,0:T(8,128)(2,1)}, u32[]{:S(2)}) copy-start(bf16[1024,128]{1,0:T(8,128)(2,1)} %k_ref.3) | copy-start | bytes 786436
  18.8 11.7 %copy-start.19 = (s32[512]{0:T(512)S(1)}, s32[512]{0:T(512)}, u32[]{:S(2)}) copy-start(s32[512]{0:T(512)} %param.14) | copy-start | bytes 6148
  18.8 11.7 %copy-start.20 = (s32[512]{0:T(512)S(1)}, s32[512]{0:T(512)}, u32[]{:S(2)}) copy-start(s32[512]{0:T(512)} %param.15) | copy-start | bytes 6148
  18.8 2.5 %collective-permute-start = (f32[16,512]{1,0:T(8,128)}, f32[16,512]{1,0:T(8,128)S(1)}, u32[]{:S(2)}, u32[]{:S(2)}) collective-permute-start(f32[16,512]{1,0:T(8,128)} %get-tuple-element.24), channel_id=1, source_target_pairs={{0,1},{1,0},{2,3},{3,2},{4,5},{5,4},{6,7},{7,6},{8,9},{9,8},{10,11... | collective-permute-start | bytes 98312 | tf_op jit(solution)/shard_map/ppermute | solution.py:490
  22.9 14.2 %all-to-all-start = ((f32[8,16,512]{2,1,0:T(8,128)}), f32[8,16,512]{2,1,0:T(8,128)S(1)}, u32[]{:S(2)}, u32[]{:S(2)}) async-start(f32[8,16,512]{2,1,0:T(8,128)} %broadcast_in_dim.3), calls=%async_computation | async-start | bytes 524288 | tf_op jit(solution)/shard_map/all_to_all | solution.py:486
  31.1 14.2 %copy-start.1 = (bf16[2,512,256]{2,1,0:T(8,128)(2,1)S(1)}, bf16[2,512,256]{2,1,0:T(8,128)(2,1)}, u32[]{:S(2)}) copy-start(bf16[2,512,256]{2,1,0:T(8,128)(2,1)} %get-tuple-element.22.sel_ref) | copy-start | bytes 1572868
  31.1 14.2 %copy-start.5 = (f32[128,256]{1,0:T(8,128)S(1)}, f32[128,256]{1,0:T(8,128)}, u32[]{:S(2)}) copy-start(f32[128,256]{1,0:T(8,128)} %get-tuple-element.23.m_ref) | copy-start | bytes 393220
  37.1 15.0 %all-to-all-start.2 = ((f32[16,8,128]{2,1,0:T(8,128)}), f32[16,8,128]{2,1,0:T(8,128)S(1)}, u32[]{:S(2)}, u32[]{:S(2)}) async-start(f32[16,8,128]{2,1,0:T(8,128)} %get-tuple-element.26), calls=%async_computation.2 | async-start | bytes 131072 | tf_op jit(solution)/shard_map/all_to_all | solution.py:486
  52.1 20.4 %all-to-all-start.3 = ((f32[8,64,512]{2,1,0:T(8,128)}), f32[8,64,512]{2,1,0:T(8,128)}, u32[]{:S(2)}, u32[]{:S(2)}) async-start(f32[8,64,512]{2,1,0:T(8,128)} %shard_map.104), calls=%async_computation.3 | async-start | bytes 2097152 | tf_op jit(solution)/shard_map/all_to_all | solution.py:486
  64.0 12.3 %copy-start.18 = (f32[64,64]{1,0:T(8,128)S(1)}, f32[64,64]{1,0:T(8,128)}, u32[]{:S(2)}) copy-start(f32[64,64]{1,0:T(8,128)} %w_ref.1) | copy-start | bytes 49156
  64.0 12.7 %copy-start.2 = (bf16[64,8192]{1,0:T(8,128)(2,1)S(1)}, bf16[64,8192]{1,0:T(8,128)(2,1)}, u32[]{:S(2)}) copy-start(bf16[64,8192]{1,0:T(8,128)(2,1)} %q_ref.5) | copy-start | bytes 3145732
  64.0 12.7 %copy-start.4 = (bf16[1024,128]{0,1:T(8,128)(2,1)S(1)}, bf16[1024,128]{0,1:T(8,128)(2,1)}, u32[]{:S(2)}) copy-start(bf16[1024,128]{0,1:T(8,128)(2,1)} %copy.12) | copy-start | bytes 786436
  64.0 12.7 %copy-start.6 = (f32[64,1024]{1,0:T(8,128)S(1)}, f32[64,1024]{1,0:T(8,128)}, u32[]{:S(2)}) copy-start(f32[64,1024]{1,0:T(8,128)} %get-tuple-element.25.s_ref) | copy-start | bytes 786436
  64.0 12.7 %copy-start.11 = (f32[64]{0:T(128)S(1)}, f32[64]{0:T(128)}, u32[]{:S(2)}) copy-start(f32[64]{0:T(128)} %param.13) | copy-start | bytes 772
  72.5 18.4 %all-to-all-start.1 = ((f32[8,64,512]{2,1,0:T(8,128)}), f32[8,64,512]{2,1,0:T(8,128)S(1)}, u32[]{:S(2)}, u32[]{:S(2)}) async-start(f32[8,64,512]{2,1,0:T(8,128)} %shard_map.103), calls=%async_computation.1 | async-start | bytes 2097152 | tf_op jit(solution)/shard_map/all_to_all | solution.py:486
  85.7 1.4 %copy-start = (f32[16,72,512]{2,1,0:T(8,128)}, f32[16,72,512]{2,1,0:T(8,128)S(1)}, u32[]{:S(2)}) copy-start(f32[16,72,512]{2,1,0:T(8,128)S(1)} %get-tuple-element.27.refs_0_) | copy-start | bytes 7077892
  87.2 0.7 copy-start.7
  90.9 1.0 copy-start.8
  103.0 5.9 %copy-start.9 = (f32[2,128,128]{2,1,0:T(8,128)}, f32[2,128,128]{2,1,0:T(8,128)S(1)}, u32[]{:S(2)}) copy-start(f32[2,128,128]{2,1,0:T(8,128)S(1)} %get-tuple-element.34) | copy-start | bytes 393220
  103.0 5.9 %copy-start.12 = (f32[2,128,128]{2,1,0:T(8,128)}, f32[2,128,128]{2,1,0:T(8,128)S(1)}, u32[]{:S(2)}) copy-start(f32[2,128,128]{2,1,0:T(8,128)S(1)} %get-tuple-element.37) | copy-start | bytes 393220
  103.0 5.9 %copy-start.14 = (f32[2,128,128]{2,1,0:T(8,128)}, f32[2,128,128]{2,1,0:T(8,128)S(1)}, u32[]{:S(2)}) copy-start(f32[2,128,128]{2,1,0:T(8,128)S(1)} %get-tuple-element.36) | copy-start | bytes 393220
  103.0 5.9 %copy-start.16 = (f32[2,128,128]{2,1,0:T(8,128)}, f32[2,128,128]{2,1,0:T(8,128)S(1)}, u32[]{:S(2)}) copy-start(f32[2,128,128]{2,1,0:T(8,128)S(1)} %get-tuple-element.35) | copy-start | bytes 393220
  103.0 3.3 %collective-permute-start.1 = (f32[8,72,512]{2,1,0:T(8,128)S(1)}, f32[8,72,512]{2,1,0:T(8,128)S(1)}, u32[]{:S(2)}, u32[]{:S(2)}) collective-permute-start(f32[8,72,512]{2,1,0:T(8,128)S(1)} %get-tuple-element.30), channel_id=1, source_target_pairs={{0,1},{1,0},{2,3},{3,2},{4,5},{5,4},{6,7},{7,6},{8,9},{9,8},{10,11... | collective-permute-start | bytes 3538952 | tf_op jit(solution)/shard_map/ppermute | solution.py:490
  108.9 4.4 %copy-start.17 = (f32[2,128,128]{2,1,0:T(8,128)S(1)}, f32[2,128,128]{2,1,0:T(8,128)}, u32[]{:S(2)}) copy-start(f32[2,128,128]{2,1,0:T(8,128)} %copy-done.16) | copy-start | bytes 393220
  108.9 4.9 %copy-start.15 = (f32[2,128,128]{2,1,0:T(8,128)S(1)}, f32[2,128,128]{2,1,0:T(8,128)}, u32[]{:S(2)}) copy-start(f32[2,128,128]{2,1,0:T(8,128)} %copy-done.14) | copy-start | bytes 393220
  108.9 6.8 %copy-start.13 = (f32[2,128,128]{2,1,0:T(8,128)S(1)}, f32[2,128,128]{2,1,0:T(8,128)}, u32[]{:S(2)}) copy-start(f32[2,128,128]{2,1,0:T(8,128)} %copy-done.12) | copy-start | bytes 393220
  108.9 13.1 %copy-start.10 = (f32[2,128,128]{2,1,0:T(8,128)S(1)}, f32[2,128,128]{2,1,0:T(8,128)}, u32[]{:S(2)}) copy-start(f32[2,128,128]{2,1,0:T(8,128)} %copy-done.9) | copy-start | bytes 393220
  108.9 20.3 %all-to-all-start.4 = ((f32[4,2,72,512]{3,2,1,0:T(8,128)}), f32[4,2,72,512]{3,2,1,0:T(8,128)S(1)}, u32[]{:S(2)}, u32[]{:S(2)}) async-start(f32[4,2,72,512]{3,2,1,0:T(8,128)} %bitcast.16), calls=%async_computation.4 | async-start | bytes 2359296 | tf_op jit(solution)/shard_map/all_to_all | solution.py:486
  113.3 5.9 %collective-permute-start.3 = (f32[2,128,128]{2,1,0:T(8,128)S(1)}, f32[2,128,128]{2,1,0:T(8,128)S(1)}, u32[]{:S(2)}, u32[]{:S(2)}) collective-permute-start(f32[2,128,128]{2,1,0:T(8,128)S(1)} %copy-done.17), channel_id=1, source_target_pairs={{0,16},{16,32},{32,48},{48,0},{64,80},{80,96},{96,112},{112,64},{1... | collective-permute-start | bytes 393224 | tf_op jit(solution)/shard_map/ppermute | solution.py:500
  113.8 7.7 %collective-permute-start.4 = (f32[2,128,128]{2,1,0:T(8,128)S(1)}, f32[2,128,128]{2,1,0:T(8,128)S(1)}, u32[]{:S(2)}, u32[]{:S(2)}) collective-permute-start(f32[2,128,128]{2,1,0:T(8,128)S(1)} %copy-done.15), channel_id=1, source_target_pairs={{0,32},{16,48},{32,0},{48,16},{64,96},{80,112},{96,64},{112,80},{1... | collective-permute-start | bytes 393224 | tf_op jit(solution)/shard_map/ppermute | solution.py:500
  115.7 6.3 %collective-permute-start.5 = (f32[2,128,128]{2,1,0:T(8,128)S(1)}, f32[2,128,128]{2,1,0:T(8,128)S(1)}, u32[]{:S(2)}, u32[]{:S(2)}) collective-permute-start(f32[2,128,128]{2,1,0:T(8,128)S(1)} %copy-done.13), channel_id=1, source_target_pairs={{0,48},{16,0},{32,16},{48,32},{64,112},{80,64},{96,80},{112,96},{1... | collective-permute-start | bytes 393224 | tf_op jit(solution)/shard_map/ppermute | solution.py:500
  122.0 11.1 %collective-permute-start.6 = (f32[2,128,128]{2,1,0:T(8,128)S(1)}, f32[2,128,128]{2,1,0:T(8,128)S(1)}, u32[]{:S(2)}, u32[]{:S(2)}) collective-permute-start(f32[2,128,128]{2,1,0:T(8,128)S(1)} %add_add_fusion), channel_id=1, source_target_pairs={{0,64},{16,80},{32,96},{48,112},{64,0},{80,16},{96,32},{112,48},{1... | collective-permute-start | bytes 393224 | tf_op jit(solution)/shard_map/ppermute | solution.py:490
  129.8 13.3 %collective-permute-start.2 = (f32[72,512]{1,0:T(8,128)S(1)}, f32[72,512]{1,0:T(8,128)S(1)}, u32[]{:S(2)}, u32[]{:S(2)}) collective-permute-start(f32[72,512]{1,0:T(8,128)S(1)} %get-tuple-element.32), channel_id=1, source_target_pairs={{0,2},{1,3},{2,0},{3,1},{4,6},{5,7},{6,4},{7,5},{8,10},{9,11},{10,... | collective-permute-start | bytes 442376 | tf_op jit(solution)/shard_map/ppermute | solution.py:490
  133.2 4.2 %collective-permute-start.9 = (f32[2,128,128]{2,1,0:T(8,128)S(1)}, f32[2,128,128]{2,1,0:T(8,128)S(1)}, u32[]{:S(2)}, u32[]{:S(2)}) collective-permute-start(f32[2,128,128]{2,1,0:T(8,128)S(1)} %add.46.refs_0_), channel_id=1, source_target_pairs={{0,48},{16,0},{32,16},{48,32},{64,112},{80,64},{96,80},{112,96},{1... | collective-permute-start | bytes 393224 | tf_op jit(solution)/shard_map/ppermute | solution.py:500
  134.4 5.4 %collective-permute-start.8 = (f32[2,128,128]{2,1,0:T(8,128)S(1)}, f32[2,128,128]{2,1,0:T(8,128)S(1)}, u32[]{:S(2)}, u32[]{:S(2)}) collective-permute-start(f32[2,128,128]{2,1,0:T(8,128)S(1)} %add.46.refs_0_), channel_id=1, source_target_pairs={{0,32},{16,48},{32,0},{48,16},{64,96},{80,112},{96,64},{112,80},{1... | collective-permute-start | bytes 393224 | tf_op jit(solution)/shard_map/ppermute | solution.py:500
  135.5 6.2 %collective-permute-start.7 = (f32[2,128,128]{2,1,0:T(8,128)S(1)}, f32[2,128,128]{2,1,0:T(8,128)S(1)}, u32[]{:S(2)}, u32[]{:S(2)}) collective-permute-start(f32[2,128,128]{2,1,0:T(8,128)S(1)} %add.46.refs_0_), channel_id=1, source_target_pairs={{0,16},{16,32},{32,48},{48,0},{64,80},{80,96},{96,112},{112,64},{1... | collective-permute-start | bytes 393224 | tf_op jit(solution)/shard_map/ppermute | solution.py:500

commit v7 on v5

--- a/solution.py
+++ b/solution.py
@@ -18,6 +18,7 @@
 TILE = 256
 RUN = 4
 GROUP = 4
+PAIR = 2
 PARTS = 2
 ROUNDS = 4
 VMEM = 48 << 20
@@ -305,7 +306,6 @@
     dim = kt_ref.shape[0]
     width = dim * GROUP
     index_scale = 1.0 / math.sqrt(dim)
-    dest = far_first(i, steps, place_ref) if last else i
 
     @pl.when(i == 0)
     def _():
@@ -318,42 +318,51 @@
         g_ref[...] = jnp.where(scores > FLOOR, as_column(c_ref[...]) * (probs - target), 0.0)
         gkt_ref[...] = jnp.zeros_like(gkt_ref)
 
-    q = q_ref[:, pl.ds(pl.multiple_of(dest * width, width), width)]
-    q = jnp.concatenate([q[:, j * dim : (j + 1) * dim] for j in range(GROUP)], axis=0)
-    d = jnp.dot(q, kt_ref[...], preferred_element_type=jnp.float32)
     g = g_ref[...]
-    w = w_ref[dest]
-    parts, sums = [], []
-    for j in range(GROUP):
-        dots = d[j * rows : (j + 1) * rows]
-        kept = jnp.where(dots > 0.0, g, 0.0)
-        parts.append((kept * (w[:, j : j + 1] * index_scale)).astype(jnp.bfloat16))
-        sums.append(as_row(jnp.sum(kept * dots, axis=1, keepdims=True)))
-    head_grad = jnp.concatenate(parts, axis=0)
-    gq = jnp.dot(head_grad, k_ref[...], preferred_element_type=jnp.float32)
-    pad = jnp.zeros((1, width - rows), jnp.float32)
-    low = [jnp.concatenate([x * index_scale, pad], axis=1) for x in sums]
-    low = jnp.concatenate([*low, jnp.zeros((8 - GROUP, width), jnp.float32)], axis=0)
-    gq = jnp.concatenate([gq[j * rows : (j + 1) * rows] for j in range(GROUP)], axis=1)
-    gq = jnp.concatenate([gq, low], axis=0)
-    gkt_ref[...] += lax.dot_general(q, head_grad, (((0,), (0,)), ((), ())), preferred_element_type=jnp.float32)
+    blocks, keys_total = [], gkt_ref[...]
+    for n in range(PAIR):
+        dest = far_first(i * PAIR + n, steps * PAIR, place_ref) if last else i * PAIR + n
+        q = q_ref[:, pl.ds(pl.multiple_of(dest * width, width), width)]
+        q = jnp.concatenate([q[:, j * dim : (j + 1) * dim] for j in range(GROUP)], axis=0)
+        d = jnp.dot(q, kt_ref[...], preferred_element_type=jnp.float32)
+        w = w_ref[dest]
+        parts, sums = [], []
+        for j in range(GROUP):
+            dots = d[j * rows : (j + 1) * rows]
+            kept = jnp.where(dots > 0.0, g, 0.0)
+            parts.append((kept * (w[:, j : j + 1] * index_scale)).astype(jnp.bfloat16))
+            sums.append(as_row(jnp.sum(kept * dots, axis=1, keepdims=True)))
+        head_grad = jnp.concatenate(parts, axis=0)
+        gq = jnp.dot(head_grad, k_ref[...], preferred_element_type=jnp.float32)
+        pad = jnp.zeros((1, width - rows), jnp.float32)
+        low = [jnp.concatenate([x * index_scale, pad], axis=1) for x in sums]
+        low = jnp.concatenate([*low, jnp.zeros((8 - GROUP, width), jnp.float32)], axis=0)
+        gq = jnp.concatenate([gq[j * rows : (j + 1) * rows] for j in range(GROUP)], axis=1)
+        gq = jnp.concatenate([gq, low], axis=0)
+        keys_total = keys_total + lax.dot_general(
+            q, head_grad, (((0,), (0,)), ((), ())), preferred_element_type=jnp.float32
+        )
+        blocks.append(gq + former_ref[dest] if last else gq)
+    gkt_ref[...] = keys_total
     if not last:
-        gq_ref[0] = gq
+        for n in range(PAIR):
+            gq_ref[n] = blocks[n]
 
         @pl.when(i == steps - 1)
         def _():
             gk_ref[...] = gkt_ref[...].T.reshape(gk_ref.shape)
 
         return
-    gq = gq + former_ref[dest]
 
     @pl.when(i < steps // 2)
     def _():
-        far_ref[0] = gq
+        for n in range(PAIR):
+            far_ref[n] = blocks[n]
 
     @pl.when(i >= steps // 2)
     def _():
-        near_ref[0] = gq
+        for n in range(PAIR):
+            near_ref[n] = blocks[n]
 
     @pl.when(i == steps - 1)
     def _():
@@ -375,11 +384,12 @@
     rows, width = q.shape
     keys, dim = k.shape
     keys = keys // PARTS
-    steps = width // (dim * GROUP)
+    blocks = width // (dim * GROUP)
+    steps = blocks // PAIR
     last = former is not None
     whole = lambda *shape: pl.BlockSpec(shape, lambda i, place: (0,) * len(shape))
-    w = jnp.moveaxis(w.reshape(rows, steps, GROUP), 1, 0)
-    block, shape = (1, rows + 8, dim * GROUP), (owners, keys // owners, dim)
+    w = jnp.moveaxis(w.reshape(rows, blocks, GROUP), 1, 0)
+    block, shape = (PAIR, rows + 8, dim * GROUP), (owners, keys // owners, dim)
     array = lambda *shape: jax.ShapeDtypeStruct(shape, jnp.float32)
     in_specs = [
         whole(*t.shape),
@@ -403,10 +413,10 @@
             pl.BlockSpec(block, lambda i, place: (jnp.minimum(i, half - 1), 0, 0)),
             pl.BlockSpec(block, lambda i, place: (jnp.maximum(i - half, 0), 0, 0)),
         ] + [whole(*piece)] * ROUNDS
-        out_shape = [array(half, *block[1:])] * 2 + [array(*piece)] * ROUNDS
+        out_shape = [array(blocks // 2, *block[1:])] * 2 + [array(*piece)] * ROUNDS
     else:
         out_specs = [pl.BlockSpec(block, lambda i, place: (i, 0, 0)), whole(*shape)]
-        out_shape = [array(steps, *block[1:]), array(*shape)]
+        out_shape = [array(blocks, *block[1:]), array(*shape)]
     return pl.pallas_call(
         functools.partial(back_kernel, last),
         grid_spec=pltpu.PrefetchScalarGridSpec(
@@ -534,7 +544,8 @@
     gk = gk + flipped(gk, "head", ROUNDS)
     gk = joined(place, [gk] + [turned(gk, k) for k in range(1, ROUNDS)]).reshape(keys, -1)
     mine, other = halves(place, gq)
-    gq, gw = ended(mine, flipped(other, "key", 2))
+    other = flipped(other, "key", 2)
+    gq, gw = ended(mine, other)
     return (gq, gk, gw.T)
 
 

time: 145 us -> 143 us (0.986)
  Pallas kernels: 60 us -> 56.9 us
    pallas_call x2, Pallas kernels: 20.1 us -> 16.9 us  [backward(): pl.pallas_call(functools.partial(back_kernel, last), grid_spec=pltpu.Pref...]
  transfers between devices with their start and end apart: 14 -> 14, of which waited for: 12 -> 12; matrix products, arithmetic and copies ran while one was open for 2% -> 2% of each run, Pallas kernels for 21% -> 20%
where the time goes in v7:
time: 143 us; the launch traced here: 141 us
  Pallas kernels  56.9 us (40%)
  starting transfers between devices  37.9 us (27%)
  waiting for transfers between devices  36.7 us (26%)
  local copies, waits for them, and re-layouts  5 us (3%)
  other arithmetic  3.27 us (2%)
    all_to_all x5, starting transfers between devices, exchanged(): return lax.all_to_all(x, axis, 0, 0, axis_index_groups=groups, tiled=True)  26.1 us
    all_to_all x5, waiting for transfers between devices, exchanged(): return lax.all_to_all(x, axis, 0, 0, axis_index_groups=groups, tiled=True)  23 us
    pallas_call x1, Pallas kernels, main_forward(): pl.pallas_call(main_kernel, grid_spec=pltpu.PrefetchScalarGridSpec(num_sc...  18.3 us
    pallas_call x2, Pallas kernels, backward(): pl.pallas_call(functools.partial(back_kernel, last), grid_spec=pltpu.Pref...  16.9 us
    pallas_call x2, Pallas kernels, weighted_sum(): pl.pallas_call(functools.partial(sum_kernel, first), grid_spec=pltpu.Pref...  13.3 us
    ppermute x6, waiting for transfers between devices, turned(): lax.ppermute(x, 'head', [(i, i // ROUNDS * ROUNDS + (i + k) % ROUNDS) for...  11.1 us
    ppermute x6, starting transfers between devices, turned(): lax.ppermute(x, 'head', [(i, i // ROUNDS * ROUNDS + (i + k) % ROUNDS) for...  6.17 us
    pallas_call x1, Pallas kernels, index_forward(): pl.pallas_call(index_kernel, grid=(keys // CHUNK,), in_specs=[pl.BlockSpe...  5.66 us
  transfers between devices with their start and end apart: 14, of which 12 were waited for; matrix products, arithmetic and copies ran while one was open for 2% of the time, Pallas kernels for 20%

profile of v7, /device:TPU:1, one launch (start us, length us, event | category | flops | bytes accessed | tf_op | source)
XLA Modules:
  0.0 140.6 jit_solution(8333403614297891624)
XLA Ops:
  0.6 18.3 %main_forward.1 = (bf16[2,16,1024,256]{3,2,1,0:T(8,128)(2,1)}, bf16[2,512,256]{2,1,0:T(8,128)(2,1)}, f32[128,256]{1,0:T(8,128)}, f32[16,16,512]{2,1,0:T(8,128)}) custom-call(s32[1]{0:T(128)} %bitcast.3.base_ref, bf16[576,1024]{1,0:T(8,128)(2,1)} %bitcast.33, bf16[16,576,512]{2,1,0:T(8,128)(2,1)} %bitcast.28, bf16[16,576,512]{2,1,0:T(8,128)(2,1)} %bitcast.29, ...), custom_call_target="tpu_custom_call" | custom-call | flops 9663676416 | bytes 27262976 | tf_op jit(solution)/shard_map/main_forward/pallas_call | solution.py:141
  19.0 0.0 copy-start.3
  19.0 8.6 %all-to-all-start = ((f32[16,16,512]{2,1,0:T(8,128)}), f32[16,16,512]{2,1,0:T(8,128)S(1)}, u32[]{:S(2)}, u32[]{:S(2)}) async-start(f32[16,16,512]{2,1,0:T(8,128)} %get-tuple-element.24), calls=%async_computation | async-start | bytes 1048576 | tf_op jit(solution)/shard_map/all_to_all | solution.py:498
  27.6 0.9 copy.12
  28.5 0.6 dynamic-slice_bitcast_fusion
  29.1 5.7 %index_forward.1 = (f32[64,1024]{1,0:T(8,128)}, f32[16,8,128]{2,1,0:T(8,128)}) custom-call(s32[1]{0:T(128)} %bitcast.3.base_ref, bf16[64,8192]{1,0:T(8,128)(2,1)} %q_ref.5, bf16[128,1024]{1,0:T(8,128)(2,1)} %bitcast.23, f32[64,64]{1,0:T(8,128)} %w_ref.1, s32[1,64]{1,0:T(1,128)} %get-tuple-element.40.start_ref, s32[1,64]{1,0:T(1,128)} %get-tuple-element.39.pos_ref), custom_call_target="tpu_custom_call" | custom-call | flops 1073741824 | bytes 2097152 | tf_op jit(solution)/shard_map/index_forward/pallas_call | solution.py:210
  34.8 4.0 %all-to-all-done.stats_ref = f32[16,16,512]{2,1,0:T(8,128)S(1)} async-done(((f32[16,16,512]{2,1,0:T(8,128)}), f32[16,16,512]{2,1,0:T(8,128)S(1)}, u32[]{:S(2)}, u32[]{:S(2)}) %all-to-all-start) | async-done | bytes 524320 | tf_op jit(solution)/shard_map/all_to_all | solution.py:498
  38.8 4.5 %all-to-all-start.2 = ((f32[16,8,128]{2,1,0:T(8,128)}), f32[16,8,128]{2,1,0:T(8,128)S(1)}, u32[]{:S(2)}, u32[]{:S(2)}) async-start(f32[16,8,128]{2,1,0:T(8,128)} %get-tuple-element.26), calls=%async_computation.2 | async-start | bytes 131072 | tf_op jit(solution)/shard_map/all_to_all | solution.py:498
  43.3 0.6 convert_reduce_fusion
  43.9 6.6 %shard_map.104 = f32[8,64,512]{2,1,0:T(8,128)} custom-call(s32[1]{0:T(128)} %bitcast.5.info_ref, bf16[2,16,1024,256]{3,2,1,0:T(8,128)(2,1)} %get-tuple-element.21.e_ref, bf16[2,512,256]{2,1,0:T(8,128)(2,1)S(1)} %copy-done.1, f32[128,256]{1,0:T(8,128)S(1)} %copy-done.5, f32[16,16,512]{2,1,0:T(8,128)S(1)} %all-to-all-done.stats_ref), custom_call_target="tpu_custom_call" | custom-call | flops 8388608 | bytes 9437184 | tf_op jit(solution)/shard_map/pallas_call | solution.py:277
  50.5 0.2 all-to-all-done.2.stats_ref
  50.7 5.2 %all-to-all-start.3 = ((f32[8,64,512]{2,1,0:T(8,128)}), f32[8,64,512]{2,1,0:T(8,128)}, u32[]{:S(2)}, u32[]{:S(2)}) async-start(f32[8,64,512]{2,1,0:T(8,128)} %shard_map.104), calls=%async_computation.3 | async-start | bytes 2097152 | tf_op jit(solution)/shard_map/all_to_all | solution.py:498
  55.9 6.7 %shard_map.103 = f32[8,64,512]{2,1,0:T(8,128)} custom-call(s32[1]{0:T(128)} %bitcast.5.info_ref, bf16[2,16,1024,256]{3,2,1,0:T(8,128)(2,1)} %get-tuple-element.21.e_ref, bf16[2,512,256]{2,1,0:T(8,128)(2,1)S(1)} %copy-done.1, f32[128,256]{1,0:T(8,128)S(1)} %copy-done.5, f32[16,16,512]{2,1,0:T(8,128)S(1)} %all-to-all-done.stats_ref), custom_call_target="tpu_custom_call" | custom-call | flops 8388608 | bytes 9437184 | tf_op jit(solution)/shard_map/pallas_call | solution.py:277
  62.6 0.0 copy-start.11
  62.6 8.6 %all-to-all-done.3.t_ref = f32[8,64,512]{2,1,0:T(8,128)} async-done(((f32[8,64,512]{2,1,0:T(8,128)}), f32[8,64,512]{2,1,0:T(8,128)}, u32[]{:S(2)}, u32[]{:S(2)}) %all-to-all-start.3) | async-done | bytes 1048608 | tf_op jit(solution)/shard_map/all_to_all | solution.py:498
  71.2 3.7 %all-to-all-start.1 = ((f32[8,64,512]{2,1,0:T(8,128)}), f32[8,64,512]{2,1,0:T(8,128)S(1)}, u32[]{:S(2)}, u32[]{:S(2)}) async-start(f32[8,64,512]{2,1,0:T(8,128)} %shard_map.103), calls=%async_computation.1 | async-start | bytes 2097152 | tf_op jit(solution)/shard_map/all_to_all | solution.py:498
  74.9 0.1 copy.13
  75.0 0.2 copy.14
  75.3 0.1 pad_add_fusion.place_ref
  75.4 7.6 %shard_map.105 = (f32[16,72,512]{2,1,0:T(8,128)S(1)}, f32[8,64,128]{2,1,0:T(8,128)S(1)}) custom-call(s32[3]{0:T(128)S(1)} %pad_add_fusion.place_ref, f32[8,64,512]{2,1,0:T(8,128)} %all-to-all-done.3.t_ref, f32[64,1024]{1,0:T(8,128)S(1)} %copy-done.6, f32[16,8,128]{2,1,0:T(8,128)S(1)} %all-to-all-done.2.stats_ref, f32[1,64]{1,0:T(1,128)S(1)} %bitcast.26, ...), custom_call_target="tpu_custom_call" | custom-call | flops 1610612736 | bytes 4194304 | tf_op jit(solution)/shard_map/pallas_call | solution.py:420
  83.0 1.4 %copy-done = f32[16,72,512]{2,1,0:T(8,128)} copy-done((f32[16,72,512]{2,1,0:T(8,128)}, f32[16,72,512]{2,1,0:T(8,128)S(1)}, u32[]{:S(2)}) %copy-start) | copy-done | bytes 2359320
  84.4 0.7 copy-done.7
  85.1 4.5 %all-to-all-done.1.t_ref = f32[8,64,512]{2,1,0:T(8,128)S(1)} async-done(((f32[8,64,512]{2,1,0:T(8,128)}), f32[8,64,512]{2,1,0:T(8,128)S(1)}, u32[]{:S(2)}, u32[]{:S(2)}) %all-to-all-start.1) | async-done | bytes 1048608 | tf_op jit(solution)/shard_map/all_to_all | solution.py:498
  89.6 0.9 copy-done.8
  90.6 9.3 %shard_map.106 = (f32[8,72,512]{2,1,0:T(8,128)S(1)}, f32[8,72,512]{2,1,0:T(8,128)}, f32[2,128,128]{2,1,0:T(8,128)S(1)}, f32[2,128,128]{2,1,0:T(8,128)S(1)}, f32[...) custom-call(s32[3]{0:T(128)S(1)} %pad_add_fusion.place_ref, f32[8,64,512]{2,1,0:T(8,128)S(1)} %all-to-all-done.1.t_ref, ...), custom_call_target="tpu_custom_call" | custom-call | flops 1610612736 | bytes 4194304 | tf_op jit(solution)/shard_map/pallas_call | solution.py:420
  99.9 0.9 collective-permute-start
  100.8 2.5 %collective-permute-done = f32[8,72,512]{2,1,0:T(8,128)S(1)} collective-permute-done((f32[8,72,512]{2,1,0:T(8,128)S(1)}, f32[8,72,512]{2,1,0:T(8,128)S(1)}, u32[]{:S(2)}, u32[]{:S(2)}) %collective-permute-start) | collective-permute-done | bytes 1179680 | tf_op jit(solution)/shard_map/ppermute | solution.py:502
  103.2 2.6 %add.34 = f32[8,72,512]{2,1,0:T(8,128)} add(f32[8,72,512]{2,1,0:T(8,128)} %get-tuple-element.29, f32[8,72,512]{2,1,0:T(8,128)S(1)} %collective-permute-done) | non-fusion elementwise | flops 294912 | bytes 3538944 | tf_op jit(solution)/shard_map/add | solution.py:540
  105.8 0.0 copy-start.15
  105.8 4.1 %all-to-all-start.4 = ((f32[4,2,72,512]{3,2,1,0:T(8,128)}), f32[4,2,72,512]{3,2,1,0:T(8,128)S(1)}, u32[]{:S(2)}, u32[]{:S(2)}) async-start(f32[4,2,72,512]{3,2,1,0:T(8,128)} %bitcast.16), calls=%async_computation.4 | async-start | bytes 2359296 | tf_op jit(solution)/shard_map/all_to_all | solution.py:498
  110.0 0.6 collective-permute-start.2
  110.6 1.9 %collective-permute-start.3 = (f32[2,128,128]{2,1,0:T(8,128)S(1)}, f32[2,128,128]{2,1,0:T(8,128)S(1)}, u32[]{:S(2)}, u32[]{:S(2)}) collective-permute-start(f32[2,128,128]{2,1,0:T(8,128)S(1)} %copy-done.15), channel_id=1, source_target_pairs={{0,32},{16,48},{32,0},{48,16},{64,96},{80,112},{96,64},{112,80},{1... | collective-permute-start | bytes 393224 | tf_op jit(solution)/shard_map/ppermute | solution.py:507
  112.4 1.2 collective-permute-start.4
  113.7 2.2 %collective-permute-done.2 = f32[2,128,128]{2,1,0:T(8,128)S(1)} collective-permute-done((f32[2,128,128]{2,1,0:T(8,128)S(1)}, f32[2,128,128]{2,1,0:T(8,128)S(1)}, u32[]{:S(2)}, u32[]{:S(2)}) %collective-permute-start.2) | collective-permute-done | bytes 131104 | tf_op jit(solution)/shard_map/ppermute | solution.py:507
  115.8 2.3 %collective-permute-done.3 = f32[2,128,128]{2,1,0:T(8,128)S(1)} collective-permute-done((f32[2,128,128]{2,1,0:T(8,128)S(1)}, f32[2,128,128]{2,1,0:T(8,128)S(1)}, u32[]{:S(2)}, u32[]{:S(2)}) %collective-permute-start.3) | collective-permute-done | bytes 131104 | tf_op jit(solution)/shard_map/ppermute | solution.py:507
  118.2 0.5 collective-permute-done.4
  118.7 1.4 %collective-permute-start.5 = (f32[2,128,128]{2,1,0:T(8,128)S(1)}, f32[2,128,128]{2,1,0:T(8,128)S(1)}, u32[]{:S(2)}, u32[]{:S(2)}) collective-permute-start(f32[2,128,128]{2,1,0:T(8,128)S(1)} %add_add_fusion), channel_id=1, source_target_pairs={{0,64},{16,80},{32,96},{48,112},{64,0},{80,16},{96,32},{112,48},{1... | collective-permute-start | bytes 393224 | tf_op jit(solution)/shard_map/ppermute | solution.py:502
  120.2 5.8 %all-to-all-done.4.x_ref = f32[4,2,72,512]{3,2,1,0:T(8,128)S(1)} async-done(((f32[4,2,72,512]{3,2,1,0:T(8,128)}), f32[4,2,72,512]{3,2,1,0:T(8,128)S(1)}, u32[]{:S(2)}, u32[]{:S(2)}) %all-to-all-start.4) | async-done | bytes 1179680 | tf_op jit(solution)/shard_map/all_to_all | solution.py:498
  125.9 0.6 halves.1
  126.5 3.3 %collective-permute-start.1 = (f32[72,512]{1,0:T(8,128)S(1)}, f32[72,512]{1,0:T(8,128)S(1)}, u32[]{:S(2)}, u32[]{:S(2)}) collective-permute-start(f32[72,512]{1,0:T(8,128)S(1)} %get-tuple-element.32), channel_id=1, source_target_pairs={{0,2},{1,3},{2,0},{3,1},{4,6},{5,7},{6,4},{7,5},{8,10},{9,11},{10,... | collective-permute-start | bytes 442376 | tf_op jit(solution)/shard_map/ppermute | solution.py:502
  129.9 1.3 collective-permute-start.8
  131.2 1.1 collective-permute-start.7
  132.4 0.1 collective-permute-start.6
  132.4 1.7 %collective-permute-done.8.refs_3_ = f32[2,128,128]{2,1,0:T(8,128)S(1)} collective-permute-done((f32[2,128,128]{2,1,0:T(8,128)S(1)}, f32[2,128,128]{2,1,0:T(8,128)S(1)}, u32[]{:S(2)}, u32[]{:S(2)}) %collective-permute-start.8) | collective-permute-done | bytes 131104 | tf_op jit(solution)/shard_map/ppermute | solution.py:507
  134.1 2.5 %collective-permute-done.7.refs_2_ = f32[2,128,128]{2,1,0:T(8,128)S(1)} collective-permute-done((f32[2,128,128]{2,1,0:T(8,128)S(1)}, f32[2,128,128]{2,1,0:T(8,128)S(1)}, u32[]{:S(2)}, u32[]{:S(2)}) %collective-permute-start.7) | collective-permute-done | bytes 131104 | tf_op jit(solution)/shard_map/ppermute | solution.py:507
  136.6 1.9 %collective-permute-done.6.refs_1_ = f32[2,128,128]{2,1,0:T(8,128)S(1)} collective-permute-done((f32[2,128,128]{2,1,0:T(8,128)S(1)}, f32[2,128,128]{2,1,0:T(8,128)S(1)}, u32[]{:S(2)}, u32[]{:S(2)}) %collective-permute-start.6) | collective-permute-done | bytes 131104 | tf_op jit(solution)/shard_map/ppermute | solution.py:507
  138.5 1.4 join.1
  139.9 0.7 end.1
  (40 shorter events, 0.1 us)
Async XLA Ops:
  19.0 8.6 %copy-start.3 = (bf16[1024,128]{1,0:T(8,128)(2,1)S(1)}, bf16[1024,128]{1,0:T(8,128)(2,1)}, u32[]{:S(2)}) copy-start(bf16[1024,128]{1,0:T(8,128)(2,1)} %k_ref.3) | copy-start | bytes 786436
  19.0 9.5 %copy-start.19 = (s32[512]{0:T(512)S(1)}, s32[512]{0:T(512)}, u32[]{:S(2)}) copy-start(s32[512]{0:T(512)} %param.14) | copy-start | bytes 6148
  19.0 9.5 %copy-start.20 = (s32[512]{0:T(512)S(1)}, s32[512]{0:T(512)}, u32[]{:S(2)}) copy-start(s32[512]{0:T(512)} %param.15) | copy-start | bytes 6148
  19.0 19.8 %all-to-all-start = ((f32[16,16,512]{2,1,0:T(8,128)}), f32[16,16,512]{2,1,0:T(8,128)S(1)}, u32[]{:S(2)}, u32[]{:S(2)}) async-start(f32[16,16,512]{2,1,0:T(8,128)} %get-tuple-element.24), calls=%async_computation | async-start | bytes 1048576 | tf_op jit(solution)/shard_map/all_to_all | solution.py:498
  29.1 14.8 %copy-start.1 = (bf16[2,512,256]{2,1,0:T(8,128)(2,1)S(1)}, bf16[2,512,256]{2,1,0:T(8,128)(2,1)}, u32[]{:S(2)}) copy-start(bf16[2,512,256]{2,1,0:T(8,128)(2,1)} %get-tuple-element.22.sel_ref) | copy-start | bytes 1572868
  29.1 14.8 %copy-start.5 = (f32[128,256]{1,0:T(8,128)S(1)}, f32[128,256]{1,0:T(8,128)}, u32[]{:S(2)}) copy-start(f32[128,256]{1,0:T(8,128)} %get-tuple-element.23.m_ref) | copy-start | bytes 393220
  38.8 11.9 %all-to-all-start.2 = ((f32[16,8,128]{2,1,0:T(8,128)}), f32[16,8,128]{2,1,0:T(8,128)S(1)}, u32[]{:S(2)}, u32[]{:S(2)}) async-start(f32[16,8,128]{2,1,0:T(8,128)} %get-tuple-element.26), calls=%async_computation.2 | async-start | bytes 131072 | tf_op jit(solution)/shard_map/all_to_all | solution.py:498
  50.7 20.4 %all-to-all-start.3 = ((f32[8,64,512]{2,1,0:T(8,128)}), f32[8,64,512]{2,1,0:T(8,128)}, u32[]{:S(2)}, u32[]{:S(2)}) async-start(f32[8,64,512]{2,1,0:T(8,128)} %shard_map.104), calls=%async_computation.3 | async-start | bytes 2097152 | tf_op jit(solution)/shard_map/all_to_all | solution.py:498
  62.6 12.4 %copy-start.18 = (f32[64,64]{1,0:T(8,128)S(1)}, f32[64,64]{1,0:T(8,128)}, u32[]{:S(2)}) copy-start(f32[64,64]{1,0:T(8,128)} %w_ref.1) | copy-start | bytes 49156
  62.6 12.8 %copy-start.2 = (bf16[64,8192]{1,0:T(8,128)(2,1)S(1)}, bf16[64,8192]{1,0:T(8,128)(2,1)}, u32[]{:S(2)}) copy-start(bf16[64,8192]{1,0:T(8,128)(2,1)} %q_ref.5) | copy-start | bytes 3145732
  62.6 12.8 %copy-start.4 = (bf16[1024,128]{0,1:T(8,128)(2,1)S(1)}, bf16[1024,128]{0,1:T(8,128)(2,1)}, u32[]{:S(2)}) copy-start(bf16[1024,128]{0,1:T(8,128)(2,1)} %copy.12) | copy-start | bytes 786436
  62.6 12.8 %copy-start.6 = (f32[64,1024]{1,0:T(8,128)S(1)}, f32[64,1024]{1,0:T(8,128)}, u32[]{:S(2)}) copy-start(f32[64,1024]{1,0:T(8,128)} %get-tuple-element.25.s_ref) | copy-start | bytes 786436
  62.6 12.8 %copy-start.11 = (f32[64]{0:T(128)S(1)}, f32[64]{0:T(128)}, u32[]{:S(2)}) copy-start(f32[64]{0:T(128)} %param.13) | copy-start | bytes 772
  71.2 18.4 %all-to-all-start.1 = ((f32[8,64,512]{2,1,0:T(8,128)}), f32[8,64,512]{2,1,0:T(8,128)S(1)}, u32[]{:S(2)}, u32[]{:S(2)}) async-start(f32[8,64,512]{2,1,0:T(8,128)} %shard_map.103), calls=%async_computation.1 | async-start | bytes 2097152 | tf_op jit(solution)/shard_map/all_to_all | solution.py:498
  83.0 1.4 %copy-start = (f32[16,72,512]{2,1,0:T(8,128)}, f32[16,72,512]{2,1,0:T(8,128)S(1)}, u32[]{:S(2)}) copy-start(f32[16,72,512]{2,1,0:T(8,128)S(1)} %get-tuple-element.27.refs_0_) | copy-start | bytes 7077892
  84.4 0.7 copy-start.7
  89.6 1.0 copy-start.8
  99.9 5.9 %copy-start.9 = (f32[2,128,128]{2,1,0:T(8,128)}, f32[2,128,128]{2,1,0:T(8,128)S(1)}, u32[]{:S(2)}) copy-start(f32[2,128,128]{2,1,0:T(8,128)S(1)} %get-tuple-element.34) | copy-start | bytes 393220
  99.9 5.9 %copy-start.12 = (f32[2,128,128]{2,1,0:T(8,128)}, f32[2,128,128]{2,1,0:T(8,128)S(1)}, u32[]{:S(2)}) copy-start(f32[2,128,128]{2,1,0:T(8,128)S(1)} %get-tuple-element.37) | copy-start | bytes 393220
  99.9 5.9 %copy-start.14 = (f32[2,128,128]{2,1,0:T(8,128)}, f32[2,128,128]{2,1,0:T(8,128)S(1)}, u32[]{:S(2)}) copy-start(f32[2,128,128]{2,1,0:T(8,128)S(1)} %get-tuple-element.36) | copy-start | bytes 393220
  99.9 5.9 %copy-start.16 = (f32[2,128,128]{2,1,0:T(8,128)}, f32[2,128,128]{2,1,0:T(8,128)S(1)}, u32[]{:S(2)}) copy-start(f32[2,128,128]{2,1,0:T(8,128)S(1)} %get-tuple-element.35) | copy-start | bytes 393220
  99.9 3.3 %collective-permute-start = (f32[8,72,512]{2,1,0:T(8,128)S(1)}, f32[8,72,512]{2,1,0:T(8,128)S(1)}, u32[]{:S(2)}, u32[]{:S(2)}) collective-permute-start(f32[8,72,512]{2,1,0:T(8,128)S(1)} %get-tuple-element.30), channel_id=1, source_target_pairs={{0,1},{1,0},{2,3},{3,2},{4,5},{5,4},{6,7},{7,6},{8,9},{9,8},{10,11... | collective-permute-start | bytes 3538952 | tf_op jit(solution)/shard_map/ppermute | solution.py:502
  105.8 4.2 %copy-start.17 = (f32[2,128,128]{2,1,0:T(8,128)S(1)}, f32[2,128,128]{2,1,0:T(8,128)}, u32[]{:S(2)}) copy-start(f32[2,128,128]{2,1,0:T(8,128)} %copy-done.16) | copy-start | bytes 393220
  105.8 4.8 %copy-start.15 = (f32[2,128,128]{2,1,0:T(8,128)S(1)}, f32[2,128,128]{2,1,0:T(8,128)}, u32[]{:S(2)}) copy-start(f32[2,128,128]{2,1,0:T(8,128)} %copy-done.14) | copy-start | bytes 393220
  105.8 6.6 %copy-start.13 = (f32[2,128,128]{2,1,0:T(8,128)S(1)}, f32[2,128,128]{2,1,0:T(8,128)}, u32[]{:S(2)}) copy-start(f32[2,128,128]{2,1,0:T(8,128)} %copy-done.12) | copy-start | bytes 393220
  105.8 12.9 %copy-start.10 = (f32[2,128,128]{2,1,0:T(8,128)S(1)}, f32[2,128,128]{2,1,0:T(8,128)}, u32[]{:S(2)}) copy-start(f32[2,128,128]{2,1,0:T(8,128)} %copy-done.9) | copy-start | bytes 393220
  105.8 20.1 %all-to-all-start.4 = ((f32[4,2,72,512]{3,2,1,0:T(8,128)}), f32[4,2,72,512]{3,2,1,0:T(8,128)S(1)}, u32[]{:S(2)}, u32[]{:S(2)}) async-start(f32[4,2,72,512]{3,2,1,0:T(8,128)} %bitcast.16), calls=%async_computation.4 | async-start | bytes 2359296 | tf_op jit(solution)/shard_map/all_to_all | solution.py:498
  110.0 5.8 %collective-permute-start.2 = (f32[2,128,128]{2,1,0:T(8,128)S(1)}, f32[2,128,128]{2,1,0:T(8,128)S(1)}, u32[]{:S(2)}, u32[]{:S(2)}) collective-permute-start(f32[2,128,128]{2,1,0:T(8,128)S(1)} %copy-done.17), channel_id=1, source_target_pairs={{0,16},{16,32},{32,48},{48,0},{64,80},{80,96},{96,112},{112,64},{1... | collective-permute-start | bytes 393224 | tf_op jit(solution)/shard_map/ppermute | solution.py:507
  110.6 7.6 %collective-permute-start.3 = (f32[2,128,128]{2,1,0:T(8,128)S(1)}, f32[2,128,128]{2,1,0:T(8,128)S(1)}, u32[]{:S(2)}, u32[]{:S(2)}) collective-permute-start(f32[2,128,128]{2,1,0:T(8,128)S(1)} %copy-done.15), channel_id=1, source_target_pairs={{0,32},{16,48},{32,0},{48,16},{64,96},{80,112},{96,64},{112,80},{1... | collective-permute-start | bytes 393224 | tf_op jit(solution)/shard_map/ppermute | solution.py:507
  112.4 6.3 %collective-permute-start.4 = (f32[2,128,128]{2,1,0:T(8,128)S(1)}, f32[2,128,128]{2,1,0:T(8,128)S(1)}, u32[]{:S(2)}, u32[]{:S(2)}) collective-permute-start(f32[2,128,128]{2,1,0:T(8,128)S(1)} %copy-done.13), channel_id=1, source_target_pairs={{0,48},{16,0},{32,16},{48,32},{64,112},{80,64},{96,80},{112,96},{1... | collective-permute-start | bytes 393224 | tf_op jit(solution)/shard_map/ppermute | solution.py:507
  118.7 11.1 %collective-permute-start.5 = (f32[2,128,128]{2,1,0:T(8,128)S(1)}, f32[2,128,128]{2,1,0:T(8,128)S(1)}, u32[]{:S(2)}, u32[]{:S(2)}) collective-permute-start(f32[2,128,128]{2,1,0:T(8,128)S(1)} %add_add_fusion), channel_id=1, source_target_pairs={{0,64},{16,80},{32,96},{48,112},{64,0},{80,16},{96,32},{112,48},{1... | collective-permute-start | bytes 393224 | tf_op jit(solution)/shard_map/ppermute | solution.py:502
  126.5 13.4 %collective-permute-start.1 = (f32[72,512]{1,0:T(8,128)S(1)}, f32[72,512]{1,0:T(8,128)S(1)}, u32[]{:S(2)}, u32[]{:S(2)}) collective-permute-start(f32[72,512]{1,0:T(8,128)S(1)} %get-tuple-element.32), channel_id=1, source_target_pairs={{0,2},{1,3},{2,0},{3,1},{4,6},{5,7},{6,4},{7,5},{8,10},{9,11},{10,... | collective-permute-start | bytes 442376 | tf_op jit(solution)/shard_map/ppermute | solution.py:502
  129.9 4.2 %collective-permute-start.8 = (f32[2,128,128]{2,1,0:T(8,128)S(1)}, f32[2,128,128]{2,1,0:T(8,128)S(1)}, u32[]{:S(2)}, u32[]{:S(2)}) collective-permute-start(f32[2,128,128]{2,1,0:T(8,128)S(1)} %add.38.refs_0_), channel_id=1, source_target_pairs={{0,48},{16,0},{32,16},{48,32},{64,112},{80,64},{96,80},{112,96},{1... | collective-permute-start | bytes 393224 | tf_op jit(solution)/shard_map/ppermute | solution.py:507
  131.2 5.4 %collective-permute-start.7 = (f32[2,128,128]{2,1,0:T(8,128)S(1)}, f32[2,128,128]{2,1,0:T(8,128)S(1)}, u32[]{:S(2)}, u32[]{:S(2)}) collective-permute-start(f32[2,128,128]{2,1,0:T(8,128)S(1)} %add.38.refs_0_), channel_id=1, source_target_pairs={{0,32},{16,48},{32,0},{48,16},{64,96},{80,112},{96,64},{112,80},{1... | collective-permute-start | bytes 393224 | tf_op jit(solution)/shard_map/ppermute | solution.py:507
  132.4 6.2 %collective-permute-start.6 = (f32[2,128,128]{2,1,0:T(8,128)S(1)}, f32[2,128,128]{2,1,0:T(8,128)S(1)}, u32[]{:S(2)}, u32[]{:S(2)}) collective-permute-start(f32[2,128,128]{2,1,0:T(8,128)S(1)} %add.38.refs_0_), channel_id=1, source_target_pairs={{0,16},{16,32},{32,48},{48,0},{64,80},{80,96},{96,112},{112,64},{1... | collective-permute-start | bytes 393224 | tf_op jit(solution)/shard_map/ppermute | solution.py:507

commit v8 on v7

--- a/solution.py
+++ b/solution.py
@@ -198,11 +198,10 @@
         high = jnp.maximum(jnp.max(scores, axis=1, keepdims=True), FLOOR)
         total = jnp.sum(jnp.exp2(scores - high), axis=1, keepdims=True)
         row = as_row(jnp.where(total > 0.0, high + jnp.log2(total), FLOOR))
-        row = jnp.concatenate([row, jnp.zeros_like(row)], axis=1)
-        lse_ref[...] = jnp.broadcast_to(row[None], lse_ref.shape)
-
-
-def index_forward(base, q, kt, w, start, pos, peers):
+        lse_ref[...] = row
+
+
+def index_forward(base, q, kt, w, start, pos):
     rows, width = q.shape
     dim, keys = kt.shape
     heads = w.shape[1]
@@ -218,10 +217,10 @@
             whole(1, rows),
             whole(1, rows),
         ],
-        out_specs=[whole(rows, keys), whole(peers, 8, 2 * rows)],
+        out_specs=[whole(rows, keys), whole(1, rows)],
         out_shape=[
             jax.ShapeDtypeStruct((rows, keys), jnp.float32),
-            jax.ShapeDtypeStruct((peers, 8, 2 * rows), jnp.float32),
+            jax.ShapeDtypeStruct((1, rows), jnp.float32),
         ],
         cost_estimate=pl.CostEstimate(flops=2 * rows * width * keys, bytes_accessed=2 << 20, transcendentals=rows * keys),
         name="index_forward",
@@ -311,10 +310,7 @@
     def _():
         target = jnp.sum(t_ref[...], axis=0) * (1.0 / H)
         scores = s_ref[...]
-        stats = [stats_ref[n, 0:1, :rows] for n in range(stats_ref.shape[0])]
-        high = functools.reduce(jnp.maximum, stats)
-        lse = high + jnp.log2(sum(jnp.exp2(x - high) for x in stats))
-        probs = jnp.exp2(scores - as_column(lse))
+        probs = jnp.exp2(scores - as_column(stats_ref[...]))
         g_ref[...] = jnp.where(scores > FLOOR, as_column(c_ref[...]) * (probs - target), 0.0)
         gkt_ref[...] = jnp.zeros_like(gkt_ref)
 
@@ -502,6 +498,11 @@
     return lax.ppermute(x, axis, [(i, i ^ mask) for i in range(lax.axis_size(axis))])
 
 
+def joined_lse(a, b):
+    high = jnp.maximum(a, b)
+    return high + jnp.log2(jnp.exp2(a - high) + jnp.exp2(b - high))
+
+
 def turned(x, k):
     n = lax.axis_size("head")
     return lax.ppermute(x, "head", [(i, i // ROUNDS * ROUNDS + (i + k) % ROUNDS) for i in range(n)])
@@ -522,8 +523,13 @@
     info = count.reshape(1)
     e, sel, high, lse = main_forward(base, k_latent.T, jnp.swapaxes(q_latent, 1, 2), start, pos, peers)
     stats = exchanged(lse, "key")
-    scores, index_lse = index_forward(base, q_index, kt_index, head_weight, own_start, own_pos, peers)
-    index_stats = exchanged(index_lse, "key")
+    scores, index_lse = index_forward(base, q_index, kt_index, head_weight, own_start, own_pos)
+    index_lse = joined_lse(index_lse, flipped(index_lse, "key", 1))
+    moved = flipped(index_lse, "key", 2)
+    index_lse = joined_lse(index_lse, moved)
+    others = [lax.ppermute(index_lse, "key", [(i, (i + 4 * k) % peers) for i in range(peers)]) for k in (1, 2, 3)]
+    top = functools.reduce(jnp.maximum, others, index_lse)
+    index_stats = top + jnp.log2(sum(jnp.exp2(y - top) for y in [index_lse, *others]))
     targets = []
     for part in range(PARTS):
         partial = weighted_sum(info, e, sel, high, stats, owners, part)
@@ -539,7 +545,8 @@
     groups = [list(range(c, peers, 4)) for c in range(4)]
     gq = near + moved
     gq = exchanged(gq.reshape(peers // 4, 2, *gq.shape[1:]), "key", groups)
-    pieces = [turned(x, k) if k else x for k, x in enumerate(pieces)]
+    pieces[1:3] = [turned(pieces[k], k) for k in (1, 2)]
+    pieces[3] = turned(pieces[3], 3)
     gk = sum(pieces[1:], pieces[0])
     gk = gk + flipped(gk, "head", ROUNDS)
     gk = joined(place, [gk] + [turned(gk, k) for k in range(1, ROUNDS)]).reshape(keys, -1)

time: 143 us -> 157 us (1.098)
  waiting for transfers between devices: 36.7 us -> 46.2 us
  starting transfers between devices: 37.9 us -> 41.6 us
  local copies, waits for them, and re-layouts: 5 us -> 8.29 us
    ppermute x3 -> x5, waiting for transfers between devices: 2.48 us -> 14.6 us  [flipped(): lax.ppermute(x, axis, [(i, i ^ mask) for i in range(lax.axis_size(axis))])]
    all_to_all x5 -> x4, waiting for transfers between devices: 23 us -> 15.8 us  [exchanged(): return lax.all_to_all(x, axis, 0, 0, axis_index_groups=groups, tiled=True)]
    unnamed x44 -> x34, local copies, waits for them, and re-layouts: 4.1 us -> 7.38 us
    all_to_all x5 -> x4, starting transfers between devices: 26.1 us -> 22.9 us  [exchanged(): return lax.all_to_all(x, axis, 0, 0, axis_index_groups=groups, tiled=True)]
    ppermute x6, starting transfers between devices: 6.17 us -> 9 us  [turned(): lax.ppermute(x, 'head', [(i, i // ROUNDS * ROUNDS + (i + k) % ROUNDS) for...]
    ppermute x0 -> x3, waiting for transfers between devices: none -> 2.71 us  [shards(): lax.ppermute(index_lse, 'key', [(i, (i + 4 * k) % peers) for i in range(p...]
    ppermute x0 -> x3, starting transfers between devices: none -> 2.08 us  [shards(): lax.ppermute(index_lse, 'key', [(i, (i + 4 * k) % peers) for i in range(p...]
    ppermute x3 -> x5, starting transfers between devices: 5.64 us -> 7.57 us  [flipped(): lax.ppermute(x, axis, [(i, i ^ mask) for i in range(lax.axis_size(axis))])]
  transfers between devices with their start and end apart: 14 -> 18, of which waited for: 12 -> 12; matrix products, arithmetic and copies ran while one was open for 2% -> 2% of each run, Pallas kernels for 20% -> 13%
where the time goes in v8:
time: 157 us; the launch traced here: 156 us
  Pallas kernels  55.8 us (36%)
  waiting for transfers between devices  46.2 us (29%)
  starting transfers between devices  41.6 us (26%)
  local copies, waits for them, and re-layouts  8.29 us (5%)
  other arithmetic  3.35 us (2%)
    all_to_all x4, starting transfers between devices, exchanged(): return lax.all_to_all(x, axis, 0, 0, axis_index_groups=groups, tiled=True)  22.9 us
    pallas_call x1, Pallas kernels, main_forward(): pl.pallas_call(main_kernel, grid_spec=pltpu.PrefetchScalarGridSpec(num_sc...  18.6 us
    all_to_all x4, waiting for transfers between devices, exchanged(): return lax.all_to_all(x, axis, 0, 0, axis_index_groups=groups, tiled=True)  15.8 us
    pallas_call x2, Pallas kernels, backward(): pl.pallas_call(functools.partial(back_kernel, last), grid_spec=pltpu.Pref...  15.6 us
    ppermute x5, waiting for transfers between devices, flipped(): lax.ppermute(x, axis, [(i, i ^ mask) for i in range(lax.axis_size(axis))])  14.6 us
    pallas_call x2, Pallas kernels, weighted_sum(): pl.pallas_call(functools.partial(sum_kernel, first), grid_spec=pltpu.Pref...  13.4 us
    ppermute x6, waiting for transfers between devices, turned(): lax.ppermute(x, 'head', [(i, i // ROUNDS * ROUNDS + (i + k) % ROUNDS) for...  13 us
    ppermute x6, starting transfers between devices, turned(): lax.ppermute(x, 'head', [(i, i // ROUNDS * ROUNDS + (i + k) % ROUNDS) for...  9 us
  transfers between devices with their start and end apart: 18, of which 12 were waited for; matrix products, arithmetic and copies ran while one was open for 2% of the time, Pallas kernels for 13%

profile of v8, /device:TPU:1, one launch (start us, length us, event | category | flops | bytes accessed | tf_op | source)
XLA Modules:
  0.0 156.1 jit_solution(9012386569185387412)
XLA Ops:
  0.7 18.6 %main_forward.1 = (bf16[2,16,1024,256]{3,2,1,0:T(8,128)(2,1)}, bf16[2,512,256]{2,1,0:T(8,128)(2,1)}, f32[128,256]{1,0:T(8,128)}, f32[16,16,512]{2,1,0:T(8,128)}) custom-call(s32[1]{0:T(128)} %bitcast.3.base_ref, bf16[576,1024]{1,0:T(8,128)(2,1)} %bitcast.33, bf16[16,576,512]{2,1,0:T(8,128)(2,1)} %bitcast.28, bf16[16,576,512]{2,1,0:T(8,128)(2,1)} %bitcast.29, ...), custom_call_target="tpu_custom_call" | custom-call | flops 9663676416 | bytes 27262976 | tf_op jit(solution)/shard_map/main_forward/pallas_call | solution.py:141
  19.3 8.6 %all-to-all-start = ((f32[16,16,512]{2,1,0:T(8,128)}), f32[16,16,512]{2,1,0:T(8,128)S(1)}, u32[]{:S(2)}, u32[]{:S(2)}) async-start(f32[16,16,512]{2,1,0:T(8,128)} %get-tuple-element.24), calls=%async_computation | async-start | bytes 1048576 | tf_op jit(solution)/shard_map/all_to_all | solution.py:494
  27.9 0.6 convert_reduce_fusion
  28.5 10.6 %all-to-all-done.stats_ref = f32[16,16,512]{2,1,0:T(8,128)S(1)} async-done(((f32[16,16,512]{2,1,0:T(8,128)}), f32[16,16,512]{2,1,0:T(8,128)S(1)}, u32[]{:S(2)}, u32[]{:S(2)}) %all-to-all-start) | async-done | bytes 524320 | tf_op jit(solution)/shard_map/all_to_all | solution.py:494
  39.1 0.9 copy-done.6
  40.0 6.7 %shard_map.104 = f32[8,64,512]{2,1,0:T(8,128)} custom-call(s32[1]{0:T(128)} %bitcast.5.info_ref, bf16[2,16,1024,256]{3,2,1,0:T(8,128)(2,1)} %get-tuple-element.21.e_ref, bf16[2,512,256]{2,1,0:T(8,128)(2,1)S(1)} %copy-done.1, f32[128,256]{1,0:T(8,128)S(1)} %copy-done.6, f32[16,16,512]{2,1,0:T(8,128)S(1)} %all-to-all-done.stats_ref), custom_call_target="tpu_custom_call" | custom-call | flops 8388608 | bytes 9437184 | tf_op jit(solution)/shard_map/pallas_call | solution.py:276
  46.7 5.3 %all-to-all-start.2 = ((f32[8,64,512]{2,1,0:T(8,128)}), f32[8,64,512]{2,1,0:T(8,128)S(1)}, u32[]{:S(2)}, u32[]{:S(2)}) async-start(f32[8,64,512]{2,1,0:T(8,128)} %shard_map.104), calls=%async_computation.2 | async-start | bytes 2097152 | tf_op jit(solution)/shard_map/all_to_all | solution.py:494
  52.0 0.8 copy.12
  52.8 0.7 dynamic-slice_bitcast_fusion
  53.5 5.6 %index_forward.1 = (f32[64,1024]{1,0:T(8,128)}, f32[1,64]{1,0:T(1,128)}) custom-call(s32[1]{0:T(128)} %bitcast.3.base_ref, bf16[64,8192]{1,0:T(8,128)(2,1)} %q_ref.5, bf16[128,1024]{1,0:T(8,128)(2,1)} %bitcast.23, f32[64,64]{1,0:T(8,128)} %w_ref.1, s32[1,64]{1,0:T(1,128)} %get-tuple-element.40.start_ref, s32[1,64]{1,0:T(1,128)} %get-tuple-element.39.pos_ref), custom_call_target="tpu_custom_call" | custom-call | flops 1073741824 | bytes 2097152 | tf_op jit(solution)/shard_map/index_forward/pallas_call | solution.py:209
  59.1 1.5 collective-permute-start
  60.6 6.7 %shard_map.103 = f32[8,64,512]{2,1,0:T(8,128)} custom-call(s32[1]{0:T(128)} %bitcast.5.info_ref, bf16[2,16,1024,256]{3,2,1,0:T(8,128)(2,1)} %get-tuple-element.21.e_ref, bf16[2,512,256]{2,1,0:T(8,128)(2,1)S(1)} %copy-done.1, f32[128,256]{1,0:T(8,128)S(1)} %copy-done.7, f32[16,16,512]{2,1,0:T(8,128)S(1)} %all-to-all-done.stats_ref), custom_call_target="tpu_custom_call" | custom-call | flops 8388608 | bytes 9437184 | tf_op jit(solution)/shard_map/pallas_call | solution.py:276
  67.3 5.6 %all-to-all-start.1 = ((f32[8,64,512]{2,1,0:T(8,128)}), f32[8,64,512]{2,1,0:T(8,128)S(1)}, u32[]{:S(2)}, u32[]{:S(2)}) async-start(f32[8,64,512]{2,1,0:T(8,128)} %shard_map.103), calls=%async_computation.1 | async-start | bytes 2097152 | tf_op jit(solution)/shard_map/all_to_all | solution.py:494
  72.9 0.7 collective-permute-start.1
  73.7 12.1 %collective-permute-done.1 = f32[1,64]{1,0:T(1,128)S(1)} collective-permute-done((f32[1,64]{1,0:T(1,128)S(1)}, f32[1,64]{1,0:T(1,128)S(1)}, u32[]{:S(2)}, u32[]{:S(2)}) %collective-permute-start.1) | collective-permute-done | bytes 288 | tf_op jit(solution)/shard_map/ppermute | solution.py:498
  85.8 0.6 collective-permute-start.4
  86.4 0.9 collective-permute-start.3
  87.3 0.6 collective-permute-start.2
  88.3 2.0 %collective-permute-done.3 = f32[1,64]{1,0:T(1,128)S(1)} collective-permute-done((f32[1,64]{1,0:T(1,128)S(1)}, f32[1,64]{1,0:T(1,128)S(1)}, u32[]{:S(2)}, u32[]{:S(2)}) %collective-permute-start.3) | collective-permute-done | bytes 288 | tf_op jit(solution)/shard_map/ppermute | solution.py:530
  90.3 0.6 collective-permute-done.2
  91.0 1.2 copy-done.2
  92.2 6.3 %shard_map.105 = (f32[16,72,512]{2,1,0:T(8,128)S(1)}, f32[8,64,128]{2,1,0:T(8,128)S(1)}) custom-call(s32[3]{0:T(128)S(1)} %pad_add_fusion.place_ref, f32[8,64,512]{2,1,0:T(8,128)S(1)} %all-to-all-done.2.t_ref, f32[64,1024]{1,0:T(8,128)S(1)} %copy-done.8, f32[1,64]{1,0:T(1,128)S(1)} %multiply_add_fusion.stats_ref, f32[1,64]{1,0:T(1,128)S(1)} %bitcast.26, ...), custom_call_target="tpu_custom_call" | custom-call | flops 1610612736 | bytes 4194304 | tf_op jit(solution)/shard_map/pallas_call | solution.py:416
  98.5 1.4 copy-done
  99.9 0.7 copy-done.9
  100.6 1.2 copy-done.3
  101.9 0.9 copy-done.10
  102.8 9.3 %shard_map.106 = (f32[8,72,512]{2,1,0:T(8,128)S(1)}, f32[8,72,512]{2,1,0:T(8,128)}, f32[2,128,128]{2,1,0:T(8,128)S(1)}, f32[2,128,128]{2,1,0:T(8,128)S(1)}, f32[...) custom-call(s32[3]{0:T(128)S(1)} %pad_add_fusion.place_ref, f32[8,64,512]{2,1,0:T(8,128)S(1)} %all-to-all-done.1.t_ref, ...), custom_call_target="tpu_custom_call" | custom-call | flops 1610612736 | bytes 4194304 | tf_op jit(solution)/shard_map/pallas_call | solution.py:416
  112.1 2.3 %collective-permute-start.5 = (f32[8,72,512]{2,1,0:T(8,128)S(1)}, f32[8,72,512]{2,1,0:T(8,128)S(1)}, u32[]{:S(2)}, u32[]{:S(2)}) collective-permute-start(f32[8,72,512]{2,1,0:T(8,128)S(1)} %get-tuple-element.30), channel_id=1, source_target_pairs={{0,1},{1,0},{2,3},{3,2},{4,5},{5,4},{6,7},{7,6},{8,9},{9,8},{10,11... | collective-permute-start | bytes 3538952 | tf_op jit(solution)/shard_map/ppermute | solution.py:498
  114.4 2.5 %collective-permute-done.5 = f32[8,72,512]{2,1,0:T(8,128)S(1)} collective-permute-done((f32[8,72,512]{2,1,0:T(8,128)S(1)}, f32[8,72,512]{2,1,0:T(8,128)S(1)}, u32[]{:S(2)}, u32[]{:S(2)}) %collective-permute-start.5) | collective-permute-done | bytes 1179680 | tf_op jit(solution)/shard_map/ppermute | solution.py:498
  116.9 2.6 %add.66 = f32[8,72,512]{2,1,0:T(8,128)} add(f32[8,72,512]{2,1,0:T(8,128)} %get-tuple-element.29, f32[8,72,512]{2,1,0:T(8,128)S(1)} %collective-permute-done.5) | non-fusion elementwise | flops 294912 | bytes 3538944 | tf_op jit(solution)/shard_map/add | solution.py:546
  119.4 3.5 %all-to-all-start.3 = ((f32[4,2,72,512]{3,2,1,0:T(8,128)}), f32[4,2,72,512]{3,2,1,0:T(8,128)S(1)}, u32[]{:S(2)}, u32[]{:S(2)}) async-start(f32[4,2,72,512]{3,2,1,0:T(8,128)} %bitcast.16), calls=%async_computation.3 | async-start | bytes 2359296 | tf_op jit(solution)/shard_map/all_to_all | solution.py:494
  123.0 1.5 collective-permute-start.7
  124.4 2.7 %collective-permute-start.8 = (f32[2,128,128]{2,1,0:T(8,128)S(1)}, f32[2,128,128]{2,1,0:T(8,128)S(1)}, u32[]{:S(2)}, u32[]{:S(2)}) collective-permute-start(f32[2,128,128]{2,1,0:T(8,128)S(1)} %get-tuple-element.36), channel_id=1, source_target_pairs={{0,32},{16,48},{32,0},{48,16},{64,96},{80,112},{96,64},{112,80},{1... | collective-permute-start | bytes 393224 | tf_op jit(solution)/shard_map/ppermute | solution.py:508
  127.2 0.9 collective-permute-start.9
  128.1 1.4 collective-permute-done.7
  129.5 3.7 %collective-permute-done.8 = f32[2,128,128]{2,1,0:T(8,128)S(1)} collective-permute-done((f32[2,128,128]{2,1,0:T(8,128)S(1)}, f32[2,128,128]{2,1,0:T(8,128)S(1)}, u32[]{:S(2)}, u32[]{:S(2)}) %collective-permute-start.8) | collective-permute-done | bytes 131104 | tf_op jit(solution)/shard_map/ppermute | solution.py:508
  133.2 0.7 collective-permute-start.10
  133.9 5.2 %all-to-all-done.3.x_ref = f32[4,2,72,512]{3,2,1,0:T(8,128)S(1)} async-done(((f32[4,2,72,512]{3,2,1,0:T(8,128)}), f32[4,2,72,512]{3,2,1,0:T(8,128)S(1)}, u32[]{:S(2)}, u32[]{:S(2)}) %all-to-all-start.3) | async-done | bytes 1179680 | tf_op jit(solution)/shard_map/all_to_all | solution.py:494
  139.2 0.6 halves.1
  139.8 2.4 %collective-permute-start.6 = (f32[72,512]{1,0:T(8,128)S(1)}, f32[72,512]{1,0:T(8,128)S(1)}, u32[]{:S(2)}, u32[]{:S(2)}) collective-permute-start(f32[72,512]{1,0:T(8,128)S(1)} %get-tuple-element.32), channel_id=1, source_target_pairs={{0,2},{1,3},{2,0},{3,1},{4,6},{5,7},{6,4},{7,5},{8,10},{9,11},{10,... | collective-permute-start | bytes 442376 | tf_op jit(solution)/shard_map/ppermute | solution.py:498
  142.2 3.0 %collective-permute-start.13 = (f32[2,128,128]{2,1,0:T(8,128)S(1)}, f32[2,128,128]{2,1,0:T(8,128)S(1)}, u32[]{:S(2)}, u32[]{:S(2)}) collective-permute-start(f32[2,128,128]{2,1,0:T(8,128)S(1)} %add.70.refs_0_), channel_id=1, source_target_pairs={{0,48},{16,0},{32,16},{48,32},{64,112},{80,64},{96,80},{112,96},{1... | collective-permute-start | bytes 393224 | tf_op jit(solution)/shard_map/ppermute | solution.py:508
  145.2 0.2 collective-permute-start.12
  145.5 0.6 collective-permute-start.11
  146.1 1.7 %collective-permute-done.13.refs_3_ = f32[2,128,128]{2,1,0:T(8,128)S(1)} collective-permute-done((f32[2,128,128]{2,1,0:T(8,128)S(1)}, f32[2,128,128]{2,1,0:T(8,128)S(1)}, u32[]{:S(2)}, u32[]{:S(2)}) %collective-permute-start.13) | collective-permute-done | bytes 131104 | tf_op jit(solution)/shard_map/ppermute | solution.py:508
  147.8 2.8 %collective-permute-done.12.refs_2_ = f32[2,128,128]{2,1,0:T(8,128)S(1)} collective-permute-done((f32[2,128,128]{2,1,0:T(8,128)S(1)}, f32[2,128,128]{2,1,0:T(8,128)S(1)}, u32[]{:S(2)}, u32[]{:S(2)}) %collective-permute-start.12) | collective-permute-done | bytes 131104 | tf_op jit(solution)/shard_map/ppermute | solution.py:508
  150.7 3.4 %collective-permute-done.11.refs_1_ = f32[2,128,128]{2,1,0:T(8,128)S(1)} collective-permute-done((f32[2,128,128]{2,1,0:T(8,128)S(1)}, f32[2,128,128]{2,1,0:T(8,128)S(1)}, u32[]{:S(2)}, u32[]{:S(2)}) %collective-permute-start.11) | collective-permute-done | bytes 131104 | tf_op jit(solution)/shard_map/ppermute | solution.py:508
  154.0 1.4 join.1
  155.4 0.7 end.1
  (41 shorter events, 0.6 us)
Async XLA Ops:
  0.6 27.2 %copy-start.13 = (s32[512]{0:T(512)S(1)}, s32[512]{0:T(512)}, u32[]{:S(2)}) copy-start(s32[512]{0:T(512)} %param.14) | copy-start | bytes 6148
  0.6 27.2 %copy-start.14 = (s32[512]{0:T(512)S(1)}, s32[512]{0:T(512)}, u32[]{:S(2)}) copy-start(s32[512]{0:T(512)} %param.15) | copy-start | bytes 6148
  19.3 19.8 %copy-start.1 = (bf16[2,512,256]{2,1,0:T(8,128)(2,1)S(1)}, bf16[2,512,256]{2,1,0:T(8,128)(2,1)}, u32[]{:S(2)}) copy-start(bf16[2,512,256]{2,1,0:T(8,128)(2,1)} %get-tuple-element.22.sel_ref) | copy-start | bytes 1572868
  19.3 19.8 %all-to-all-start = ((f32[16,16,512]{2,1,0:T(8,128)}), f32[16,16,512]{2,1,0:T(8,128)S(1)}, u32[]{:S(2)}, u32[]{:S(2)}) async-start(f32[16,16,512]{2,1,0:T(8,128)} %get-tuple-element.24), calls=%async_computation | async-start | bytes 1048576 | tf_op jit(solution)/shard_map/all_to_all | solution.py:494
  39.1 0.9 copy-start.6
  46.7 5.3 %copy-start.4 = (bf16[1024,128]{1,0:T(8,128)(2,1)S(1)}, bf16[1024,128]{1,0:T(8,128)(2,1)}, u32[]{:S(2)}) copy-start(bf16[1024,128]{1,0:T(8,128)(2,1)} %k_ref.3) | copy-start | bytes 786436
  46.7 20.6 %all-to-all-start.2 = ((f32[8,64,512]{2,1,0:T(8,128)}), f32[8,64,512]{2,1,0:T(8,128)S(1)}, u32[]{:S(2)}, u32[]{:S(2)}) async-start(f32[8,64,512]{2,1,0:T(8,128)} %shard_map.104), calls=%async_computation.2 | async-start | bytes 2097152 | tf_op jit(solution)/shard_map/all_to_all | solution.py:494
  53.5 7.1 %copy-start.7 = (f32[128,256]{1,0:T(8,128)S(1)}, f32[128,256]{1,0:T(8,128)}, u32[]{:S(2)}) copy-start(f32[128,256]{1,0:T(8,128)} %get-tuple-element.23.m_ref) | copy-start | bytes 393220
  59.1 13.8 %collective-permute-start = (f32[1,64]{1,0:T(1,128)}, f32[1,64]{1,0:T(1,128)S(1)}, u32[]{:S(2)}, u32[]{:S(2)}) collective-permute-start(f32[1,64]{1,0:T(1,128)} %get-tuple-element.26), channel_id=1, source_target_pairs={{0,1},{1,0},{2,3},{3,2},{4,5},{5,4},{6,7},{7,6},{8,9},{9,8},{10,11... | collective-permute-start | bytes 776 | tf_op jit(solution)/shard_map/ppermute | solution.py:498
  67.3 5.6 %copy-start.15 = (f32[1,64]{1,0:T(1,128)S(1)}, f32[1,64]{1,0:T(1,128)}, u32[]{:S(2)}) copy-start(f32[1,64]{1,0:T(1,128)} %get-tuple-element.26) | copy-start | bytes 772
  67.3 20.6 %copy-start.12 = (f32[64,64]{1,0:T(8,128)S(1)}, f32[64,64]{1,0:T(8,128)}, u32[]{:S(2)}) copy-start(f32[64,64]{1,0:T(8,128)} %w_ref.1) | copy-start | bytes 49156
  67.3 23.7 %copy-start.5 = (bf16[1024,128]{0,1:T(8,128)(2,1)S(1)}, bf16[1024,128]{0,1:T(8,128)(2,1)}, u32[]{:S(2)}) copy-start(bf16[1024,128]{0,1:T(8,128)(2,1)} %copy.12) | copy-start | bytes 786436
  67.3 23.7 %copy-start.8 = (f32[64,1024]{1,0:T(8,128)S(1)}, f32[64,1024]{1,0:T(8,128)}, u32[]{:S(2)}) copy-start(f32[64,1024]{1,0:T(8,128)} %get-tuple-element.25.s_ref) | copy-start | bytes 786436
  67.3 23.7 %copy-start.11 = (f32[64]{0:T(128)S(1)}, f32[64]{0:T(128)}, u32[]{:S(2)}) copy-start(f32[64]{0:T(128)} %param.13) | copy-start | bytes 772
  67.3 33.3 %all-to-all-start.1 = ((f32[8,64,512]{2,1,0:T(8,128)}), f32[8,64,512]{2,1,0:T(8,128)S(1)}, u32[]{:S(2)}, u32[]{:S(2)}) async-start(f32[8,64,512]{2,1,0:T(8,128)} %shard_map.103), calls=%async_computation.1 | async-start | bytes 2097152 | tf_op jit(solution)/shard_map/all_to_all | solution.py:494
  72.9 12.9 %collective-permute-start.1 = (f32[1,64]{1,0:T(1,128)S(1)}, f32[1,64]{1,0:T(1,128)S(1)}, u32[]{:S(2)}, u32[]{:S(2)}) collective-permute-start(f32[1,64]{1,0:T(1,128)S(1)} %multiply_add_fusion.2), channel_id=1, source_target_pairs={{0,2},{1,3},{2,0},{3,1},{4,6},{5,7},{6,4},{7,5},{8,10},{9,11},{10,... | collective-permute-start | bytes 776 | tf_op jit(solution)/shard_map/ppermute | solution.py:498
  85.8 2.5 %collective-permute-start.4 = (f32[1,64]{1,0:T(1,128)S(1)}, f32[1,64]{1,0:T(1,128)S(1)}, u32[]{:S(2)}, u32[]{:S(2)}) collective-permute-start(f32[1,64]{1,0:T(1,128)S(1)} %multiply_add_fusion.1), channel_id=1, source_target_pairs={{0,12},{1,13},{2,14},{3,15},{4,0},{5,1},{6,2},{7,3},{8,4},{9,5},{1... | collective-permute-start | bytes 776 | tf_op jit(solution)/shard_map/ppermute | solution.py:530
  86.4 3.9 %collective-permute-start.3 = (f32[1,64]{1,0:T(1,128)S(1)}, f32[1,64]{1,0:T(1,128)S(1)}, u32[]{:S(2)}, u32[]{:S(2)}) collective-permute-start(f32[1,64]{1,0:T(1,128)S(1)} %multiply_add_fusion.1), channel_id=1, source_target_pairs={{0,8},{1,9},{2,10},{3,11},{4,12},{5,13},{6,14},{7,15},{8,0},{9,1},... | collective-permute-start | bytes 776 | tf_op jit(solution)/shard_map/ppermute | solution.py:530
  87.3 3.6 %collective-permute-start.2 = (f32[1,64]{1,0:T(1,128)S(1)}, f32[1,64]{1,0:T(1,128)S(1)}, u32[]{:S(2)}, u32[]{:S(2)}) collective-permute-start(f32[1,64]{1,0:T(1,128)S(1)} %multiply_add_fusion.1), channel_id=1, source_target_pairs={{0,4},{1,5},{2,6},{3,7},{4,8},{5,9},{6,10},{7,11},{8,12},{9,13},{1... | collective-permute-start | bytes 776 | tf_op jit(solution)/shard_map/ppermute | solution.py:530
  91.0 1.2 copy-start.2
  98.5 1.4 copy-start
  99.9 0.7 copy-start.9
  100.6 1.2 copy-start.3
  101.9 0.9 copy-start.10
  112.1 4.8 %collective-permute-start.5 = (f32[8,72,512]{2,1,0:T(8,128)S(1)}, f32[8,72,512]{2,1,0:T(8,128)S(1)}, u32[]{:S(2)}, u32[]{:S(2)}) collective-permute-start(f32[8,72,512]{2,1,0:T(8,128)S(1)} %get-tuple-element.30), channel_id=1, source_target_pairs={{0,1},{1,0},{2,3},{3,2},{4,5},{5,4},{6,7},{7,6},{8,9},{9,8},{10,11... | collective-permute-start | bytes 3538952 | tf_op jit(solution)/shard_map/ppermute | solution.py:498
  119.4 19.7 %all-to-all-start.3 = ((f32[4,2,72,512]{3,2,1,0:T(8,128)}), f32[4,2,72,512]{3,2,1,0:T(8,128)S(1)}, u32[]{:S(2)}, u32[]{:S(2)}) async-start(f32[4,2,72,512]{3,2,1,0:T(8,128)} %bitcast.16), calls=%async_computation.3 | async-start | bytes 2359296 | tf_op jit(solution)/shard_map/all_to_all | solution.py:494
  123.0 6.5 %collective-permute-start.7 = (f32[2,128,128]{2,1,0:T(8,128)S(1)}, f32[2,128,128]{2,1,0:T(8,128)S(1)}, u32[]{:S(2)}, u32[]{:S(2)}) collective-permute-start(f32[2,128,128]{2,1,0:T(8,128)S(1)} %get-tuple-element.35), channel_id=1, source_target_pairs={{0,16},{16,32},{32,48},{48,0},{64,80},{80,96},{96,112},{112,64},{1... | collective-permute-start | bytes 393224 | tf_op jit(solution)/shard_map/ppermute | solution.py:508
  124.4 8.7 %collective-permute-start.8 = (f32[2,128,128]{2,1,0:T(8,128)S(1)}, f32[2,128,128]{2,1,0:T(8,128)S(1)}, u32[]{:S(2)}, u32[]{:S(2)}) collective-permute-start(f32[2,128,128]{2,1,0:T(8,128)S(1)} %get-tuple-element.36), channel_id=1, source_target_pairs={{0,32},{16,48},{32,0},{48,16},{64,96},{80,112},{96,64},{112,80},{1... | collective-permute-start | bytes 393224 | tf_op jit(solution)/shard_map/ppermute | solution.py:508
  127.2 6.0 %collective-permute-start.9 = (f32[2,128,128]{2,1,0:T(8,128)S(1)}, f32[2,128,128]{2,1,0:T(8,128)S(1)}, u32[]{:S(2)}, u32[]{:S(2)}) collective-permute-start(f32[2,128,128]{2,1,0:T(8,128)S(1)} %get-tuple-element.37), channel_id=1, source_target_pairs={{0,48},{16,0},{32,16},{48,32},{64,112},{80,64},{96,80},{112,96},{1... | collective-permute-start | bytes 393224 | tf_op jit(solution)/shard_map/ppermute | solution.py:508
  133.2 8.9 %collective-permute-start.10 = (f32[2,128,128]{2,1,0:T(8,128)S(1)}, f32[2,128,128]{2,1,0:T(8,128)S(1)}, u32[]{:S(2)}, u32[]{:S(2)}) collective-permute-start(f32[2,128,128]{2,1,0:T(8,128)S(1)} %add_add_fusion), channel_id=1, source_target_pairs={{0,64},{16,80},{32,96},{48,112},{64,0},{80,16},{96,32},{112,48},{1... | collective-permute-start | bytes 393224 | tf_op jit(solution)/shard_map/ppermute | solution.py:498
  139.8 15.6 %collective-permute-start.6 = (f32[72,512]{1,0:T(8,128)S(1)}, f32[72,512]{1,0:T(8,128)S(1)}, u32[]{:S(2)}, u32[]{:S(2)}) collective-permute-start(f32[72,512]{1,0:T(8,128)S(1)} %get-tuple-element.32), channel_id=1, source_target_pairs={{0,2},{1,3},{2,0},{3,1},{4,6},{5,7},{6,4},{7,5},{8,10},{9,11},{10,... | collective-permute-start | bytes 442376 | tf_op jit(solution)/shard_map/ppermute | solution.py:498
  142.2 5.6 %collective-permute-start.13 = (f32[2,128,128]{2,1,0:T(8,128)S(1)}, f32[2,128,128]{2,1,0:T(8,128)S(1)}, u32[]{:S(2)}, u32[]{:S(2)}) collective-permute-start(f32[2,128,128]{2,1,0:T(8,128)S(1)} %add.70.refs_0_), channel_id=1, source_target_pairs={{0,48},{16,0},{32,16},{48,32},{64,112},{80,64},{96,80},{112,96},{1... | collective-permute-start | bytes 393224 | tf_op jit(solution)/shard_map/ppermute | solution.py:508
  145.2 5.4 %collective-permute-start.12 = (f32[2,128,128]{2,1,0:T(8,128)S(1)}, f32[2,128,128]{2,1,0:T(8,128)S(1)}, u32[]{:S(2)}, u32[]{:S(2)}) collective-permute-start(f32[2,128,128]{2,1,0:T(8,128)S(1)} %add.70.refs_0_), channel_id=1, source_target_pairs={{0,32},{16,48},{32,0},{48,16},{64,96},{80,112},{96,64},{112,80},{1... | collective-permute-start | bytes 393224 | tf_op jit(solution)/shard_map/ppermute | solution.py:508
  145.5 8.5 %collective-permute-start.11 = (f32[2,128,128]{2,1,0:T(8,128)S(1)}, f32[2,128,128]{2,1,0:T(8,128)S(1)}, u32[]{:S(2)}, u32[]{:S(2)}) collective-permute-start(f32[2,128,128]{2,1,0:T(8,128)S(1)} %add.70.refs_0_), channel_id=1, source_target_pairs={{0,16},{16,32},{32,48},{48,0},{64,80},{80,96},{96,112},{112,64},{1... | collective-permute-start | bytes 393224 | tf_op jit(solution)/shard_map/ppermute | solution.py:508

commit v9 on v8

--- a/solution.py
+++ b/solution.py
@@ -18,7 +18,7 @@
 TILE = 256
 RUN = 4
 GROUP = 4
-PAIR = 2
+PAIR = 4
 PARTS = 2
 ROUNDS = 4
 VMEM = 48 << 20
@@ -317,7 +317,7 @@
     g = g_ref[...]
     blocks, keys_total = [], gkt_ref[...]
     for n in range(PAIR):
-        dest = far_first(i * PAIR + n, steps * PAIR, place_ref) if last else i * PAIR + n
+        dest = far_first(i * PAIR + n, steps * PAIR, place_ref)
         q = q_ref[:, pl.ds(pl.multiple_of(dest * width, width), width)]
         q = jnp.concatenate([q[:, j * dim : (j + 1) * dim] for j in range(GROUP)], axis=0)
         d = jnp.dot(q, kt_ref[...], preferred_element_type=jnp.float32)
@@ -338,7 +338,7 @@
         keys_total = keys_total + lax.dot_general(
             q, head_grad, (((0,), (0,)), ((), ())), preferred_element_type=jnp.float32
         )
-        blocks.append(gq + former_ref[dest] if last else gq)
+        blocks.append(gq + former_ref[n] if last else gq)
     gkt_ref[...] = keys_total
     if not last:
         for n in range(PAIR):
@@ -401,7 +401,7 @@
     scratch = [pltpu.VMEM((rows, keys), jnp.float32), pltpu.VMEM((dim, keys), jnp.float32)]
     if last:
         half = steps // 2
-        in_specs += [whole(*former[0].shape), whole(*shape)]
+        in_specs += [pl.BlockSpec(block, lambda i, place: (i, 0, 0)), whole(*shape)]
         args += former
         scratch.append(pltpu.VMEM(shape, jnp.float32))
         piece = (owners // ROUNDS, PARTS * shape[1], dim)

time: 157 us -> 156 us (level)
  no operation moved by 1% of the time
where the time goes in v9:
time: 156 us; the launch traced here: 155 us
  Pallas kernels  54.7 us (35%)
  waiting for transfers between devices  46.2 us (30%)
  starting transfers between devices  41.6 us (27%)
  local copies, waits for them, and re-layouts  8.29 us (5%)
  other arithmetic  3.35 us (2%)
    all_to_all x4, starting transfers between devices, exchanged(): return lax.all_to_all(x, axis, 0, 0, axis_index_groups=groups, tiled=True)  22.9 us
    pallas_call x1, Pallas kernels, main_forward(): pl.pallas_call(main_kernel, grid_spec=pltpu.PrefetchScalarGridSpec(num_sc...  18.6 us
    all_to_all x4, waiting for transfers between devices, exchanged(): return lax.all_to_all(x, axis, 0, 0, axis_index_groups=groups, tiled=True)  15.8 us
    ppermute x5, waiting for transfers between devices, flipped(): lax.ppermute(x, axis, [(i, i ^ mask) for i in range(lax.axis_size(axis))])  14.6 us
    pallas_call x2, Pallas kernels, backward(): pl.pallas_call(functools.partial(back_kernel, last), grid_spec=pltpu.Pref...  14.4 us
    pallas_call x2, Pallas kernels, weighted_sum(): pl.pallas_call(functools.partial(sum_kernel, first), grid_spec=pltpu.Pref...  13.4 us
    ppermute x6, waiting for transfers between devices, turned(): lax.ppermute(x, 'head', [(i, i // ROUNDS * ROUNDS + (i + k) % ROUNDS) for...  13.1 us
    ppermute x6, starting transfers between devices, turned(): lax.ppermute(x, 'head', [(i, i // ROUNDS * ROUNDS + (i + k) % ROUNDS) for...  9 us
  transfers between devices with their start and end apart: 18, of which 12 were waited for; matrix products, arithmetic and copies ran while one was open for 2% of the time, Pallas kernels for 13%

profile of v9, /device:TPU:1, one launch (start us, length us, event | category | flops | bytes accessed | tf_op | source)
XLA Modules:
  0.0 154.9 jit_solution(10610611683685604130)
XLA Ops:
  0.7 18.6 %main_forward.1 = (bf16[2,16,1024,256]{3,2,1,0:T(8,128)(2,1)}, bf16[2,512,256]{2,1,0:T(8,128)(2,1)}, f32[128,256]{1,0:T(8,128)}, f32[16,16,512]{2,1,0:T(8,128)}) custom-call(s32[1]{0:T(128)} %bitcast.3.base_ref, bf16[576,1024]{1,0:T(8,128)(2,1)} %bitcast.33, bf16[16,576,512]{2,1,0:T(8,128)(2,1)} %bitcast.28, bf16[16,576,512]{2,1,0:T(8,128)(2,1)} %bitcast.29, ...), custom_call_target="tpu_custom_call" | custom-call | flops 9663676416 | bytes 27262976 | tf_op jit(solution)/shard_map/main_forward/pallas_call | solution.py:141
  19.3 8.6 %all-to-all-start = ((f32[16,16,512]{2,1,0:T(8,128)}), f32[16,16,512]{2,1,0:T(8,128)S(1)}, u32[]{:S(2)}, u32[]{:S(2)}) async-start(f32[16,16,512]{2,1,0:T(8,128)} %get-tuple-element.24), calls=%async_computation | async-start | bytes 1048576 | tf_op jit(solution)/shard_map/all_to_all | solution.py:494
  27.9 0.6 convert_reduce_fusion
  28.5 10.6 %all-to-all-done.stats_ref = f32[16,16,512]{2,1,0:T(8,128)S(1)} async-done(((f32[16,16,512]{2,1,0:T(8,128)}), f32[16,16,512]{2,1,0:T(8,128)S(1)}, u32[]{:S(2)}, u32[]{:S(2)}) %all-to-all-start) | async-done | bytes 524320 | tf_op jit(solution)/shard_map/all_to_all | solution.py:494
  39.1 0.9 copy-done.6
  40.0 6.7 %shard_map.104 = f32[8,64,512]{2,1,0:T(8,128)} custom-call(s32[1]{0:T(128)} %bitcast.5.info_ref, bf16[2,16,1024,256]{3,2,1,0:T(8,128)(2,1)} %get-tuple-element.21.e_ref, bf16[2,512,256]{2,1,0:T(8,128)(2,1)S(1)} %copy-done.1, f32[128,256]{1,0:T(8,128)S(1)} %copy-done.6, f32[16,16,512]{2,1,0:T(8,128)S(1)} %all-to-all-done.stats_ref), custom_call_target="tpu_custom_call" | custom-call | flops 8388608 | bytes 9437184 | tf_op jit(solution)/shard_map/pallas_call | solution.py:276
  46.7 5.3 %all-to-all-start.2 = ((f32[8,64,512]{2,1,0:T(8,128)}), f32[8,64,512]{2,1,0:T(8,128)S(1)}, u32[]{:S(2)}, u32[]{:S(2)}) async-start(f32[8,64,512]{2,1,0:T(8,128)} %shard_map.104), calls=%async_computation.2 | async-start | bytes 2097152 | tf_op jit(solution)/shard_map/all_to_all | solution.py:494
  52.0 0.8 copy.12
  52.8 0.7 dynamic-slice_bitcast_fusion
  53.5 5.6 %index_forward.1 = (f32[64,1024]{1,0:T(8,128)}, f32[1,64]{1,0:T(1,128)}) custom-call(s32[1]{0:T(128)} %bitcast.3.base_ref, bf16[64,8192]{1,0:T(8,128)(2,1)} %q_ref.5, bf16[128,1024]{1,0:T(8,128)(2,1)} %bitcast.23, f32[64,64]{1,0:T(8,128)} %w_ref.1, s32[1,64]{1,0:T(1,128)} %get-tuple-element.40.start_ref, s32[1,64]{1,0:T(1,128)} %get-tuple-element.39.pos_ref), custom_call_target="tpu_custom_call" | custom-call | flops 1073741824 | bytes 2097152 | tf_op jit(solution)/shard_map/index_forward/pallas_call | solution.py:209
  59.1 1.5 collective-permute-start
  60.6 6.7 %shard_map.103 = f32[8,64,512]{2,1,0:T(8,128)} custom-call(s32[1]{0:T(128)} %bitcast.5.info_ref, bf16[2,16,1024,256]{3,2,1,0:T(8,128)(2,1)} %get-tuple-element.21.e_ref, bf16[2,512,256]{2,1,0:T(8,128)(2,1)S(1)} %copy-done.1, f32[128,256]{1,0:T(8,128)S(1)} %copy-done.7, f32[16,16,512]{2,1,0:T(8,128)S(1)} %all-to-all-done.stats_ref), custom_call_target="tpu_custom_call" | custom-call | flops 8388608 | bytes 9437184 | tf_op jit(solution)/shard_map/pallas_call | solution.py:276
  67.3 5.6 %all-to-all-start.1 = ((f32[8,64,512]{2,1,0:T(8,128)}), f32[8,64,512]{2,1,0:T(8,128)S(1)}, u32[]{:S(2)}, u32[]{:S(2)}) async-start(f32[8,64,512]{2,1,0:T(8,128)} %shard_map.103), calls=%async_computation.1 | async-start | bytes 2097152 | tf_op jit(solution)/shard_map/all_to_all | solution.py:494
  72.9 0.7 collective-permute-start.1
  73.7 12.1 %collective-permute-done.1 = f32[1,64]{1,0:T(1,128)S(1)} collective-permute-done((f32[1,64]{1,0:T(1,128)S(1)}, f32[1,64]{1,0:T(1,128)S(1)}, u32[]{:S(2)}, u32[]{:S(2)}) %collective-permute-start.1) | collective-permute-done | bytes 288 | tf_op jit(solution)/shard_map/ppermute | solution.py:498
  85.8 0.6 collective-permute-start.4
  86.4 0.9 collective-permute-start.3
  87.3 0.6 collective-permute-start.2
  88.0 0.2 copy.14
  88.3 2.0 %collective-permute-done.3 = f32[1,64]{1,0:T(1,128)S(1)} collective-permute-done((f32[1,64]{1,0:T(1,128)S(1)}, f32[1,64]{1,0:T(1,128)S(1)}, u32[]{:S(2)}, u32[]{:S(2)}) %collective-permute-start.3) | collective-permute-done | bytes 288 | tf_op jit(solution)/shard_map/ppermute | solution.py:530
  90.3 0.6 collective-permute-done.2
  91.0 1.2 copy-done.2
  92.2 6.1 %shard_map.105 = (f32[16,72,512]{2,1,0:T(8,128)S(1)}, f32[8,64,128]{2,1,0:T(8,128)S(1)}) custom-call(s32[3]{0:T(128)S(1)} %pad_add_fusion.place_ref, f32[8,64,512]{2,1,0:T(8,128)S(1)} %all-to-all-done.2.t_ref, f32[64,1024]{1,0:T(8,128)S(1)} %copy-done.8, f32[1,64]{1,0:T(1,128)S(1)} %multiply_add_fusion.stats_ref, f32[1,64]{1,0:T(1,128)S(1)} %bitcast.26, ...), custom_call_target="tpu_custom_call" | custom-call | flops 1610612736 | bytes 4194304 | tf_op jit(solution)/shard_map/pallas_call | solution.py:416
  98.4 1.4 copy-done
  99.8 0.7 copy-done.9
  100.5 1.2 copy-done.3
  101.7 0.9 copy-done.10
  102.7 8.3 %shard_map.106 = (f32[8,72,512]{2,1,0:T(8,128)S(1)}, f32[8,72,512]{2,1,0:T(8,128)}, f32[2,128,128]{2,1,0:T(8,128)S(1)}, f32[2,128,128]{2,1,0:T(8,128)S(1)}, f32[...) custom-call(s32[3]{0:T(128)S(1)} %pad_add_fusion.place_ref, f32[8,64,512]{2,1,0:T(8,128)S(1)} %all-to-all-done.1.t_ref, ...), custom_call_target="tpu_custom_call" | custom-call | flops 1610612736 | bytes 4194304 | tf_op jit(solution)/shard_map/pallas_call | solution.py:416
  110.9 2.3 %collective-permute-start.5 = (f32[8,72,512]{2,1,0:T(8,128)S(1)}, f32[8,72,512]{2,1,0:T(8,128)S(1)}, u32[]{:S(2)}, u32[]{:S(2)}) collective-permute-start(f32[8,72,512]{2,1,0:T(8,128)S(1)} %get-tuple-element.30), channel_id=1, source_target_pairs={{0,1},{1,0},{2,3},{3,2},{4,5},{5,4},{6,7},{7,6},{8,9},{9,8},{10,11... | collective-permute-start | bytes 3538952 | tf_op jit(solution)/shard_map/ppermute | solution.py:498
  113.2 2.5 %collective-permute-done.5 = f32[8,72,512]{2,1,0:T(8,128)S(1)} collective-permute-done((f32[8,72,512]{2,1,0:T(8,128)S(1)}, f32[8,72,512]{2,1,0:T(8,128)S(1)}, u32[]{:S(2)}, u32[]{:S(2)}) %collective-permute-start.5) | collective-permute-done | bytes 1179680 | tf_op jit(solution)/shard_map/ppermute | solution.py:498
  115.7 2.6 %add.66 = f32[8,72,512]{2,1,0:T(8,128)} add(f32[8,72,512]{2,1,0:T(8,128)} %get-tuple-element.29, f32[8,72,512]{2,1,0:T(8,128)S(1)} %collective-permute-done.5) | non-fusion elementwise | flops 294912 | bytes 3538944 | tf_op jit(solution)/shard_map/add | solution.py:546
  118.2 3.5 %all-to-all-start.3 = ((f32[4,2,72,512]{3,2,1,0:T(8,128)}), f32[4,2,72,512]{3,2,1,0:T(8,128)S(1)}, u32[]{:S(2)}, u32[]{:S(2)}) async-start(f32[4,2,72,512]{3,2,1,0:T(8,128)} %bitcast.16), calls=%async_computation.3 | async-start | bytes 2359296 | tf_op jit(solution)/shard_map/all_to_all | solution.py:494
  121.8 1.5 collective-permute-start.7
  123.3 2.7 %collective-permute-start.8 = (f32[2,128,128]{2,1,0:T(8,128)S(1)}, f32[2,128,128]{2,1,0:T(8,128)S(1)}, u32[]{:S(2)}, u32[]{:S(2)}) collective-permute-start(f32[2,128,128]{2,1,0:T(8,128)S(1)} %get-tuple-element.36), channel_id=1, source_target_pairs={{0,32},{16,48},{32,0},{48,16},{64,96},{80,112},{96,64},{112,80},{1... | collective-permute-start | bytes 393224 | tf_op jit(solution)/shard_map/ppermute | solution.py:508
  126.0 0.9 collective-permute-start.9
  126.9 1.5 collective-permute-done.7
  128.3 3.7 %collective-permute-done.8 = f32[2,128,128]{2,1,0:T(8,128)S(1)} collective-permute-done((f32[2,128,128]{2,1,0:T(8,128)S(1)}, f32[2,128,128]{2,1,0:T(8,128)S(1)}, u32[]{:S(2)}, u32[]{:S(2)}) %collective-permute-start.8) | collective-permute-done | bytes 131104 | tf_op jit(solution)/shard_map/ppermute | solution.py:508
  132.1 0.6 collective-permute-start.10
  132.7 5.2 %all-to-all-done.3.x_ref = f32[4,2,72,512]{3,2,1,0:T(8,128)S(1)} async-done(((f32[4,2,72,512]{3,2,1,0:T(8,128)}), f32[4,2,72,512]{3,2,1,0:T(8,128)S(1)}, u32[]{:S(2)}, u32[]{:S(2)}) %all-to-all-start.3) | async-done | bytes 1179680 | tf_op jit(solution)/shard_map/all_to_all | solution.py:494
  138.0 0.6 halves.1
  138.6 2.4 %collective-permute-start.6 = (f32[72,512]{1,0:T(8,128)S(1)}, f32[72,512]{1,0:T(8,128)S(1)}, u32[]{:S(2)}, u32[]{:S(2)}) collective-permute-start(f32[72,512]{1,0:T(8,128)S(1)} %get-tuple-element.32), channel_id=1, source_target_pairs={{0,2},{1,3},{2,0},{3,1},{4,6},{5,7},{6,4},{7,5},{8,10},{9,11},{10,... | collective-permute-start | bytes 442376 | tf_op jit(solution)/shard_map/ppermute | solution.py:498
  141.0 3.0 %collective-permute-start.13 = (f32[2,128,128]{2,1,0:T(8,128)S(1)}, f32[2,128,128]{2,1,0:T(8,128)S(1)}, u32[]{:S(2)}, u32[]{:S(2)}) collective-permute-start(f32[2,128,128]{2,1,0:T(8,128)S(1)} %add.70.refs_0_), channel_id=1, source_target_pairs={{0,48},{16,0},{32,16},{48,32},{64,112},{80,64},{96,80},{112,96},{1... | collective-permute-start | bytes 393224 | tf_op jit(solution)/shard_map/ppermute | solution.py:508
  144.3 0.6 collective-permute-start.11
  144.9 1.8 %collective-permute-done.13.refs_3_ = f32[2,128,128]{2,1,0:T(8,128)S(1)} collective-permute-done((f32[2,128,128]{2,1,0:T(8,128)S(1)}, f32[2,128,128]{2,1,0:T(8,128)S(1)}, u32[]{:S(2)}, u32[]{:S(2)}) %collective-permute-start.13) | collective-permute-done | bytes 131104 | tf_op jit(solution)/shard_map/ppermute | solution.py:508
  146.7 2.8 %collective-permute-done.12.refs_2_ = f32[2,128,128]{2,1,0:T(8,128)S(1)} collective-permute-done((f32[2,128,128]{2,1,0:T(8,128)S(1)}, f32[2,128,128]{2,1,0:T(8,128)S(1)}, u32[]{:S(2)}, u32[]{:S(2)}) %collective-permute-start.12) | collective-permute-done | bytes 131104 | tf_op jit(solution)/shard_map/ppermute | solution.py:508
  149.5 3.3 %collective-permute-done.11.refs_1_ = f32[2,128,128]{2,1,0:T(8,128)S(1)} collective-permute-done((f32[2,128,128]{2,1,0:T(8,128)S(1)}, f32[2,128,128]{2,1,0:T(8,128)S(1)}, u32[]{:S(2)}, u32[]{:S(2)}) %collective-permute-start.11) | collective-permute-done | bytes 131104 | tf_op jit(solution)/shard_map/ppermute | solution.py:508
  152.8 1.4 join.1
  154.2 0.7 end.1
  (41 shorter events, 0.6 us)
Async XLA Ops:
  0.6 27.2 %copy-start.13 = (s32[512]{0:T(512)S(1)}, s32[512]{0:T(512)}, u32[]{:S(2)}) copy-start(s32[512]{0:T(512)} %param.14) | copy-start | bytes 6148
  0.6 27.2 %copy-start.14 = (s32[512]{0:T(512)S(1)}, s32[512]{0:T(512)}, u32[]{:S(2)}) copy-start(s32[512]{0:T(512)} %param.15) | copy-start | bytes 6148
  19.3 19.8 %copy-start.1 = (bf16[2,512,256]{2,1,0:T(8,128)(2,1)S(1)}, bf16[2,512,256]{2,1,0:T(8,128)(2,1)}, u32[]{:S(2)}) copy-start(bf16[2,512,256]{2,1,0:T(8,128)(2,1)} %get-tuple-element.22.sel_ref) | copy-start | bytes 1572868
  19.3 19.8 %all-to-all-start = ((f32[16,16,512]{2,1,0:T(8,128)}), f32[16,16,512]{2,1,0:T(8,128)S(1)}, u32[]{:S(2)}, u32[]{:S(2)}) async-start(f32[16,16,512]{2,1,0:T(8,128)} %get-tuple-element.24), calls=%async_computation | async-start | bytes 1048576 | tf_op jit(solution)/shard_map/all_to_all | solution.py:494
  39.1 0.9 copy-start.6
  46.7 5.3 %copy-start.4 = (bf16[1024,128]{1,0:T(8,128)(2,1)S(1)}, bf16[1024,128]{1,0:T(8,128)(2,1)}, u32[]{:S(2)}) copy-start(bf16[1024,128]{1,0:T(8,128)(2,1)} %k_ref.3) | copy-start | bytes 786436
  46.7 20.6 %all-to-all-start.2 = ((f32[8,64,512]{2,1,0:T(8,128)}), f32[8,64,512]{2,1,0:T(8,128)S(1)}, u32[]{:S(2)}, u32[]{:S(2)}) async-start(f32[8,64,512]{2,1,0:T(8,128)} %shard_map.104), calls=%async_computation.2 | async-start | bytes 2097152 | tf_op jit(solution)/shard_map/all_to_all | solution.py:494
  53.5 7.1 %copy-start.7 = (f32[128,256]{1,0:T(8,128)S(1)}, f32[128,256]{1,0:T(8,128)}, u32[]{:S(2)}) copy-start(f32[128,256]{1,0:T(8,128)} %get-tuple-element.23.m_ref) | copy-start | bytes 393220
  59.1 13.8 %collective-permute-start = (f32[1,64]{1,0:T(1,128)}, f32[1,64]{1,0:T(1,128)S(1)}, u32[]{:S(2)}, u32[]{:S(2)}) collective-permute-start(f32[1,64]{1,0:T(1,128)} %get-tuple-element.26), channel_id=1, source_target_pairs={{0,1},{1,0},{2,3},{3,2},{4,5},{5,4},{6,7},{7,6},{8,9},{9,8},{10,11... | collective-permute-start | bytes 776 | tf_op jit(solution)/shard_map/ppermute | solution.py:498
  67.3 5.6 %copy-start.15 = (f32[1,64]{1,0:T(1,128)S(1)}, f32[1,64]{1,0:T(1,128)}, u32[]{:S(2)}) copy-start(f32[1,64]{1,0:T(1,128)} %get-tuple-element.26) | copy-start | bytes 772
  67.3 20.6 %copy-start.12 = (f32[64,64]{1,0:T(8,128)S(1)}, f32[64,64]{1,0:T(8,128)}, u32[]{:S(2)}) copy-start(f32[64,64]{1,0:T(8,128)} %w_ref.1) | copy-start | bytes 49156
  67.3 23.7 %copy-start.5 = (bf16[1024,128]{0,1:T(8,128)(2,1)S(1)}, bf16[1024,128]{0,1:T(8,128)(2,1)}, u32[]{:S(2)}) copy-start(bf16[1024,128]{0,1:T(8,128)(2,1)} %copy.12) | copy-start | bytes 786436
  67.3 23.7 %copy-start.8 = (f32[64,1024]{1,0:T(8,128)S(1)}, f32[64,1024]{1,0:T(8,128)}, u32[]{:S(2)}) copy-start(f32[64,1024]{1,0:T(8,128)} %get-tuple-element.25.s_ref) | copy-start | bytes 786436
  67.3 23.7 %copy-start.11 = (f32[64]{0:T(128)S(1)}, f32[64]{0:T(128)}, u32[]{:S(2)}) copy-start(f32[64]{0:T(128)} %param.13) | copy-start | bytes 772
  67.3 33.2 %all-to-all-start.1 = ((f32[8,64,512]{2,1,0:T(8,128)}), f32[8,64,512]{2,1,0:T(8,128)S(1)}, u32[]{:S(2)}, u32[]{:S(2)}) async-start(f32[8,64,512]{2,1,0:T(8,128)} %shard_map.103), calls=%async_computation.1 | async-start | bytes 2097152 | tf_op jit(solution)/shard_map/all_to_all | solution.py:494
  72.9 12.9 %collective-permute-start.1 = (f32[1,64]{1,0:T(1,128)S(1)}, f32[1,64]{1,0:T(1,128)S(1)}, u32[]{:S(2)}, u32[]{:S(2)}) collective-permute-start(f32[1,64]{1,0:T(1,128)S(1)} %multiply_add_fusion.2), channel_id=1, source_target_pairs={{0,2},{1,3},{2,0},{3,1},{4,6},{5,7},{6,4},{7,5},{8,10},{9,11},{10,... | collective-permute-start | bytes 776 | tf_op jit(solution)/shard_map/ppermute | solution.py:498
  85.8 2.5 %collective-permute-start.4 = (f32[1,64]{1,0:T(1,128)S(1)}, f32[1,64]{1,0:T(1,128)S(1)}, u32[]{:S(2)}, u32[]{:S(2)}) collective-permute-start(f32[1,64]{1,0:T(1,128)S(1)} %multiply_add_fusion.1), channel_id=1, source_target_pairs={{0,12},{1,13},{2,14},{3,15},{4,0},{5,1},{6,2},{7,3},{8,4},{9,5},{1... | collective-permute-start | bytes 776 | tf_op jit(solution)/shard_map/ppermute | solution.py:530
  86.4 3.9 %collective-permute-start.3 = (f32[1,64]{1,0:T(1,128)S(1)}, f32[1,64]{1,0:T(1,128)S(1)}, u32[]{:S(2)}, u32[]{:S(2)}) collective-permute-start(f32[1,64]{1,0:T(1,128)S(1)} %multiply_add_fusion.1), channel_id=1, source_target_pairs={{0,8},{1,9},{2,10},{3,11},{4,12},{5,13},{6,14},{7,15},{8,0},{9,1},... | collective-permute-start | bytes 776 | tf_op jit(solution)/shard_map/ppermute | solution.py:530
  87.3 3.6 %collective-permute-start.2 = (f32[1,64]{1,0:T(1,128)S(1)}, f32[1,64]{1,0:T(1,128)S(1)}, u32[]{:S(2)}, u32[]{:S(2)}) collective-permute-start(f32[1,64]{1,0:T(1,128)S(1)} %multiply_add_fusion.1), channel_id=1, source_target_pairs={{0,4},{1,5},{2,6},{3,7},{4,8},{5,9},{6,10},{7,11},{8,12},{9,13},{1... | collective-permute-start | bytes 776 | tf_op jit(solution)/shard_map/ppermute | solution.py:530
  91.0 1.2 copy-start.2
  98.4 1.4 copy-start
  99.8 0.7 copy-start.9
  100.5 1.2 copy-start.3
  101.7 0.9 copy-start.10
  110.9 4.8 %collective-permute-start.5 = (f32[8,72,512]{2,1,0:T(8,128)S(1)}, f32[8,72,512]{2,1,0:T(8,128)S(1)}, u32[]{:S(2)}, u32[]{:S(2)}) collective-permute-start(f32[8,72,512]{2,1,0:T(8,128)S(1)} %get-tuple-element.30), channel_id=1, source_target_pairs={{0,1},{1,0},{2,3},{3,2},{4,5},{5,4},{6,7},{7,6},{8,9},{9,8},{10,11... | collective-permute-start | bytes 3538952 | tf_op jit(solution)/shard_map/ppermute | solution.py:498
  118.2 19.7 %all-to-all-start.3 = ((f32[4,2,72,512]{3,2,1,0:T(8,128)}), f32[4,2,72,512]{3,2,1,0:T(8,128)S(1)}, u32[]{:S(2)}, u32[]{:S(2)}) async-start(f32[4,2,72,512]{3,2,1,0:T(8,128)} %bitcast.16), calls=%async_computation.3 | async-start | bytes 2359296 | tf_op jit(solution)/shard_map/all_to_all | solution.py:494
  121.8 6.6 %collective-permute-start.7 = (f32[2,128,128]{2,1,0:T(8,128)S(1)}, f32[2,128,128]{2,1,0:T(8,128)S(1)}, u32[]{:S(2)}, u32[]{:S(2)}) collective-permute-start(f32[2,128,128]{2,1,0:T(8,128)S(1)} %get-tuple-element.35), channel_id=1, source_target_pairs={{0,16},{16,32},{32,48},{48,0},{64,80},{80,96},{96,112},{112,64},{1... | collective-permute-start | bytes 393224 | tf_op jit(solution)/shard_map/ppermute | solution.py:508
  123.3 8.8 %collective-permute-start.8 = (f32[2,128,128]{2,1,0:T(8,128)S(1)}, f32[2,128,128]{2,1,0:T(8,128)S(1)}, u32[]{:S(2)}, u32[]{:S(2)}) collective-permute-start(f32[2,128,128]{2,1,0:T(8,128)S(1)} %get-tuple-element.36), channel_id=1, source_target_pairs={{0,32},{16,48},{32,0},{48,16},{64,96},{80,112},{96,64},{112,80},{1... | collective-permute-start | bytes 393224 | tf_op jit(solution)/shard_map/ppermute | solution.py:508
  126.0 6.0 %collective-permute-start.9 = (f32[2,128,128]{2,1,0:T(8,128)S(1)}, f32[2,128,128]{2,1,0:T(8,128)S(1)}, u32[]{:S(2)}, u32[]{:S(2)}) collective-permute-start(f32[2,128,128]{2,1,0:T(8,128)S(1)} %get-tuple-element.37), channel_id=1, source_target_pairs={{0,48},{16,0},{32,16},{48,32},{64,112},{80,64},{96,80},{112,96},{1... | collective-permute-start | bytes 393224 | tf_op jit(solution)/shard_map/ppermute | solution.py:508
  132.1 8.9 %collective-permute-start.10 = (f32[2,128,128]{2,1,0:T(8,128)S(1)}, f32[2,128,128]{2,1,0:T(8,128)S(1)}, u32[]{:S(2)}, u32[]{:S(2)}) collective-permute-start(f32[2,128,128]{2,1,0:T(8,128)S(1)} %add_add_fusion), channel_id=1, source_target_pairs={{0,64},{16,80},{32,96},{48,112},{64,0},{80,16},{96,32},{112,48},{1... | collective-permute-start | bytes 393224 | tf_op jit(solution)/shard_map/ppermute | solution.py:498
  138.6 15.6 %collective-permute-start.6 = (f32[72,512]{1,0:T(8,128)S(1)}, f32[72,512]{1,0:T(8,128)S(1)}, u32[]{:S(2)}, u32[]{:S(2)}) collective-permute-start(f32[72,512]{1,0:T(8,128)S(1)} %get-tuple-element.32), channel_id=1, source_target_pairs={{0,2},{1,3},{2,0},{3,1},{4,6},{5,7},{6,4},{7,5},{8,10},{9,11},{10,... | collective-permute-start | bytes 442376 | tf_op jit(solution)/shard_map/ppermute | solution.py:498
  141.0 5.6 %collective-permute-start.13 = (f32[2,128,128]{2,1,0:T(8,128)S(1)}, f32[2,128,128]{2,1,0:T(8,128)S(1)}, u32[]{:S(2)}, u32[]{:S(2)}) collective-permute-start(f32[2,128,128]{2,1,0:T(8,128)S(1)} %add.70.refs_0_), channel_id=1, source_target_pairs={{0,48},{16,0},{32,16},{48,32},{64,112},{80,64},{96,80},{112,96},{1... | collective-permute-start | bytes 393224 | tf_op jit(solution)/shard_map/ppermute | solution.py:508
  144.1 5.4 %collective-permute-start.12 = (f32[2,128,128]{2,1,0:T(8,128)S(1)}, f32[2,128,128]{2,1,0:T(8,128)S(1)}, u32[]{:S(2)}, u32[]{:S(2)}) collective-permute-start(f32[2,128,128]{2,1,0:T(8,128)S(1)} %add.70.refs_0_), channel_id=1, source_target_pairs={{0,32},{16,48},{32,0},{48,16},{64,96},{80,112},{96,64},{112,80},{1... | collective-permute-start | bytes 393224 | tf_op jit(solution)/shard_map/ppermute | solution.py:508
  144.3 8.5 %collective-permute-start.11 = (f32[2,128,128]{2,1,0:T(8,128)S(1)}, f32[2,128,128]{2,1,0:T(8,128)S(1)}, u32[]{:S(2)}, u32[]{:S(2)}) collective-permute-start(f32[2,128,128]{2,1,0:T(8,128)S(1)} %add.70.refs_0_), channel_id=1, source_target_pairs={{0,16},{16,32},{32,48},{48,0},{64,80},{80,96},{96,112},{112,64},{1... | collective-permute-start | bytes 393224 | tf_op jit(solution)/shard_map/ppermute | solution.py:508

commit v10 on v9

--- a/solution.py
+++ b/solution.py
@@ -16,6 +16,7 @@
 FLOOR = -1e29
 CHUNK = 256
 TILE = 256
+WIDTH = 256
 RUN = 4
 GROUP = 4
 PAIR = 4
@@ -244,7 +245,7 @@
     @pl.when(in_use(t, info_ref))
     def _():
         lse = lse_ref[t]
-        row = t * heads * chunks + first + c
+        row = t * heads * chunks + (first + c) * width // CHUNK
         weights = [jnp.exp2(m_ref[pl.ds(row + h * chunks, 1), :] - lse[h : h + 1]) for h in range(heads)]
         strips = []
         for r in range(width // lanes):
@@ -270,7 +271,7 @@
     tiles, heads, keys, tile = e.shape
     queries = sel.shape[1]
     rows = queries // owners
-    steps = keys // PARTS // CHUNK
+    steps = keys // PARTS // WIDTH
     first = part * steps
     used = lambda t, info: jnp.where(in_use(t, info), t, 0)
     return pl.pallas_call(
@@ -279,12 +280,12 @@
             num_scalar_prefetch=1,
             grid=(steps, tiles),
             in_specs=[
-                pl.BlockSpec((1, heads, CHUNK, tile), lambda c, t, info: (used(t, info), 0, first + c, 0)),
+                pl.BlockSpec((1, heads, WIDTH, tile), lambda c, t, info: (used(t, info), 0, first + c, 0)),
                 pl.BlockSpec((1, queries, tile), lambda c, t, info: (used(t, info), 0, 0)),
                 pl.BlockSpec(m.shape, lambda c, t, info: (0, 0)),
                 pl.BlockSpec(stats.shape, lambda c, t, info: (0, 0, 0)),
             ],
-            out_specs=pl.BlockSpec((owners, rows, CHUNK), lambda c, t, info: (0, 0, c)),
+            out_specs=pl.BlockSpec((owners, rows, WIDTH), lambda c, t, info: (0, 0, c)),
             scratch_shapes=[pltpu.VMEM((tiles, heads, tile), jnp.float32)],
         ),
         out_shape=jax.ShapeDtypeStruct((owners, rows, keys // PARTS), jnp.float32),
@@ -295,11 +296,13 @@
     )(info, e, sel, m, stats)
 
 
-def back_kernel(last, place_ref, t_ref, s_ref, stats_ref, c_ref, q_ref, k_ref, kt_ref, w_ref, *refs):
+def back_kernel(last, place_ref, t_ref, s_ref, stats_ref, c_ref, q_hbm, k_ref, kt_ref, w_ref, *refs):
     if last:
-        former_ref, fk_ref, far_ref, near_ref, *gk_refs, g_ref, gkt_ref, turned_ref = refs
+        former_ref, gk_hbm, far_ref, near_ref, *gk_refs, g_ref, gkt_ref, q_ref, q_sem, turned_ref, fk_ref, fk_sem = refs
+        fk_copy = pltpu.make_async_copy(gk_hbm, fk_ref, fk_sem)
     else:
-        gq_ref, gk_ref, g_ref, gkt_ref = refs
+        gq_ref, gk_ref, g_ref, gkt_ref, q_ref, q_sem = refs
+    q_copy = pltpu.make_async_copy(q_hbm, q_ref, q_sem)
     i, steps = pl.program_id(0), pl.num_programs(0)
     rows, _ = g_ref.shape
     dim = kt_ref.shape[0]
@@ -308,11 +311,15 @@
 
     @pl.when(i == 0)
     def _():
+        q_copy.start()
+        if last:
+            fk_copy.start()
         target = jnp.sum(t_ref[...], axis=0) * (1.0 / H)
         scores = s_ref[...]
         probs = jnp.exp2(scores - as_column(stats_ref[...]))
         g_ref[...] = jnp.where(scores > FLOOR, as_column(c_ref[...]) * (probs - target), 0.0)
         gkt_ref[...] = jnp.zeros_like(gkt_ref)
+        q_copy.wait()
 
     g = g_ref[...]
     blocks, keys_total = [], gkt_ref[...]
@@ -363,6 +370,7 @@
     @pl.when(i == steps - 1)
     def _():
         turned_ref[...] = gkt_ref[...].T.reshape(turned_ref.shape)
+        fk_copy.wait()
         rounds, lines = len(gk_refs), turned_ref.shape[1]
         for n, ref in enumerate(gk_refs):
             for y in range(ref.shape[0]):
@@ -392,18 +400,23 @@
         pl.BlockSpec((rows, keys), lambda i, place: (0, part)),
         whole(*stats.shape),
         whole(1, rows),
-        whole(rows, width),
+        pl.BlockSpec(memory_space=pltpu.HBM),
         pl.BlockSpec((keys, dim), lambda i, place: (part, 0)),
         pl.BlockSpec((dim, keys), lambda i, place: (0, part)),
         whole(*w.shape),
     ]
     args = [t, s, stats, c, q, k, kt, w]
-    scratch = [pltpu.VMEM((rows, keys), jnp.float32), pltpu.VMEM((dim, keys), jnp.float32)]
+    scratch = [
+        pltpu.VMEM((rows, keys), jnp.float32),
+        pltpu.VMEM((dim, keys), jnp.float32),
+        pltpu.VMEM((rows, width), q.dtype),
+        pltpu.SemaphoreType.DMA,
+    ]
     if last:
         half = steps // 2
-        in_specs += [pl.BlockSpec(block, lambda i, place: (i, 0, 0)), whole(*shape)]
+        in_specs += [pl.BlockSpec(block, lambda i, place: (i, 0, 0)), pl.BlockSpec(memory_space=pltpu.HBM)]
         args += former
-        scratch.append(pltpu.VMEM(shape, jnp.float32))
+        scratch += [pltpu.VMEM(shape, jnp.float32), pltpu.VMEM(shape, jnp.float32), pltpu.SemaphoreType.DMA]
         piece = (owners // ROUNDS, PARTS * shape[1], dim)
         out_specs = [
             pl.BlockSpec(block, lambda i, place: (jnp.minimum(i, half - 1), 0, 0)),
@@ -419,7 +432,7 @@
             num_scalar_prefetch=1, grid=(steps,), in_specs=in_specs, out_specs=out_specs, scratch_shapes=scratch
         ),
         out_shape=out_shape,
-        compiler_params=pltpu.CompilerParams(vmem_limit_bytes=VMEM),
+        compiler_params=pltpu.CompilerParams(vmem_limit_bytes=56 << 20),
         cost_estimate=pl.CostEstimate(
             flops=6 * rows * width * keys, bytes_accessed=4 << 20, transcendentals=rows * keys
         ),

time: 156 us -> 158 us (1.013)
  Pallas kernels: 54.7 us -> 60.9 us
  local copies, waits for them, and re-layouts: 8.29 us -> 4.59 us
    pallas_call x2, Pallas kernels: 14.4 us -> 20.6 us  [backward(): pl.pallas_call(functools.partial(back_kernel, last), grid_spec=pltpu.Pref...]
    unnamed x34 -> x32, local copies, waits for them, and re-layouts: 7.38 us -> 2.87 us
  transfers between devices with their start and end apart: 18 -> 18, of which waited for: 12 -> 11; matrix products, arithmetic and copies ran while one was open for 2% -> 3% of each run, Pallas kernels for 13% -> 15%
where the time goes in v10:
time: 158 us; the launch traced here: 157 us
  Pallas kernels  60.9 us (39%)
  waiting for transfers between devices  45 us (28%)
  starting transfers between devices  41.7 us (26%)
  local copies, waits for them, and re-layouts  4.59 us (3%)
  other arithmetic  4.37 us (3%)
    all_to_all x4, starting transfers between devices, exchanged(): return lax.all_to_all(x, axis, 0, 0, axis_index_groups=groups, tiled=True)  23 us
    pallas_call x2, Pallas kernels, backward(): pl.pallas_call(functools.partial(back_kernel, last), grid_spec=pltpu.Pref...  20.6 us
    pallas_call x1, Pallas kernels, main_forward(): pl.pallas_call(main_kernel, grid_spec=pltpu.PrefetchScalarGridSpec(num_sc...  18.6 us
    all_to_all x4, waiting for transfers between devices, exchanged(): return lax.all_to_all(x, axis, 0, 0, axis_index_groups=groups, tiled=True)  15.8 us
    ppermute x5, waiting for transfers between devices, flipped(): lax.ppermute(x, axis, [(i, i ^ mask) for i in range(lax.axis_size(axis))])  14.3 us
    pallas_call x2, Pallas kernels, weighted_sum(): pl.pallas_call(functools.partial(sum_kernel, first), grid_spec=pltpu.Pref...  13.4 us
    ppermute x6, waiting for transfers between devices, turned(): lax.ppermute(x, 'head', [(i, i // ROUNDS * ROUNDS + (i + k) % ROUNDS) for...  13 us
    ppermute x6, starting transfers between devices, turned(): lax.ppermute(x, 'head', [(i, i // ROUNDS * ROUNDS + (i + k) % ROUNDS) for...  9.01 us
  transfers between devices with their start and end apart: 18, of which 11 were waited for; matrix products, arithmetic and copies ran while one was open for 3% of the time, Pallas kernels for 15%

profile of v10, /device:TPU:1, one launch (start us, length us, event | category | flops | bytes accessed | tf_op | source)
XLA Modules:
  0.0 157.4 jit_solution(15583458824638839493)
XLA Ops:
  0.7 18.6 %main_forward.1 = (bf16[2,16,1024,256]{3,2,1,0:T(8,128)(2,1)}, bf16[2,512,256]{2,1,0:T(8,128)(2,1)}, f32[128,256]{1,0:T(8,128)}, f32[16,16,512]{2,1,0:T(8,128)}) custom-call(s32[1]{0:T(128)} %bitcast.3.base_ref, bf16[576,1024]{1,0:T(8,128)(2,1)} %bitcast.28, bf16[16,576,512]{2,1,0:T(8,128)(2,1)} %bitcast.21, bf16[16,576,512]{2,1,0:T(8,128)(2,1)} %bitcast.22, ...), custom_call_target="tpu_custom_call" | custom-call | flops 9663676416 | bytes 27262976 | tf_op jit(solution)/shard_map/main_forward/pallas_call | solution.py:142
  19.3 8.6 %all-to-all-start = ((f32[16,16,512]{2,1,0:T(8,128)}), f32[16,16,512]{2,1,0:T(8,128)S(1)}, u32[]{:S(2)}, u32[]{:S(2)}) async-start(f32[16,16,512]{2,1,0:T(8,128)} %get-tuple-element.24), calls=%async_computation | async-start | bytes 1048576 | tf_op jit(solution)/shard_map/all_to_all | solution.py:507
  27.9 0.6 convert_reduce_fusion
  28.5 10.6 %all-to-all-done.stats_ref = f32[16,16,512]{2,1,0:T(8,128)S(1)} async-done(((f32[16,16,512]{2,1,0:T(8,128)}), f32[16,16,512]{2,1,0:T(8,128)S(1)}, u32[]{:S(2)}, u32[]{:S(2)}) %all-to-all-start) | async-done | bytes 524320 | tf_op jit(solution)/shard_map/all_to_all | solution.py:507
  39.1 0.9 copy-done.1
  40.0 6.7 %shard_map.104 = f32[8,64,512]{2,1,0:T(8,128)} custom-call(s32[1]{0:T(128)} %bitcast.5.info_ref, bf16[2,16,1024,256]{3,2,1,0:T(8,128)(2,1)} %get-tuple-element.21.e_ref, bf16[2,512,256]{2,1,0:T(8,128)(2,1)S(1)} %copy-done, f32[128,256]{1,0:T(8,128)S(1)} %copy-done.1, f32[16,16,512]{2,1,0:T(8,128)S(1)} %all-to-all-done.stats_ref), custom_call_target="tpu_custom_call" | custom-call | flops 8388608 | bytes 9437184 | tf_op jit(solution)/shard_map/pallas_call | solution.py:277
  46.7 5.3 %all-to-all-start.2 = ((f32[8,64,512]{2,1,0:T(8,128)}), f32[8,64,512]{2,1,0:T(8,128)S(1)}, u32[]{:S(2)}, u32[]{:S(2)}) async-start(f32[8,64,512]{2,1,0:T(8,128)} %shard_map.104), calls=%async_computation.2 | async-start | bytes 2097152 | tf_op jit(solution)/shard_map/all_to_all | solution.py:507
  52.0 0.8 copy.12
  52.8 0.7 dynamic-slice_bitcast_fusion
  53.5 5.6 %index_forward.1 = (f32[64,1024]{1,0:T(8,128)}, f32[1,64]{1,0:T(1,128)}) custom-call(s32[1]{0:T(128)} %bitcast.3.base_ref, bf16[64,8192]{1,0:T(8,128)(2,1)} %q_hbm.3, bf16[128,1024]{1,0:T(8,128)(2,1)} %bitcast.29, f32[64,64]{1,0:T(8,128)} %w_ref.1, s32[1,64]{1,0:T(1,128)} %get-tuple-element.40.start_ref, s32[1,64]{1,0:T(1,128)} %get-tuple-element.39.pos_ref), custom_call_target="tpu_custom_call" | custom-call | flops 1073741824 | bytes 2097152 | tf_op jit(solution)/shard_map/index_forward/pallas_call | solution.py:210
  59.1 1.5 collective-permute-start
  60.6 6.7 %shard_map.103 = f32[8,64,512]{2,1,0:T(8,128)} custom-call(s32[1]{0:T(128)} %bitcast.5.info_ref, bf16[2,16,1024,256]{3,2,1,0:T(8,128)(2,1)} %get-tuple-element.21.e_ref, bf16[2,512,256]{2,1,0:T(8,128)(2,1)S(1)} %copy-done, f32[128,256]{1,0:T(8,128)S(1)} %copy-done.2, f32[16,16,512]{2,1,0:T(8,128)S(1)} %all-to-all-done.stats_ref), custom_call_target="tpu_custom_call" | custom-call | flops 8388608 | bytes 9437184 | tf_op jit(solution)/shard_map/pallas_call | solution.py:277
  67.4 5.4 %all-to-all-start.1 = ((f32[8,64,512]{2,1,0:T(8,128)}), f32[8,64,512]{2,1,0:T(8,128)S(1)}, u32[]{:S(2)}, u32[]{:S(2)}) async-start(f32[8,64,512]{2,1,0:T(8,128)} %shard_map.103), calls=%async_computation.1 | async-start | bytes 2097152 | tf_op jit(solution)/shard_map/all_to_all | solution.py:507
  72.8 0.7 collective-permute-start.1
  73.5 0.6 pad_add_fusion.place_ref
  74.1 11.6 %collective-permute-done.1 = f32[1,64]{1,0:T(1,128)S(1)} collective-permute-done((f32[1,64]{1,0:T(1,128)S(1)}, f32[1,64]{1,0:T(1,128)S(1)}, u32[]{:S(2)}, u32[]{:S(2)}) %collective-permute-start.1) | collective-permute-done | bytes 288 | tf_op jit(solution)/shard_map/ppermute | solution.py:511
  85.7 0.6 collective-permute-start.4
  86.3 0.9 collective-permute-start.3
  87.2 0.6 collective-permute-start.2
  87.8 0.1 copy.13
  87.9 1.1 copy.14
  88.9 1.3 collective-permute-done.3
  90.2 0.6 collective-permute-done.2
  90.8 0.5 multiply_add_fusion.stats_ref
  91.4 9.9 %shard_map.105 = (f32[16,72,512]{2,1,0:T(8,128)}, f32[8,64,128]{2,1,0:T(8,128)}) custom-call(s32[3]{0:T(128)} %pad_add_fusion.place_ref, f32[8,64,512]{2,1,0:T(8,128)} %copy-done.5, f32[64,1024]{1,0:T(8,128)} %get-tuple-element.25.s_ref, f32[1,64]{1,0:T(1,128)} %multiply_add_fusion.stats_ref, f32[1,64]{1,0:T(1,128)} %bitcast.36, bf16[64,8192]{1,0:T(8,128)(2,1)} %q_hbm.3, ...), custom_call_target="tpu_custom_call" | custom-call | flops 1610612736 | bytes 4194304 | tf_op jit(solution)/shard_map/pallas_call | solution.py:429
  101.3 1.0 copy-done.4
  102.3 10.7 %shard_map.106 = (f32[8,72,512]{2,1,0:T(8,128)}, f32[8,72,512]{2,1,0:T(8,128)}, f32[2,128,128]{2,1,0:T(8,128)}, f32[2,128,128]{2,1,0:T(8,128)}, f32[2,128,128]{2,1,0:T(8,128)}, /*index=5*/f32[2,128,128]{2,1,0:T(8,128)}) custom-call(s32[3]{0:T(128)} %pad_add_fusion.place_ref, f32[8,64,512]{2,1,0:T(8,128)} %copy-done.4, f32[64,1024]{1,0:T(8,128)} %get-tuple-element.25.s_ref, ...), custom_call_target="tpu_custom_call" | custom-call | flops 1610612736 | bytes 4194304 | tf_op jit(solution)/shard_map/pallas_call | solution.py:429
  113.0 2.4 %collective-permute-start.5 = (f32[8,72,512]{2,1,0:T(8,128)}, f32[8,72,512]{2,1,0:T(8,128)S(1)}, u32[]{:S(2)}, u32[]{:S(2)}) collective-permute-start(f32[8,72,512]{2,1,0:T(8,128)} %get-tuple-element.30), channel_id=1, source_target_pairs={{0,1},{1,0},{2,3},{3,2},{4,5},{5,4},{6,7},{7,6},{8,9},{9,8},{10,11... | collective-permute-start | bytes 3538952 | tf_op jit(solution)/shard_map/ppermute | solution.py:511
  115.4 2.7 %collective-permute-done.5 = f32[8,72,512]{2,1,0:T(8,128)S(1)} collective-permute-done((f32[8,72,512]{2,1,0:T(8,128)}, f32[8,72,512]{2,1,0:T(8,128)S(1)}, u32[]{:S(2)}, u32[]{:S(2)}) %collective-permute-start.5) | collective-permute-done | bytes 1179680 | tf_op jit(solution)/shard_map/ppermute | solution.py:511
  118.0 2.5 %add.66 = f32[8,72,512]{2,1,0:T(8,128)} add(f32[8,72,512]{2,1,0:T(8,128)} %get-tuple-element.29, f32[8,72,512]{2,1,0:T(8,128)S(1)} %collective-permute-done.5) | non-fusion elementwise | flops 294912 | bytes 3538944 | tf_op jit(solution)/shard_map/add | solution.py:559
  120.6 3.7 %all-to-all-start.3 = ((f32[4,2,72,512]{3,2,1,0:T(8,128)}), f32[4,2,72,512]{3,2,1,0:T(8,128)S(1)}, u32[]{:S(2)}, u32[]{:S(2)}) async-start(f32[4,2,72,512]{3,2,1,0:T(8,128)} %bitcast.16), calls=%async_computation.3 | async-start | bytes 2359296 | tf_op jit(solution)/shard_map/all_to_all | solution.py:507
  124.3 1.5 collective-permute-start.7
  125.8 2.7 %collective-permute-start.8 = (f32[2,128,128]{2,1,0:T(8,128)S(1)}, f32[2,128,128]{2,1,0:T(8,128)S(1)}, u32[]{:S(2)}, u32[]{:S(2)}) collective-permute-start(f32[2,128,128]{2,1,0:T(8,128)S(1)} %copy-done.12), channel_id=1, source_target_pairs={{0,32},{16,48},{32,0},{48,16},{64,96},{80,112},{96,64},{112,80},{1... | collective-permute-start | bytes 393224 | tf_op jit(solution)/shard_map/ppermute | solution.py:521
  128.5 0.9 collective-permute-start.9
  129.4 1.4 collective-permute-done.7
  130.8 3.7 %collective-permute-done.8 = f32[2,128,128]{2,1,0:T(8,128)S(1)} collective-permute-done((f32[2,128,128]{2,1,0:T(8,128)S(1)}, f32[2,128,128]{2,1,0:T(8,128)S(1)}, u32[]{:S(2)}, u32[]{:S(2)}) %collective-permute-start.8) | collective-permute-done | bytes 131104 | tf_op jit(solution)/shard_map/ppermute | solution.py:521
  134.6 0.7 collective-permute-start.10
  135.2 5.2 %all-to-all-done.3.x_ref = f32[4,2,72,512]{3,2,1,0:T(8,128)S(1)} async-done(((f32[4,2,72,512]{3,2,1,0:T(8,128)}), f32[4,2,72,512]{3,2,1,0:T(8,128)S(1)}, u32[]{:S(2)}, u32[]{:S(2)}) %all-to-all-start.3) | async-done | bytes 1179680 | tf_op jit(solution)/shard_map/all_to_all | solution.py:507
  140.5 0.6 halves.1
  141.1 2.4 %collective-permute-start.6 = (f32[72,512]{1,0:T(8,128)S(1)}, f32[72,512]{1,0:T(8,128)S(1)}, u32[]{:S(2)}, u32[]{:S(2)}) collective-permute-start(f32[72,512]{1,0:T(8,128)S(1)} %get-tuple-element.32), channel_id=1, source_target_pairs={{0,2},{1,3},{2,0},{3,1},{4,6},{5,7},{6,4},{7,5},{8,10},{9,11},{10,... | collective-permute-start | bytes 442376 | tf_op jit(solution)/shard_map/ppermute | solution.py:511
  143.5 3.0 %collective-permute-start.13 = (f32[2,128,128]{2,1,0:T(8,128)S(1)}, f32[2,128,128]{2,1,0:T(8,128)S(1)}, u32[]{:S(2)}, u32[]{:S(2)}) collective-permute-start(f32[2,128,128]{2,1,0:T(8,128)S(1)} %add.70.refs_0_), channel_id=1, source_target_pairs={{0,48},{16,0},{32,16},{48,32},{64,112},{80,64},{96,80},{112,96},{1... | collective-permute-start | bytes 393224 | tf_op jit(solution)/shard_map/ppermute | solution.py:521
  146.6 0.2 collective-permute-start.12
  146.8 0.6 collective-permute-start.11
  147.4 1.7 %collective-permute-done.13.refs_3_ = f32[2,128,128]{2,1,0:T(8,128)S(1)} collective-permute-done((f32[2,128,128]{2,1,0:T(8,128)S(1)}, f32[2,128,128]{2,1,0:T(8,128)S(1)}, u32[]{:S(2)}, u32[]{:S(2)}) %collective-permute-start.13) | collective-permute-done | bytes 131104 | tf_op jit(solution)/shard_map/ppermute | solution.py:521
  149.2 2.8 %collective-permute-done.12.refs_2_ = f32[2,128,128]{2,1,0:T(8,128)S(1)} collective-permute-done((f32[2,128,128]{2,1,0:T(8,128)S(1)}, f32[2,128,128]{2,1,0:T(8,128)S(1)}, u32[]{:S(2)}, u32[]{:S(2)}) %collective-permute-start.12) | collective-permute-done | bytes 131104 | tf_op jit(solution)/shard_map/ppermute | solution.py:521
  152.0 3.3 %collective-permute-done.11.refs_1_ = f32[2,128,128]{2,1,0:T(8,128)S(1)} collective-permute-done((f32[2,128,128]{2,1,0:T(8,128)S(1)}, f32[2,128,128]{2,1,0:T(8,128)S(1)}, u32[]{:S(2)}, u32[]{:S(2)}) %collective-permute-start.11) | collective-permute-done | bytes 131104 | tf_op jit(solution)/shard_map/ppermute | solution.py:521
  155.3 1.4 join.1
  156.7 0.7 end.1
  (39 shorter events, 0.1 us)
Async XLA Ops:
  0.6 27.2 %copy-start.9 = (s32[512]{0:T(512)S(1)}, s32[512]{0:T(512)}, u32[]{:S(2)}) copy-start(s32[512]{0:T(512)} %param.14) | copy-start | bytes 6148
  0.6 27.2 %copy-start.10 = (s32[512]{0:T(512)S(1)}, s32[512]{0:T(512)}, u32[]{:S(2)}) copy-start(s32[512]{0:T(512)} %param.15) | copy-start | bytes 6148
  19.3 19.8 %copy-start = (bf16[2,512,256]{2,1,0:T(8,128)(2,1)S(1)}, bf16[2,512,256]{2,1,0:T(8,128)(2,1)}, u32[]{:S(2)}) copy-start(bf16[2,512,256]{2,1,0:T(8,128)(2,1)} %get-tuple-element.22.sel_ref) | copy-start | bytes 1572868
  19.3 19.8 %all-to-all-start = ((f32[16,16,512]{2,1,0:T(8,128)}), f32[16,16,512]{2,1,0:T(8,128)S(1)}, u32[]{:S(2)}, u32[]{:S(2)}) async-start(f32[16,16,512]{2,1,0:T(8,128)} %get-tuple-element.24), calls=%async_computation | async-start | bytes 1048576 | tf_op jit(solution)/shard_map/all_to_all | solution.py:507
  39.1 0.9 copy-start.1
  46.7 5.3 %copy-start.6 = (bf16[1024,128]{1,0:T(8,128)(2,1)S(1)}, bf16[1024,128]{1,0:T(8,128)(2,1)}, u32[]{:S(2)}) copy-start(bf16[1024,128]{1,0:T(8,128)(2,1)} %k_ref.3) | copy-start | bytes 786436
  46.7 20.6 %all-to-all-start.2 = ((f32[8,64,512]{2,1,0:T(8,128)}), f32[8,64,512]{2,1,0:T(8,128)S(1)}, u32[]{:S(2)}, u32[]{:S(2)}) async-start(f32[8,64,512]{2,1,0:T(8,128)} %shard_map.104), calls=%async_computation.2 | async-start | bytes 2097152 | tf_op jit(solution)/shard_map/all_to_all | solution.py:507
  53.5 7.1 %copy-start.2 = (f32[128,256]{1,0:T(8,128)S(1)}, f32[128,256]{1,0:T(8,128)}, u32[]{:S(2)}) copy-start(f32[128,256]{1,0:T(8,128)} %get-tuple-element.23.m_ref) | copy-start | bytes 393220
  59.1 13.7 %collective-permute-start = (f32[1,64]{1,0:T(1,128)}, f32[1,64]{1,0:T(1,128)S(1)}, u32[]{:S(2)}, u32[]{:S(2)}) collective-permute-start(f32[1,64]{1,0:T(1,128)} %get-tuple-element.26), channel_id=1, source_target_pairs={{0,1},{1,0},{2,3},{3,2},{4,5},{5,4},{6,7},{7,6},{8,9},{9,8},{10,11... | collective-permute-start | bytes 776 | tf_op jit(solution)/shard_map/ppermute | solution.py:511
  67.3 5.5 %copy-start.14 = (f32[1,64]{1,0:T(1,128)S(1)}, f32[1,64]{1,0:T(1,128)}, u32[]{:S(2)}) copy-start(f32[1,64]{1,0:T(1,128)} %get-tuple-element.26) | copy-start | bytes 772
  67.3 20.5 %copy-start.8 = (f32[64,64]{1,0:T(8,128)S(1)}, f32[64,64]{1,0:T(8,128)}, u32[]{:S(2)}) copy-start(f32[64,64]{1,0:T(8,128)} %w_ref.1) | copy-start | bytes 49156
  67.4 21.6 %copy-start.5 = (f32[8,64,512]{2,1,0:T(8,128)}, f32[8,64,512]{2,1,0:T(8,128)S(1)}, u32[]{:S(2)}) copy-start(f32[8,64,512]{2,1,0:T(8,128)S(1)} %all-to-all-done.2.t_ref) | copy-start | bytes 3145732
  67.4 33.9 %all-to-all-start.1 = ((f32[8,64,512]{2,1,0:T(8,128)}), f32[8,64,512]{2,1,0:T(8,128)S(1)}, u32[]{:S(2)}, u32[]{:S(2)}) async-start(f32[8,64,512]{2,1,0:T(8,128)} %shard_map.103), calls=%async_computation.1 | async-start | bytes 2097152 | tf_op jit(solution)/shard_map/all_to_all | solution.py:507
  72.8 12.9 %collective-permute-start.1 = (f32[1,64]{1,0:T(1,128)S(1)}, f32[1,64]{1,0:T(1,128)S(1)}, u32[]{:S(2)}, u32[]{:S(2)}) collective-permute-start(f32[1,64]{1,0:T(1,128)S(1)} %multiply_add_fusion.2), channel_id=1, source_target_pairs={{0,2},{1,3},{2,0},{3,1},{4,6},{5,7},{6,4},{7,5},{8,10},{9,11},{10,... | collective-permute-start | bytes 776 | tf_op jit(solution)/shard_map/ppermute | solution.py:511
  85.7 3.2 %collective-permute-start.4 = (f32[1,64]{1,0:T(1,128)S(1)}, f32[1,64]{1,0:T(1,128)S(1)}, u32[]{:S(2)}, u32[]{:S(2)}) collective-permute-start(f32[1,64]{1,0:T(1,128)S(1)} %multiply_add_fusion.1), channel_id=1, source_target_pairs={{0,12},{1,13},{2,14},{3,15},{4,0},{5,1},{6,2},{7,3},{8,4},{9,5},{1... | collective-permute-start | bytes 776 | tf_op jit(solution)/shard_map/ppermute | solution.py:543
  86.3 3.9 %collective-permute-start.3 = (f32[1,64]{1,0:T(1,128)S(1)}, f32[1,64]{1,0:T(1,128)S(1)}, u32[]{:S(2)}, u32[]{:S(2)}) collective-permute-start(f32[1,64]{1,0:T(1,128)S(1)} %multiply_add_fusion.1), channel_id=1, source_target_pairs={{0,8},{1,9},{2,10},{3,11},{4,12},{5,13},{6,14},{7,15},{8,0},{9,1},... | collective-permute-start | bytes 776 | tf_op jit(solution)/shard_map/ppermute | solution.py:543
  87.2 3.6 %collective-permute-start.2 = (f32[1,64]{1,0:T(1,128)S(1)}, f32[1,64]{1,0:T(1,128)S(1)}, u32[]{:S(2)}, u32[]{:S(2)}) collective-permute-start(f32[1,64]{1,0:T(1,128)S(1)} %multiply_add_fusion.1), channel_id=1, source_target_pairs={{0,4},{1,5},{2,6},{3,7},{4,8},{5,9},{6,10},{7,11},{8,12},{9,13},{1... | collective-permute-start | bytes 776 | tf_op jit(solution)/shard_map/ppermute | solution.py:543
  101.3 1.0 copy-start.4
  113.0 5.1 %collective-permute-start.5 = (f32[8,72,512]{2,1,0:T(8,128)}, f32[8,72,512]{2,1,0:T(8,128)S(1)}, u32[]{:S(2)}, u32[]{:S(2)}) collective-permute-start(f32[8,72,512]{2,1,0:T(8,128)} %get-tuple-element.30), channel_id=1, source_target_pairs={{0,1},{1,0},{2,3},{3,2},{4,5},{5,4},{6,7},{7,6},{8,9},{9,8},{10,11... | collective-permute-start | bytes 3538952 | tf_op jit(solution)/shard_map/ppermute | solution.py:511
  120.6 3.7 %copy-start.13 = (f32[2,128,128]{2,1,0:T(8,128)S(1)}, f32[2,128,128]{2,1,0:T(8,128)}, u32[]{:S(2)}) copy-start(f32[2,128,128]{2,1,0:T(8,128)} %get-tuple-element.35) | copy-start | bytes 393220
  120.6 5.2 %copy-start.12 = (f32[2,128,128]{2,1,0:T(8,128)S(1)}, f32[2,128,128]{2,1,0:T(8,128)}, u32[]{:S(2)}) copy-start(f32[2,128,128]{2,1,0:T(8,128)} %get-tuple-element.36) | copy-start | bytes 393220
  120.6 7.9 %copy-start.11 = (f32[2,128,128]{2,1,0:T(8,128)S(1)}, f32[2,128,128]{2,1,0:T(8,128)}, u32[]{:S(2)}) copy-start(f32[2,128,128]{2,1,0:T(8,128)} %get-tuple-element.37) | copy-start | bytes 393220
  120.6 13.9 %copy-start.7 = (f32[2,128,128]{2,1,0:T(8,128)S(1)}, f32[2,128,128]{2,1,0:T(8,128)}, u32[]{:S(2)}) copy-start(f32[2,128,128]{2,1,0:T(8,128)} %get-tuple-element.34) | copy-start | bytes 393220
  120.6 19.9 %copy-start.3 = (s32[3]{0:T(128)S(1)}, s32[3]{0:T(128)}, u32[]{:S(2)}) copy-start(s32[3]{0:T(128)} %pad_add_fusion.place_ref) | copy-start | bytes 40
  120.6 19.9 %all-to-all-start.3 = ((f32[4,2,72,512]{3,2,1,0:T(8,128)}), f32[4,2,72,512]{3,2,1,0:T(8,128)S(1)}, u32[]{:S(2)}, u32[]{:S(2)}) async-start(f32[4,2,72,512]{3,2,1,0:T(8,128)} %bitcast.16), calls=%async_computation.3 | async-start | bytes 2359296 | tf_op jit(solution)/shard_map/all_to_all | solution.py:507
  124.3 6.5 %collective-permute-start.7 = (f32[2,128,128]{2,1,0:T(8,128)S(1)}, f32[2,128,128]{2,1,0:T(8,128)S(1)}, u32[]{:S(2)}, u32[]{:S(2)}) collective-permute-start(f32[2,128,128]{2,1,0:T(8,128)S(1)} %copy-done.13), channel_id=1, source_target_pairs={{0,16},{16,32},{32,48},{48,0},{64,80},{80,96},{96,112},{112,64},{1... | collective-permute-start | bytes 393224 | tf_op jit(solution)/shard_map/ppermute | solution.py:521
  125.8 8.7 %collective-permute-start.8 = (f32[2,128,128]{2,1,0:T(8,128)S(1)}, f32[2,128,128]{2,1,0:T(8,128)S(1)}, u32[]{:S(2)}, u32[]{:S(2)}) collective-permute-start(f32[2,128,128]{2,1,0:T(8,128)S(1)} %copy-done.12), channel_id=1, source_target_pairs={{0,32},{16,48},{32,0},{48,16},{64,96},{80,112},{96,64},{112,80},{1... | collective-permute-start | bytes 393224 | tf_op jit(solution)/shard_map/ppermute | solution.py:521
  128.5 6.0 %collective-permute-start.9 = (f32[2,128,128]{2,1,0:T(8,128)S(1)}, f32[2,128,128]{2,1,0:T(8,128)S(1)}, u32[]{:S(2)}, u32[]{:S(2)}) collective-permute-start(f32[2,128,128]{2,1,0:T(8,128)S(1)} %copy-done.11), channel_id=1, source_target_pairs={{0,48},{16,0},{32,16},{48,32},{64,112},{80,64},{96,80},{112,96},{1... | collective-permute-start | bytes 393224 | tf_op jit(solution)/shard_map/ppermute | solution.py:521
  134.6 8.9 %collective-permute-start.10 = (f32[2,128,128]{2,1,0:T(8,128)S(1)}, f32[2,128,128]{2,1,0:T(8,128)S(1)}, u32[]{:S(2)}, u32[]{:S(2)}) collective-permute-start(f32[2,128,128]{2,1,0:T(8,128)S(1)} %add_add_fusion), channel_id=1, source_target_pairs={{0,64},{16,80},{32,96},{48,112},{64,0},{80,16},{96,32},{112,48},{1... | collective-permute-start | bytes 393224 | tf_op jit(solution)/shard_map/ppermute | solution.py:511
  141.1 15.6 %collective-permute-start.6 = (f32[72,512]{1,0:T(8,128)S(1)}, f32[72,512]{1,0:T(8,128)S(1)}, u32[]{:S(2)}, u32[]{:S(2)}) collective-permute-start(f32[72,512]{1,0:T(8,128)S(1)} %get-tuple-element.32), channel_id=1, source_target_pairs={{0,2},{1,3},{2,0},{3,1},{4,6},{5,7},{6,4},{7,5},{8,10},{9,11},{10,... | collective-permute-start | bytes 442376 | tf_op jit(solution)/shard_map/ppermute | solution.py:511
  143.5 5.6 %collective-permute-start.13 = (f32[2,128,128]{2,1,0:T(8,128)S(1)}, f32[2,128,128]{2,1,0:T(8,128)S(1)}, u32[]{:S(2)}, u32[]{:S(2)}) collective-permute-start(f32[2,128,128]{2,1,0:T(8,128)S(1)} %add.70.refs_0_), channel_id=1, source_target_pairs={{0,48},{16,0},{32,16},{48,32},{64,112},{80,64},{96,80},{112,96},{1... | collective-permute-start | bytes 393224 | tf_op jit(solution)/shard_map/ppermute | solution.py:521
  146.6 5.4 %collective-permute-start.12 = (f32[2,128,128]{2,1,0:T(8,128)S(1)}, f32[2,128,128]{2,1,0:T(8,128)S(1)}, u32[]{:S(2)}, u32[]{:S(2)}) collective-permute-start(f32[2,128,128]{2,1,0:T(8,128)S(1)} %add.70.refs_0_), channel_id=1, source_target_pairs={{0,32},{16,48},{32,0},{48,16},{64,96},{80,112},{96,64},{112,80},{1... | collective-permute-start | bytes 393224 | tf_op jit(solution)/shard_map/ppermute | solution.py:521
  146.8 8.5 %collective-permute-start.11 = (f32[2,128,128]{2,1,0:T(8,128)S(1)}, f32[2,128,128]{2,1,0:T(8,128)S(1)}, u32[]{:S(2)}, u32[]{:S(2)}) collective-permute-start(f32[2,128,128]{2,1,0:T(8,128)S(1)} %add.70.refs_0_), channel_id=1, source_target_pairs={{0,16},{16,32},{32,48},{48,0},{64,80},{80,96},{96,112},{112,64},{1... | collective-permute-start | bytes 393224 | tf_op jit(solution)/shard_map/ppermute | solution.py:521

commit v11 on v9

--- a/solution.py
+++ b/solution.py
@@ -15,10 +15,11 @@
 LOW = -1e30
 FLOOR = -1e29
 CHUNK = 256
+STRIP = 512
 TILE = 256
 RUN = 4
 GROUP = 4
-PAIR = 4
+PAIR = 8
 PARTS = 2
 ROUNDS = 4
 VMEM = 48 << 20
@@ -179,7 +180,7 @@
 
 def index_kernel(base_ref, q_ref, kt_ref, w_ref, start_ref, pos_ref, s_ref, lse_ref):
     c = pl.program_id(0)
-    rows, width = s_ref.shape[0], CHUNK
+    rows, width = s_ref.shape[0], STRIP
     heads = w_ref.shape[1]
     dim = kt_ref.shape[0]
     here = pl.ds(pl.multiple_of(c * width, width), width)
@@ -208,7 +209,7 @@
     whole = lambda *shape: pl.BlockSpec(shape, lambda c: (0,) * len(shape))
     return pl.pallas_call(
         index_kernel,
-        grid=(keys // CHUNK,),
+        grid=(keys // STRIP,),
         in_specs=[
             pl.BlockSpec(memory_space=pltpu.SMEM),
             whole(rows, width),

time: 156 us -> 155 us (level)
  transfers between devices with their start and end apart: 18 -> 18, of which waited for: 12 -> 11; matrix products, arithmetic and copies ran while one was open for 2% -> 2% of each run, Pallas kernels for 13% -> 12%
where the time goes in v11:
time: 155 us; the launch traced here: 154 us
  Pallas kernels  53.3 us (34%)
  waiting for transfers between devices  45.9 us (30%)
  starting transfers between devices  42 us (27%)
  local copies, waits for them, and re-layouts  8.29 us (5%)
  other arithmetic  3.35 us (2%)
    all_to_all x4, starting transfers between devices, exchanged(): return lax.all_to_all(x, axis, 0, 0, axis_index_groups=groups, tiled=True)  23 us
    pallas_call x1, Pallas kernels, main_forward(): pl.pallas_call(main_kernel, grid_spec=pltpu.PrefetchScalarGridSpec(num_sc...  18.6 us
    all_to_all x4, waiting for transfers between devices, exchanged(): return lax.all_to_all(x, axis, 0, 0, axis_index_groups=groups, tiled=True)  15.9 us
    ppermute x5, waiting for transfers between devices, flipped(): lax.ppermute(x, axis, [(i, i ^ mask) for i in range(lax.axis_size(axis))])  14.6 us
    pallas_call x2, Pallas kernels, backward(): pl.pallas_call(functools.partial(back_kernel, last), grid_spec=pltpu.Pref...  13.8 us
    pallas_call x2, Pallas kernels, weighted_sum(): pl.pallas_call(functools.partial(sum_kernel, first), grid_spec=pltpu.Pref...  13.4 us
    ppermute x6, waiting for transfers between devices, turned(): lax.ppermute(x, 'head', [(i, i // ROUNDS * ROUNDS + (i + k) % ROUNDS) for...  12.9 us
    ppermute x6, starting transfers between devices, turned(): lax.ppermute(x, 'head', [(i, i // ROUNDS * ROUNDS + (i + k) % ROUNDS) for...  9.02 us
  transfers between devices with their start and end apart: 18, of which 11 were waited for; matrix products, arithmetic and copies ran while one was open for 2% of the time, Pallas kernels for 12%

profile of v11, /device:TPU:1, one launch (start us, length us, event | category | flops | bytes accessed | tf_op | source)
XLA Modules:
  0.0 153.7 jit_solution(11137648769174204783)
XLA Ops:
  0.7 18.6 %main_forward.1 = (bf16[2,16,1024,256]{3,2,1,0:T(8,128)(2,1)}, bf16[2,512,256]{2,1,0:T(8,128)(2,1)}, f32[128,256]{1,0:T(8,128)}, f32[16,16,512]{2,1,0:T(8,128)}) custom-call(s32[1]{0:T(128)} %bitcast.3.base_ref, bf16[576,1024]{1,0:T(8,128)(2,1)} %bitcast.33, bf16[16,576,512]{2,1,0:T(8,128)(2,1)} %bitcast.28, bf16[16,576,512]{2,1,0:T(8,128)(2,1)} %bitcast.29, ...), custom_call_target="tpu_custom_call" | custom-call | flops 9663676416 | bytes 27262976 | tf_op jit(solution)/shard_map/main_forward/pallas_call | solution.py:142
  19.3 8.6 %all-to-all-start = ((f32[16,16,512]{2,1,0:T(8,128)}), f32[16,16,512]{2,1,0:T(8,128)S(1)}, u32[]{:S(2)}, u32[]{:S(2)}) async-start(f32[16,16,512]{2,1,0:T(8,128)} %get-tuple-element.24), calls=%async_computation | async-start | bytes 1048576 | tf_op jit(solution)/shard_map/all_to_all | solution.py:495
  27.9 0.6 convert_reduce_fusion
  28.5 10.6 %all-to-all-done.stats_ref = f32[16,16,512]{2,1,0:T(8,128)S(1)} async-done(((f32[16,16,512]{2,1,0:T(8,128)}), f32[16,16,512]{2,1,0:T(8,128)S(1)}, u32[]{:S(2)}, u32[]{:S(2)}) %all-to-all-start) | async-done | bytes 524320 | tf_op jit(solution)/shard_map/all_to_all | solution.py:495
  39.1 0.9 copy-done.6
  40.0 6.7 %shard_map.104 = f32[8,64,512]{2,1,0:T(8,128)} custom-call(s32[1]{0:T(128)} %bitcast.5.info_ref, bf16[2,16,1024,256]{3,2,1,0:T(8,128)(2,1)} %get-tuple-element.21.e_ref, bf16[2,512,256]{2,1,0:T(8,128)(2,1)S(1)} %copy-done.1, f32[128,256]{1,0:T(8,128)S(1)} %copy-done.6, f32[16,16,512]{2,1,0:T(8,128)S(1)} %all-to-all-done.stats_ref), custom_call_target="tpu_custom_call" | custom-call | flops 8388608 | bytes 9437184 | tf_op jit(solution)/shard_map/pallas_call | solution.py:277
  46.7 5.3 %all-to-all-start.2 = ((f32[8,64,512]{2,1,0:T(8,128)}), f32[8,64,512]{2,1,0:T(8,128)S(1)}, u32[]{:S(2)}, u32[]{:S(2)}) async-start(f32[8,64,512]{2,1,0:T(8,128)} %shard_map.104), calls=%async_computation.2 | async-start | bytes 2097152 | tf_op jit(solution)/shard_map/all_to_all | solution.py:495
  52.0 0.8 copy.12
  52.8 0.7 dynamic-slice_bitcast_fusion
  53.5 4.9 %index_forward.1 = (f32[64,1024]{1,0:T(8,128)}, f32[1,64]{1,0:T(1,128)}) custom-call(s32[1]{0:T(128)} %bitcast.3.base_ref, bf16[64,8192]{1,0:T(8,128)(2,1)} %q_ref.5, bf16[128,1024]{1,0:T(8,128)(2,1)} %bitcast.23, f32[64,64]{1,0:T(8,128)} %w_ref.1, s32[1,64]{1,0:T(1,128)} %get-tuple-element.40.start_ref, s32[1,64]{1,0:T(1,128)} %get-tuple-element.39.pos_ref), custom_call_target="tpu_custom_call" | custom-call | flops 1073741824 | bytes 2097152 | tf_op jit(solution)/shard_map/index_forward/pallas_call | solution.py:210
  58.4 1.5 collective-permute-start
  59.9 6.7 %shard_map.103 = f32[8,64,512]{2,1,0:T(8,128)} custom-call(s32[1]{0:T(128)} %bitcast.5.info_ref, bf16[2,16,1024,256]{3,2,1,0:T(8,128)(2,1)} %get-tuple-element.21.e_ref, bf16[2,512,256]{2,1,0:T(8,128)(2,1)S(1)} %copy-done.1, f32[128,256]{1,0:T(8,128)S(1)} %copy-done.7, f32[16,16,512]{2,1,0:T(8,128)S(1)} %all-to-all-done.stats_ref), custom_call_target="tpu_custom_call" | custom-call | flops 8388608 | bytes 9437184 | tf_op jit(solution)/shard_map/pallas_call | solution.py:277
  66.6 5.6 %all-to-all-start.1 = ((f32[8,64,512]{2,1,0:T(8,128)}), f32[8,64,512]{2,1,0:T(8,128)S(1)}, u32[]{:S(2)}, u32[]{:S(2)}) async-start(f32[8,64,512]{2,1,0:T(8,128)} %shard_map.103), calls=%async_computation.1 | async-start | bytes 2097152 | tf_op jit(solution)/shard_map/all_to_all | solution.py:495
  72.2 0.7 collective-permute-start.1
  72.9 12.1 %collective-permute-done.1 = f32[1,64]{1,0:T(1,128)S(1)} collective-permute-done((f32[1,64]{1,0:T(1,128)S(1)}, f32[1,64]{1,0:T(1,128)S(1)}, u32[]{:S(2)}, u32[]{:S(2)}) %collective-permute-start.1) | collective-permute-done | bytes 288 | tf_op jit(solution)/shard_map/ppermute | solution.py:499
  85.0 0.8 collective-permute-start.4
  85.8 0.7 collective-permute-start.3
  86.6 0.8 collective-permute-start.2
  87.4 0.2 copy.14
  87.7 2.0 %collective-permute-done.3 = f32[1,64]{1,0:T(1,128)S(1)} collective-permute-done((f32[1,64]{1,0:T(1,128)S(1)}, f32[1,64]{1,0:T(1,128)S(1)}, u32[]{:S(2)}, u32[]{:S(2)}) %collective-permute-start.3) | collective-permute-done | bytes 288 | tf_op jit(solution)/shard_map/ppermute | solution.py:531
  89.8 0.4 collective-permute-done.2
  90.3 1.2 copy-done.2
  91.5 5.7 %shard_map.105 = (f32[16,72,512]{2,1,0:T(8,128)S(1)}, f32[8,64,128]{2,1,0:T(8,128)S(1)}) custom-call(s32[3]{0:T(128)S(1)} %pad_add_fusion.place_ref, f32[8,64,512]{2,1,0:T(8,128)S(1)} %all-to-all-done.2.t_ref, f32[64,1024]{1,0:T(8,128)S(1)} %copy-done.8, f32[1,64]{1,0:T(1,128)S(1)} %multiply_add_fusion.stats_ref, f32[1,64]{1,0:T(1,128)S(1)} %bitcast.26, ...), custom_call_target="tpu_custom_call" | custom-call | flops 1610612736 | bytes 4194304 | tf_op jit(solution)/shard_map/pallas_call | solution.py:417
  97.2 1.4 copy-done
  98.6 0.7 copy-done.9
  99.3 1.2 copy-done.3
  100.5 0.9 copy-done.10
  101.5 8.1 %shard_map.106 = (f32[8,72,512]{2,1,0:T(8,128)S(1)}, f32[8,72,512]{2,1,0:T(8,128)}, f32[2,128,128]{2,1,0:T(8,128)S(1)}, f32[2,128,128]{2,1,0:T(8,128)S(1)}, f32[...) custom-call(s32[3]{0:T(128)S(1)} %pad_add_fusion.place_ref, f32[8,64,512]{2,1,0:T(8,128)S(1)} %all-to-all-done.1.t_ref, ...), custom_call_target="tpu_custom_call" | custom-call | flops 1610612736 | bytes 4194304 | tf_op jit(solution)/shard_map/pallas_call | solution.py:417
  109.6 2.4 %collective-permute-start.5 = (f32[8,72,512]{2,1,0:T(8,128)S(1)}, f32[8,72,512]{2,1,0:T(8,128)S(1)}, u32[]{:S(2)}, u32[]{:S(2)}) collective-permute-start(f32[8,72,512]{2,1,0:T(8,128)S(1)} %get-tuple-element.30), channel_id=1, source_target_pairs={{0,1},{1,0},{2,3},{3,2},{4,5},{5,4},{6,7},{7,6},{8,9},{9,8},{10,11... | collective-permute-start | bytes 3538952 | tf_op jit(solution)/shard_map/ppermute | solution.py:499
  112.0 2.5 %collective-permute-done.5 = f32[8,72,512]{2,1,0:T(8,128)S(1)} collective-permute-done((f32[8,72,512]{2,1,0:T(8,128)S(1)}, f32[8,72,512]{2,1,0:T(8,128)S(1)}, u32[]{:S(2)}, u32[]{:S(2)}) %collective-permute-start.5) | collective-permute-done | bytes 1179680 | tf_op jit(solution)/shard_map/ppermute | solution.py:499
  114.5 2.6 %add.66 = f32[8,72,512]{2,1,0:T(8,128)} add(f32[8,72,512]{2,1,0:T(8,128)} %get-tuple-element.29, f32[8,72,512]{2,1,0:T(8,128)S(1)} %collective-permute-done.5) | non-fusion elementwise | flops 294912 | bytes 3538944 | tf_op jit(solution)/shard_map/add | solution.py:547
  117.1 3.5 %all-to-all-start.3 = ((f32[4,2,72,512]{3,2,1,0:T(8,128)}), f32[4,2,72,512]{3,2,1,0:T(8,128)S(1)}, u32[]{:S(2)}, u32[]{:S(2)}) async-start(f32[4,2,72,512]{3,2,1,0:T(8,128)} %bitcast.16), calls=%async_computation.3 | async-start | bytes 2359296 | tf_op jit(solution)/shard_map/all_to_all | solution.py:495
  120.6 1.5 collective-permute-start.7
  122.1 2.6 %collective-permute-start.8 = (f32[2,128,128]{2,1,0:T(8,128)S(1)}, f32[2,128,128]{2,1,0:T(8,128)S(1)}, u32[]{:S(2)}, u32[]{:S(2)}) collective-permute-start(f32[2,128,128]{2,1,0:T(8,128)S(1)} %get-tuple-element.36), channel_id=1, source_target_pairs={{0,32},{16,48},{32,0},{48,16},{64,96},{80,112},{96,64},{112,80},{1... | collective-permute-start | bytes 393224 | tf_op jit(solution)/shard_map/ppermute | solution.py:509
  124.7 1.0 collective-permute-start.9
  125.7 1.2 collective-permute-done.7
  126.9 3.8 %collective-permute-done.8 = f32[2,128,128]{2,1,0:T(8,128)S(1)} collective-permute-done((f32[2,128,128]{2,1,0:T(8,128)S(1)}, f32[2,128,128]{2,1,0:T(8,128)S(1)}, u32[]{:S(2)}, u32[]{:S(2)}) %collective-permute-start.8) | collective-permute-done | bytes 131104 | tf_op jit(solution)/shard_map/ppermute | solution.py:509
  130.8 0.7 collective-permute-start.10
  131.4 5.4 %all-to-all-done.3.x_ref = f32[4,2,72,512]{3,2,1,0:T(8,128)S(1)} async-done(((f32[4,2,72,512]{3,2,1,0:T(8,128)}), f32[4,2,72,512]{3,2,1,0:T(8,128)S(1)}, u32[]{:S(2)}, u32[]{:S(2)}) %all-to-all-start.3) | async-done | bytes 1179680 | tf_op jit(solution)/shard_map/all_to_all | solution.py:495
  136.8 0.6 halves.1
  137.4 2.5 %collective-permute-start.6 = (f32[72,512]{1,0:T(8,128)S(1)}, f32[72,512]{1,0:T(8,128)S(1)}, u32[]{:S(2)}, u32[]{:S(2)}) collective-permute-start(f32[72,512]{1,0:T(8,128)S(1)} %get-tuple-element.32), channel_id=1, source_target_pairs={{0,2},{1,3},{2,0},{3,1},{4,6},{5,7},{6,4},{7,5},{8,10},{9,11},{10,... | collective-permute-start | bytes 442376 | tf_op jit(solution)/shard_map/ppermute | solution.py:499
  139.9 3.0 %collective-permute-start.13 = (f32[2,128,128]{2,1,0:T(8,128)S(1)}, f32[2,128,128]{2,1,0:T(8,128)S(1)}, u32[]{:S(2)}, u32[]{:S(2)}) collective-permute-start(f32[2,128,128]{2,1,0:T(8,128)S(1)} %add.70.refs_0_), channel_id=1, source_target_pairs={{0,48},{16,0},{32,16},{48,32},{64,112},{80,64},{96,80},{112,96},{1... | collective-permute-start | bytes 393224 | tf_op jit(solution)/shard_map/ppermute | solution.py:509
  143.2 0.6 collective-permute-start.11
  143.8 1.7 %collective-permute-done.13.refs_3_ = f32[2,128,128]{2,1,0:T(8,128)S(1)} collective-permute-done((f32[2,128,128]{2,1,0:T(8,128)S(1)}, f32[2,128,128]{2,1,0:T(8,128)S(1)}, u32[]{:S(2)}, u32[]{:S(2)}) %collective-permute-start.13) | collective-permute-done | bytes 131104 | tf_op jit(solution)/shard_map/ppermute | solution.py:509
  145.5 2.8 %collective-permute-done.12.refs_2_ = f32[2,128,128]{2,1,0:T(8,128)S(1)} collective-permute-done((f32[2,128,128]{2,1,0:T(8,128)S(1)}, f32[2,128,128]{2,1,0:T(8,128)S(1)}, u32[]{:S(2)}, u32[]{:S(2)}) %collective-permute-start.12) | collective-permute-done | bytes 131104 | tf_op jit(solution)/shard_map/ppermute | solution.py:509
  148.3 3.3 %collective-permute-done.11.refs_1_ = f32[2,128,128]{2,1,0:T(8,128)S(1)} collective-permute-done((f32[2,128,128]{2,1,0:T(8,128)S(1)}, f32[2,128,128]{2,1,0:T(8,128)S(1)}, u32[]{:S(2)}, u32[]{:S(2)}) %collective-permute-start.11) | collective-permute-done | bytes 131104 | tf_op jit(solution)/shard_map/ppermute | solution.py:509
  151.7 1.4 join.1
  153.1 0.7 end.1
  (41 shorter events, 0.6 us)
Async XLA Ops:
  0.6 27.2 %copy-start.13 = (s32[512]{0:T(512)S(1)}, s32[512]{0:T(512)}, u32[]{:S(2)}) copy-start(s32[512]{0:T(512)} %param.14) | copy-start | bytes 6148
  0.6 27.2 %copy-start.14 = (s32[512]{0:T(512)S(1)}, s32[512]{0:T(512)}, u32[]{:S(2)}) copy-start(s32[512]{0:T(512)} %param.15) | copy-start | bytes 6148
  19.3 19.8 %copy-start.1 = (bf16[2,512,256]{2,1,0:T(8,128)(2,1)S(1)}, bf16[2,512,256]{2,1,0:T(8,128)(2,1)}, u32[]{:S(2)}) copy-start(bf16[2,512,256]{2,1,0:T(8,128)(2,1)} %get-tuple-element.22.sel_ref) | copy-start | bytes 1572868
  19.3 19.8 %all-to-all-start = ((f32[16,16,512]{2,1,0:T(8,128)}), f32[16,16,512]{2,1,0:T(8,128)S(1)}, u32[]{:S(2)}, u32[]{:S(2)}) async-start(f32[16,16,512]{2,1,0:T(8,128)} %get-tuple-element.24), calls=%async_computation | async-start | bytes 1048576 | tf_op jit(solution)/shard_map/all_to_all | solution.py:495
  39.1 0.9 copy-start.6
  46.7 5.3 %copy-start.4 = (bf16[1024,128]{1,0:T(8,128)(2,1)S(1)}, bf16[1024,128]{1,0:T(8,128)(2,1)}, u32[]{:S(2)}) copy-start(bf16[1024,128]{1,0:T(8,128)(2,1)} %k_ref.3) | copy-start | bytes 786436
  46.7 19.9 %all-to-all-start.2 = ((f32[8,64,512]{2,1,0:T(8,128)}), f32[8,64,512]{2,1,0:T(8,128)S(1)}, u32[]{:S(2)}, u32[]{:S(2)}) async-start(f32[8,64,512]{2,1,0:T(8,128)} %shard_map.104), calls=%async_computation.2 | async-start | bytes 2097152 | tf_op jit(solution)/shard_map/all_to_all | solution.py:495
  53.5 6.4 %copy-start.7 = (f32[128,256]{1,0:T(8,128)S(1)}, f32[128,256]{1,0:T(8,128)}, u32[]{:S(2)}) copy-start(f32[128,256]{1,0:T(8,128)} %get-tuple-element.23.m_ref) | copy-start | bytes 393220
  58.4 13.8 %collective-permute-start = (f32[1,64]{1,0:T(1,128)}, f32[1,64]{1,0:T(1,128)S(1)}, u32[]{:S(2)}, u32[]{:S(2)}) collective-permute-start(f32[1,64]{1,0:T(1,128)} %get-tuple-element.26), channel_id=1, source_target_pairs={{0,1},{1,0},{2,3},{3,2},{4,5},{5,4},{6,7},{7,6},{8,9},{9,8},{10,11... | collective-permute-start | bytes 776 | tf_op jit(solution)/shard_map/ppermute | solution.py:499
  66.5 5.6 %copy-start.15 = (f32[1,64]{1,0:T(1,128)S(1)}, f32[1,64]{1,0:T(1,128)}, u32[]{:S(2)}) copy-start(f32[1,64]{1,0:T(1,128)} %get-tuple-element.26) | copy-start | bytes 772
  66.6 20.8 %copy-start.12 = (f32[64,64]{1,0:T(8,128)S(1)}, f32[64,64]{1,0:T(8,128)}, u32[]{:S(2)}) copy-start(f32[64,64]{1,0:T(8,128)} %w_ref.1) | copy-start | bytes 49156
  66.6 23.7 %copy-start.5 = (bf16[1024,128]{0,1:T(8,128)(2,1)S(1)}, bf16[1024,128]{0,1:T(8,128)(2,1)}, u32[]{:S(2)}) copy-start(bf16[1024,128]{0,1:T(8,128)(2,1)} %copy.12) | copy-start | bytes 786436
  66.6 23.7 %copy-start.8 = (f32[64,1024]{1,0:T(8,128)S(1)}, f32[64,1024]{1,0:T(8,128)}, u32[]{:S(2)}) copy-start(f32[64,1024]{1,0:T(8,128)} %get-tuple-element.25.s_ref) | copy-start | bytes 786436
  66.6 23.7 %copy-start.11 = (f32[64]{0:T(128)S(1)}, f32[64]{0:T(128)}, u32[]{:S(2)}) copy-start(f32[64]{0:T(128)} %param.13) | copy-start | bytes 772
  66.6 32.7 %all-to-all-start.1 = ((f32[8,64,512]{2,1,0:T(8,128)}), f32[8,64,512]{2,1,0:T(8,128)S(1)}, u32[]{:S(2)}, u32[]{:S(2)}) async-start(f32[8,64,512]{2,1,0:T(8,128)} %shard_map.103), calls=%async_computation.1 | async-start | bytes 2097152 | tf_op jit(solution)/shard_map/all_to_all | solution.py:495
  72.2 12.8 %collective-permute-start.1 = (f32[1,64]{1,0:T(1,128)S(1)}, f32[1,64]{1,0:T(1,128)S(1)}, u32[]{:S(2)}, u32[]{:S(2)}) collective-permute-start(f32[1,64]{1,0:T(1,128)S(1)} %multiply_add_fusion.2), channel_id=1, source_target_pairs={{0,2},{1,3},{2,0},{3,1},{4,6},{5,7},{6,4},{7,5},{8,10},{9,11},{10,... | collective-permute-start | bytes 776 | tf_op jit(solution)/shard_map/ppermute | solution.py:499
  85.0 2.7 %collective-permute-start.4 = (f32[1,64]{1,0:T(1,128)S(1)}, f32[1,64]{1,0:T(1,128)S(1)}, u32[]{:S(2)}, u32[]{:S(2)}) collective-permute-start(f32[1,64]{1,0:T(1,128)S(1)} %multiply_add_fusion.1), channel_id=1, source_target_pairs={{0,12},{1,13},{2,14},{3,15},{4,0},{5,1},{6,2},{7,3},{8,4},{9,5},{1... | collective-permute-start | bytes 776 | tf_op jit(solution)/shard_map/ppermute | solution.py:531
  85.8 3.9 %collective-permute-start.3 = (f32[1,64]{1,0:T(1,128)S(1)}, f32[1,64]{1,0:T(1,128)S(1)}, u32[]{:S(2)}, u32[]{:S(2)}) collective-permute-start(f32[1,64]{1,0:T(1,128)S(1)} %multiply_add_fusion.1), channel_id=1, source_target_pairs={{0,8},{1,9},{2,10},{3,11},{4,12},{5,13},{6,14},{7,15},{8,0},{9,1},... | collective-permute-start | bytes 776 | tf_op jit(solution)/shard_map/ppermute | solution.py:531
  86.6 3.6 %collective-permute-start.2 = (f32[1,64]{1,0:T(1,128)S(1)}, f32[1,64]{1,0:T(1,128)S(1)}, u32[]{:S(2)}, u32[]{:S(2)}) collective-permute-start(f32[1,64]{1,0:T(1,128)S(1)} %multiply_add_fusion.1), channel_id=1, source_target_pairs={{0,4},{1,5},{2,6},{3,7},{4,8},{5,9},{6,10},{7,11},{8,12},{9,13},{1... | collective-permute-start | bytes 776 | tf_op jit(solution)/shard_map/ppermute | solution.py:531
  90.3 1.2 copy-start.2
  97.2 1.4 copy-start
  98.6 0.7 copy-start.9
  99.3 1.2 copy-start.3
  100.5 0.9 copy-start.10
  109.6 4.9 %collective-permute-start.5 = (f32[8,72,512]{2,1,0:T(8,128)S(1)}, f32[8,72,512]{2,1,0:T(8,128)S(1)}, u32[]{:S(2)}, u32[]{:S(2)}) collective-permute-start(f32[8,72,512]{2,1,0:T(8,128)S(1)} %get-tuple-element.30), channel_id=1, source_target_pairs={{0,1},{1,0},{2,3},{3,2},{4,5},{5,4},{6,7},{7,6},{8,9},{9,8},{10,11... | collective-permute-start | bytes 3538952 | tf_op jit(solution)/shard_map/ppermute | solution.py:499
  117.1 19.7 %all-to-all-start.3 = ((f32[4,2,72,512]{3,2,1,0:T(8,128)}), f32[4,2,72,512]{3,2,1,0:T(8,128)S(1)}, u32[]{:S(2)}, u32[]{:S(2)}) async-start(f32[4,2,72,512]{3,2,1,0:T(8,128)} %bitcast.16), calls=%async_computation.3 | async-start | bytes 2359296 | tf_op jit(solution)/shard_map/all_to_all | solution.py:495
  120.6 6.3 %collective-permute-start.7 = (f32[2,128,128]{2,1,0:T(8,128)S(1)}, f32[2,128,128]{2,1,0:T(8,128)S(1)}, u32[]{:S(2)}, u32[]{:S(2)}) collective-permute-start(f32[2,128,128]{2,1,0:T(8,128)S(1)} %get-tuple-element.35), channel_id=1, source_target_pairs={{0,16},{16,32},{32,48},{48,0},{64,80},{80,96},{96,112},{112,64},{1... | collective-permute-start | bytes 393224 | tf_op jit(solution)/shard_map/ppermute | solution.py:509
  122.1 8.6 %collective-permute-start.8 = (f32[2,128,128]{2,1,0:T(8,128)S(1)}, f32[2,128,128]{2,1,0:T(8,128)S(1)}, u32[]{:S(2)}, u32[]{:S(2)}) collective-permute-start(f32[2,128,128]{2,1,0:T(8,128)S(1)} %get-tuple-element.36), channel_id=1, source_target_pairs={{0,32},{16,48},{32,0},{48,16},{64,96},{80,112},{96,64},{112,80},{1... | collective-permute-start | bytes 393224 | tf_op jit(solution)/shard_map/ppermute | solution.py:509
  124.7 6.0 %collective-permute-start.9 = (f32[2,128,128]{2,1,0:T(8,128)S(1)}, f32[2,128,128]{2,1,0:T(8,128)S(1)}, u32[]{:S(2)}, u32[]{:S(2)}) collective-permute-start(f32[2,128,128]{2,1,0:T(8,128)S(1)} %get-tuple-element.37), channel_id=1, source_target_pairs={{0,48},{16,0},{32,16},{48,32},{64,112},{80,64},{96,80},{112,96},{1... | collective-permute-start | bytes 393224 | tf_op jit(solution)/shard_map/ppermute | solution.py:509
  130.8 9.1 %collective-permute-start.10 = (f32[2,128,128]{2,1,0:T(8,128)S(1)}, f32[2,128,128]{2,1,0:T(8,128)S(1)}, u32[]{:S(2)}, u32[]{:S(2)}) collective-permute-start(f32[2,128,128]{2,1,0:T(8,128)S(1)} %add_add_fusion), channel_id=1, source_target_pairs={{0,64},{16,80},{32,96},{48,112},{64,0},{80,16},{96,32},{112,48},{1... | collective-permute-start | bytes 393224 | tf_op jit(solution)/shard_map/ppermute | solution.py:499
  137.4 15.7 %collective-permute-start.6 = (f32[72,512]{1,0:T(8,128)S(1)}, f32[72,512]{1,0:T(8,128)S(1)}, u32[]{:S(2)}, u32[]{:S(2)}) collective-permute-start(f32[72,512]{1,0:T(8,128)S(1)} %get-tuple-element.32), channel_id=1, source_target_pairs={{0,2},{1,3},{2,0},{3,1},{4,6},{5,7},{6,4},{7,5},{8,10},{9,11},{10,... | collective-permute-start | bytes 442376 | tf_op jit(solution)/shard_map/ppermute | solution.py:499
  139.9 5.6 %collective-permute-start.13 = (f32[2,128,128]{2,1,0:T(8,128)S(1)}, f32[2,128,128]{2,1,0:T(8,128)S(1)}, u32[]{:S(2)}, u32[]{:S(2)}) collective-permute-start(f32[2,128,128]{2,1,0:T(8,128)S(1)} %add.70.refs_0_), channel_id=1, source_target_pairs={{0,48},{16,0},{32,16},{48,32},{64,112},{80,64},{96,80},{112,96},{1... | collective-permute-start | bytes 393224 | tf_op jit(solution)/shard_map/ppermute | solution.py:509
  142.9 5.4 %collective-permute-start.12 = (f32[2,128,128]{2,1,0:T(8,128)S(1)}, f32[2,128,128]{2,1,0:T(8,128)S(1)}, u32[]{:S(2)}, u32[]{:S(2)}) collective-permute-start(f32[2,128,128]{2,1,0:T(8,128)S(1)} %add.70.refs_0_), channel_id=1, source_target_pairs={{0,32},{16,48},{32,0},{48,16},{64,96},{80,112},{96,64},{112,80},{1... | collective-permute-start | bytes 393224 | tf_op jit(solution)/shard_map/ppermute | solution.py:509
  143.2 8.5 %collective-permute-start.11 = (f32[2,128,128]{2,1,0:T(8,128)S(1)}, f32[2,128,128]{2,1,0:T(8,128)S(1)}, u32[]{:S(2)}, u32[]{:S(2)}) collective-permute-start(f32[2,128,128]{2,1,0:T(8,128)S(1)} %add.70.refs_0_), channel_id=1, source_target_pairs={{0,16},{16,32},{32,48},{48,0},{64,80},{80,96},{96,112},{112,64},{1... | collective-permute-start | bytes 393224 | tf_op jit(solution)/shard_map/ppermute | solution.py:509
